TPU v7x, 512 devices: a whole 4x8x8 slice. The times are simulated.
512 devices in a mesh: front: 2 (over core), row: 32 (over y, x), col: 8 (over z).
Axes of the slice: x: 4, y: 8, z: 8, core: 2. Of those that a mesh axis runs over, the one named last changes fastest.
Arguments:
- window: bfloat16 [2, 32768, 4096], P('front', 'row', 'col'), may hold values from -4 to 7.3, as said below
- children: bfloat16 [32768, 128, 128], P(('front', 'row', 'col')), may hold values from -4 to 4
- routes: int32 [32768, 1], P(('front', 'row', 'col')), may hold values from 0 to 63; in each aligned block of 64 rows (0 to 63, 64 to 127, ...) at most 2 rows name the same one
- slots: int32 [32768], P(('front', 'row', 'col')), may hold values from 0 to 15
- pattern: int32 [2, 64, 8], P('front', 'row', 'col'), may hold values 0 or 1
Outputs:
- factored: bfloat16 [2, 32768, 4096], P('front', 'row', 'col')
Inputs may be any that keep to these rules, and one draw needn't show every extreme that they name: `routes`: among the rows of one device (aligned blocks of 64 rows) no owner group is named by more than 2 rows, a bound that some block reaches. `slots`: child blocks land only below the first tile row of each owner's part. `window`: each front's rows and columns [0, 512) hold a symmetric positive definite tile.
All inputs are finite; a program needn't handle non-finite values. No bound on the sum of `pattern` on one device may be relied on, other than what follows from the above.
Results may differ from a plain program's by a relative error of at most 0.0056.
Values may be sent and summed in bfloat16 or wider, within the bound.
No kernel may reach another device: no remote copies, remote signals or barrier semaphores. Data moves between devices by JAX's collectives and lax.ppermute only.
A program may use at most 64 MiB of HBM per device.

v0:
```python
import jax
import jax.numpy as jnp
from jax import lax
from jax.sharding import PartitionSpec as P

TILE = 512
SB = 128
CAP = 2


def broadcast(block, axis, holder):
    block = jnp.where(lax.axis_index(axis) == holder, block, jnp.zeros_like(block))
    return lax.psum(block, axis)


def shards(window, children, routes, slots, pattern):
    tile = TILE
    sub = SB
    side = tile // sub
    rows_local = window.shape[1]
    tiles_local = rows_local // tile
    fronts = lax.axis_size("front")
    rows_axis = lax.axis_size("row")
    groups = fronts * rows_axis
    count = children.shape[0]
    buffer_rows = groups * CAP
    target = routes[:, 0]
    labels_grid = lax.broadcasted_iota(jnp.int32, (count, groups), 1)
    hits = (target[:, None] == labels_grid).astype(jnp.int32)
    before = jnp.cumsum(hits, axis=0) - hits
    place = target * CAP + jnp.sum(before * hits, axis=1)
    select = (lax.broadcasted_iota(jnp.int32, (buffer_rows, count), 0) == place[None, :]).astype(
        jnp.bfloat16
    )
    flat = children.reshape(count, sub * sub)
    outgoing = jnp.dot(select, flat, preferred_element_type=jnp.float32).astype(jnp.bfloat16)
    marks = (slots + 1).astype(jnp.bfloat16)
    tagged = jnp.dot(select, marks, preferred_element_type=jnp.float32).astype(jnp.bfloat16)
    incoming, tags = (
        lax.all_to_all(outgoing, ("front", "row"), split_axis=0, concat_axis=0, tiled=True),
        lax.all_to_all(tagged, ("front", "row"), split_axis=0, concat_axis=0, tiled=True),
    )
    slot_count = (tiles_local - 1) * side * side
    slot_marks = (lax.broadcasted_iota(jnp.int32, (slot_count,), 0) + 1).astype(jnp.bfloat16)
    match = (tags[None, :] == slot_marks[:, None]).astype(jnp.bfloat16)
    added = jnp.dot(match, incoming, preferred_element_type=jnp.float32)
    added = (
        added.reshape(tiles_local - 1, side, side, sub, sub)
        .transpose(0, 1, 3, 2, 4)
        .reshape((tiles_local - 1) * tile, tile)
    )
    base = window[0].astype(jnp.float32)
    assembled = jnp.concatenate([base[:tile], base[tile:] + added], axis=0)
    source = broadcast(assembled, "col", 0)
    pivot = broadcast(source[:tile].astype(jnp.bfloat16), "row", 0).astype(jnp.float32)
    factor = jnp.linalg.cholesky(pivot)
    lower = jax.scipy.linalg.solve_triangular(factor, source.T, lower=True).T.astype(jnp.bfloat16)
    column = lax.axis_index("col")
    owner = column // tiles_local
    within = column % tiles_local
    piece = lax.dynamic_slice_in_dim(lower, within * tile, tile, 0)
    partner = broadcast(piece, "row", owner)
    product = lax.dot_general(
        lower, partner, (((1,), (1,)), ((), ())), preferred_element_type=jnp.float32
    )
    live = jnp.repeat(pattern[0, :, 0].astype(jnp.float32), tile)[:, None]
    updated = (assembled - live * product).astype(jnp.bfloat16)
    result = jnp.where(column == 0, lower, updated)
    return result[None]


def solution(mesh):
    placed = (
        P("front", "row", "col"),
        P(("front", "row", "col"), None, None),
        P(("front", "row", "col"), None),
        P(("front", "row", "col")),
        P("front", "row", "col"),
    )
    return jax.shard_map(
        shards, mesh=mesh, in_specs=placed, out_specs=P("front", "row", "col"), check_vma=False
    )
```

profile of v0, /device:TPU:64, one launch (start us, length us, event | category | flops | bytes accessed | tf_op | source)
XLA Modules:
  0.0 729.8 jit_solution(7414971362005157550)
XLA Ops:
  10.5 10.6 %all-to-all-start = ((bf16[64,2,1]{1,2,0:T(2,128)(2,1)}), bf16[64,2,1]{1,2,0:T(2,128)(2,1)S(1)}, u32[]{:S(2)}, u32[]{:S(2)}) async-start(bf16[64,2,1]{1,2,0:T(2,128)(2,1)} %all_to_all.19), calls=%async_computation | async-start | bytes 65536 | tf_op jit(solution)/shard_map/all_to_all | solution.py:41
  21.0 5.3 convolution_convert_fusion
  26.3 7.6 %all_to_all.16 = bf16[64,2,16384]{2,1,0:T(2,128)(2,1)} reshape(bf16[128,16384]{1,0:T(8,128)(2,1)} %convolution_convert_fusion) | data formatting | bytes 8388608 | tf_op jit(solution)/shard_map/all_to_all | solution.py:40
  33.9 10.6 %all-to-all-start.1 = ((bf16[64,2,16384]{2,1,0:T(2,128)(2,1)}), bf16[64,2,16384]{2,1,0:T(2,128)(2,1)}, u32[]{:S(2)}, u32[]{:S(2)}) async-start(bf16[64,2,16384]{2,1,0:T(2,128)(2,1)} %all_to_all.16), calls=%async_computation.1 | async-start | bytes 8388608 | tf_op jit(solution)/shard_map/all_to_all | solution.py:40
  46.2 92.9 %all-to-all-done.1 = bf16[64,2,16384]{2,1,0:T(2,128)(2,1)} async-done(((bf16[64,2,16384]{2,1,0:T(2,128)(2,1)}), bf16[64,2,16384]{2,1,0:T(2,128)(2,1)}, u32[]{:S(2)}, u32[]{:S(2)}) %all-to-all-start.1) | async-done | bytes 4194336 | tf_op jit(solution)/shard_map/all_to_all | solution.py:40
  139.1 7.2 all_to_all.18
  146.3 6.4 copy.21
  152.6 3.4 fusion.40
  157.3 1.5 fusion.2
  158.9 89.5 %all-reduce.5.cloned.1.call-done = f32[1024,512]{1,0:T(8,128)} async-done(((f32[1024,512]{1,0:T(8,128)}), f32[1024,512]{1,0:T(8,128)}) %all-reduce.5.cloned.1.call-update) | async-done | bytes 2097168 | tf_op jit(solution)/shard_map/psum | solution.py:13
  248.4 1.3 slice.154
  251.1 158.4 %all-reduce.7.cloned.1.call-done = bf16[512,512]{0,1:T(8,128)(2,1)} async-done(((bf16[512,512]{0,1:T(8,128)(2,1)}), bf16[512,512]{0,1:T(8,128)(2,1)}) %all-reduce.7.cloned.1.call-update) | async-done | bytes 524304 | tf_op jit(solution)/shard_map/psum | solution.py:13
  412.0 11.7 %cholesky.104 = f32[128,128]{1,0:T(8,128)S(1)} custom-call(f32[128,128]{1,0:T(8,128)S(1)} %cholesky.266), custom_call_target="Cholesky" | custom-call | tf_op jit(solution)/shard_map/jit(cholesky)/cholesky | solution.py:56
  423.7 9.8 %custom-call.31 = f32[1,128,128]{1,2,0:T(8,128)S(1)} custom-call(f32[1,128,128]{2,1,0:T(8,128)S(1)} %get-tuple-element.32), custom_call_target="InvertDiagBlocksLowerTriangular" | custom-call | tf_op jit(solution)/shard_map/jit(cholesky)/cholesky | solution.py:56
  434.3 11.7 %cholesky.217 = f32[128,128]{1,0:T(8,128)S(1)} custom-call(f32[128,128]{1,0:T(8,128)S(1)} %cholesky.270), custom_call_target="Cholesky" | custom-call | tf_op jit(solution)/shard_map/jit(cholesky)/cholesky | solution.py:56
  446.1 10.0 %custom-call.32 = f32[1,128,128]{1,2,0:T(8,128)S(1)} custom-call(f32[1,128,128]{2,1,0:T(8,128)S(1)} %get-tuple-element.29), custom_call_target="InvertDiagBlocksLowerTriangular" | custom-call | tf_op jit(solution)/shard_map/jit(cholesky)/cholesky | solution.py:56
  456.7 11.7 %cholesky.238 = f32[128,128]{1,0:T(8,128)S(1)} custom-call(f32[128,128]{1,0:T(8,128)S(1)} %cholesky.275), custom_call_target="Cholesky" | custom-call | tf_op jit(solution)/shard_map/jit(cholesky)/cholesky | solution.py:56
  469.1 9.8 %custom-call.33 = f32[1,128,128]{1,2,0:T(8,128)S(1)} custom-call(f32[1,128,128]{2,1,0:T(8,128)S(1)} %get-tuple-element.26), custom_call_target="InvertDiagBlocksLowerTriangular" | custom-call | tf_op jit(solution)/shard_map/jit(cholesky)/cholesky | solution.py:56
  479.6 11.7 %cholesky.255 = f32[128,128]{1,0:T(8,128)S(1)} custom-call(f32[128,128]{1,0:T(8,128)S(1)} %convolution_subtract_fusion.4), custom_call_target="Cholesky" | custom-call | tf_op jit(solution)/shard_map/jit(cholesky)/cholesky | solution.py:56
  495.2 10.5 %while.1 = (s32[]{:T(128)}, f32[512,512]{1,0:T(8,128)S(1)}, s32[4,2]{0,1:T(2,128)S(1)}, f32[4,128,128]{2,1,0:T(8,128)}, s32[]{:T(128)}) while((s32[]{:T(128)}, f32[512,512]{1,0:T(8,128)S(1)}, s32[4,2]{0,1:T(2,128)S(1)}, f32[4,128,128]{2,1,0:T(8,128)}, s32[]{:T(128)}) %tuple.27), condition=%wide.while_cond, body=%wide.while_body.sunk | while | flops 2 | bytes 132705 | solution.py:57
  496.0 1.9 bitcast_dynamic-update-slice_fusion.2
  498.6 1.9 bitcast_dynamic-update-slice_fusion.2
  501.2 1.9 bitcast_dynamic-update-slice_fusion.2
  503.7 1.9 bitcast_dynamic-update-slice_fusion.2
  505.6 40.2 %custom-call.34 = f32[4,128,128]{1,2,0:T(8,128)S(1)} custom-call(f32[4,128,128]{2,1,0:T(8,128)} %get-tuple-element.12), custom_call_target="InvertDiagBlocksLowerTriangular" | custom-call | tf_op jit(solution)/shard_map/jit(_solve_triangular)/triangular_solve | solution.py:57
  545.8 1.8 fusion.19
  547.6 2.0 convolution_subtract_fusion.1
  550.3 2.9 convolution_subtract_fusion
  553.8 3.8 fusion.9
  559.6 1.5 convolution_convert_fusion.1
  563.9 155.6 %all-reduce.9.cloned.1.call-done = bf16[512,512]{1,0:T(8,128)(2,1)} async-done(((bf16[512,512]{1,0:T(8,128)(2,1)}), bf16[512,512]{1,0:T(8,128)(2,1)}) %all-reduce.9.cloned.1.call-update) | async-done | bytes 524304 | tf_op jit(solution)/shard_map/psum | solution.py:13
  719.6 3.3 fusion.13
  (76 shorter events, 23.3 us)
Async XLA Ops:
  10.5 23.5 %all-to-all-start = ((bf16[64,2,1]{1,2,0:T(2,128)(2,1)}), bf16[64,2,1]{1,2,0:T(2,128)(2,1)S(1)}, u32[]{:S(2)}, u32[]{:S(2)}) async-start(bf16[64,2,1]{1,2,0:T(2,128)(2,1)} %all_to_all.19), calls=%async_computation | async-start | bytes 65536 | tf_op jit(solution)/shard_map/all_to_all | solution.py:41
  33.9 10.6 %copy-start.3 = (bf16[1,1024,512]{2,1,0:T(8,128)(2,1)S(1)}, bf16[1,1024,512]{2,1,0:T(8,128)(2,1)}, u32[]{:S(2)}) copy-start(bf16[1,1024,512]{2,1,0:T(8,128)(2,1)} %param.5) | copy-start | bytes 3145732
  33.9 105.1 %all-to-all-start.1 = ((bf16[64,2,16384]{2,1,0:T(2,128)(2,1)}), bf16[64,2,16384]{2,1,0:T(2,128)(2,1)}, u32[]{:S(2)}, u32[]{:S(2)}) async-start(bf16[64,2,16384]{2,1,0:T(2,128)(2,1)} %all_to_all.16), calls=%async_computation.1 | async-start | bytes 8388608 | tf_op jit(solution)/shard_map/all_to_all | solution.py:40
  44.5 203.9 %all-reduce.5.cloned.1.call-start = ((), (), s32[]{:S(2)}) async-start(), calls=%async_computation.2 | async-start | bytes 4194304 | tf_op jit(solution)/shard_map/psum | solution.py:13
  156.1 1.2 copy-start
  158.9 250.6 %all-reduce.7.cloned.1.call-start = ((), (), s32[]{:S(2)}) async-start(), calls=%async_computation.3 | async-start | bytes 1048576 | tf_op jit(solution)/shard_map/psum | solution.py:13
  250.8 468.8 %all-reduce.9.cloned.1.call-start = ((), (), s32[]{:S(2)}) async-start(), calls=%async_computation.4 | async-start | bytes 1048576 | tf_op jit(solution)/shard_map/psum | solution.py:13
  505.6 44.7 %copy-start.2 = (f32[512,512]{1,0:T(8,128)}, f32[512,512]{1,0:T(8,128)S(1)}, u32[]{:S(2)}) copy-start(f32[512,512]{1,0:T(8,128)S(1)} %get-tuple-element.89) | copy-start | bytes 3145732
  545.8 7.4 %copy-start.5 = (f32[4,128,128]{1,2,0:T(8,128)}, f32[4,128,128]{1,2,0:T(8,128)S(1)}, u32[]{:S(2)}) copy-start(f32[4,128,128]{1,2,0:T(8,128)S(1)} %custom-call.34) | copy-start | bytes 786436
  559.6 4.3 copy-start.6
  559.6 160.0 %copy-start.1 = (f32[512,512]{1,0:T(8,128)S(1)}, f32[512,512]{1,0:T(8,128)}, u32[]{:S(2)}) copy-start(f32[512,512]{1,0:T(8,128)} %slice_bitcast_fusion.1) | copy-start | bytes 3145732
  561.1 0.7 copy-start.4
Sparse Core Ops, SparseCore 0:
  159.0 89.4 all-reduce.4
  251.8 157.6 all-reduce.6
  564.0 155.5 all-reduce.8
where the time goes:
time: 736 us; the launch traced here: 730 us
  waiting for transfers between devices  496 us (67%)
  other arithmetic  127 us (17%)
  local copies, waits for them, and re-layouts  40 us (5%)
  matrix products  27.9 us (4%)
  starting transfers between devices  21.4 us (3%)
  between operations  16.3 us (2%)
    psum x3, waiting for transfers between devices, broadcast(): return lax.psum(block, axis)  404 us
    all_to_all x1, waiting for transfers between devices, shards(): lax.all_to_all(outgoing, ('front', 'row'), split_axis=0, concat_axis=0, t...  92.9 us
    another operation x14, other arithmetic, shards(): factor = jnp.linalg.cholesky(pivot)  78.6 us
    another operation x4, other arithmetic, shards(): jax.scipy.linalg.solve_triangular(factor, source.T, lower=True)  41.4 us
    all_to_all x3, local copies, waits for them, and re-layouts, shards(): lax.all_to_all(outgoing, ('front', 'row'), split_axis=0, concat_axis=0, t...  21.2 us
  transfers between devices with their start and end apart: 5, of which 4 were waited for; matrix products, arithmetic and copies ran while one was open for 1% of the time, Pallas kernels for 0%

commit v1 on v0

v1 whole, which is shorter than its diff:
```python
import functools

import jax
import jax.numpy as jnp
from jax import lax
from jax.experimental import pallas as pl
from jax.experimental.pallas import tpu as pltpu
from jax.sharding import PartitionSpec as P

TILE = 512
SB = 128
CAP = 2
HI = lax.Precision.HIGHEST
F32 = jnp.float32
BF16 = jnp.bfloat16


def place_kernel(routes, slots, children, outgoing, tags, count, sem):
    n = children.shape[0]
    rows = tags.shape[0]

    def clear_tag(i, _):
        tags[i] = 0
        return 0

    lax.fori_loop(0, rows, clear_tag, 0)

    def clear_count(i, _):
        count[i] = 0
        return 0

    lax.fori_loop(0, count.shape[0], clear_count, 0)

    def send(k, _):
        g = routes[k]
        c = count[g]
        count[g] = c + 1
        at = g * CAP + c
        tags[at] = slots[k] + 1
        pltpu.make_async_copy(children.at[k], outgoing.at[at], sem).start()
        return 0

    lax.fori_loop(0, n, send, 0)
    pltpu.make_async_copy(children, outgoing.at[pl.ds(0, n)], sem).wait()


def place(routes, slots, children, groups):
    rows = groups * CAP
    smem = pl.BlockSpec(memory_space=pltpu.SMEM)
    return pl.pallas_call(
        place_kernel,
        out_shape=(
            jax.ShapeDtypeStruct((rows,) + children.shape[1:], children.dtype),
            jax.ShapeDtypeStruct((rows,), jnp.int32),
        ),
        in_specs=[smem, smem, pl.BlockSpec(memory_space=pl.ANY)],
        out_specs=(pl.BlockSpec(memory_space=pl.ANY), smem),
        scratch_shapes=[pltpu.SMEM((groups,), jnp.int32), pltpu.SemaphoreType.DMA],
        name="place",
    )(routes, slots, children)


def assemble_kernel(tags, incoming, base, out, acc):
    side = TILE // SB
    acc[...] = jnp.zeros_like(acc)

    def add(s, _):
        t = tags[s]

        @pl.when(t > 0)
        def _():
            acc[t - 1] = acc[t - 1] + incoming[s].astype(F32)

        return 0

    lax.fori_loop(0, incoming.shape[0], add, 0)
    for i in range(side):
        for j in range(side):
            rows, cols = slice(i * SB, (i + 1) * SB), slice(j * SB, (j + 1) * SB)
            out[rows, cols] = base[rows, cols].astype(F32) + acc[i * side + j]


def assemble(tags, incoming, base):
    vmem = pl.BlockSpec(memory_space=pltpu.VMEM)
    return pl.pallas_call(
        assemble_kernel,
        out_shape=jax.ShapeDtypeStruct((TILE, TILE), F32),
        in_specs=[pl.BlockSpec(memory_space=pltpu.SMEM), vmem, vmem],
        out_specs=vmem,
        scratch_shapes=[pltpu.VMEM(((TILE // SB) ** 2, SB, SB), F32)],
        compiler_params=pltpu.CompilerParams(vmem_limit_bytes=24 << 20),
        name="assemble",
    )(tags, incoming, base)


STEP = 4


def invert_block(block):
    n = block.shape[0]
    s = block
    row_at = lax.broadcasted_iota(jnp.int32, (n, n), 0)
    col_at = lax.broadcasted_iota(jnp.int32, (n, n), 1)
    w = jnp.where(row_at == col_at, 1.0, 0.0).astype(F32)
    done = []
    top = 0
    for j in range(0, n, STEP):
        local = j - top
        cols = [jnp.broadcast_to(s[:, j + a : j + a + 1], s.shape) for a in range(STEP)]
        r = [s[local + a : local + a + 1, :] for a in range(STEP)]
        v = [w[local + a : local + a + 1, :] for a in range(STEP)]
        p = [[cols[b][local + a : local + a + 1, :] for b in range(STEP)] for a in range(STEP)]
        inv = []
        m = [[None] * STEP for _ in range(STEP)]
        for b in range(STEP):
            inv.append(1.0 / p[b][b])
            for a in range(b + 1, STEP):
                m[a][b] = p[a][b] * inv[b]
                for c in range(b + 1, a + 1):
                    p[a][c] = p[a][c] - m[a][b] * p[c][b]
                r[a] = r[a] - m[a][b] * r[b]
                v[a] = v[a] - m[a][b] * v[b]
        done += [v[a] * lax.rsqrt(p[a][a]) for a in range(STEP)]
        if j + STEP >= n:
            break
        y = [None] * STEP
        z = [None] * STEP
        for a in reversed(range(STEP)):
            y[a] = r[a] * inv[a]
            z[a] = v[a] * inv[a]
            for b in range(a + 1, STEP):
                y[a] = y[a] - m[b][a] * y[b]
                z[a] = z[a] - m[b][a] * z[b]
        skip = (j + STEP) // 8 * 8 - top
        s, w = s[skip:], w[skip:]
        cols = [c[skip:] for c in cols]
        top += skip
        if top < j + STEP:
            keep = lax.broadcasted_iota(jnp.int32, s.shape, 0) >= j + STEP - top
            cols = [jnp.where(keep, c, 0.0) for c in cols]
        for a in range(STEP):
            s = s - cols[a] * y[a]
            w = w - cols[a] * z[a]
    return jnp.concatenate(done, axis=0)


def dot(a, b, dims):
    return lax.dot_general(a, b, (dims, ((), ())), precision=HI, preferred_element_type=F32)


def inverse_kernel(pivot, out, work, rest):
    n = pivot.shape[0]
    blocks = n // SB
    row_at = lax.broadcasted_iota(jnp.int32, (n, n), 0)
    col_at = lax.broadcasted_iota(jnp.int32, (n, n), 1)
    work[...] = pivot[...].astype(F32)
    rest[...] = jnp.where(row_at == col_at, 1.0, 0.0).astype(F32)

    def step(k, _):
        here = pl.ds(pl.multiple_of(k * SB, SB), SB)
        small = invert_block(work[here, here])
        panel = dot(work[:, here], small, ((1,), (1,)))
        below = lax.broadcasted_iota(jnp.int32, (n, SB), 0) >= (k + 1) * SB
        panel = jnp.where(below, panel, 0.0)
        work[...] = work[...] - dot(panel, panel, ((1,), (1,)))
        solved = dot(small, rest[here, :], ((1,), (0,)))
        out[here, :] = solved
        rest[...] = rest[...] - dot(panel, solved, ((1,), (0,)))
        return 0

    lax.fori_loop(0, blocks, step, 0)


def inverse_factor(pivot):
    n = pivot.shape[0]
    vmem = pl.BlockSpec(memory_space=pltpu.VMEM)
    return pl.pallas_call(
        inverse_kernel,
        out_shape=jax.ShapeDtypeStruct((n, n), F32),
        in_specs=[vmem],
        out_specs=vmem,
        scratch_shapes=[pltpu.VMEM((n, n), F32), pltpu.VMEM((n, n), F32)],
        compiler_params=pltpu.CompilerParams(vmem_limit_bytes=24 << 20),
        cost_estimate=pl.CostEstimate(flops=4 * n**3, bytes_accessed=6 * n * n, transcendentals=0),
        name="inverse",
    )(pivot)


def swap(block, axis):
    return lax.all_to_all(block, axis, split_axis=0, concat_axis=0, tiled=True)


def broadcast(block, axis, holder):
    parts = lax.axis_size(axis)
    rows, cols = block.shape
    got = swap(block.reshape(parts, rows // parts, cols), axis)
    mine = lax.dynamic_index_in_dim(got, holder, 0, keepdims=True)
    return swap(jnp.broadcast_to(mine, got.shape), axis).reshape(rows, cols)


def shards(window, children, routes, slots, pattern):
    groups = lax.axis_size("front") * lax.axis_size("row")
    column = lax.axis_index("col")
    first = window[0, :TILE]
    second = window[0, TILE:]
    pivot = broadcast(first, "row", 0)
    outgoing, marks = place(routes[:, 0], slots, children, groups)
    tags = swap(marks.reshape(groups, CAP), ("front", "row")).reshape(-1)
    incoming = swap(outgoing, ("front", "row"))
    inverse = inverse_factor(pivot)
    lower_first = lax.dot_general(
        first.astype(F32), inverse, (((1,), (1,)), ((), ())), precision=HI
    ).astype(BF16)
    added = assemble(tags, incoming, second)
    lower_second = lax.dot_general(
        added, inverse, (((1,), (1,)), ((), ())), precision=HI
    ).astype(BF16)
    lower_first = broadcast(lower_first, "col", 0)
    lower_second = broadcast(lower_second, "col", 0)
    owner = column // 2
    piece = jnp.where(column % 2 == 0, lower_first, lower_second)
    partner = broadcast(piece, "row", owner)

    def finish(lower, assembled, live):
        product = lax.dot_general(
            lower, partner, (((1,), (1,)), ((), ())), preferred_element_type=F32
        )
        updated = (assembled - live.astype(F32) * product).astype(BF16)
        return jnp.where(column == 0, lower, updated)

    return jnp.concatenate(
        [
            finish(lower_first, first.astype(F32), pattern[0, 0, 0]),
            finish(lower_second, added, pattern[0, 1, 0]),
        ],
        axis=0,
    )[None]


def solution(mesh):
    placed = (
        P("front", "row", "col"),
        P(("front", "row", "col"), None, None),
        P(("front", "row", "col"), None),
        P(("front", "row", "col")),
        P("front", "row", "col"),
    )
    return jax.shard_map(
        shards, mesh=mesh, in_specs=placed, out_specs=P("front", "row", "col"), check_vma=False
    )
```

time: 736 us -> 368 us (0.50)
  the two profiles are of different devices: /device:TPU:64 before, /device:TPU:8 now
where the time goes in v1:
time: 368 us; the launch traced here: 367 us
  waiting for transfers between devices  163 us (44%)
  Pallas kernels  104 us (28%)
  starting transfers between devices  60.5 us (16%)
  blocking collectives  21.7 us (6%)
  local copies, waits for them, and re-layouts  7.91 us (2%)
  matrix products  5.57 us (2%)
    all_to_all x9, waiting for transfers between devices, swap(): return lax.all_to_all(block, axis, split_axis=0, concat_axis=0, tiled=True)  163 us
    pallas_call x1, Pallas kernels, place(): pl.pallas_call(place_kernel, out_shape=(jax.ShapeDtypeStruct((rows,) + ch...  67 us
    all_to_all x9, starting transfers between devices, swap(): return lax.all_to_all(block, axis, split_axis=0, concat_axis=0, tiled=True)  60.5 us
    pallas_call x1, Pallas kernels, inverse_factor(): pl.pallas_call(inverse_kernel, out_shape=jax.ShapeDtypeStruct((n, n), F32...  32.1 us
    all_to_all x1, blocking collectives, swap(): return lax.all_to_all(block, axis, split_axis=0, concat_axis=0, tiled=True)  21.7 us
  transfers between devices with their start and end apart: 9, of which 8 were waited for; matrix products, arithmetic and copies ran while one was open for 2% of the time, Pallas kernels for 28%

profile of v1, /device:TPU:8, one launch (start us, length us, event | category | flops | bytes accessed | tf_op | source)
XLA Modules:
  0.0 366.6 jit_solution(2574305933559412608)
XLA Ops:
  0.0 2.1 fusion.8
  2.1 10.2 %all-to-all-start = ((bf16[32,16,512]{2,1,0:T(8,128)(2,1)}), bf16[32,16,512]{2,1,0:T(8,128)(2,1)S(1)}, u32[]{:S(2)}, u32[]{:S(2)}) async-start(bf16[32,16,512]{2,1,0:T(8,128)(2,1)} %bitcast.1), calls=%async_computation | async-start | bytes 1048576 | tf_op jit(solution)/shard_map/all_to_all | solution.py:190
  12.2 67.0 %place.1 = (bf16[128,128,128]{2,1,0:T(8,128)(2,1)}, s32[128]{0:T(128)}) custom-call(s32[64]{0:T(128)} %bitcast.40, s32[64]{0:T(128)} %slots.1, bf16[64,128,128]{2,1,0:T(8,128)(2,1)} %children.1), custom_call_target="tpu_custom_call" | custom-call | tf_op jit(solution)/shard_map/place/pallas_call | solution.py:50
  79.3 1.3 all_to_all.37
  80.6 10.2 %all-to-all-start.4 = ((s32[64,1,2]{2,1,0:T(1,128)}), s32[64,1,2]{2,1,0:T(1,128)S(1)}, u32[]{:S(2)}, u32[]{:S(2)}) async-start(s32[64,1,2]{2,1,0:T(1,128)} %bitcast.9), calls=%async_computation.4 | async-start | bytes 65536 | tf_op jit(solution)/shard_map/all_to_all | solution.py:190
  90.8 8.3 %all-to-all-done.4 = s32[64,1,2]{2,1,0:T(1,128)S(1)} async-done(((s32[64,1,2]{2,1,0:T(1,128)}), s32[64,1,2]{2,1,0:T(1,128)S(1)}, u32[]{:S(2)}, u32[]{:S(2)}) %all-to-all-start.4) | async-done | bytes 544 | tf_op jit(solution)/shard_map/all_to_all | solution.py:190
  99.2 21.7 %all_to_all.54 = bf16[32,16,512]{2,1,0:T(8,128)(2,1)S(1)} all-to-all(bf16[32,16,512]{2,1,0:T(8,128)(2,1)S(1)} %broadcast_in_dim.32), channel_id=1, replica_groups=mesh['front'=2,'row'=32,'col'=8] {'row'}, dimensions={0} | all-to-all | bytes 1048576 | tf_op jit(solution)/shard_map/all_to_all | solution.py:190
  120.9 5.9 %all-to-all-start.5 = ((bf16[128,128,128]{2,1,0:T(8,128)(2,1)}), bf16[128,128,128]{2,1,0:T(8,128)(2,1)}, u32[]{:S(2)}, u32[]{:S(2)}) async-start(bf16[128,128,128]{2,1,0:T(8,128)(2,1)} %get-tuple-element.8), calls=%async_computation.5 | async-start | bytes 8388608 | tf_op jit(solution)/shard_map/all_to_all | solution.py:190
  126.9 32.1 %inverse.1 = f32[512,512]{1,0:T(8,128)S(1)} custom-call(bf16[512,512]{1,0:T(8,128)(2,1)S(1)} %bitcast.35), custom_call_target="tpu_custom_call" | custom-call | flops 536870912 | bytes 1572864 | tf_op jit(solution)/shard_map/inverse/pallas_call | solution.py:177
  159.0 1.9 convolution_convert_fusion
  160.9 60.1 %all-to-all-done.5.incoming = bf16[128,128,128]{2,1,0:T(8,128)(2,1)} async-done(((bf16[128,128,128]{2,1,0:T(8,128)(2,1)}), bf16[128,128,128]{2,1,0:T(8,128)(2,1)}, u32[]{:S(2)}, u32[]{:S(2)}) %all-to-all-start.5) | async-done | bytes 4194336 | tf_op jit(solution)/shard_map/all_to_all | solution.py:190
  221.0 10.3 %all-to-all-start.2 = ((bf16[8,64,512]{2,1,0:T(8,128)(2,1)}), bf16[8,64,512]{2,1,0:T(8,128)(2,1)S(1)}, u32[]{:S(2)}, u32[]{:S(2)}) async-start(bf16[8,64,512]{2,1,0:T(8,128)(2,1)} %bitcast.4), calls=%async_computation.2 | async-start | bytes 1048576 | tf_op jit(solution)/shard_map/all_to_all | solution.py:190
  231.8 0.7 reduce.3
  232.7 4.4 %assemble.1 = f32[512,512]{1,0:T(8,128)S(1)} custom-call(s32[128]{0:T(128)S(1)} %reshape.36.tags, bf16[128,128,128]{2,1,0:T(8,128)(2,1)} %all-to-all-done.5.incoming, bf16[512,512]{1,0:T(8,128)(2,1)S(1)} %get-tuple-element.10.base), custom_call_target="tpu_custom_call" | custom-call | tf_op jit(solution)/shard_map/assemble/pallas_call | solution.py:85
  237.1 2.7 convolution_convert_fusion.1
  239.7 9.4 %all-to-all-done.2 = bf16[8,64,512]{2,1,0:T(8,128)(2,1)S(1)} async-done(((bf16[8,64,512]{2,1,0:T(8,128)(2,1)}), bf16[8,64,512]{2,1,0:T(8,128)(2,1)S(1)}, u32[]{:S(2)}, u32[]{:S(2)}) %all-to-all-start.2) | async-done | bytes 524320 | tf_op jit(solution)/shard_map/all_to_all | solution.py:190
  249.1 3.5 all-to-all-start.6
  252.6 17.9 %all-to-all-done.6 = bf16[8,64,512]{2,1,0:T(8,128)(2,1)S(1)} async-done(((bf16[8,64,512]{2,1,0:T(8,128)(2,1)}), bf16[8,64,512]{2,1,0:T(8,128)(2,1)S(1)}, u32[]{:S(2)}, u32[]{:S(2)}) %all-to-all-start.6) | async-done | bytes 524320 | tf_op jit(solution)/shard_map/all_to_all | solution.py:190
  270.4 0.8 broadcast_in_dim.34
  271.3 3.5 all-to-all-start.3
  274.8 17.9 %all-to-all-done.3 = bf16[8,64,512]{2,1,0:T(8,128)(2,1)S(1)} async-done(((bf16[8,64,512]{2,1,0:T(8,128)(2,1)}), bf16[8,64,512]{2,1,0:T(8,128)(2,1)S(1)}, u32[]{:S(2)}, u32[]{:S(2)}) %all-to-all-start.3) | async-done | bytes 524320 | tf_op jit(solution)/shard_map/all_to_all | solution.py:190
  292.7 0.9 broadcast_in_dim.36
  293.6 3.5 all-to-all-start.7
  297.1 17.8 %all-to-all-done.7 = bf16[8,64,512]{2,1,0:T(8,128)(2,1)S(1)} async-done(((bf16[8,64,512]{2,1,0:T(8,128)(2,1)}), bf16[8,64,512]{2,1,0:T(8,128)(2,1)S(1)}, u32[]{:S(2)}, u32[]{:S(2)}) %all-to-all-start.7) | async-done | bytes 524320 | tf_op jit(solution)/shard_map/all_to_all | solution.py:190
  314.9 0.8 broadcast_select_fusion
  315.8 8.3 %all-to-all-start.8 = ((bf16[32,16,512]{2,1,0:T(8,128)(2,1)}), bf16[32,16,512]{2,1,0:T(8,128)(2,1)S(1)}, u32[]{:S(2)}, u32[]{:S(2)}) async-start(bf16[32,16,512]{2,1,0:T(8,128)(2,1)} %bitcast.13), calls=%async_computation.8 | async-start | bytes 1048576 | tf_op jit(solution)/shard_map/all_to_all | solution.py:190
  324.1 17.4 %all-to-all-done.8 = bf16[32,16,512]{2,1,0:T(8,128)(2,1)S(1)} async-done(((bf16[32,16,512]{2,1,0:T(8,128)(2,1)}), bf16[32,16,512]{2,1,0:T(8,128)(2,1)S(1)}, u32[]{:S(2)}, u32[]{:S(2)}) %all-to-all-start.8) | async-done | bytes 524320 | tf_op jit(solution)/shard_map/all_to_all | solution.py:190
  341.4 0.9 broadcast_in_dim.38
  342.3 5.2 %all-to-all-start.9 = ((bf16[32,16,512]{2,1,0:T(8,128)(2,1)}), bf16[32,16,512]{2,1,0:T(8,128)(2,1)S(1)}, u32[]{:S(2)}, u32[]{:S(2)}) async-start(bf16[32,16,512]{2,1,0:T(8,128)(2,1)} %broadcast_in_dim.38), calls=%async_computation.9 | async-start | bytes 1048576 | tf_op jit(solution)/shard_map/all_to_all | solution.py:190
  347.5 0.6 fusion.9
  349.4 14.6 %all-to-all-done.9 = bf16[32,16,512]{2,1,0:T(8,128)(2,1)S(1)} async-done(((bf16[32,16,512]{2,1,0:T(8,128)(2,1)}), bf16[32,16,512]{2,1,0:T(8,128)(2,1)S(1)}, u32[]{:S(2)}, u32[]{:S(2)}) %all-to-all-start.9) | async-done | bytes 524320 | tf_op jit(solution)/shard_map/all_to_all | solution.py:190
  365.6 1.0 maximum_bitcast_fusion
  (20 shorter events, 2.3 us)
Async XLA Ops:
  2.1 78.6 %all-to-all-start = ((bf16[32,16,512]{2,1,0:T(8,128)(2,1)}), bf16[32,16,512]{2,1,0:T(8,128)(2,1)S(1)}, u32[]{:S(2)}, u32[]{:S(2)}) async-start(bf16[32,16,512]{2,1,0:T(8,128)(2,1)} %bitcast.1), calls=%async_computation | async-start | bytes 1048576 | tf_op jit(solution)/shard_map/all_to_all | solution.py:190
  80.6 18.5 %all-to-all-start.4 = ((s32[64,1,2]{2,1,0:T(1,128)}), s32[64,1,2]{2,1,0:T(1,128)S(1)}, u32[]{:S(2)}, u32[]{:S(2)}) async-start(s32[64,1,2]{2,1,0:T(1,128)} %bitcast.9), calls=%async_computation.4 | async-start | bytes 65536 | tf_op jit(solution)/shard_map/all_to_all | solution.py:190
  120.9 100.1 %all-to-all-start.5 = ((bf16[128,128,128]{2,1,0:T(8,128)(2,1)}), bf16[128,128,128]{2,1,0:T(8,128)(2,1)}, u32[]{:S(2)}, u32[]{:S(2)}) async-start(bf16[128,128,128]{2,1,0:T(8,128)(2,1)} %get-tuple-element.8), calls=%async_computation.5 | async-start | bytes 8388608 | tf_op jit(solution)/shard_map/all_to_all | solution.py:190
  126.8 32.2 %copy-start = (bf16[1,1024,512]{2,1,0:T(8,128)(2,1)S(1)}, bf16[1,1024,512]{2,1,0:T(8,128)(2,1)}, u32[]{:S(2)}) copy-start(bf16[1,1024,512]{2,1,0:T(8,128)(2,1)} %param.5) | copy-start | bytes 3145732
  221.0 28.1 %all-to-all-start.2 = ((bf16[8,64,512]{2,1,0:T(8,128)(2,1)}), bf16[8,64,512]{2,1,0:T(8,128)(2,1)S(1)}, u32[]{:S(2)}, u32[]{:S(2)}) async-start(bf16[8,64,512]{2,1,0:T(8,128)(2,1)} %bitcast.4), calls=%async_computation.2 | async-start | bytes 1048576 | tf_op jit(solution)/shard_map/all_to_all | solution.py:190
  249.1 21.4 %all-to-all-start.6 = ((bf16[8,64,512]{2,1,0:T(8,128)(2,1)}), bf16[8,64,512]{2,1,0:T(8,128)(2,1)S(1)}, u32[]{:S(2)}, u32[]{:S(2)}) async-start(bf16[8,64,512]{2,1,0:T(8,128)(2,1)} %bitcast.11), calls=%async_computation.6 | async-start | bytes 1048576 | tf_op jit(solution)/shard_map/all_to_all | solution.py:190
  271.3 21.4 %all-to-all-start.3 = ((bf16[8,64,512]{2,1,0:T(8,128)(2,1)}), bf16[8,64,512]{2,1,0:T(8,128)(2,1)S(1)}, u32[]{:S(2)}, u32[]{:S(2)}) async-start(bf16[8,64,512]{2,1,0:T(8,128)(2,1)} %broadcast_in_dim.34), calls=%async_computation.3 | async-start | bytes 1048576 | tf_op jit(solution)/shard_map/all_to_all | solution.py:190
  292.7 23.1 %copy-start.2 = (bf16[8,64,512]{2,1,0:T(8,128)(2,1)}, bf16[8,64,512]{2,1,0:T(8,128)(2,1)S(1)}, u32[]{:S(2)}) copy-start(bf16[8,64,512]{2,1,0:T(8,128)(2,1)S(1)} %all-to-all-done.3) | copy-start | bytes 1572868
  293.6 21.4 %all-to-all-start.7 = ((bf16[8,64,512]{2,1,0:T(8,128)(2,1)}), bf16[8,64,512]{2,1,0:T(8,128)(2,1)S(1)}, u32[]{:S(2)}, u32[]{:S(2)}) async-start(bf16[8,64,512]{2,1,0:T(8,128)(2,1)} %broadcast_in_dim.36), calls=%async_computation.7 | async-start | bytes 1048576 | tf_op jit(solution)/shard_map/all_to_all | solution.py:190
  297.1 50.4 %copy-start.4 = (s32[1,2,1]{1,2,0:T(1,128)S(1)}, s32[1,2,1]{1,2,0:T(1,128)}, u32[]{:S(2)}) copy-start(s32[1,2,1]{1,2,0:T(1,128)} %param.9) | copy-start | bytes 28
  315.8 25.7 %all-to-all-start.8 = ((bf16[32,16,512]{2,1,0:T(8,128)(2,1)}), bf16[32,16,512]{2,1,0:T(8,128)(2,1)S(1)}, u32[]{:S(2)}, u32[]{:S(2)}) async-start(bf16[32,16,512]{2,1,0:T(8,128)(2,1)} %bitcast.13), calls=%async_computation.8 | async-start | bytes 1048576 | tf_op jit(solution)/shard_map/all_to_all | solution.py:190
  341.4 23.0 %copy-start.1 = (bf16[1,1024,512]{2,1,0:T(8,128)(2,1)S(1)}, bf16[1,1024,512]{2,1,0:T(8,128)(2,1)}, u32[]{:S(2)}) copy-start(bf16[1,1024,512]{2,1,0:T(8,128)(2,1)} %param.5) | copy-start | bytes 3145732
  342.3 21.7 %all-to-all-start.9 = ((bf16[32,16,512]{2,1,0:T(8,128)(2,1)}), bf16[32,16,512]{2,1,0:T(8,128)(2,1)S(1)}, u32[]{:S(2)}, u32[]{:S(2)}) async-start(bf16[32,16,512]{2,1,0:T(8,128)(2,1)} %broadcast_in_dim.38), calls=%async_computation.9 | async-start | bytes 1048576 | tf_op jit(solution)/shard_map/all_to_all | solution.py:190
  364.0 1.0 copy-start.3

commit v2 on v1

--- a/solution.py
+++ b/solution.py
@@ -53,7 +53,7 @@
             jax.ShapeDtypeStruct((rows,) + children.shape[1:], children.dtype),
             jax.ShapeDtypeStruct((rows,), jnp.int32),
         ),
-        in_specs=[smem, smem, pl.BlockSpec(memory_space=pl.ANY)],
+        in_specs=[smem, smem, pl.BlockSpec(memory_space=pltpu.VMEM)],
         out_specs=(pl.BlockSpec(memory_space=pl.ANY), smem),
         scratch_shapes=[pltpu.SMEM((groups,), jnp.int32), pltpu.SemaphoreType.DMA],
         name="place",
@@ -158,7 +158,9 @@
 
     def step(k, _):
         here = pl.ds(pl.multiple_of(k * SB, SB), SB)
-        small = invert_block(work[here, here])
+        block = work[here, here]
+        at = [lax.broadcasted_iota(jnp.int32, block.shape, d) for d in (0, 1)]
+        small = invert_block(jnp.where(at[0] >= at[1], block, block.T))
         panel = dot(work[:, here], small, ((1,), (1,)))
         below = lax.broadcasted_iota(jnp.int32, (n, SB), 0) >= (k + 1) * SB
         panel = jnp.where(below, panel, 0.0)
@@ -190,51 +192,129 @@
     return lax.all_to_all(block, axis, split_axis=0, concat_axis=0, tiled=True)
 
 
-def broadcast(block, axis, holder):
-    parts = lax.axis_size(axis)
-    rows, cols = block.shape
-    got = swap(block.reshape(parts, rows // parts, cols), axis)
-    mine = lax.dynamic_index_in_dim(got, holder, 0, keepdims=True)
-    return swap(jnp.broadcast_to(mine, got.shape), axis).reshape(rows, cols)
+def circulate(part, axis):
+    size = lax.axis_size(axis)
+    parts = [part]
+    for t in range(1, size):
+        parts.append(lax.ppermute(part, axis, [(i, (i - t) % size) for i in range(size)]))
+    return parts
+
+
+def finish_kernel(size, state, *refs):
+    parts = refs[:size]
+    partner, base, added, out = refs[size:]
+    column = state[0]
+    rows = parts[0].shape[0] // 2
+    for t in range(size):
+        source = lax.rem(column + t, size)
+        at = pl.ds(pl.multiple_of(source * rows, rows), rows)
+        under = pl.ds(pl.multiple_of(source * rows + TILE, rows), rows)
+
+        @pl.when(column == 0)
+        def _():
+            out[0, at, :] = parts[t][:rows, :]
+            out[0, under, :] = parts[t][rows:, :]
+
+        @pl.when(column != 0)
+        def _():
+            product = lax.dot_general(
+                parts[t][...], partner[...], (((1,), (1,)), ((), ())), preferred_element_type=F32
+            )
+            upper = base[0, at, :].astype(F32) - state[1].astype(F32) * product[:rows]
+            out[0, at, :] = upper.astype(BF16)
+            lower = added[at, :] - state[2].astype(F32) * product[rows:]
+            out[0, under, :] = lower.astype(BF16)
+
+
+def finish(state, parts, partner, window, added):
+    size = len(parts)
+    vmem = pl.BlockSpec(memory_space=pltpu.VMEM)
+    return pl.pallas_call(
+        functools.partial(finish_kernel, size),
+        out_shape=jax.ShapeDtypeStruct((1, 2 * TILE, TILE), BF16),
+        grid=(1,),
+        in_specs=[pl.BlockSpec(memory_space=pltpu.SMEM)]
+        + [vmem] * (size + 1)
+        + [pl.BlockSpec((1, TILE, TILE), lambda i: (0, 0, 0)), vmem],
+        out_specs=vmem,
+        compiler_params=pltpu.CompilerParams(vmem_limit_bytes=24 << 20),
+        name="finish",
+    )(state, *parts, partner, window, added)
+
+
+def hand_out(parts, axis):
+    mine = jnp.zeros_like(parts[-1] if parts[0] is None else parts[0])
+    if parts[0] is not None:
+        mine = jnp.where(lax.axis_index(axis) == 0, parts[0], mine)
+    for p in range(1, len(parts)):
+        if parts[p] is not None:
+            mine = mine + lax.ppermute(parts[p], axis, [(0, p)])
+    return mine
 
 
 def shards(window, children, routes, slots, pattern):
-    groups = lax.axis_size("front") * lax.axis_size("row")
+    fronts = lax.axis_size("front")
+    rows_axis = lax.axis_size("row")
+    columns = lax.axis_size("col")
+    front = lax.axis_index("front")
     column = lax.axis_index("col")
     first = window[0, :TILE]
     second = window[0, TILE:]
-    pivot = broadcast(first, "row", 0)
-    outgoing, marks = place(routes[:, 0], slots, children, groups)
-    tags = swap(marks.reshape(groups, CAP), ("front", "row")).reshape(-1)
+    part_rows = TILE // rows_axis
+    marks_each = fronts * CAP
+    even_raw = swap(first.reshape(rows_axis, part_rows, TILE), "row")[: columns // 2]
+    outgoing, marks = place(routes[:, 0], slots, children, fronts * rows_axis)
+    marks = marks.reshape(fronts, rows_axis, CAP)
+    near = jnp.where(front == 0, marks[0], marks[1])
+    far = jnp.where(front == 0, marks[1], marks[0])
+    far = lax.ppermute(far, "front", [(0, 1), (1, 0)])
+    both = jnp.concatenate([near, far], axis=1).astype(BF16)
+    both = jnp.pad(both, ((0, 0), (TILE - marks_each, 0)))[:, None, :]
+    place_row = lax.broadcasted_iota(jnp.int32, (rows_axis, part_rows, TILE), 1)
+    place_col = lax.broadcasted_iota(jnp.int32, (rows_axis, part_rows, TILE), 2)
+    spread = jnp.where(
+        (place_row == 0) & (place_col >= TILE - marks_each), both, even_raw[0][None]
+    )
+    pivot = swap(spread, "row")
+    got = pivot[:, 0, TILE - marks_each :].astype(jnp.int32).reshape(rows_axis, fronts, CAP)
+    near, far = got[:, 0], got[:, 1]
+    tags = jnp.stack([jnp.where(front == 0, near, far), jnp.where(front == 0, far, near)])
+    tags = tags.reshape(-1)
+    pivot = pivot.reshape(TILE, TILE)
+    outgoing, tags, pivot = lax.optimization_barrier((outgoing, tags, pivot))
     incoming = swap(outgoing, ("front", "row"))
     inverse = inverse_factor(pivot)
-    lower_first = lax.dot_general(
-        first.astype(F32), inverse, (((1,), (1,)), ((), ())), precision=HI
-    ).astype(BF16)
+
+    def solve(rows):
+        return lax.dot_general(
+            rows.astype(F32), inverse, (((1,), (1,)), ((), ())), precision=HI
+        ).astype(BF16)
+
+    def to_columns(lower):
+        return hand_out(list(lower.reshape(columns, TILE // columns, TILE)), "col")
+
+    even = solve(even_raw.reshape(-1, TILE)).reshape(even_raw.shape)
+    even_part = hand_out(
+        [even[c // 2] if c % 2 == 0 else None for c in range(columns)], "col"
+    )
+    first_part = to_columns(solve(first))
+    incoming, even_part, first_part = lax.optimization_barrier((incoming, even_part, first_part))
     added = assemble(tags, incoming, second)
-    lower_second = lax.dot_general(
-        added, inverse, (((1,), (1,)), ((), ())), precision=HI
-    ).astype(BF16)
-    lower_first = broadcast(lower_first, "col", 0)
-    lower_second = broadcast(lower_second, "col", 0)
-    owner = column // 2
-    piece = jnp.where(column % 2 == 0, lower_first, lower_second)
-    partner = broadcast(piece, "row", owner)
-
-    def finish(lower, assembled, live):
-        product = lax.dot_general(
-            lower, partner, (((1,), (1,)), ((), ())), preferred_element_type=F32
-        )
-        updated = (assembled - live.astype(F32) * product).astype(BF16)
-        return jnp.where(column == 0, lower, updated)
-
-    return jnp.concatenate(
-        [
-            finish(lower_first, first.astype(F32), pattern[0, 0, 0]),
-            finish(lower_second, added, pattern[0, 1, 0]),
-        ],
-        axis=0,
-    )[None]
+    lower_second = solve(added)
+    odd = swap(lower_second.reshape(rows_axis, part_rows, TILE), "row")
+    second_part = to_columns(lower_second)
+    odd, second_part = lax.optimization_barrier((odd, second_part))
+    odd_part = hand_out(
+        [odd[c // 2] if c % 2 == 1 else None for c in range(columns)], "col"
+    )
+    lower = circulate(jnp.concatenate([first_part, second_part], axis=0), "col")
+    partner_part = jnp.where(column % 2 == 0, even_part, odd_part)
+    partner = swap(
+        jnp.broadcast_to(partner_part[None], (rows_axis,) + partner_part.shape), "row"
+    ).reshape(TILE, TILE)
+
+    state = jnp.concatenate([jnp.full((1,), column, jnp.int32), pattern[0, :, 0]])
+    return finish(state, lower, partner, window, added)
 
 
 def solution(mesh):

time: 368 us -> 255 us (0.69)
  the two profiles are of different devices: /device:TPU:8 before, /device:TPU:66 now
where the time goes in v2:
time: 255 us; the launch traced here: 254 us
  waiting for transfers between devices  90.5 us (35%)
  starting transfers between devices  81.1 us (32%)
  Pallas kernels  46 us (18%)
  blocking collectives  21.3 us (8%)
  local copies, waits for them, and re-layouts  7.8 us (3%)
  matrix products  4.39 us (2%)
    all_to_all x4, waiting for transfers between devices, swap(): return lax.all_to_all(block, axis, split_axis=0, concat_axis=0, tiled=True)  66.5 us
    all_to_all x4, starting transfers between devices, swap(): return lax.all_to_all(block, axis, split_axis=0, concat_axis=0, tiled=True)  35.5 us
    pallas_call x1, Pallas kernels, inverse_factor(): pl.pallas_call(inverse_kernel, out_shape=jax.ShapeDtypeStruct((n, n), F32...  32.5 us
    ppermute x7, starting transfers between devices, circulate(): lax.ppermute(part, axis, [(i, (i - t) % size) for i in range(size)])  27.7 us
    all_to_all x1, blocking collectives, swap(): return lax.all_to_all(block, axis, split_axis=0, concat_axis=0, tiled=True)  21.3 us
    ppermute x21, starting transfers between devices, hand_out(): mine = mine + lax.ppermute(parts[p], axis, [(0, p)])  16 us
    ppermute x21, waiting for transfers between devices, hand_out(): mine = mine + lax.ppermute(parts[p], axis, [(0, p)])  14.5 us
    ppermute x7, waiting for transfers between devices, circulate(): lax.ppermute(part, axis, [(i, (i - t) % size) for i in range(size)])  8.67 us
  transfers between devices with their start and end apart: 33, of which 9 were waited for; matrix products, arithmetic and copies ran while one was open for 2% of the time, Pallas kernels for 15%

profile of v2, /device:TPU:66, one launch (start us, length us, event | category | flops | bytes accessed | tf_op | source)
XLA Modules:
  0.0 253.7 jit_solution(6260087366983378211)
XLA Ops:
  0.0 2.2 slice_bitcast_fusion
  2.2 10.2 %all-to-all-start = ((bf16[32,16,512]{2,1,0:T(8,128)(2,1)}), bf16[32,16,512]{2,1,0:T(8,128)(2,1)S(1)}, u32[]{:S(2)}, u32[]{:S(2)}) async-start(bf16[32,16,512]{2,1,0:T(8,128)(2,1)} %bitcast.3), calls=%async_computation | async-start | bytes 1048576 | tf_op jit(solution)/shard_map/all_to_all | solution.py:192
  12.5 4.7 %place.1 = (bf16[128,128,128]{2,1,0:T(8,128)(2,1)}, s32[128]{0:T(128)}) custom-call(s32[64]{0:T(128)} %bitcast.43, s32[64]{0:T(128)} %slots.1, bf16[64,128,128]{2,1,0:T(8,128)(2,1)} %children.1), custom_call_target="tpu_custom_call" | custom-call | tf_op jit(solution)/shard_map/place/pallas_call | solution.py:50
  18.2 1.9 collective-permute-start
  21.4 7.9 %all-to-all-done = bf16[32,16,512]{2,1,0:T(8,128)(2,1)S(1)} async-done(((bf16[32,16,512]{2,1,0:T(8,128)(2,1)}), bf16[32,16,512]{2,1,0:T(8,128)(2,1)S(1)}, u32[]{:S(2)}, u32[]{:S(2)}) %all-to-all-start) | async-done | bytes 524320 | tf_op jit(solution)/shard_map/all_to_all | solution.py:192
  29.5 21.3 %all_to_all.25 = bf16[32,16,512]{2,1,0:T(8,128)(2,1)S(1)} all-to-all(bf16[32,16,512]{2,1,0:T(8,128)(2,1)S(1)} %and_select_fusion), channel_id=1, replica_groups=mesh['front'=2,'row'=32,'col'=8] {'row'}, dimensions={0} | all-to-all | bytes 1048576 | tf_op jit(solution)/shard_map/all_to_all | solution.py:192
  51.3 6.4 %all-to-all-start.2 = ((bf16[128,128,128]{2,1,0:T(8,128)(2,1)}), bf16[128,128,128]{2,1,0:T(8,128)(2,1)}, u32[]{:S(2)}, u32[]{:S(2)}) async-start(bf16[128,128,128]{2,1,0:T(8,128)(2,1)} %get-tuple-element.17), calls=%async_computation.2 | async-start | bytes 8388608 | tf_op jit(solution)/shard_map/all_to_all | solution.py:192
  57.7 32.5 %inverse.1 = f32[512,512]{1,0:T(8,128)S(1)} custom-call(bf16[512,512]{1,0:T(8,128)(2,1)S(1)} %bitcast.39), custom_call_target="tpu_custom_call" | custom-call | flops 536870912 | bytes 1572864 | tf_op jit(solution)/shard_map/inverse/pallas_call | solution.py:179
  90.2 1.1 fusion
  91.4 1.3 collective-permute-start.4
  99.7 51.0 %all-to-all-done.2.incoming = bf16[128,128,128]{2,1,0:T(8,128)(2,1)} async-done(((bf16[128,128,128]{2,1,0:T(8,128)(2,1)}), bf16[128,128,128]{2,1,0:T(8,128)(2,1)}, u32[]{:S(2)}, u32[]{:S(2)}) %all-to-all-start.2) | async-done | bytes 4194336 | tf_op jit(solution)/shard_map/all_to_all | solution.py:192
  151.8 4.7 %assemble.1.refs_10_ = f32[512,512]{1,0:T(8,128)S(1)} custom-call(s32[128]{0:T(128)S(1)} %reshape.128.tags, bf16[128,128,128]{2,1,0:T(8,128)(2,1)} %all-to-all-done.2.incoming, bf16[512,512]{1,0:T(8,128)(2,1)S(1)} %copy-done.1), custom_call_target="tpu_custom_call" | custom-call | tf_op jit(solution)/shard_map/assemble/pallas_call | solution.py:85
  156.5 2.7 %convolution_convert_fusion.1 = bf16[512,512]{1,0:T(8,128)(2,1)} fusion(f32[512,512]{1,0:T(8,128)S(1)} %assemble.1.refs_10_, f32[512,512]{1,0:T(8,128)S(1)} %inverse.1), kind=kOutput, calls=%fused_computation.1 | convolution fusion | flops 1610874880 | bytes 2621440 | tf_op jit(solution)/shard_map/dot_general | solution.py:289
  159.2 9.0 %all-to-all-start.3 = ((bf16[32,16,512]{2,1,0:T(8,128)(2,1)}), bf16[32,16,512]{2,1,0:T(8,128)(2,1)S(1)}, u32[]{:S(2)}, u32[]{:S(2)}) async-start(bf16[32,16,512]{2,1,0:T(8,128)(2,1)} %bitcast.40), calls=%async_computation.3 | async-start | bytes 1048576 | tf_op jit(solution)/shard_map/all_to_all | solution.py:192
  168.2 1.1 fusion.22
  169.3 1.3 collective-permute-start.11
  173.3 2.2 collective-permute-done.11
  177.8 7.6 %all-to-all-done.3 = bf16[32,16,512]{2,1,0:T(8,128)(2,1)S(1)} async-done(((bf16[32,16,512]{2,1,0:T(8,128)(2,1)}), bf16[32,16,512]{2,1,0:T(8,128)(2,1)S(1)}, u32[]{:S(2)}, u32[]{:S(2)}) %all-to-all-start.3) | async-done | bytes 524320 | tf_op jit(solution)/shard_map/all_to_all | solution.py:192
  187.3 1.3 collective-permute-start.25
  188.7 12.3 %collective-permute-done.25 = bf16[16,512]{1,0:T(8,128)(2,1)S(1)} collective-permute-done((bf16[16,512]{1,0:T(8,128)(2,1)S(1)}, bf16[16,512]{1,0:T(8,128)(2,1)S(1)}, u32[]{:S(2)}, u32[]{:S(2)}) %collective-permute-start.25) | collective-permute-done | bytes 16416 | tf_op jit(solution)/shard_map/ppermute | solution.py:251
  201.8 9.8 %all-to-all-start.4 = ((bf16[32,16,512]{2,1,0:T(8,128)(2,1)}), bf16[32,16,512]{2,1,0:T(8,128)(2,1)S(1)}, u32[]{:S(2)}, u32[]{:S(2)}) async-start(bf16[32,16,512]{2,1,0:T(8,128)(2,1)} %broadcast_in_dim.36), calls=%async_computation.4 | async-start | bytes 1048576 | tf_op jit(solution)/shard_map/all_to_all | solution.py:192
  211.6 1.9 collective-permute-start.24
  213.5 1.9 collective-permute-start.23
  215.5 5.6 %collective-permute-start.22 = (bf16[128,512]{1,0:T(8,128)(2,1)S(1)}, bf16[128,512]{1,0:T(8,128)(2,1)S(1)}, u32[]{:S(2)}, u32[]{:S(2)}) collective-permute-start(bf16[128,512]{1,0:T(8,128)(2,1)S(1)} %constant_dynamic-update-slice_fusion.refs_0_), channel_id=1, source_target_pairs={{0,3},{1,4},{2,5},{3,6},{4,7},{5,0},{6,1},{7,2},{8,11},{9,12},{10,... | collective-permute-start | bytes 393224 | tf_op jit(solution)/shard_map/ppermute | solution.py:199
  221.1 4.7 %collective-permute-start.21 = (bf16[128,512]{1,0:T(8,128)(2,1)S(1)}, bf16[128,512]{1,0:T(8,128)(2,1)S(1)}, u32[]{:S(2)}, u32[]{:S(2)}) collective-permute-start(bf16[128,512]{1,0:T(8,128)(2,1)S(1)} %constant_dynamic-update-slice_fusion.refs_0_), channel_id=1, source_target_pairs={{0,4},{1,5},{2,6},{3,7},{4,0},{5,1},{6,2},{7,3},{8,12},{9,13},{10,... | collective-permute-start | bytes 393224 | tf_op jit(solution)/shard_map/ppermute | solution.py:199
  225.8 5.2 %collective-permute-start.20 = (bf16[128,512]{1,0:T(8,128)(2,1)S(1)}, bf16[128,512]{1,0:T(8,128)(2,1)S(1)}, u32[]{:S(2)}, u32[]{:S(2)}) collective-permute-start(bf16[128,512]{1,0:T(8,128)(2,1)S(1)} %constant_dynamic-update-slice_fusion.refs_0_), channel_id=1, source_target_pairs={{0,5},{1,6},{2,7},{3,0},{4,1},{5,2},{6,3},{7,4},{8,13},{9,14},{10,... | collective-permute-start | bytes 393224 | tf_op jit(solution)/shard_map/ppermute | solution.py:199
  231.0 3.3 %collective-permute-start.19 = (bf16[128,512]{1,0:T(8,128)(2,1)S(1)}, bf16[128,512]{1,0:T(8,128)(2,1)S(1)}, u32[]{:S(2)}, u32[]{:S(2)}) collective-permute-start(bf16[128,512]{1,0:T(8,128)(2,1)S(1)} %constant_dynamic-update-slice_fusion.refs_0_), channel_id=1, source_target_pairs={{0,6},{1,7},{2,0},{3,1},{4,2},{5,3},{6,4},{7,5},{8,14},{9,15},{10,... | collective-permute-start | bytes 393224 | tf_op jit(solution)/shard_map/ppermute | solution.py:199
  234.3 5.1 %collective-permute-start.18 = (bf16[128,512]{1,0:T(8,128)(2,1)S(1)}, bf16[128,512]{1,0:T(8,128)(2,1)S(1)}, u32[]{:S(2)}, u32[]{:S(2)}) collective-permute-start(bf16[128,512]{1,0:T(8,128)(2,1)S(1)} %constant_dynamic-update-slice_fusion.refs_0_), channel_id=1, source_target_pairs={{0,7},{1,0},{2,1},{3,2},{4,3},{5,4},{6,5},{7,6},{8,15},{9,8},{10,9... | collective-permute-start | bytes 393224 | tf_op jit(solution)/shard_map/ppermute | solution.py:199
  239.5 4.8 %collective-permute-done.20.refs_3_ = bf16[128,512]{1,0:T(8,128)(2,1)S(1)} collective-permute-done((bf16[128,512]{1,0:T(8,128)(2,1)S(1)}, bf16[128,512]{1,0:T(8,128)(2,1)S(1)}, u32[]{:S(2)}, u32[]{:S(2)}) %collective-permute-start.20) | collective-permute-done | bytes 131104 | tf_op jit(solution)/shard_map/ppermute | solution.py:199
  244.3 2.3 collective-permute-done.19.refs_2_
  246.6 1.5 collective-permute-done.18.refs_1_
  249.7 4.0 %finish.1 = bf16[1,1024,512]{2,1,0:T(8,128)(2,1)} custom-call(s32[3]{0:T(128)S(1)} %pad_add_fusion.1.state, bf16[128,512]{1,0:T(8,128)(2,1)S(1)} %constant_dynamic-update-slice_fusion.refs_0_, bf16[128,512]{1,0:T(8,128)(2,1)S(1)} %copy-done.3, bf16[128,512]{1,0:T(8,128)(2,1)S(1)} %collective-permute-done.19.refs_2_, ...), custom_call_target="tpu_custom_call" | custom-call | tf_op jit(solution)/shard_map/finish/pallas_call | solution.py:232
  (89 shorter events, 20.2 us)
Async XLA Ops:
  2.2 27.1 %all-to-all-start = ((bf16[32,16,512]{2,1,0:T(8,128)(2,1)}), bf16[32,16,512]{2,1,0:T(8,128)(2,1)S(1)}, u32[]{:S(2)}, u32[]{:S(2)}) async-start(bf16[32,16,512]{2,1,0:T(8,128)(2,1)} %bitcast.3), calls=%async_computation | async-start | bytes 1048576 | tf_op jit(solution)/shard_map/all_to_all | solution.py:192
  18.2 3.0 %collective-permute-start = (s32[32,2]{0,1:T(2,128)S(1)}, s32[32,2]{0,1:T(2,128)S(1)}, u32[]{:S(2)}, u32[]{:S(2)}) collective-permute-start(s32[32,2]{0,1:T(2,128)S(1)} %copy.17), channel_id=1, source_target_pairs={{0,256},{256,0},{1,257},{257,1},{2,258},{258,2},{3,259},{259,3},{4... | collective-permute-start | bytes 776 | tf_op jit(solution)/shard_map/ppermute | solution.py:270
  51.3 99.5 %all-to-all-start.2 = ((bf16[128,128,128]{2,1,0:T(8,128)(2,1)}), bf16[128,128,128]{2,1,0:T(8,128)(2,1)}, u32[]{:S(2)}, u32[]{:S(2)}) async-start(bf16[128,128,128]{2,1,0:T(8,128)(2,1)} %get-tuple-element.17), calls=%async_computation.2 | async-start | bytes 8388608 | tf_op jit(solution)/shard_map/all_to_all | solution.py:192
  91.4 6.7 %collective-permute-start.4 = (bf16[64,512]{1,0:T(8,128)(2,1)S(1)}, bf16[64,512]{1,0:T(8,128)(2,1)S(1)}, u32[]{:S(2)}, u32[]{:S(2)}) collective-permute-start(bf16[64,512]{1,0:T(8,128)(2,1)S(1)} %get-tuple-element.38), channel_id=1, source_target_pairs={{0,1},{8,9},{16,17},{24,25},{32,33},{40,41},{48,49},{56,57},{64,65... | collective-permute-start | bytes 196616 | tf_op jit(solution)/shard_map/ppermute | solution.py:251
  92.7 6.1 %collective-permute-start.10 = (bf16[64,512]{1,0:T(8,128)(2,1)S(1)}, bf16[64,512]{1,0:T(8,128)(2,1)S(1)}, u32[]{:S(2)}, u32[]{:S(2)}) collective-permute-start(bf16[64,512]{1,0:T(8,128)(2,1)S(1)} %get-tuple-element.39), channel_id=1, source_target_pairs={{0,7},{8,15},{16,23},{24,31},{32,39},{40,47},{48,55},{56,63},{64,7... | collective-permute-start | bytes 196616 | tf_op jit(solution)/shard_map/ppermute | solution.py:251
  94.0 2.0 collective-permute-start.1
  94.7 2.0 collective-permute-start.3
  95.3 2.0 collective-permute-start.2
  96.0 3.6 %collective-permute-start.9 = (bf16[64,512]{1,0:T(8,128)(2,1)S(1)}, bf16[64,512]{1,0:T(8,128)(2,1)S(1)}, u32[]{:S(2)}, u32[]{:S(2)}) collective-permute-start(bf16[64,512]{1,0:T(8,128)(2,1)S(1)} %get-tuple-element.40), channel_id=1, source_target_pairs={{0,6},{8,14},{16,22},{24,30},{32,38},{40,46},{48,54},{56,62},{64,7... | collective-permute-start | bytes 196616 | tf_op jit(solution)/shard_map/ppermute | solution.py:251
  96.7 2.9 %collective-permute-start.8 = (bf16[64,512]{1,0:T(8,128)(2,1)S(1)}, bf16[64,512]{1,0:T(8,128)(2,1)S(1)}, u32[]{:S(2)}, u32[]{:S(2)}) collective-permute-start(bf16[64,512]{1,0:T(8,128)(2,1)S(1)} %get-tuple-element.41), channel_id=1, source_target_pairs={{0,5},{8,13},{16,21},{24,29},{32,37},{40,45},{48,53},{56,61},{64,6... | collective-permute-start | bytes 196616 | tf_op jit(solution)/shard_map/ppermute | solution.py:251
  97.4 2.3 collective-permute-start.7
  98.1 1.6 collective-permute-start.6
  98.8 0.9 collective-permute-start.5
  159.2 26.1 %all-to-all-start.3 = ((bf16[32,16,512]{2,1,0:T(8,128)(2,1)}), bf16[32,16,512]{2,1,0:T(8,128)(2,1)S(1)}, u32[]{:S(2)}, u32[]{:S(2)}) async-start(bf16[32,16,512]{2,1,0:T(8,128)(2,1)} %bitcast.40), calls=%async_computation.3 | async-start | bytes 1048576 | tf_op jit(solution)/shard_map/all_to_all | solution.py:192
  169.3 6.2 %collective-permute-start.11 = (bf16[64,512]{1,0:T(8,128)(2,1)S(1)}, bf16[64,512]{1,0:T(8,128)(2,1)S(1)}, u32[]{:S(2)}, u32[]{:S(2)}) collective-permute-start(bf16[64,512]{1,0:T(8,128)(2,1)S(1)} %get-tuple-element.31), channel_id=1, source_target_pairs={{0,1},{8,9},{16,17},{24,25},{32,33},{40,41},{48,49},{56,57},{64,65... | collective-permute-start | bytes 196616 | tf_op jit(solution)/shard_map/ppermute | solution.py:251
  170.6 5.5 %collective-permute-start.17 = (bf16[64,512]{1,0:T(8,128)(2,1)S(1)}, bf16[64,512]{1,0:T(8,128)(2,1)S(1)}, u32[]{:S(2)}, u32[]{:S(2)}) collective-permute-start(bf16[64,512]{1,0:T(8,128)(2,1)S(1)} %get-tuple-element.32), channel_id=1, source_target_pairs={{0,7},{8,15},{16,23},{24,31},{32,39},{40,47},{48,55},{56,63},{64,7... | collective-permute-start | bytes 196616 | tf_op jit(solution)/shard_map/ppermute | solution.py:251
  171.3 5.5 %collective-permute-start.16 = (bf16[64,512]{1,0:T(8,128)(2,1)S(1)}, bf16[64,512]{1,0:T(8,128)(2,1)S(1)}, u32[]{:S(2)}, u32[]{:S(2)}) collective-permute-start(bf16[64,512]{1,0:T(8,128)(2,1)S(1)} %get-tuple-element.33), channel_id=1, source_target_pairs={{0,6},{8,14},{16,22},{24,30},{32,38},{40,46},{48,54},{56,62},{64,7... | collective-permute-start | bytes 196616 | tf_op jit(solution)/shard_map/ppermute | solution.py:251
  172.0 4.9 %collective-permute-start.15 = (bf16[64,512]{1,0:T(8,128)(2,1)S(1)}, bf16[64,512]{1,0:T(8,128)(2,1)S(1)}, u32[]{:S(2)}, u32[]{:S(2)}) collective-permute-start(bf16[64,512]{1,0:T(8,128)(2,1)S(1)} %get-tuple-element.34), channel_id=1, source_target_pairs={{0,5},{8,13},{16,21},{24,29},{32,37},{40,45},{48,53},{56,61},{64,6... | collective-permute-start | bytes 196616 | tf_op jit(solution)/shard_map/ppermute | solution.py:251
  172.6 4.2 %collective-permute-start.14 = (bf16[64,512]{1,0:T(8,128)(2,1)S(1)}, bf16[64,512]{1,0:T(8,128)(2,1)S(1)}, u32[]{:S(2)}, u32[]{:S(2)}) collective-permute-start(bf16[64,512]{1,0:T(8,128)(2,1)S(1)} %get-tuple-element.35), channel_id=1, source_target_pairs={{0,4},{8,12},{16,20},{24,28},{32,36},{40,44},{48,52},{56,60},{64,6... | collective-permute-start | bytes 196616 | tf_op jit(solution)/shard_map/ppermute | solution.py:251
  175.5 1.4 collective-permute-start.13
  185.3 3.3 %collective-permute-start.26 = (bf16[16,512]{1,0:T(8,128)(2,1)S(1)}, bf16[16,512]{1,0:T(8,128)(2,1)S(1)}, u32[]{:S(2)}, u32[]{:S(2)}) collective-permute-start(bf16[16,512]{1,0:T(8,128)(2,1)S(1)} %get-tuple-element.27), channel_id=1, source_target_pairs={{0,3},{8,11},{16,19},{24,27},{32,35},{40,43},{48,51},{56,59},{64,6... | collective-permute-start | bytes 49160 | tf_op jit(solution)/shard_map/ppermute | solution.py:251
  186.0 2.7 %collective-permute-start.28 = (bf16[16,512]{1,0:T(8,128)(2,1)S(1)}, bf16[16,512]{1,0:T(8,128)(2,1)S(1)}, u32[]{:S(2)}, u32[]{:S(2)}) collective-permute-start(bf16[16,512]{1,0:T(8,128)(2,1)S(1)} %get-tuple-element.28), channel_id=1, source_target_pairs={{0,7},{8,15},{16,23},{24,31},{32,39},{40,47},{48,55},{56,63},{64,7... | collective-permute-start | bytes 49160 | tf_op jit(solution)/shard_map/ppermute | solution.py:251
  186.7 2.0 collective-permute-start.27
  187.3 13.6 %collective-permute-start.25 = (bf16[16,512]{1,0:T(8,128)(2,1)S(1)}, bf16[16,512]{1,0:T(8,128)(2,1)S(1)}, u32[]{:S(2)}, u32[]{:S(2)}) collective-permute-start(bf16[16,512]{1,0:T(8,128)(2,1)S(1)} %get-tuple-element.30), channel_id=1, source_target_pairs={{0,1},{8,9},{16,17},{24,25},{32,33},{40,41},{48,49},{56,57},{64,65... | collective-permute-start | bytes 49160 | tf_op jit(solution)/shard_map/ppermute | solution.py:251
  201.8 47.0 %all-to-all-start.4 = ((bf16[32,16,512]{2,1,0:T(8,128)(2,1)}), bf16[32,16,512]{2,1,0:T(8,128)(2,1)S(1)}, u32[]{:S(2)}, u32[]{:S(2)}) async-start(bf16[32,16,512]{2,1,0:T(8,128)(2,1)} %broadcast_in_dim.36), calls=%async_computation.4 | async-start | bytes 1048576 | tf_op jit(solution)/shard_map/all_to_all | solution.py:192
  211.6 19.4 %collective-permute-start.24 = (bf16[128,512]{1,0:T(8,128)(2,1)S(1)}, bf16[128,512]{1,0:T(8,128)(2,1)S(1)}, u32[]{:S(2)}, u32[]{:S(2)}) collective-permute-start(bf16[128,512]{1,0:T(8,128)(2,1)S(1)} %constant_dynamic-update-slice_fusion.refs_0_), channel_id=1, source_target_pairs={{0,1},{1,2},{2,3},{3,4},{4,5},{5,6},{6,7},{7,0},{8,9},{9,10},{10,1... | collective-permute-start | bytes 393224 | tf_op jit(solution)/shard_map/ppermute | solution.py:199
  213.5 20.7 %collective-permute-start.23 = (bf16[128,512]{1,0:T(8,128)(2,1)S(1)}, bf16[128,512]{1,0:T(8,128)(2,1)S(1)}, u32[]{:S(2)}, u32[]{:S(2)}) collective-permute-start(bf16[128,512]{1,0:T(8,128)(2,1)S(1)} %constant_dynamic-update-slice_fusion.refs_0_), channel_id=1, source_target_pairs={{0,2},{1,3},{2,4},{3,5},{4,6},{5,7},{6,0},{7,1},{8,10},{9,11},{10,... | collective-permute-start | bytes 393224 | tf_op jit(solution)/shard_map/ppermute | solution.py:199
  215.5 24.0 %collective-permute-start.22 = (bf16[128,512]{1,0:T(8,128)(2,1)S(1)}, bf16[128,512]{1,0:T(8,128)(2,1)S(1)}, u32[]{:S(2)}, u32[]{:S(2)}) collective-permute-start(bf16[128,512]{1,0:T(8,128)(2,1)S(1)} %constant_dynamic-update-slice_fusion.refs_0_), channel_id=1, source_target_pairs={{0,3},{1,4},{2,5},{3,6},{4,7},{5,0},{6,1},{7,2},{8,11},{9,12},{10,... | collective-permute-start | bytes 393224 | tf_op jit(solution)/shard_map/ppermute | solution.py:199
  221.1 18.4 %collective-permute-start.21 = (bf16[128,512]{1,0:T(8,128)(2,1)S(1)}, bf16[128,512]{1,0:T(8,128)(2,1)S(1)}, u32[]{:S(2)}, u32[]{:S(2)}) collective-permute-start(bf16[128,512]{1,0:T(8,128)(2,1)S(1)} %constant_dynamic-update-slice_fusion.refs_0_), channel_id=1, source_target_pairs={{0,4},{1,5},{2,6},{3,7},{4,0},{5,1},{6,2},{7,3},{8,12},{9,13},{10,... | collective-permute-start | bytes 393224 | tf_op jit(solution)/shard_map/ppermute | solution.py:199
  225.8 18.5 %collective-permute-start.20 = (bf16[128,512]{1,0:T(8,128)(2,1)S(1)}, bf16[128,512]{1,0:T(8,128)(2,1)S(1)}, u32[]{:S(2)}, u32[]{:S(2)}) collective-permute-start(bf16[128,512]{1,0:T(8,128)(2,1)S(1)} %constant_dynamic-update-slice_fusion.refs_0_), channel_id=1, source_target_pairs={{0,5},{1,6},{2,7},{3,0},{4,1},{5,2},{6,3},{7,4},{8,13},{9,14},{10,... | collective-permute-start | bytes 393224 | tf_op jit(solution)/shard_map/ppermute | solution.py:199
  231.0 15.6 %collective-permute-start.19 = (bf16[128,512]{1,0:T(8,128)(2,1)S(1)}, bf16[128,512]{1,0:T(8,128)(2,1)S(1)}, u32[]{:S(2)}, u32[]{:S(2)}) collective-permute-start(bf16[128,512]{1,0:T(8,128)(2,1)S(1)} %constant_dynamic-update-slice_fusion.refs_0_), channel_id=1, source_target_pairs={{0,6},{1,7},{2,0},{3,1},{4,2},{5,3},{6,4},{7,5},{8,14},{9,15},{10,... | collective-permute-start | bytes 393224 | tf_op jit(solution)/shard_map/ppermute | solution.py:199
  234.3 13.9 %collective-permute-start.18 = (bf16[128,512]{1,0:T(8,128)(2,1)S(1)}, bf16[128,512]{1,0:T(8,128)(2,1)S(1)}, u32[]{:S(2)}, u32[]{:S(2)}) collective-permute-start(bf16[128,512]{1,0:T(8,128)(2,1)S(1)} %constant_dynamic-update-slice_fusion.refs_0_), channel_id=1, source_target_pairs={{0,7},{1,0},{2,1},{3,2},{4,3},{5,4},{6,5},{7,6},{8,15},{9,8},{10,9... | collective-permute-start | bytes 393224 | tf_op jit(solution)/shard_map/ppermute | solution.py:199
  (8 other events, 189.2 us)

commit v3 on v2

--- a/solution.py
+++ b/solution.py
@@ -62,10 +62,15 @@
 
 def assemble_kernel(tags, incoming, base, out, acc):
     side = TILE // SB
-    acc[...] = jnp.zeros_like(acc)
+    step = pl.program_id(0)
+    blocks = incoming.shape[0]
+
+    @pl.when(step == 0)
+    def _():
+        acc[...] = jnp.zeros_like(acc)
 
     def add(s, _):
-        t = tags[s]
+        t = tags[step * blocks + s]
 
         @pl.when(t > 0)
         def _():
@@ -73,24 +78,33 @@
 
         return 0
 
-    lax.fori_loop(0, incoming.shape[0], add, 0)
-    for i in range(side):
-        for j in range(side):
-            rows, cols = slice(i * SB, (i + 1) * SB), slice(j * SB, (j + 1) * SB)
-            out[rows, cols] = base[rows, cols].astype(F32) + acc[i * side + j]
-
-
-def assemble(tags, incoming, base):
-    vmem = pl.BlockSpec(memory_space=pltpu.VMEM)
+    lax.fori_loop(0, blocks, add, 0)
+
+    @pl.when(step == pl.num_programs(0) - 1)
+    def _():
+        for i in range(side):
+            for j in range(side):
+                rows, cols = slice(i * SB, (i + 1) * SB), slice(j * SB, (j + 1) * SB)
+                out[rows, cols] = base[0, rows, cols].astype(F32) + acc[i * side + j]
+
+
+def assemble(tags, incoming, window):
+    steps = 8
+    blocks = incoming.shape[0] // steps
     return pl.pallas_call(
         assemble_kernel,
         out_shape=jax.ShapeDtypeStruct((TILE, TILE), F32),
-        in_specs=[pl.BlockSpec(memory_space=pltpu.SMEM), vmem, vmem],
-        out_specs=vmem,
+        grid=(steps,),
+        in_specs=[
+            pl.BlockSpec(memory_space=pltpu.SMEM),
+            pl.BlockSpec((blocks, SB, SB), lambda i: (i, 0, 0)),
+            pl.BlockSpec((1, TILE, TILE), lambda i: (0, 1, 0)),
+        ],
+        out_specs=pl.BlockSpec((TILE, TILE), lambda i: (0, 0)),
         scratch_shapes=[pltpu.VMEM(((TILE // SB) ** 2, SB, SB), F32)],
         compiler_params=pltpu.CompilerParams(vmem_limit_bytes=24 << 20),
         name="assemble",
-    )(tags, incoming, base)
+    )(tags, incoming, window)
 
 
 STEP = 4
@@ -192,64 +206,87 @@
     return lax.all_to_all(block, axis, split_axis=0, concat_axis=0, tiled=True)
 
 
-def circulate(part, axis):
-    size = lax.axis_size(axis)
-    parts = [part]
+HOLDERS = 4
+
+
+def hand_out(parts, axis, devices):
+    mine = jnp.zeros_like(parts[0])
+    for part, device in zip(parts, devices):
+        if device == 0:
+            mine = mine + jnp.where(lax.axis_index(axis) == 0, part, jnp.zeros_like(part))
+        else:
+            mine = mine + lax.ppermute(part, axis, [(0, device)])
+    return mine
+
+
+def column_holders():
+    size = lax.axis_size("col")
+    return list(range(0, size, size // HOLDERS))
+
+
+def to_holders(block):
+    parts = list(block.reshape(HOLDERS, -1, block.shape[1]))
+    return hand_out(parts, "col", column_holders())
+
+
+def from_holders(mine):
+    size = lax.axis_size("col")
+    got = [mine]
     for t in range(1, size):
-        parts.append(lax.ppermute(part, axis, [(i, (i - t) % size) for i in range(size)]))
-    return parts
+        got.append(lax.ppermute(mine, "col", [(i, (i - t) % size) for i in column_holders()]))
+    return got
 
 
 def finish_kernel(size, state, *refs):
-    parts = refs[:size]
-    partner, base, added, out = refs[size:]
+    halves = refs[:size], refs[size : 2 * size]
+    partner, base, added, out = refs[2 * size :]
     column = state[0]
-    rows = parts[0].shape[0] // 2
-    for t in range(size):
-        source = lax.rem(column + t, size)
-        at = pl.ds(pl.multiple_of(source * rows, rows), rows)
-        under = pl.ds(pl.multiple_of(source * rows + TILE, rows), rows)
-
-        @pl.when(column == 0)
-        def _():
-            out[0, at, :] = parts[t][:rows, :]
-            out[0, under, :] = parts[t][rows:, :]
-
-        @pl.when(column != 0)
-        def _():
-            product = lax.dot_general(
-                parts[t][...], partner[...], (((1,), (1,)), ((), ())), preferred_element_type=F32
-            )
-            upper = base[0, at, :].astype(F32) - state[1].astype(F32) * product[:rows]
-            out[0, at, :] = upper.astype(BF16)
-            lower = added[at, :] - state[2].astype(F32) * product[rows:]
-            out[0, under, :] = lower.astype(BF16)
-
-
-def finish(state, parts, partner, window, added):
-    size = len(parts)
+    step = size // HOLDERS
+    rows = TILE // HOLDERS
+    shift = lax.rem(step - lax.rem(column, step), step)
+    first = lax.div(column + shift, step)
+    for s in range(step):
+        for k in range(HOLDERS):
+            source = lax.rem(first + k, HOLDERS)
+            at = pl.ds(pl.multiple_of(source * rows, rows), rows)
+            under = pl.ds(pl.multiple_of(source * rows + TILE, rows), rows)
+            upper_part, under_part = halves[0][k * step + s], halves[1][k * step + s]
+
+            @pl.when((shift == s) & (column == 0))
+            def _():
+                out[0, at, :] = upper_part[...]
+                out[0, under, :] = under_part[...]
+
+            @pl.when((shift == s) & (column != 0))
+            def _():
+                def product(part):
+                    return lax.dot_general(
+                        part[...],
+                        partner[...],
+                        (((1,), (1,)), ((), ())),
+                        preferred_element_type=F32,
+                    )
+
+                upper = base[0, at, :].astype(F32) - state[1].astype(F32) * product(upper_part)
+                out[0, at, :] = upper.astype(BF16)
+                lower = added[at, :] - state[2].astype(F32) * product(under_part)
+                out[0, under, :] = lower.astype(BF16)
+
+
+def finish(state, upper, under, partner, window, added):
+    size = len(upper)
     vmem = pl.BlockSpec(memory_space=pltpu.VMEM)
     return pl.pallas_call(
         functools.partial(finish_kernel, size),
         out_shape=jax.ShapeDtypeStruct((1, 2 * TILE, TILE), BF16),
         grid=(1,),
         in_specs=[pl.BlockSpec(memory_space=pltpu.SMEM)]
-        + [vmem] * (size + 1)
+        + [vmem] * (2 * size + 1)
         + [pl.BlockSpec((1, TILE, TILE), lambda i: (0, 0, 0)), vmem],
         out_specs=vmem,
         compiler_params=pltpu.CompilerParams(vmem_limit_bytes=24 << 20),
         name="finish",
-    )(state, *parts, partner, window, added)
-
-
-def hand_out(parts, axis):
-    mine = jnp.zeros_like(parts[-1] if parts[0] is None else parts[0])
-    if parts[0] is not None:
-        mine = jnp.where(lax.axis_index(axis) == 0, parts[0], mine)
-    for p in range(1, len(parts)):
-        if parts[p] is not None:
-            mine = mine + lax.ppermute(parts[p], axis, [(0, p)])
-    return mine
+    )(state, *upper, *under, partner, window, added)
 
 
 def shards(window, children, routes, slots, pattern):
@@ -259,7 +296,6 @@
     front = lax.axis_index("front")
     column = lax.axis_index("col")
     first = window[0, :TILE]
-    second = window[0, TILE:]
     part_rows = TILE // rows_axis
     marks_each = fronts * CAP
     even_raw = swap(first.reshape(rows_axis, part_rows, TILE), "row")[: columns // 2]
@@ -290,31 +326,24 @@
             rows.astype(F32), inverse, (((1,), (1,)), ((), ())), precision=HI
         ).astype(BF16)
 
-    def to_columns(lower):
-        return hand_out(list(lower.reshape(columns, TILE // columns, TILE)), "col")
-
     even = solve(even_raw.reshape(-1, TILE)).reshape(even_raw.shape)
-    even_part = hand_out(
-        [even[c // 2] if c % 2 == 0 else None for c in range(columns)], "col"
-    )
-    first_part = to_columns(solve(first))
-    incoming, even_part, first_part = lax.optimization_barrier((incoming, even_part, first_part))
-    added = assemble(tags, incoming, second)
+    even_part = hand_out(list(even), "col", range(0, columns, 2))
+    upper = from_holders(to_holders(solve(first)))
+    incoming, even_part, upper = lax.optimization_barrier((incoming, even_part, upper))
+    added = assemble(tags, incoming, window)
     lower_second = solve(added)
     odd = swap(lower_second.reshape(rows_axis, part_rows, TILE), "row")
-    second_part = to_columns(lower_second)
-    odd, second_part = lax.optimization_barrier((odd, second_part))
-    odd_part = hand_out(
-        [odd[c // 2] if c % 2 == 1 else None for c in range(columns)], "col"
-    )
-    lower = circulate(jnp.concatenate([first_part, second_part], axis=0), "col")
+    under = to_holders(lower_second)
+    odd, under = lax.optimization_barrier((odd, under))
+    odd_part = hand_out(list(odd[: columns // 2]), "col", range(1, columns, 2))
+    under = from_holders(under)
     partner_part = jnp.where(column % 2 == 0, even_part, odd_part)
     partner = swap(
         jnp.broadcast_to(partner_part[None], (rows_axis,) + partner_part.shape), "row"
     ).reshape(TILE, TILE)
 
     state = jnp.concatenate([jnp.full((1,), column, jnp.int32), pattern[0, :, 0]])
-    return finish(state, lower, partner, window, added)
+    return finish(state, upper, under, partner, window, added)
 
 
 def solution(mesh):

time: 255 us -> 247 us (0.969)
  the two profiles are of different devices: /device:TPU:66 before, /device:TPU:2 now
where the time goes in v3:
time: 247 us; the launch traced here: 245 us
  starting transfers between devices  122 us (49%)
  Pallas kernels  44.9 us (18%)
  waiting for transfers between devices  26.3 us (11%)
  local copies, waits for them, and re-layouts  21.4 us (9%)
  blocking collectives  21.3 us (9%)
  matrix products  4.38 us (2%)
  other arithmetic  4.13 us (2%)
    ppermute x13, starting transfers between devices, hand_out(): mine = mine + lax.ppermute(part, axis, [(0, device)])  51.2 us
    ppermute x14, starting transfers between devices, from_holders(): lax.ppermute(mine, 'col', [(i, (i - t) % size) for i in column_holders()])  37.3 us
    pallas_call x1, Pallas kernels, inverse_factor(): pl.pallas_call(inverse_kernel, out_shape=jax.ShapeDtypeStruct((n, n), F32...  32.5 us
    all_to_all x4, starting transfers between devices, swap(): return lax.all_to_all(block, axis, split_axis=0, concat_axis=0, tiled=True)  31.8 us
    all_to_all x1, blocking collectives, swap(): return lax.all_to_all(block, axis, split_axis=0, concat_axis=0, tiled=True)  21.3 us
    unnamed x54, local copies, waits for them, and re-layouts  16.2 us
    all_to_all x4, waiting for transfers between devices, swap(): return lax.all_to_all(block, axis, split_axis=0, concat_axis=0, tiled=True)  16.2 us
    ppermute x13, waiting for transfers between devices, hand_out(): mine = mine + lax.ppermute(part, axis, [(0, device)])  6.59 us
  transfers between devices with their start and end apart: 32, of which 10 were waited for; matrix products, arithmetic and copies ran while one was open for 3% of the time, Pallas kernels for 15%

profile of v3, /device:TPU:2, one launch (start us, length us, event | category | flops | bytes accessed | tf_op | source)
XLA Modules:
  0.0 245.1 jit_solution(10102394756324578245)
XLA Ops:
  0.0 1.9 slice.64
  1.9 10.2 %all-to-all-start = ((bf16[32,16,512]{2,1,0:T(8,128)(2,1)}), bf16[32,16,512]{2,1,0:T(8,128)(2,1)S(1)}, u32[]{:S(2)}, u32[]{:S(2)}) async-start(bf16[32,16,512]{2,1,0:T(8,128)(2,1)} %bitcast.3), calls=%async_computation | async-start | bytes 1048576 | tf_op jit(solution)/shard_map/all_to_all | solution.py:206
  12.1 4.8 %place.1 = (bf16[128,128,128]{2,1,0:T(8,128)(2,1)}, s32[128]{0:T(128)}) custom-call(s32[64]{0:T(128)} %bitcast.41, s32[64]{0:T(128)} %slots.1, bf16[64,128,128]{2,1,0:T(8,128)(2,1)} %children.1), custom_call_target="tpu_custom_call" | custom-call | tf_op jit(solution)/shard_map/place/pallas_call | solution.py:50
  17.9 1.9 collective-permute-start
  21.1 7.8 %all-to-all-done = bf16[32,16,512]{2,1,0:T(8,128)(2,1)S(1)} async-done(((bf16[32,16,512]{2,1,0:T(8,128)(2,1)}), bf16[32,16,512]{2,1,0:T(8,128)(2,1)S(1)}, u32[]{:S(2)}, u32[]{:S(2)}) %all-to-all-start) | async-done | bytes 524320 | tf_op jit(solution)/shard_map/all_to_all | solution.py:206
  29.2 21.3 %all_to_all.25 = bf16[32,16,512]{2,1,0:T(8,128)(2,1)S(1)} all-to-all(bf16[32,16,512]{2,1,0:T(8,128)(2,1)S(1)} %and_select_fusion), channel_id=1, replica_groups=mesh['front'=2,'row'=32,'col'=8] {'row'}, dimensions={0} | all-to-all | bytes 1048576 | tf_op jit(solution)/shard_map/all_to_all | solution.py:206
  50.9 6.4 %all-to-all-start.2 = ((bf16[128,128,128]{2,1,0:T(8,128)(2,1)}), bf16[128,128,128]{2,1,0:T(8,128)(2,1)}, u32[]{:S(2)}, u32[]{:S(2)}) async-start(bf16[128,128,128]{2,1,0:T(8,128)(2,1)} %get-tuple-element.24), calls=%async_computation.2 | async-start | bytes 8388608 | tf_op jit(solution)/shard_map/all_to_all | solution.py:206
  57.4 32.5 %inverse.1 = f32[512,512]{1,0:T(8,128)S(1)} custom-call(bf16[512,512]{1,0:T(8,128)(2,1)S(1)} %bitcast.37), custom_call_target="tpu_custom_call" | custom-call | flops 536870912 | bytes 1572864 | tf_op jit(solution)/shard_map/inverse/pallas_call | solution.py:193
  91.0 6.1 %collective-permute-start.4 = (bf16[128,512]{1,0:T(8,128)(2,1)S(1)}, bf16[128,512]{1,0:T(8,128)(2,1)S(1)}, u32[]{:S(2)}, u32[]{:S(2)}) collective-permute-start(bf16[128,512]{1,0:T(8,128)(2,1)S(1)} %get-tuple-element.46), channel_id=1, source_target_pairs={{0,2},{8,10},{16,18},{24,26},{32,34},{40,42},{48,50},{56,58},{64,6... | collective-permute-start | bytes 393224 | tf_op jit(solution)/shard_map/ppermute | solution.py:218
  97.1 5.5 %collective-permute-start.6 = (bf16[128,512]{1,0:T(8,128)(2,1)S(1)}, bf16[128,512]{1,0:T(8,128)(2,1)S(1)}, u32[]{:S(2)}, u32[]{:S(2)}) collective-permute-start(bf16[128,512]{1,0:T(8,128)(2,1)S(1)} %get-tuple-element.47), channel_id=1, source_target_pairs={{0,6},{8,14},{16,22},{24,30},{32,38},{40,46},{48,54},{56,62},{64,7... | collective-permute-start | bytes 393224 | tf_op jit(solution)/shard_map/ppermute | solution.py:218
  105.8 1.3 collective-permute-done.5
  108.5 1.9 collective-permute-start.12
  110.4 9.0 %collective-permute-start.1 = (bf16[16,512]{1,0:T(8,128)(2,1)S(1)}, bf16[16,512]{1,0:T(8,128)(2,1)S(1)}, u32[]{:S(2)}, u32[]{:S(2)}) collective-permute-start(bf16[16,512]{1,0:T(8,128)(2,1)S(1)} %get-tuple-element.49), channel_id=1, source_target_pairs={{0,2},{8,10},{16,18},{24,26},{32,34},{40,42},{48,50},{56,58},{64,6... | collective-permute-start | bytes 49160 | tf_op jit(solution)/shard_map/ppermute | solution.py:218
  123.3 1.9 collective-permute-start.10
  126.6 7.5 %collective-permute-start.8 = (bf16[128,512]{1,0:T(8,128)(2,1)S(1)}, bf16[128,512]{1,0:T(8,128)(2,1)S(1)}, u32[]{:S(2)}, u32[]{:S(2)}) collective-permute-start(bf16[128,512]{1,0:T(8,128)(2,1)S(1)} %fusion.8.refs_0_), channel_id=1, source_target_pairs={{0,6},{2,0},{4,2},{6,4},{8,14},{10,8},{12,10},{14,12},{16,22},{18,... | collective-permute-start | bytes 393224 | tf_op jit(solution)/shard_map/ppermute | solution.py:236
  134.1 1.5 collective-permute-start.7
  138.1 2.6 %collective-permute-done.8.refs_2_ = bf16[128,512]{1,0:T(8,128)(2,1)S(1)} collective-permute-done((bf16[128,512]{1,0:T(8,128)(2,1)S(1)}, bf16[128,512]{1,0:T(8,128)(2,1)S(1)}, u32[]{:S(2)}, u32[]{:S(2)}) %collective-permute-start.8) | collective-permute-done | bytes 131104 | tf_op jit(solution)/shard_map/ppermute | solution.py:236
  142.0 8.4 %all-to-all-done.2.incoming = bf16[128,128,128]{2,1,0:T(8,128)(2,1)} async-done(((bf16[128,128,128]{2,1,0:T(8,128)(2,1)}), bf16[128,128,128]{2,1,0:T(8,128)(2,1)}, u32[]{:S(2)}, u32[]{:S(2)}) %all-to-all-start.2) | async-done | bytes 4194336 | tf_op jit(solution)/shard_map/all_to_all | solution.py:206
  150.4 6.0 %assemble.1.refs_18_ = f32[512,512]{1,0:T(8,128)S(1)} custom-call(s32[128]{0:T(128)S(1)} %reshape.112.tags, bf16[128,128,128]{2,1,0:T(8,128)(2,1)} %all-to-all-done.2.incoming, bf16[1,1024,512]{2,1,0:T(8,128)(2,1)S(1)} %copy-done), custom_call_target="tpu_custom_call" | custom-call | tf_op jit(solution)/shard_map/assemble/pallas_call | solution.py:94
  156.4 2.7 %convolution_convert_fusion.1 = bf16[512,512]{1,0:T(8,128)(2,1)} fusion(f32[512,512]{1,0:T(8,128)S(1)} %assemble.1.refs_18_, f32[512,512]{1,0:T(8,128)S(1)} %inverse.1), kind=kOutput, calls=%fused_computation.1 | convolution fusion | flops 1610874880 | bytes 2621440 | tf_op jit(solution)/shard_map/dot_general | solution.py:325
  159.0 9.5 %all-to-all-start.3 = ((bf16[32,16,512]{2,1,0:T(8,128)(2,1)}), bf16[32,16,512]{2,1,0:T(8,128)(2,1)S(1)}, u32[]{:S(2)}, u32[]{:S(2)}) async-start(bf16[32,16,512]{2,1,0:T(8,128)(2,1)} %bitcast.38), calls=%async_computation.3 | async-start | bytes 1048576 | tf_op jit(solution)/shard_map/all_to_all | solution.py:206
  169.7 6.1 %collective-permute-start.14 = (bf16[128,512]{1,0:T(8,128)(2,1)S(1)}, bf16[128,512]{1,0:T(8,128)(2,1)S(1)}, u32[]{:S(2)}, u32[]{:S(2)}) collective-permute-start(bf16[128,512]{1,0:T(8,128)(2,1)S(1)} %get-tuple-element.43), channel_id=1, source_target_pairs={{0,2},{8,10},{16,18},{24,26},{32,34},{40,42},{48,50},{56,58},{64,6... | collective-permute-start | bytes 393224 | tf_op jit(solution)/shard_map/ppermute | solution.py:218
  175.8 5.5 %collective-permute-start.16 = (bf16[128,512]{1,0:T(8,128)(2,1)S(1)}, bf16[128,512]{1,0:T(8,128)(2,1)S(1)}, u32[]{:S(2)}, u32[]{:S(2)}) collective-permute-start(bf16[128,512]{1,0:T(8,128)(2,1)S(1)} %get-tuple-element.44), channel_id=1, source_target_pairs={{0,6},{8,14},{16,22},{24,30},{32,38},{40,46},{48,54},{56,62},{64,7... | collective-permute-start | bytes 393224 | tf_op jit(solution)/shard_map/ppermute | solution.py:218
  182.6 1.3 collective-permute-done.16
  186.8 7.6 %collective-permute-start.25 = (bf16[16,512]{1,0:T(8,128)(2,1)}, bf16[16,512]{1,0:T(8,128)(2,1)S(1)}, u32[]{:S(2)}, u32[]{:S(2)}) collective-permute-start(bf16[16,512]{1,0:T(8,128)(2,1)} %get-tuple-element.39), channel_id=1, source_target_pairs={{0,3},{8,11},{16,19},{24,27},{32,35},{40,43},{48,51},{56,59},{64,6... | collective-permute-start | bytes 49160 | tf_op jit(solution)/shard_map/ppermute | solution.py:218
  194.4 3.7 %collective-permute-start.27 = (bf16[16,512]{1,0:T(8,128)(2,1)}, bf16[16,512]{1,0:T(8,128)(2,1)S(1)}, u32[]{:S(2)}, u32[]{:S(2)}) collective-permute-start(bf16[16,512]{1,0:T(8,128)(2,1)} %get-tuple-element.40), channel_id=1, source_target_pairs={{0,7},{8,15},{16,23},{24,31},{32,39},{40,47},{48,55},{56,63},{64,7... | collective-permute-start | bytes 49160 | tf_op jit(solution)/shard_map/ppermute | solution.py:218
  203.7 5.6 %all-to-all-start.4 = ((bf16[32,16,512]{2,1,0:T(8,128)(2,1)}), bf16[32,16,512]{2,1,0:T(8,128)(2,1)S(1)}, u32[]{:S(2)}, u32[]{:S(2)}) async-start(bf16[32,16,512]{2,1,0:T(8,128)(2,1)} %broadcast_in_dim.36), calls=%async_computation.4 | async-start | bytes 1048576 | tf_op jit(solution)/shard_map/all_to_all | solution.py:206
  209.3 3.5 %collective-permute-start.23 = (bf16[128,512]{1,0:T(8,128)(2,1)S(1)}, bf16[128,512]{1,0:T(8,128)(2,1)S(1)}, u32[]{:S(2)}, u32[]{:S(2)}) collective-permute-start(bf16[128,512]{1,0:T(8,128)(2,1)S(1)} %fusion.5.refs_8_), channel_id=1, source_target_pairs={{0,1},{2,3},{4,5},{6,7},{8,9},{10,11},{12,13},{14,15},{16,17},{18,... | collective-permute-start | bytes 393224 | tf_op jit(solution)/shard_map/ppermute | solution.py:236
  212.8 1.9 collective-permute-start.22
  216.0 5.3 %collective-permute-start.20 = (bf16[128,512]{1,0:T(8,128)(2,1)S(1)}, bf16[128,512]{1,0:T(8,128)(2,1)S(1)}, u32[]{:S(2)}, u32[]{:S(2)}) collective-permute-start(bf16[128,512]{1,0:T(8,128)(2,1)S(1)} %fusion.5.refs_8_), channel_id=1, source_target_pairs={{0,4},{2,6},{4,0},{6,2},{8,12},{10,14},{12,8},{14,10},{16,20},{18,... | collective-permute-start | bytes 393224 | tf_op jit(solution)/shard_map/ppermute | solution.py:236
  223.3 6.0 %collective-permute-start.18 = (bf16[128,512]{1,0:T(8,128)(2,1)S(1)}, bf16[128,512]{1,0:T(8,128)(2,1)S(1)}, u32[]{:S(2)}, u32[]{:S(2)}) collective-permute-start(bf16[128,512]{1,0:T(8,128)(2,1)S(1)} %fusion.5.refs_8_), channel_id=1, source_target_pairs={{0,6},{2,0},{4,2},{6,4},{8,14},{10,8},{12,10},{14,12},{16,22},{18,... | collective-permute-start | bytes 393224 | tf_op jit(solution)/shard_map/ppermute | solution.py:236
  243.5 1.7 finish.1
  (125 shorter events, 45.8 us)
Async XLA Ops:
  1.9 27.1 %all-to-all-start = ((bf16[32,16,512]{2,1,0:T(8,128)(2,1)}), bf16[32,16,512]{2,1,0:T(8,128)(2,1)S(1)}, u32[]{:S(2)}, u32[]{:S(2)}) async-start(bf16[32,16,512]{2,1,0:T(8,128)(2,1)} %bitcast.3), calls=%async_computation | async-start | bytes 1048576 | tf_op jit(solution)/shard_map/all_to_all | solution.py:206
  17.9 3.0 %collective-permute-start = (s32[32,2]{0,1:T(2,128)S(1)}, s32[32,2]{0,1:T(2,128)S(1)}, u32[]{:S(2)}, u32[]{:S(2)}) collective-permute-start(s32[32,2]{0,1:T(2,128)S(1)} %copy.20), channel_id=1, source_target_pairs={{0,256},{256,0},{1,257},{257,1},{2,258},{258,2},{3,259},{259,3},{4... | collective-permute-start | bytes 776 | tf_op jit(solution)/shard_map/ppermute | solution.py:306
  50.9 99.5 %all-to-all-start.2 = ((bf16[128,128,128]{2,1,0:T(8,128)(2,1)}), bf16[128,128,128]{2,1,0:T(8,128)(2,1)}, u32[]{:S(2)}, u32[]{:S(2)}) async-start(bf16[128,128,128]{2,1,0:T(8,128)(2,1)} %get-tuple-element.24), calls=%async_computation.2 | async-start | bytes 8388608 | tf_op jit(solution)/shard_map/all_to_all | solution.py:206
  91.0 13.6 %collective-permute-start.4 = (bf16[128,512]{1,0:T(8,128)(2,1)S(1)}, bf16[128,512]{1,0:T(8,128)(2,1)S(1)}, u32[]{:S(2)}, u32[]{:S(2)}) collective-permute-start(bf16[128,512]{1,0:T(8,128)(2,1)S(1)} %get-tuple-element.46), channel_id=1, source_target_pairs={{0,2},{8,10},{16,18},{24,26},{32,34},{40,42},{48,50},{56,58},{64,6... | collective-permute-start | bytes 393224 | tf_op jit(solution)/shard_map/ppermute | solution.py:218
  97.1 8.8 %collective-permute-start.6 = (bf16[128,512]{1,0:T(8,128)(2,1)S(1)}, bf16[128,512]{1,0:T(8,128)(2,1)S(1)}, u32[]{:S(2)}, u32[]{:S(2)}) collective-permute-start(bf16[128,512]{1,0:T(8,128)(2,1)S(1)} %get-tuple-element.47), channel_id=1, source_target_pairs={{0,6},{8,14},{16,22},{24,30},{32,38},{40,46},{48,54},{56,62},{64,7... | collective-permute-start | bytes 393224 | tf_op jit(solution)/shard_map/ppermute | solution.py:218
  102.6 4.5 %collective-permute-start.5 = (bf16[128,512]{1,0:T(8,128)(2,1)S(1)}, bf16[128,512]{1,0:T(8,128)(2,1)S(1)}, u32[]{:S(2)}, u32[]{:S(2)}) collective-permute-start(bf16[128,512]{1,0:T(8,128)(2,1)S(1)} %get-tuple-element.48), channel_id=1, source_target_pairs={{0,4},{8,12},{16,20},{24,28},{32,36},{40,44},{48,52},{56,60},{64,6... | collective-permute-start | bytes 393224 | tf_op jit(solution)/shard_map/ppermute | solution.py:218
  107.2 19.4 %collective-permute-start.13 = (bf16[128,512]{1,0:T(8,128)(2,1)S(1)}, bf16[128,512]{1,0:T(8,128)(2,1)S(1)}, u32[]{:S(2)}, u32[]{:S(2)}) collective-permute-start(bf16[128,512]{1,0:T(8,128)(2,1)S(1)} %fusion.8.refs_0_), channel_id=1, source_target_pairs={{0,1},{2,3},{4,5},{6,7},{8,9},{10,11},{12,13},{14,15},{16,17},{18,... | collective-permute-start | bytes 393224 | tf_op jit(solution)/shard_map/ppermute | solution.py:236
  108.5 25.6 %collective-permute-start.12 = (bf16[128,512]{1,0:T(8,128)(2,1)S(1)}, bf16[128,512]{1,0:T(8,128)(2,1)S(1)}, u32[]{:S(2)}, u32[]{:S(2)}) collective-permute-start(bf16[128,512]{1,0:T(8,128)(2,1)S(1)} %fusion.8.refs_0_), channel_id=1, source_target_pairs={{0,2},{2,4},{4,6},{6,0},{8,10},{10,12},{12,14},{14,8},{16,18},{18,... | collective-permute-start | bytes 393224 | tf_op jit(solution)/shard_map/ppermute | solution.py:236
  110.4 11.6 %collective-permute-start.1 = (bf16[16,512]{1,0:T(8,128)(2,1)S(1)}, bf16[16,512]{1,0:T(8,128)(2,1)S(1)}, u32[]{:S(2)}, u32[]{:S(2)}) collective-permute-start(bf16[16,512]{1,0:T(8,128)(2,1)S(1)} %get-tuple-element.49), channel_id=1, source_target_pairs={{0,2},{8,10},{16,18},{24,26},{32,34},{40,42},{48,50},{56,58},{64,6... | collective-permute-start | bytes 49160 | tf_op jit(solution)/shard_map/ppermute | solution.py:218
  119.4 3.9 %collective-permute-start.3 = (bf16[16,512]{1,0:T(8,128)(2,1)S(1)}, bf16[16,512]{1,0:T(8,128)(2,1)S(1)}, u32[]{:S(2)}, u32[]{:S(2)}) collective-permute-start(bf16[16,512]{1,0:T(8,128)(2,1)S(1)} %get-tuple-element.50), channel_id=1, source_target_pairs={{0,6},{8,14},{16,22},{24,30},{32,38},{40,46},{48,54},{56,62},{64,7... | collective-permute-start | bytes 49160 | tf_op jit(solution)/shard_map/ppermute | solution.py:218
  120.7 4.6 %collective-permute-start.2 = (bf16[16,512]{1,0:T(8,128)(2,1)S(1)}, bf16[16,512]{1,0:T(8,128)(2,1)S(1)}, u32[]{:S(2)}, u32[]{:S(2)}) collective-permute-start(bf16[16,512]{1,0:T(8,128)(2,1)S(1)} %get-tuple-element.51), channel_id=1, source_target_pairs={{0,4},{8,12},{16,20},{24,28},{32,36},{40,44},{48,52},{56,60},{64,6... | collective-permute-start | bytes 49160 | tf_op jit(solution)/shard_map/ppermute | solution.py:218
  122.0 14.2 %collective-permute-start.11 = (bf16[128,512]{1,0:T(8,128)(2,1)S(1)}, bf16[128,512]{1,0:T(8,128)(2,1)S(1)}, u32[]{:S(2)}, u32[]{:S(2)}) collective-permute-start(bf16[128,512]{1,0:T(8,128)(2,1)S(1)} %fusion.8.refs_0_), channel_id=1, source_target_pairs={{0,3},{2,5},{4,7},{6,1},{8,11},{10,13},{12,15},{14,9},{16,19},{18,... | collective-permute-start | bytes 393224 | tf_op jit(solution)/shard_map/ppermute | solution.py:236
  123.3 13.5 %collective-permute-start.10 = (bf16[128,512]{1,0:T(8,128)(2,1)S(1)}, bf16[128,512]{1,0:T(8,128)(2,1)S(1)}, u32[]{:S(2)}, u32[]{:S(2)}) collective-permute-start(bf16[128,512]{1,0:T(8,128)(2,1)S(1)} %fusion.8.refs_0_), channel_id=1, source_target_pairs={{0,4},{2,6},{4,0},{6,2},{8,12},{10,14},{12,8},{14,10},{16,20},{18,... | collective-permute-start | bytes 393224 | tf_op jit(solution)/shard_map/ppermute | solution.py:236
  125.3 12.2 %collective-permute-start.9 = (bf16[128,512]{1,0:T(8,128)(2,1)S(1)}, bf16[128,512]{1,0:T(8,128)(2,1)S(1)}, u32[]{:S(2)}, u32[]{:S(2)}) collective-permute-start(bf16[128,512]{1,0:T(8,128)(2,1)S(1)} %fusion.8.refs_0_), channel_id=1, source_target_pairs={{0,5},{2,7},{4,1},{6,3},{8,13},{10,15},{12,9},{14,11},{16,21},{18,... | collective-permute-start | bytes 393224 | tf_op jit(solution)/shard_map/ppermute | solution.py:236
  126.6 14.1 %collective-permute-start.8 = (bf16[128,512]{1,0:T(8,128)(2,1)S(1)}, bf16[128,512]{1,0:T(8,128)(2,1)S(1)}, u32[]{:S(2)}, u32[]{:S(2)}) collective-permute-start(bf16[128,512]{1,0:T(8,128)(2,1)S(1)} %fusion.8.refs_0_), channel_id=1, source_target_pairs={{0,6},{2,0},{4,2},{6,4},{8,14},{10,8},{12,10},{14,12},{16,22},{18,... | collective-permute-start | bytes 393224 | tf_op jit(solution)/shard_map/ppermute | solution.py:236
  134.1 7.3 %collective-permute-start.7 = (bf16[128,512]{1,0:T(8,128)(2,1)S(1)}, bf16[128,512]{1,0:T(8,128)(2,1)S(1)}, u32[]{:S(2)}, u32[]{:S(2)}) collective-permute-start(bf16[128,512]{1,0:T(8,128)(2,1)S(1)} %fusion.8.refs_0_), channel_id=1, source_target_pairs={{0,7},{2,1},{4,3},{6,5},{8,15},{10,9},{12,11},{14,13},{16,23},{18,... | collective-permute-start | bytes 393224 | tf_op jit(solution)/shard_map/ppermute | solution.py:236
  159.0 27.1 %all-to-all-start.3 = ((bf16[32,16,512]{2,1,0:T(8,128)(2,1)}), bf16[32,16,512]{2,1,0:T(8,128)(2,1)S(1)}, u32[]{:S(2)}, u32[]{:S(2)}) async-start(bf16[32,16,512]{2,1,0:T(8,128)(2,1)} %bitcast.38), calls=%async_computation.3 | async-start | bytes 1048576 | tf_op jit(solution)/shard_map/all_to_all | solution.py:206
  169.7 12.9 %collective-permute-start.14 = (bf16[128,512]{1,0:T(8,128)(2,1)S(1)}, bf16[128,512]{1,0:T(8,128)(2,1)S(1)}, u32[]{:S(2)}, u32[]{:S(2)}) collective-permute-start(bf16[128,512]{1,0:T(8,128)(2,1)S(1)} %get-tuple-element.43), channel_id=1, source_target_pairs={{0,2},{8,10},{16,18},{24,26},{32,34},{40,42},{48,50},{56,58},{64,6... | collective-permute-start | bytes 393224 | tf_op jit(solution)/shard_map/ppermute | solution.py:218
  175.8 8.2 %collective-permute-start.16 = (bf16[128,512]{1,0:T(8,128)(2,1)S(1)}, bf16[128,512]{1,0:T(8,128)(2,1)S(1)}, u32[]{:S(2)}, u32[]{:S(2)}) collective-permute-start(bf16[128,512]{1,0:T(8,128)(2,1)S(1)} %get-tuple-element.44), channel_id=1, source_target_pairs={{0,6},{8,14},{16,22},{24,30},{32,38},{40,46},{48,54},{56,62},{64,7... | collective-permute-start | bytes 393224 | tf_op jit(solution)/shard_map/ppermute | solution.py:218
  181.3 3.9 %collective-permute-start.15 = (bf16[128,512]{1,0:T(8,128)(2,1)S(1)}, bf16[128,512]{1,0:T(8,128)(2,1)S(1)}, u32[]{:S(2)}, u32[]{:S(2)}) collective-permute-start(bf16[128,512]{1,0:T(8,128)(2,1)S(1)} %get-tuple-element.45), channel_id=1, source_target_pairs={{0,4},{8,12},{16,20},{24,28},{32,36},{40,44},{48,52},{56,60},{64,6... | collective-permute-start | bytes 393224 | tf_op jit(solution)/shard_map/ppermute | solution.py:218
  186.8 13.9 %collective-permute-start.25 = (bf16[16,512]{1,0:T(8,128)(2,1)}, bf16[16,512]{1,0:T(8,128)(2,1)S(1)}, u32[]{:S(2)}, u32[]{:S(2)}) collective-permute-start(bf16[16,512]{1,0:T(8,128)(2,1)} %get-tuple-element.39), channel_id=1, source_target_pairs={{0,3},{8,11},{16,19},{24,27},{32,35},{40,43},{48,51},{56,59},{64,6... | collective-permute-start | bytes 49160 | tf_op jit(solution)/shard_map/ppermute | solution.py:218
  194.4 6.3 %collective-permute-start.27 = (bf16[16,512]{1,0:T(8,128)(2,1)}, bf16[16,512]{1,0:T(8,128)(2,1)S(1)}, u32[]{:S(2)}, u32[]{:S(2)}) collective-permute-start(bf16[16,512]{1,0:T(8,128)(2,1)} %get-tuple-element.40), channel_id=1, source_target_pairs={{0,7},{8,15},{16,23},{24,31},{32,39},{40,47},{48,55},{56,63},{64,7... | collective-permute-start | bytes 49160 | tf_op jit(solution)/shard_map/ppermute | solution.py:218
  198.1 2.9 %collective-permute-start.26 = (bf16[16,512]{1,0:T(8,128)(2,1)}, bf16[16,512]{1,0:T(8,128)(2,1)S(1)}, u32[]{:S(2)}, u32[]{:S(2)}) collective-permute-start(bf16[16,512]{1,0:T(8,128)(2,1)} %get-tuple-element.41), channel_id=1, source_target_pairs={{0,5},{8,13},{16,21},{24,29},{32,37},{40,45},{48,53},{56,61},{64,6... | collective-permute-start | bytes 49160 | tf_op jit(solution)/shard_map/ppermute | solution.py:218
  199.4 2.7 %collective-permute-start.24 = (bf16[16,512]{1,0:T(8,128)(2,1)S(1)}, bf16[16,512]{1,0:T(8,128)(2,1)S(1)}, u32[]{:S(2)}, u32[]{:S(2)}) collective-permute-start(bf16[16,512]{1,0:T(8,128)(2,1)S(1)} %get-tuple-element.42), channel_id=1, source_target_pairs={{0,1},{8,9},{16,17},{24,25},{32,33},{40,41},{48,49},{56,57},{64,65... | collective-permute-start | bytes 49160 | tf_op jit(solution)/shard_map/ppermute | solution.py:218
  203.7 31.6 %all-to-all-start.4 = ((bf16[32,16,512]{2,1,0:T(8,128)(2,1)}), bf16[32,16,512]{2,1,0:T(8,128)(2,1)S(1)}, u32[]{:S(2)}, u32[]{:S(2)}) async-start(bf16[32,16,512]{2,1,0:T(8,128)(2,1)} %broadcast_in_dim.36), calls=%async_computation.4 | async-start | bytes 1048576 | tf_op jit(solution)/shard_map/all_to_all | solution.py:206
  209.3 13.3 %collective-permute-start.23 = (bf16[128,512]{1,0:T(8,128)(2,1)S(1)}, bf16[128,512]{1,0:T(8,128)(2,1)S(1)}, u32[]{:S(2)}, u32[]{:S(2)}) collective-permute-start(bf16[128,512]{1,0:T(8,128)(2,1)S(1)} %fusion.5.refs_8_), channel_id=1, source_target_pairs={{0,1},{2,3},{4,5},{6,7},{8,9},{10,11},{12,13},{14,15},{16,17},{18,... | collective-permute-start | bytes 393224 | tf_op jit(solution)/shard_map/ppermute | solution.py:236
  212.8 16.5 %collective-permute-start.22 = (bf16[128,512]{1,0:T(8,128)(2,1)S(1)}, bf16[128,512]{1,0:T(8,128)(2,1)S(1)}, u32[]{:S(2)}, u32[]{:S(2)}) collective-permute-start(bf16[128,512]{1,0:T(8,128)(2,1)S(1)} %fusion.5.refs_8_), channel_id=1, source_target_pairs={{0,2},{2,4},{4,6},{6,0},{8,10},{10,12},{12,14},{14,8},{16,18},{18,... | collective-permute-start | bytes 393224 | tf_op jit(solution)/shard_map/ppermute | solution.py:236
  214.7 17.3 %collective-permute-start.21 = (bf16[128,512]{1,0:T(8,128)(2,1)S(1)}, bf16[128,512]{1,0:T(8,128)(2,1)S(1)}, u32[]{:S(2)}, u32[]{:S(2)}) collective-permute-start(bf16[128,512]{1,0:T(8,128)(2,1)S(1)} %fusion.5.refs_8_), channel_id=1, source_target_pairs={{0,3},{2,5},{4,7},{6,1},{8,11},{10,13},{12,15},{14,9},{16,19},{18,... | collective-permute-start | bytes 393224 | tf_op jit(solution)/shard_map/ppermute | solution.py:236
  216.0 16.7 %collective-permute-start.20 = (bf16[128,512]{1,0:T(8,128)(2,1)S(1)}, bf16[128,512]{1,0:T(8,128)(2,1)S(1)}, u32[]{:S(2)}, u32[]{:S(2)}) collective-permute-start(bf16[128,512]{1,0:T(8,128)(2,1)S(1)} %fusion.5.refs_8_), channel_id=1, source_target_pairs={{0,4},{2,6},{4,0},{6,2},{8,12},{10,14},{12,8},{14,10},{16,20},{18,... | collective-permute-start | bytes 393224 | tf_op jit(solution)/shard_map/ppermute | solution.py:236
  221.3 12.0 %collective-permute-start.19 = (bf16[128,512]{1,0:T(8,128)(2,1)S(1)}, bf16[128,512]{1,0:T(8,128)(2,1)S(1)}, u32[]{:S(2)}, u32[]{:S(2)}) collective-permute-start(bf16[128,512]{1,0:T(8,128)(2,1)S(1)} %fusion.5.refs_8_), channel_id=1, source_target_pairs={{0,5},{2,7},{4,1},{6,3},{8,13},{10,15},{12,9},{14,11},{16,21},{18,... | collective-permute-start | bytes 393224 | tf_op jit(solution)/shard_map/ppermute | solution.py:236
  223.3 10.7 %collective-permute-start.18 = (bf16[128,512]{1,0:T(8,128)(2,1)S(1)}, bf16[128,512]{1,0:T(8,128)(2,1)S(1)}, u32[]{:S(2)}, u32[]{:S(2)}) collective-permute-start(bf16[128,512]{1,0:T(8,128)(2,1)S(1)} %fusion.5.refs_8_), channel_id=1, source_target_pairs={{0,6},{2,0},{4,2},{6,4},{8,14},{10,8},{12,10},{14,12},{16,22},{18,... | collective-permute-start | bytes 393224 | tf_op jit(solution)/shard_map/ppermute | solution.py:236
  230.0 4.7 %collective-permute-start.17 = (bf16[128,512]{1,0:T(8,128)(2,1)S(1)}, bf16[128,512]{1,0:T(8,128)(2,1)S(1)}, u32[]{:S(2)}, u32[]{:S(2)}) collective-permute-start(bf16[128,512]{1,0:T(8,128)(2,1)S(1)} %fusion.5.refs_8_), channel_id=1, source_target_pairs={{0,7},{2,1},{4,3},{6,5},{8,15},{10,9},{12,11},{14,13},{16,23},{18,... | collective-permute-start | bytes 393224 | tf_op jit(solution)/shard_map/ppermute | solution.py:236
  (27 other events, 358.8 us)

commit v4 on v3

--- a/solution.py
+++ b/solution.py
@@ -89,7 +89,7 @@
 
 
 def assemble(tags, incoming, window):
-    steps = 8
+    steps = 1
     blocks = incoming.shape[0] // steps
     return pl.pallas_call(
         assemble_kernel,
@@ -162,19 +162,24 @@
     return lax.dot_general(a, b, (dims, ((), ())), precision=HI, preferred_element_type=F32)
 
 
-def inverse_kernel(pivot, out, work, rest):
-    n = pivot.shape[0]
-    blocks = n // SB
+def lower_blocks(n):
+    return [(i, j) for i in range(n // SB) for j in range(i + 1)]
+
+
+def inverse_kernel(packed, out, work, rest):
+    n = out.shape[0]
     row_at = lax.broadcasted_iota(jnp.int32, (n, n), 0)
     col_at = lax.broadcasted_iota(jnp.int32, (n, n), 1)
-    work[...] = pivot[...].astype(F32)
+    work[...] = jnp.zeros_like(work)
+    for at, (i, j) in enumerate(lower_blocks(n)):
+        work[i * SB : (i + 1) * SB, j * SB : (j + 1) * SB] = packed[
+            at * SB : (at + 1) * SB, :
+        ].astype(F32)
     rest[...] = jnp.where(row_at == col_at, 1.0, 0.0).astype(F32)
 
     def step(k, _):
         here = pl.ds(pl.multiple_of(k * SB, SB), SB)
-        block = work[here, here]
-        at = [lax.broadcasted_iota(jnp.int32, block.shape, d) for d in (0, 1)]
-        small = invert_block(jnp.where(at[0] >= at[1], block, block.T))
+        small = invert_block(work[here, here])
         panel = dot(work[:, here], small, ((1,), (1,)))
         below = lax.broadcasted_iota(jnp.int32, (n, SB), 0) >= (k + 1) * SB
         panel = jnp.where(below, panel, 0.0)
@@ -184,11 +189,11 @@
         rest[...] = rest[...] - dot(panel, solved, ((1,), (0,)))
         return 0
 
-    lax.fori_loop(0, blocks, step, 0)
-
-
-def inverse_factor(pivot):
-    n = pivot.shape[0]
+    lax.fori_loop(0, n // SB, step, 0)
+
+
+def inverse_factor(packed):
+    n = TILE
     vmem = pl.BlockSpec(memory_space=pltpu.VMEM)
     return pl.pallas_call(
         inverse_kernel,
@@ -199,7 +204,24 @@
         compiler_params=pltpu.CompilerParams(vmem_limit_bytes=24 << 20),
         cost_estimate=pl.CostEstimate(flops=4 * n**3, bytes_accessed=6 * n * n, transcendentals=0),
         name="inverse",
-    )(pivot)
+    )(packed)
+
+
+def pack_kernel(base, out):
+    for at, (i, j) in enumerate(lower_blocks(TILE)):
+        out[at * SB : (at + 1) * SB, :] = base[0, i * SB : (i + 1) * SB, j * SB : (j + 1) * SB]
+
+
+def pack_pivot(window):
+    rows = len(lower_blocks(TILE)) * SB
+    return pl.pallas_call(
+        pack_kernel,
+        out_shape=jax.ShapeDtypeStruct((rows, SB), window.dtype),
+        grid=(1,),
+        in_specs=[pl.BlockSpec((1, TILE, TILE), lambda i: (0, 0, 0))],
+        out_specs=pl.BlockSpec((rows, SB), lambda i: (0, 0)),
+        name="pack",
+    )(window)
 
 
 def swap(block, axis):
@@ -239,52 +261,72 @@
 
 def finish_kernel(size, state, *refs):
     halves = refs[:size], refs[size : 2 * size]
-    partner, base, added, out = refs[2 * size :]
+    partner, base, added, out, parts, sem = refs[2 * size :]
     column = state[0]
     step = size // HOLDERS
     rows = TILE // HOLDERS
     shift = lax.rem(step - lax.rem(column, step), step)
     first = lax.div(column + shift, step)
     for s in range(step):
-        for k in range(HOLDERS):
-            source = lax.rem(first + k, HOLDERS)
-            at = pl.ds(pl.multiple_of(source * rows, rows), rows)
-            under = pl.ds(pl.multiple_of(source * rows + TILE, rows), rows)
-            upper_part, under_part = halves[0][k * step + s], halves[1][k * step + s]
-
-            @pl.when((shift == s) & (column == 0))
-            def _():
-                out[0, at, :] = upper_part[...]
-                out[0, under, :] = under_part[...]
-
-            @pl.when((shift == s) & (column != 0))
-            def _():
-                def product(part):
-                    return lax.dot_general(
-                        part[...],
-                        partner[...],
-                        (((1,), (1,)), ((), ())),
-                        preferred_element_type=F32,
-                    )
-
-                upper = base[0, at, :].astype(F32) - state[1].astype(F32) * product(upper_part)
-                out[0, at, :] = upper.astype(BF16)
-                lower = added[at, :] - state[2].astype(F32) * product(under_part)
-                out[0, under, :] = lower.astype(BF16)
+
+        @pl.when(shift == s)
+        def _():
+            copies = [
+                pltpu.make_async_copy(
+                    halves[h][k * step + s], parts.at[h, k], sem.at[h * HOLDERS + k]
+                )
+                for h in range(2)
+                for k in range(HOLDERS)
+            ]
+            for copy in copies:
+                copy.start()
+            for copy in copies:
+                copy.wait()
+
+    for k in range(HOLDERS):
+        source = lax.rem(first + k, HOLDERS)
+        at = pl.ds(pl.multiple_of(source * rows, rows), rows)
+        under = pl.ds(pl.multiple_of(source * rows + TILE, rows), rows)
+
+        @pl.when(column == 0)
+        def _():
+            out[0, at, :] = parts[0, k]
+            out[0, under, :] = parts[1, k]
+
+        @pl.when(column != 0)
+        def _():
+            def product(part):
+                return lax.dot_general(
+                    part, partner[...], (((1,), (1,)), ((), ())), preferred_element_type=F32
+                )
+
+            upper = base[0, at, :].astype(F32) - state[1].astype(F32) * product(parts[0, k])
+            out[0, at, :] = upper.astype(BF16)
+            lower = added[at, :] - state[2].astype(F32) * product(parts[1, k])
+            out[0, under, :] = lower.astype(BF16)
 
 
 def finish(state, upper, under, partner, window, added):
     size = len(upper)
-    vmem = pl.BlockSpec(memory_space=pltpu.VMEM)
+
+    def whole(x):
+        return pl.BlockSpec(x.shape, lambda i: (0,) * x.ndim)
+
+    tile = pl.BlockSpec((1, TILE, TILE), lambda i: (0, 0, 0))
+    out = jax.ShapeDtypeStruct((1, 2 * TILE, TILE), BF16)
     return pl.pallas_call(
         functools.partial(finish_kernel, size),
-        out_shape=jax.ShapeDtypeStruct((1, 2 * TILE, TILE), BF16),
+        out_shape=out,
         grid=(1,),
         in_specs=[pl.BlockSpec(memory_space=pltpu.SMEM)]
-        + [vmem] * (2 * size + 1)
-        + [pl.BlockSpec((1, TILE, TILE), lambda i: (0, 0, 0)), vmem],
-        out_specs=vmem,
-        compiler_params=pltpu.CompilerParams(vmem_limit_bytes=24 << 20),
+        + [pl.BlockSpec(memory_space=pl.ANY)] * (2 * size)
+        + [whole(partner), tile, whole(added)],
+        out_specs=whole(out),
+        scratch_shapes=[
+            pltpu.VMEM((2, HOLDERS, TILE // HOLDERS, TILE), BF16),
+            pltpu.SemaphoreType.DMA((2 * HOLDERS,)),
+        ],
+        compiler_params=pltpu.CompilerParams(vmem_limit_bytes=56 << 20),
         name="finish",
     )(state, *upper, *under, partner, window, added)
 
@@ -296,27 +338,24 @@
     front = lax.axis_index("front")
     column = lax.axis_index("col")
     first = window[0, :TILE]
-    part_rows = TILE // rows_axis
-    marks_each = fronts * CAP
-    even_raw = swap(first.reshape(rows_axis, part_rows, TILE), "row")[: columns // 2]
+    packed = pack_pivot(window).reshape(rows_axis, -1, SB)
+    share = packed.shape[1]
+    pivot_part = swap(packed, "row")[0]
     outgoing, marks = place(routes[:, 0], slots, children, fronts * rows_axis)
     marks = marks.reshape(fronts, rows_axis, CAP)
     near = jnp.where(front == 0, marks[0], marks[1])
     far = jnp.where(front == 0, marks[1], marks[0])
     far = lax.ppermute(far, "front", [(0, 1), (1, 0)])
-    both = jnp.concatenate([near, far], axis=1).astype(BF16)
-    both = jnp.pad(both, ((0, 0), (TILE - marks_each, 0)))[:, None, :]
-    place_row = lax.broadcasted_iota(jnp.int32, (rows_axis, part_rows, TILE), 1)
-    place_col = lax.broadcasted_iota(jnp.int32, (rows_axis, part_rows, TILE), 2)
-    spread = jnp.where(
-        (place_row == 0) & (place_col >= TILE - marks_each), both, even_raw[0][None]
-    )
-    pivot = swap(spread, "row")
-    got = pivot[:, 0, TILE - marks_each :].astype(jnp.int32).reshape(rows_axis, fronts, CAP)
+    both = jnp.concatenate([near, far], axis=1).astype(BF16)[:, None, :]
+    both = jnp.pad(both, ((0, 0), (share, 7), (0, SB - both.shape[2])))
+    piece = jnp.pad(pivot_part, ((0, 8), (0, 0)))[None]
+    row_at = lax.broadcasted_iota(jnp.int32, both.shape, 1)
+    arrived = swap(jnp.where(row_at < share, piece, both), "row")
+    got = arrived[:, share, : fronts * CAP].astype(jnp.int32).reshape(rows_axis, fronts, CAP)
     near, far = got[:, 0], got[:, 1]
     tags = jnp.stack([jnp.where(front == 0, near, far), jnp.where(front == 0, far, near)])
     tags = tags.reshape(-1)
-    pivot = pivot.reshape(TILE, TILE)
+    pivot = arrived[:, :share].reshape(-1, SB)
     outgoing, tags, pivot = lax.optimization_barrier((outgoing, tags, pivot))
     incoming = swap(outgoing, ("front", "row"))
     inverse = inverse_factor(pivot)
@@ -326,22 +365,26 @@
             rows.astype(F32), inverse, (((1,), (1,)), ((), ())), precision=HI
         ).astype(BF16)
 
-    even = solve(even_raw.reshape(-1, TILE)).reshape(even_raw.shape)
-    even_part = hand_out(list(even), "col", range(0, columns, 2))
-    upper = from_holders(to_holders(solve(first)))
-    incoming, even_part, upper = lax.optimization_barrier((incoming, even_part, upper))
+    def to_plane(lower, odd):
+        pairs = [
+            ((c // 2) * columns, (c // 2) * columns + c) for c in range(max(odd, 1), columns) if c % 2 == odd
+        ]
+        return lax.ppermute(lower, ("row", "col"), pairs)
+
+    lower_first = solve(first)
+    even = to_plane(lower_first, 0)
+    upper = from_holders(to_holders(lower_first))
+    incoming, even, upper = lax.optimization_barrier((incoming, even, upper))
     added = assemble(tags, incoming, window)
     lower_second = solve(added)
-    odd = swap(lower_second.reshape(rows_axis, part_rows, TILE), "row")
-    under = to_holders(lower_second)
-    odd, under = lax.optimization_barrier((odd, under))
-    odd_part = hand_out(list(odd[: columns // 2]), "col", range(1, columns, 2))
+    odd = to_plane(lower_second, 1)
+    piece = jnp.where(column % 2 == 0, even, odd)
+    piece, under = lax.optimization_barrier((piece, to_holders(lower_second)))
     under = from_holders(under)
-    partner_part = jnp.where(column % 2 == 0, even_part, odd_part)
-    partner = swap(
-        jnp.broadcast_to(partner_part[None], (rows_axis,) + partner_part.shape), "row"
-    ).reshape(TILE, TILE)
-
+    got = swap(piece.reshape(rows_axis, -1, TILE), "row")
+    got, *under[: HOLDERS + 1] = lax.optimization_barrier((got, *under[: HOLDERS + 1]))
+    owned = lax.dynamic_index_in_dim(got, column // 2, 0)
+    partner = swap(jnp.broadcast_to(owned, got.shape), "row").reshape(TILE, TILE)
     state = jnp.concatenate([jnp.full((1,), column, jnp.int32), pattern[0, :, 0]])
     return finish(state, upper, under, partner, window, added)
 

time: 247 us -> 238 us (0.964)
  the two profiles are of different devices: /device:TPU:2 before, /device:TPU:8 now
where the time goes in v4:
time: 238 us; the launch traced here: 237 us
  starting transfers between devices  107 us (45%)
  waiting for transfers between devices  50.2 us (21%)
  Pallas kernels  47 us (20%)
  blocking collectives  20 us (8%)
  local copies, waits for them, and re-layouts  5.38 us (2%)
  other arithmetic  4.26 us (2%)
  matrix products  2.94 us (1%)
    all_to_all x4, starting transfers between devices, swap(): return lax.all_to_all(block, axis, split_axis=0, concat_axis=0, tiled=True)  37.7 us
    ppermute x14, starting transfers between devices, from_holders(): lax.ppermute(mine, 'col', [(i, (i - t) % size) for i in column_holders()])  37.2 us
    pallas_call x1, Pallas kernels, inverse_factor(): pl.pallas_call(inverse_kernel, out_shape=jax.ShapeDtypeStruct((n, n), F32...  32.2 us
    ppermute x6, starting transfers between devices, hand_out(): mine = mine + lax.ppermute(part, axis, [(0, device)])  28.5 us
    ppermute x14, waiting for transfers between devices, from_holders(): lax.ppermute(mine, 'col', [(i, (i - t) % size) for i in column_holders()])  23.1 us
    all_to_all x1, blocking collectives, swap(): return lax.all_to_all(block, axis, split_axis=0, concat_axis=0, tiled=True)  20 us
    all_to_all x4, waiting for transfers between devices, swap(): return lax.all_to_all(block, axis, split_axis=0, concat_axis=0, tiled=True)  18.6 us
    ppermute x6, waiting for transfers between devices, hand_out(): mine = mine + lax.ppermute(part, axis, [(0, device)])  7.45 us
  transfers between devices with their start and end apart: 27, of which 17 were waited for; matrix products, arithmetic and copies ran while one was open for 3% of the time, Pallas kernels for 16%

profile of v4, /device:TPU:8, one launch (start us, length us, event | category | flops | bytes accessed | tf_op | source)
XLA Modules:
  0.0 237.2 jit_solution(13713501501226872798)
XLA Ops:
  1.8 10.2 %all-to-all-start = ((bf16[32,40,128]{2,1,0:T(8,128)(2,1)}), bf16[32,40,128]{2,1,0:T(8,128)(2,1)S(1)}, u32[]{:S(2)}, u32[]{:S(2)}) async-start(bf16[32,40,128]{2,1,0:T(8,128)(2,1)} %bitcast.29), calls=%async_computation | async-start | bytes 655360 | tf_op jit(solution)/shard_map/all_to_all | solution.py:228
  12.0 4.7 %place.1 = (bf16[128,128,128]{2,1,0:T(8,128)(2,1)}, s32[128]{0:T(128)}) custom-call(s32[64]{0:T(128)} %bitcast.31, s32[64]{0:T(128)} %slots.1, bf16[64,128,128]{2,1,0:T(8,128)(2,1)} %children.1), custom_call_target="tpu_custom_call" | custom-call | tf_op jit(solution)/shard_map/place/pallas_call | solution.py:50
  17.7 1.9 collective-permute-start
  20.8 4.6 %all-to-all-done = bf16[32,40,128]{2,1,0:T(8,128)(2,1)S(1)} async-done(((bf16[32,40,128]{2,1,0:T(8,128)(2,1)}), bf16[32,40,128]{2,1,0:T(8,128)(2,1)S(1)}, u32[]{:S(2)}, u32[]{:S(2)}) %all-to-all-start) | async-done | bytes 327712 | tf_op jit(solution)/shard_map/all_to_all | solution.py:228
  25.7 20.0 %all_to_all.25 = bf16[32,48,128]{2,1,0:T(8,128)(2,1)S(1)} all-to-all(bf16[32,48,128]{2,1,0:T(8,128)(2,1)S(1)} %copy.32), channel_id=1, replica_groups=mesh['front'=2,'row'=32,'col'=8] {'row'}, dimensions={0} | all-to-all | bytes 786432 | tf_op jit(solution)/shard_map/all_to_all | solution.py:228
  46.1 6.1 %all-to-all-start.2 = ((bf16[128,128,128]{2,1,0:T(8,128)(2,1)}), bf16[128,128,128]{2,1,0:T(8,128)(2,1)}, u32[]{:S(2)}, u32[]{:S(2)}) async-start(bf16[128,128,128]{2,1,0:T(8,128)(2,1)} %get-tuple-element.30), calls=%async_computation.2 | async-start | bytes 8388608 | tf_op jit(solution)/shard_map/all_to_all | solution.py:228
  52.2 32.2 %inverse.1 = f32[512,512]{1,0:T(8,128)S(1)} custom-call(bf16[1280,128]{1,0:T(8,128)(2,1)S(1)} %bitcast.27), custom_call_target="tpu_custom_call" | custom-call | flops 536870912 | bytes 1572864 | tf_op jit(solution)/shard_map/inverse/pallas_call | solution.py:198
  86.2 11.0 %collective-permute-start.4 = (bf16[128,512]{1,0:T(8,128)(2,1)}, bf16[128,512]{1,0:T(8,128)(2,1)S(1)}, u32[]{:S(2)}, u32[]{:S(2)}) collective-permute-start(bf16[128,512]{1,0:T(8,128)(2,1)} %get-tuple-element.55), channel_id=1, source_target_pairs={{0,6},{8,14},{16,22},{24,30},{32,38},{40,46},{48,54},{56,62},{64,7... | collective-permute-start | bytes 393224 | tf_op jit(solution)/shard_map/ppermute | solution.py:240
  98.5 1.9 collective-permute-start.2
  102.6 2.1 collective-permute-done.2
  107.0 2.4 %collective-permute-start.6 = (bf16[128,512]{1,0:T(8,128)(2,1)S(1)}, bf16[128,512]{1,0:T(8,128)(2,1)S(1)}, u32[]{:S(2)}, u32[]{:S(2)}) collective-permute-start(bf16[128,512]{1,0:T(8,128)(2,1)S(1)} %fusion.16.refs_0_), channel_id=1, source_target_pairs={{0,6},{2,0},{4,2},{6,4},{8,14},{10,8},{12,10},{14,12},{16,22},{18,... | collective-permute-start | bytes 393224 | tf_op jit(solution)/shard_map/ppermute | solution.py:258
  110.7 8.5 %collective-permute-start.8 = (bf16[128,512]{1,0:T(8,128)(2,1)S(1)}, bf16[128,512]{1,0:T(8,128)(2,1)S(1)}, u32[]{:S(2)}, u32[]{:S(2)}) collective-permute-start(bf16[128,512]{1,0:T(8,128)(2,1)S(1)} %fusion.16.refs_0_), channel_id=1, source_target_pairs={{0,4},{2,6},{4,0},{6,2},{8,12},{10,14},{12,8},{14,10},{16,20},{18,... | collective-permute-start | bytes 393224 | tf_op jit(solution)/shard_map/ppermute | solution.py:258
  120.5 2.8 %collective-permute-start.10 = (bf16[128,512]{1,0:T(8,128)(2,1)S(1)}, bf16[128,512]{1,0:T(8,128)(2,1)S(1)}, u32[]{:S(2)}, u32[]{:S(2)}) collective-permute-start(bf16[128,512]{1,0:T(8,128)(2,1)S(1)} %fusion.16.refs_0_), channel_id=1, source_target_pairs={{0,2},{2,4},{4,6},{6,0},{8,10},{10,12},{12,14},{14,8},{16,18},{18,... | collective-permute-start | bytes 393224 | tf_op jit(solution)/shard_map/ppermute | solution.py:258
  123.3 3.8 %collective-permute-start.11 = (bf16[128,512]{1,0:T(8,128)(2,1)S(1)}, bf16[128,512]{1,0:T(8,128)(2,1)S(1)}, u32[]{:S(2)}, u32[]{:S(2)}) collective-permute-start(bf16[128,512]{1,0:T(8,128)(2,1)S(1)} %fusion.16.refs_0_), channel_id=1, source_target_pairs={{0,1},{2,3},{4,5},{6,7},{8,9},{10,11},{12,13},{14,15},{16,17},{18,... | collective-permute-start | bytes 393224 | tf_op jit(solution)/shard_map/ppermute | solution.py:258
  127.2 4.3 %collective-permute-done.9.refs_5_ = bf16[128,512]{1,0:T(8,128)(2,1)S(1)} collective-permute-done((bf16[128,512]{1,0:T(8,128)(2,1)S(1)}, bf16[128,512]{1,0:T(8,128)(2,1)S(1)}, u32[]{:S(2)}, u32[]{:S(2)}) %collective-permute-start.9) | collective-permute-done | bytes 131104 | tf_op jit(solution)/shard_map/ppermute | solution.py:258
  131.5 2.5 %collective-permute-done.10.refs_6_ = bf16[128,512]{1,0:T(8,128)(2,1)S(1)} collective-permute-done((bf16[128,512]{1,0:T(8,128)(2,1)S(1)}, bf16[128,512]{1,0:T(8,128)(2,1)S(1)}, u32[]{:S(2)}, u32[]{:S(2)}) %collective-permute-start.10) | collective-permute-done | bytes 131104 | tf_op jit(solution)/shard_map/ppermute | solution.py:258
  136.8 9.5 %all-to-all-done.2.incoming = bf16[128,128,128]{2,1,0:T(8,128)(2,1)} async-done(((bf16[128,128,128]{2,1,0:T(8,128)(2,1)}), bf16[128,128,128]{2,1,0:T(8,128)(2,1)}, u32[]{:S(2)}, u32[]{:S(2)}) %all-to-all-start.2) | async-done | bytes 4194336 | tf_op jit(solution)/shard_map/all_to_all | solution.py:228
  146.3 4.4 %assemble.1.refs_18_ = f32[512,512]{1,0:T(8,128)S(1)} custom-call(s32[128]{0:T(128)S(1)} %reshape.146.tags, bf16[128,128,128]{2,1,0:T(8,128)(2,1)} %all-to-all-done.2.incoming, bf16[1,1024,512]{2,1,0:T(8,128)(2,1)S(1)} %copy-done), custom_call_target="tpu_custom_call" | custom-call | tf_op jit(solution)/shard_map/assemble/pallas_call | solution.py:94
  150.8 1.9 convolution_convert_fusion.1
  154.0 11.0 %collective-permute-start.15 = (bf16[128,512]{1,0:T(8,128)(2,1)}, bf16[128,512]{1,0:T(8,128)(2,1)S(1)}, u32[]{:S(2)}, u32[]{:S(2)}) collective-permute-start(bf16[128,512]{1,0:T(8,128)(2,1)} %get-tuple-element.52), channel_id=1, source_target_pairs={{0,6},{8,14},{16,22},{24,30},{32,38},{40,46},{48,54},{56,62},{64,7... | collective-permute-start | bytes 393224 | tf_op jit(solution)/shard_map/ppermute | solution.py:240
  166.3 2.0 collective-permute-start.13
  170.2 2.0 collective-permute-done.13
  174.0 11.6 %all-to-all-start.3 = ((bf16[32,16,512]{2,1,0:T(8,128)(2,1)}), bf16[32,16,512]{2,1,0:T(8,128)(2,1)S(1)}, u32[]{:S(2)}, u32[]{:S(2)}) async-start(bf16[32,16,512]{2,1,0:T(8,128)(2,1)} %bitcast.13), calls=%async_computation.3 | async-start | bytes 1048576 | tf_op jit(solution)/shard_map/all_to_all | solution.py:228
  185.6 2.8 %collective-permute-start.16 = (bf16[128,512]{1,0:T(8,128)(2,1)S(1)}, bf16[128,512]{1,0:T(8,128)(2,1)S(1)}, u32[]{:S(2)}, u32[]{:S(2)}) collective-permute-start(bf16[128,512]{1,0:T(8,128)(2,1)S(1)} %fusion.13.refs_8_), channel_id=1, source_target_pairs={{0,7},{2,1},{4,3},{6,5},{8,15},{10,9},{12,11},{14,13},{16,23},{18,... | collective-permute-start | bytes 393224 | tf_op jit(solution)/shard_map/ppermute | solution.py:258
  188.4 4.9 %collective-permute-start.17 = (bf16[128,512]{1,0:T(8,128)(2,1)S(1)}, bf16[128,512]{1,0:T(8,128)(2,1)S(1)}, u32[]{:S(2)}, u32[]{:S(2)}) collective-permute-start(bf16[128,512]{1,0:T(8,128)(2,1)S(1)} %fusion.13.refs_8_), channel_id=1, source_target_pairs={{0,6},{2,0},{4,2},{6,4},{8,14},{10,8},{12,10},{14,12},{16,22},{18,... | collective-permute-start | bytes 393224 | tf_op jit(solution)/shard_map/ppermute | solution.py:258
  194.6 1.9 collective-permute-start.19
  199.7 7.1 %collective-permute-done.19.refs_12_ = bf16[128,512]{1,0:T(8,128)(2,1)S(1)} collective-permute-done((bf16[128,512]{1,0:T(8,128)(2,1)S(1)}, bf16[128,512]{1,0:T(8,128)(2,1)S(1)}, u32[]{:S(2)}, u32[]{:S(2)}) %collective-permute-start.19) | collective-permute-done | bytes 131104 | tf_op jit(solution)/shard_map/ppermute | solution.py:258
  207.6 9.8 %all-to-all-start.4 = ((bf16[32,16,512]{2,1,0:T(8,128)(2,1)}), bf16[32,16,512]{2,1,0:T(8,128)(2,1)S(1)}, u32[]{:S(2)}, u32[]{:S(2)}) async-start(bf16[32,16,512]{2,1,0:T(8,128)(2,1)} %broadcast_in_dim.23), calls=%async_computation.4 | async-start | bytes 1048576 | tf_op jit(solution)/shard_map/all_to_all | solution.py:228
  218.7 2.4 %collective-permute-start.21 = (bf16[128,512]{1,0:T(8,128)(2,1)S(1)}, bf16[128,512]{1,0:T(8,128)(2,1)S(1)}, u32[]{:S(2)}, u32[]{:S(2)}) collective-permute-start(bf16[128,512]{1,0:T(8,128)(2,1)S(1)} %fusion.13.refs_8_), channel_id=1, source_target_pairs={{0,2},{2,4},{4,6},{6,0},{8,10},{10,12},{12,14},{14,8},{16,18},{18,... | collective-permute-start | bytes 393224 | tf_op jit(solution)/shard_map/ppermute | solution.py:258
  224.1 3.6 %collective-permute-done.21.refs_14_ = bf16[128,512]{1,0:T(8,128)(2,1)S(1)} collective-permute-done((bf16[128,512]{1,0:T(8,128)(2,1)S(1)}, bf16[128,512]{1,0:T(8,128)(2,1)S(1)}, u32[]{:S(2)}, u32[]{:S(2)}) %collective-permute-start.21) | collective-permute-done | bytes 131104 | tf_op jit(solution)/shard_map/ppermute | solution.py:258
  227.7 4.5 %all-to-all-done.4 = bf16[32,16,512]{2,1,0:T(8,128)(2,1)S(1)} async-done(((bf16[32,16,512]{2,1,0:T(8,128)(2,1)}), bf16[32,16,512]{2,1,0:T(8,128)(2,1)S(1)}, u32[]{:S(2)}, u32[]{:S(2)}) %all-to-all-start.4) | async-done | bytes 524320 | tf_op jit(solution)/shard_map/all_to_all | solution.py:228
  233.0 4.0 %finish.1 = bf16[1,1024,512]{2,1,0:T(8,128)(2,1)} custom-call(s32[3]{0:T(128)} %pad_add_fusion.1.state, bf16[128,512]{1,0:T(8,128)(2,1)} %copy-done.5, bf16[128,512]{1,0:T(8,128)(2,1)} %copy-done.7, bf16[128,512]{1,0:T(8,128)(2,1)} %copy-done.8, bf16[128,512]{1,0:T(8,128)(2,1)} %copy-done.9, bf16[128,512]{1,0:T(8,128)(2,1)} %copy-done.10, ...), custom_call_target="tpu_custom_call" | custom-call | tf_op jit(solution)/shard_map/finish/pallas_call | solution.py:317
  (101 shorter events, 34.2 us)
Async XLA Ops:
  1.8 23.6 %all-to-all-start = ((bf16[32,40,128]{2,1,0:T(8,128)(2,1)}), bf16[32,40,128]{2,1,0:T(8,128)(2,1)S(1)}, u32[]{:S(2)}, u32[]{:S(2)}) async-start(bf16[32,40,128]{2,1,0:T(8,128)(2,1)} %bitcast.29), calls=%async_computation | async-start | bytes 655360 | tf_op jit(solution)/shard_map/all_to_all | solution.py:228
  17.7 3.0 %collective-permute-start = (s32[32,2]{0,1:T(2,128)S(1)}, s32[32,2]{0,1:T(2,128)S(1)}, u32[]{:S(2)}, u32[]{:S(2)}) collective-permute-start(s32[32,2]{0,1:T(2,128)S(1)} %copy.30), channel_id=1, source_target_pairs={{0,256},{256,0},{1,257},{257,1},{2,258},{258,2},{3,259},{259,3},{4... | collective-permute-start | bytes 776 | tf_op jit(solution)/shard_map/ppermute | solution.py:348
  46.1 100.2 %all-to-all-start.2 = ((bf16[128,128,128]{2,1,0:T(8,128)(2,1)}), bf16[128,128,128]{2,1,0:T(8,128)(2,1)}, u32[]{:S(2)}, u32[]{:S(2)}) async-start(bf16[128,128,128]{2,1,0:T(8,128)(2,1)} %get-tuple-element.30), calls=%async_computation.2 | async-start | bytes 8388608 | tf_op jit(solution)/shard_map/all_to_all | solution.py:228
  86.2 14.9 %collective-permute-start.4 = (bf16[128,512]{1,0:T(8,128)(2,1)}, bf16[128,512]{1,0:T(8,128)(2,1)S(1)}, u32[]{:S(2)}, u32[]{:S(2)}) collective-permute-start(bf16[128,512]{1,0:T(8,128)(2,1)} %get-tuple-element.55), channel_id=1, source_target_pairs={{0,6},{8,14},{16,22},{24,30},{32,38},{40,46},{48,54},{56,62},{64,7... | collective-permute-start | bytes 393224 | tf_op jit(solution)/shard_map/ppermute | solution.py:240
  97.2 5.4 %collective-permute-start.3 = (bf16[128,512]{1,0:T(8,128)(2,1)}, bf16[128,512]{1,0:T(8,128)(2,1)S(1)}, u32[]{:S(2)}, u32[]{:S(2)}) collective-permute-start(bf16[128,512]{1,0:T(8,128)(2,1)} %get-tuple-element.56), channel_id=1, source_target_pairs={{0,4},{8,12},{16,20},{24,28},{32,36},{40,44},{48,52},{56,60},{64,6... | collective-permute-start | bytes 393224 | tf_op jit(solution)/shard_map/ppermute | solution.py:240
  98.5 6.3 %collective-permute-start.2 = (bf16[128,512]{1,0:T(8,128)(2,1)S(1)}, bf16[128,512]{1,0:T(8,128)(2,1)}, u32[]{:S(2)}, u32[]{:S(2)}) collective-permute-start(bf16[128,512]{1,0:T(8,128)(2,1)S(1)} %get-tuple-element.54), channel_id=1, source_target_pairs={{0,2},{8,10},{16,18},{24,26},{32,34},{40,42},{48,50},{56,58},{64,6... | collective-permute-start | bytes 393224 | tf_op jit(solution)/shard_map/ppermute | solution.py:240
  100.4 35.6 %collective-permute-start.1 = (bf16[512,512]{1,0:T(8,128)(2,1)S(1)}, bf16[512,512]{1,0:T(8,128)(2,1)S(1)}, u32[]{:S(2)}, u32[]{:S(2)}) collective-permute-start(bf16[512,512]{1,0:T(8,128)(2,1)S(1)} %fusion), channel_id=1, source_target_pairs={{8,10},{16,20},{24,30},{264,266},{272,276},{280,286}} | collective-permute-start | bytes 1572872 | tf_op jit(solution)/shard_map/ppermute | solution.py:372
  105.7 126.6 %copy-start.5 = (bf16[128,512]{1,0:T(8,128)(2,1)}, bf16[128,512]{1,0:T(8,128)(2,1)S(1)}, u32[]{:S(2)}) copy-start(bf16[128,512]{1,0:T(8,128)(2,1)S(1)} %fusion.16.refs_0_) | copy-start | bytes 393220
  105.7 13.5 %collective-permute-start.5 = (bf16[128,512]{1,0:T(8,128)(2,1)S(1)}, bf16[128,512]{1,0:T(8,128)(2,1)S(1)}, u32[]{:S(2)}, u32[]{:S(2)}) collective-permute-start(bf16[128,512]{1,0:T(8,128)(2,1)S(1)} %fusion.16.refs_0_), channel_id=1, source_target_pairs={{0,7},{2,1},{4,3},{6,5},{8,15},{10,9},{12,11},{14,13},{16,23},{18,... | collective-permute-start | bytes 393224 | tf_op jit(solution)/shard_map/ppermute | solution.py:258
  107.0 13.5 %collective-permute-start.6 = (bf16[128,512]{1,0:T(8,128)(2,1)S(1)}, bf16[128,512]{1,0:T(8,128)(2,1)S(1)}, u32[]{:S(2)}, u32[]{:S(2)}) collective-permute-start(bf16[128,512]{1,0:T(8,128)(2,1)S(1)} %fusion.16.refs_0_), channel_id=1, source_target_pairs={{0,6},{2,0},{4,2},{6,4},{8,14},{10,8},{12,10},{14,12},{16,22},{18,... | collective-permute-start | bytes 393224 | tf_op jit(solution)/shard_map/ppermute | solution.py:258
  109.4 13.9 %collective-permute-start.7 = (bf16[128,512]{1,0:T(8,128)(2,1)S(1)}, bf16[128,512]{1,0:T(8,128)(2,1)S(1)}, u32[]{:S(2)}, u32[]{:S(2)}) collective-permute-start(bf16[128,512]{1,0:T(8,128)(2,1)S(1)} %fusion.16.refs_0_), channel_id=1, source_target_pairs={{0,5},{2,7},{4,1},{6,3},{8,13},{10,15},{12,9},{14,11},{16,21},{18,... | collective-permute-start | bytes 393224 | tf_op jit(solution)/shard_map/ppermute | solution.py:258
  110.7 16.4 %collective-permute-start.8 = (bf16[128,512]{1,0:T(8,128)(2,1)S(1)}, bf16[128,512]{1,0:T(8,128)(2,1)S(1)}, u32[]{:S(2)}, u32[]{:S(2)}) collective-permute-start(bf16[128,512]{1,0:T(8,128)(2,1)S(1)} %fusion.16.refs_0_), channel_id=1, source_target_pairs={{0,4},{2,6},{4,0},{6,2},{8,12},{10,14},{12,8},{14,10},{16,20},{18,... | collective-permute-start | bytes 393224 | tf_op jit(solution)/shard_map/ppermute | solution.py:258
  119.2 113.0 %copy-start.7 = (bf16[128,512]{1,0:T(8,128)(2,1)}, bf16[128,512]{1,0:T(8,128)(2,1)S(1)}, u32[]{:S(2)}) copy-start(bf16[128,512]{1,0:T(8,128)(2,1)S(1)} %collective-permute-done.5.refs_1_) | copy-start | bytes 393220
  119.2 12.2 %collective-permute-start.9 = (bf16[128,512]{1,0:T(8,128)(2,1)S(1)}, bf16[128,512]{1,0:T(8,128)(2,1)S(1)}, u32[]{:S(2)}, u32[]{:S(2)}) collective-permute-start(bf16[128,512]{1,0:T(8,128)(2,1)S(1)} %fusion.16.refs_0_), channel_id=1, source_target_pairs={{0,3},{2,5},{4,7},{6,1},{8,11},{10,13},{12,15},{14,9},{16,19},{18,... | collective-permute-start | bytes 393224 | tf_op jit(solution)/shard_map/ppermute | solution.py:258
  120.5 111.7 %copy-start.8 = (bf16[128,512]{1,0:T(8,128)(2,1)}, bf16[128,512]{1,0:T(8,128)(2,1)S(1)}, u32[]{:S(2)}) copy-start(bf16[128,512]{1,0:T(8,128)(2,1)S(1)} %collective-permute-done.6.refs_2_) | copy-start | bytes 393220
  120.5 13.4 %collective-permute-start.10 = (bf16[128,512]{1,0:T(8,128)(2,1)S(1)}, bf16[128,512]{1,0:T(8,128)(2,1)S(1)}, u32[]{:S(2)}, u32[]{:S(2)}) collective-permute-start(bf16[128,512]{1,0:T(8,128)(2,1)S(1)} %fusion.16.refs_0_), channel_id=1, source_target_pairs={{0,2},{2,4},{4,6},{6,0},{8,10},{10,12},{12,14},{14,8},{16,18},{18,... | collective-permute-start | bytes 393224 | tf_op jit(solution)/shard_map/ppermute | solution.py:258
  123.3 12.0 %collective-permute-start.11 = (bf16[128,512]{1,0:T(8,128)(2,1)S(1)}, bf16[128,512]{1,0:T(8,128)(2,1)S(1)}, u32[]{:S(2)}, u32[]{:S(2)}) collective-permute-start(bf16[128,512]{1,0:T(8,128)(2,1)S(1)} %fusion.16.refs_0_), channel_id=1, source_target_pairs={{0,1},{2,3},{4,5},{6,7},{8,9},{10,11},{12,13},{14,15},{16,17},{18,... | collective-permute-start | bytes 393224 | tf_op jit(solution)/shard_map/ppermute | solution.py:258
  150.7 81.5 %copy-start.1 = (f32[512,512]{1,0:T(8,128)}, f32[512,512]{1,0:T(8,128)S(1)}, u32[]{:S(2)}) copy-start(f32[512,512]{1,0:T(8,128)S(1)} %assemble.1.refs_18_) | copy-start | bytes 3145732
  150.8 71.7 %copy-start.21 = (s32[1,2,1]{1,2,0:T(1,128)S(1)}, s32[1,2,1]{1,2,0:T(1,128)}, u32[]{:S(2)}) copy-start(s32[1,2,1]{1,2,0:T(1,128)} %param.9) | copy-start | bytes 28
  152.6 20.4 %collective-permute-start.12 = (bf16[512,512]{1,0:T(8,128)(2,1)S(1)}, bf16[512,512]{1,0:T(8,128)(2,1)S(1)}, u32[]{:S(2)}, u32[]{:S(2)}) collective-permute-start(bf16[512,512]{1,0:T(8,128)(2,1)S(1)} %convolution_convert_fusion.1), channel_id=1, source_target_pairs={{0,1},{8,11},{16,21},{24,31},{256,257},{264,267},{272,277},{280,287}} | collective-permute-start | bytes 1572872 | tf_op jit(solution)/shard_map/ppermute | solution.py:372
  154.0 14.3 %collective-permute-start.15 = (bf16[128,512]{1,0:T(8,128)(2,1)}, bf16[128,512]{1,0:T(8,128)(2,1)S(1)}, u32[]{:S(2)}, u32[]{:S(2)}) collective-permute-start(bf16[128,512]{1,0:T(8,128)(2,1)} %get-tuple-element.52), channel_id=1, source_target_pairs={{0,6},{8,14},{16,22},{24,30},{32,38},{40,46},{48,54},{56,62},{64,7... | collective-permute-start | bytes 393224 | tf_op jit(solution)/shard_map/ppermute | solution.py:240
  165.0 5.1 %collective-permute-start.14 = (bf16[128,512]{1,0:T(8,128)(2,1)S(1)}, bf16[128,512]{1,0:T(8,128)(2,1)S(1)}, u32[]{:S(2)}, u32[]{:S(2)}) collective-permute-start(bf16[128,512]{1,0:T(8,128)(2,1)S(1)} %get-tuple-element.53), channel_id=1, source_target_pairs={{0,4},{8,12},{16,20},{24,28},{32,36},{40,44},{48,52},{56,60},{64,6... | collective-permute-start | bytes 393224 | tf_op jit(solution)/shard_map/ppermute | solution.py:240
  166.3 5.8 %collective-permute-start.13 = (bf16[128,512]{1,0:T(8,128)(2,1)S(1)}, bf16[128,512]{1,0:T(8,128)(2,1)}, u32[]{:S(2)}, u32[]{:S(2)}) collective-permute-start(bf16[128,512]{1,0:T(8,128)(2,1)S(1)} %get-tuple-element.51), channel_id=1, source_target_pairs={{0,2},{8,10},{16,18},{24,26},{32,34},{40,42},{48,50},{56,58},{64,6... | collective-permute-start | bytes 393224 | tf_op jit(solution)/shard_map/ppermute | solution.py:240
  174.0 32.8 %all-to-all-start.3 = ((bf16[32,16,512]{2,1,0:T(8,128)(2,1)}), bf16[32,16,512]{2,1,0:T(8,128)(2,1)S(1)}, u32[]{:S(2)}, u32[]{:S(2)}) async-start(bf16[32,16,512]{2,1,0:T(8,128)(2,1)} %bitcast.13), calls=%async_computation.3 | async-start | bytes 1048576 | tf_op jit(solution)/shard_map/all_to_all | solution.py:228
  185.6 11.0 %collective-permute-start.16 = (bf16[128,512]{1,0:T(8,128)(2,1)S(1)}, bf16[128,512]{1,0:T(8,128)(2,1)S(1)}, u32[]{:S(2)}, u32[]{:S(2)}) collective-permute-start(bf16[128,512]{1,0:T(8,128)(2,1)S(1)} %fusion.13.refs_8_), channel_id=1, source_target_pairs={{0,7},{2,1},{4,3},{6,5},{8,15},{10,9},{12,11},{14,13},{16,23},{18,... | collective-permute-start | bytes 393224 | tf_op jit(solution)/shard_map/ppermute | solution.py:258
  188.4 9.4 %collective-permute-start.17 = (bf16[128,512]{1,0:T(8,128)(2,1)S(1)}, bf16[128,512]{1,0:T(8,128)(2,1)S(1)}, u32[]{:S(2)}, u32[]{:S(2)}) collective-permute-start(bf16[128,512]{1,0:T(8,128)(2,1)S(1)} %fusion.13.refs_8_), channel_id=1, source_target_pairs={{0,6},{2,0},{4,2},{6,4},{8,14},{10,8},{12,10},{14,12},{16,22},{18,... | collective-permute-start | bytes 393224 | tf_op jit(solution)/shard_map/ppermute | solution.py:258
  193.3 6.4 %collective-permute-start.18 = (bf16[128,512]{1,0:T(8,128)(2,1)S(1)}, bf16[128,512]{1,0:T(8,128)(2,1)S(1)}, u32[]{:S(2)}, u32[]{:S(2)}) collective-permute-start(bf16[128,512]{1,0:T(8,128)(2,1)S(1)} %fusion.13.refs_8_), channel_id=1, source_target_pairs={{0,5},{2,7},{4,1},{6,3},{8,13},{10,15},{12,9},{14,11},{16,21},{18,... | collective-permute-start | bytes 393224 | tf_op jit(solution)/shard_map/ppermute | solution.py:258
  194.6 12.2 %collective-permute-start.19 = (bf16[128,512]{1,0:T(8,128)(2,1)S(1)}, bf16[128,512]{1,0:T(8,128)(2,1)S(1)}, u32[]{:S(2)}, u32[]{:S(2)}) collective-permute-start(bf16[128,512]{1,0:T(8,128)(2,1)S(1)} %fusion.13.refs_8_), channel_id=1, source_target_pairs={{0,4},{2,6},{4,0},{6,2},{8,12},{10,14},{12,8},{14,10},{16,20},{18,... | collective-permute-start | bytes 393224 | tf_op jit(solution)/shard_map/ppermute | solution.py:258
  207.6 24.6 %all-to-all-start.4 = ((bf16[32,16,512]{2,1,0:T(8,128)(2,1)}), bf16[32,16,512]{2,1,0:T(8,128)(2,1)S(1)}, u32[]{:S(2)}, u32[]{:S(2)}) async-start(bf16[32,16,512]{2,1,0:T(8,128)(2,1)} %broadcast_in_dim.23), calls=%async_computation.4 | async-start | bytes 1048576 | tf_op jit(solution)/shard_map/all_to_all | solution.py:228
  217.4 6.6 %collective-permute-start.20 = (bf16[128,512]{1,0:T(8,128)(2,1)S(1)}, bf16[128,512]{1,0:T(8,128)(2,1)S(1)}, u32[]{:S(2)}, u32[]{:S(2)}) collective-permute-start(bf16[128,512]{1,0:T(8,128)(2,1)S(1)} %fusion.13.refs_8_), channel_id=1, source_target_pairs={{0,3},{2,5},{4,7},{6,1},{8,11},{10,13},{12,15},{14,9},{16,19},{18,... | collective-permute-start | bytes 393224 | tf_op jit(solution)/shard_map/ppermute | solution.py:258
  218.7 9.0 %collective-permute-start.21 = (bf16[128,512]{1,0:T(8,128)(2,1)S(1)}, bf16[128,512]{1,0:T(8,128)(2,1)S(1)}, u32[]{:S(2)}, u32[]{:S(2)}) collective-permute-start(bf16[128,512]{1,0:T(8,128)(2,1)S(1)} %fusion.13.refs_8_), channel_id=1, source_target_pairs={{0,2},{2,4},{4,6},{6,0},{8,10},{10,12},{12,14},{14,8},{16,18},{18,... | collective-permute-start | bytes 393224 | tf_op jit(solution)/shard_map/ppermute | solution.py:258
  221.2 6.6 %collective-permute-start.22 = (bf16[128,512]{1,0:T(8,128)(2,1)S(1)}, bf16[128,512]{1,0:T(8,128)(2,1)S(1)}, u32[]{:S(2)}, u32[]{:S(2)}) collective-permute-start(bf16[128,512]{1,0:T(8,128)(2,1)S(1)} %fusion.13.refs_8_), channel_id=1, source_target_pairs={{0,1},{2,3},{4,5},{6,7},{8,9},{10,11},{12,13},{14,15},{16,17},{18,... | collective-permute-start | bytes 393224 | tf_op jit(solution)/shard_map/ppermute | solution.py:258
  (17 other events, 293.5 us)

commit v5 on v4

--- a/solution.py
+++ b/solution.py
@@ -228,82 +228,48 @@
     return lax.all_to_all(block, axis, split_axis=0, concat_axis=0, tiled=True)
 
 
-HOLDERS = 4
-
-
-def hand_out(parts, axis, devices):
-    mine = jnp.zeros_like(parts[0])
-    for part, device in zip(parts, devices):
-        if device == 0:
-            mine = mine + jnp.where(lax.axis_index(axis) == 0, part, jnp.zeros_like(part))
-        else:
-            mine = mine + lax.ppermute(part, axis, [(0, device)])
-    return mine
-
-
-def column_holders():
+def to_columns(block):
     size = lax.axis_size("col")
-    return list(range(0, size, size // HOLDERS))
-
-
-def to_holders(block):
-    parts = list(block.reshape(HOLDERS, -1, block.shape[1]))
-    return hand_out(parts, "col", column_holders())
-
-
-def from_holders(mine):
-    size = lax.axis_size("col")
-    got = [mine]
-    for t in range(1, size):
-        got.append(lax.ppermute(mine, "col", [(i, (i - t) % size) for i in column_holders()]))
+    got = [None] * size
+    for step in range(1, size):
+        c = (step + 1) // 2 if step % 2 else size - step // 2
+        got[c] = lax.ppermute(block, "col", [(0, c)])
+    got[0] = block
     return got
 
 
 def finish_kernel(size, state, *refs):
     halves = refs[:size], refs[size : 2 * size]
-    partner, base, added, out, parts, sem = refs[2 * size :]
+    partner, base, added, out, tiles, sem = refs[2 * size :]
     column = state[0]
-    step = size // HOLDERS
-    rows = TILE // HOLDERS
-    shift = lax.rem(step - lax.rem(column, step), step)
-    first = lax.div(column + shift, step)
-    for s in range(step):
-
-        @pl.when(shift == s)
+    for c in range(size):
+
+        @pl.when(column == c)
         def _():
             copies = [
-                pltpu.make_async_copy(
-                    halves[h][k * step + s], parts.at[h, k], sem.at[h * HOLDERS + k]
-                )
-                for h in range(2)
-                for k in range(HOLDERS)
+                pltpu.make_async_copy(halves[h][c], tiles.at[h], sem.at[h]) for h in range(2)
             ]
             for copy in copies:
                 copy.start()
             for copy in copies:
                 copy.wait()
 
-    for k in range(HOLDERS):
-        source = lax.rem(first + k, HOLDERS)
-        at = pl.ds(pl.multiple_of(source * rows, rows), rows)
-        under = pl.ds(pl.multiple_of(source * rows + TILE, rows), rows)
-
-        @pl.when(column == 0)
-        def _():
-            out[0, at, :] = parts[0, k]
-            out[0, under, :] = parts[1, k]
-
-        @pl.when(column != 0)
-        def _():
-            def product(part):
-                return lax.dot_general(
-                    part, partner[...], (((1,), (1,)), ((), ())), preferred_element_type=F32
-                )
-
-            upper = base[0, at, :].astype(F32) - state[1].astype(F32) * product(parts[0, k])
-            out[0, at, :] = upper.astype(BF16)
-            lower = added[at, :] - state[2].astype(F32) * product(parts[1, k])
-            out[0, under, :] = lower.astype(BF16)
+    @pl.when(column == 0)
+    def _():
+        out[0, :TILE, :] = tiles[0]
+        out[0, TILE:, :] = tiles[1]
+
+    @pl.when(column != 0)
+    def _():
+        def product(tile):
+            return lax.dot_general(
+                tile, partner[...], (((1,), (1,)), ((), ())), preferred_element_type=F32
+            )
+
+        upper = base[0].astype(F32) - state[1].astype(F32) * product(tiles[0])
+        out[0, :TILE, :] = upper.astype(BF16)
+        lower = added[...] - state[2].astype(F32) * product(tiles[1])
+        out[0, TILE:, :] = lower.astype(BF16)
 
 
 def finish(state, upper, under, partner, window, added):
@@ -323,8 +289,8 @@
         + [whole(partner), tile, whole(added)],
         out_specs=whole(out),
         scratch_shapes=[
-            pltpu.VMEM((2, HOLDERS, TILE // HOLDERS, TILE), BF16),
-            pltpu.SemaphoreType.DMA((2 * HOLDERS,)),
+            pltpu.VMEM((2, TILE, TILE), BF16),
+            pltpu.SemaphoreType.DMA((2,)),
         ],
         compiler_params=pltpu.CompilerParams(vmem_limit_bytes=56 << 20),
         name="finish",
@@ -366,23 +332,24 @@
         ).astype(BF16)
 
     def to_plane(lower, odd):
-        pairs = [
-            ((c // 2) * columns, (c // 2) * columns + c) for c in range(max(odd, 1), columns) if c % 2 == odd
-        ]
+        planes = [c for c in range(1, columns) if c % 2 == odd]
+        pairs = [((c // 2) * columns, (c // 2) * columns + c) for c in planes]
         return lax.ppermute(lower, ("row", "col"), pairs)
 
     lower_first = solve(first)
     even = to_plane(lower_first, 0)
-    upper = from_holders(to_holders(lower_first))
+    upper = to_columns(lower_first)
     incoming, even, upper = lax.optimization_barrier((incoming, even, upper))
     added = assemble(tags, incoming, window)
     lower_second = solve(added)
     odd = to_plane(lower_second, 1)
     piece = jnp.where(column % 2 == 0, even, odd)
-    piece, under = lax.optimization_barrier((piece, to_holders(lower_second)))
-    under = from_holders(under)
+    under = to_columns(lower_second)
     got = swap(piece.reshape(rows_axis, -1, TILE), "row")
-    got, *under[: HOLDERS + 1] = lax.optimization_barrier((got, *under[: HOLDERS + 1]))
+    early = [1, columns - 1, 2, columns - 2]
+    got, *arrived = lax.optimization_barrier((got, *(under[c] for c in early)))
+    for c, tile in zip(early, arrived):
+        under[c] = tile
     owned = lax.dynamic_index_in_dim(got, column // 2, 0)
     partner = swap(jnp.broadcast_to(owned, got.shape), "row").reshape(TILE, TILE)
     state = jnp.concatenate([jnp.full((1,), column, jnp.int32), pattern[0, :, 0]])

time: 238 us -> 247 us (1.038)
  the two profiles are of different devices: /device:TPU:8 before, /device:TPU:2 now
where the time goes in v5:
time: 247 us; the launch traced here: 246 us
  waiting for transfers between devices  91.6 us (37%)
  starting transfers between devices  75.7 us (31%)
  Pallas kernels  46.8 us (19%)
  blocking collectives  20.1 us (8%)
  local copies, waits for them, and re-layouts  5.12 us (2%)
  other arithmetic  3.42 us (1%)
  matrix products  2.93 us (1%)
    ppermute x14, waiting for transfers between devices, to_columns(): got[c] = lax.ppermute(block, 'col', [(0, c)])  71.9 us
    all_to_all x4, starting transfers between devices, swap(): return lax.all_to_all(block, axis, split_axis=0, concat_axis=0, tiled=True)  37.1 us
    pallas_call x1, Pallas kernels, inverse_factor(): pl.pallas_call(inverse_kernel, out_shape=jax.ShapeDtypeStruct((n, n), F32...  32.2 us
    ppermute x14, starting transfers between devices, to_columns(): got[c] = lax.ppermute(block, 'col', [(0, c)])  26.6 us
    all_to_all x1, blocking collectives, swap(): return lax.all_to_all(block, axis, split_axis=0, concat_axis=0, tiled=True)  20.1 us
    ppermute x2, waiting for transfers between devices, to_plane(): return lax.ppermute(lower, ('row', 'col'), pairs)  14.8 us
    ppermute x2, starting transfers between devices, to_plane(): return lax.ppermute(lower, ('row', 'col'), pairs)  10.1 us
  transfers between devices with their start and end apart: 21, of which 14 were waited for; matrix products, arithmetic and copies ran while one was open for 1% of the time, Pallas kernels for 15%

profile of v5, /device:TPU:2, one launch (start us, length us, event | category | flops | bytes accessed | tf_op | source)
XLA Modules:
  0.0 246.2 jit_solution(13968814297445138188)
XLA Ops:
  1.8 10.2 %all-to-all-start = ((bf16[32,40,128]{2,1,0:T(8,128)(2,1)}), bf16[32,40,128]{2,1,0:T(8,128)(2,1)S(1)}, u32[]{:S(2)}, u32[]{:S(2)}) async-start(bf16[32,40,128]{2,1,0:T(8,128)(2,1)} %bitcast.29), calls=%async_computation | async-start | bytes 655360 | tf_op jit(solution)/shard_map/all_to_all | solution.py:228
  12.1 4.7 %place.1 = (bf16[128,128,128]{2,1,0:T(8,128)(2,1)}, s32[128]{0:T(128)}) custom-call(s32[64]{0:T(128)} %bitcast.31, s32[64]{0:T(128)} %slots.1, bf16[64,128,128]{2,1,0:T(8,128)(2,1)} %children.1), custom_call_target="tpu_custom_call" | custom-call | tf_op jit(solution)/shard_map/place/pallas_call | solution.py:50
  17.7 1.9 collective-permute-start
  20.8 3.9 %all-to-all-done = bf16[32,40,128]{2,1,0:T(8,128)(2,1)S(1)} async-done(((bf16[32,40,128]{2,1,0:T(8,128)(2,1)}), bf16[32,40,128]{2,1,0:T(8,128)(2,1)S(1)}, u32[]{:S(2)}, u32[]{:S(2)}) %all-to-all-start) | async-done | bytes 327712 | tf_op jit(solution)/shard_map/all_to_all | solution.py:228
  25.0 20.1 %all_to_all.25 = bf16[32,48,128]{2,1,0:T(8,128)(2,1)S(1)} all-to-all(bf16[32,48,128]{2,1,0:T(8,128)(2,1)S(1)} %copy.32), channel_id=1, replica_groups=mesh['front'=2,'row'=32,'col'=8] {'row'}, dimensions={0} | all-to-all | bytes 786432 | tf_op jit(solution)/shard_map/all_to_all | solution.py:228
  45.5 6.7 %all-to-all-start.2 = ((bf16[128,128,128]{2,1,0:T(8,128)(2,1)}), bf16[128,128,128]{2,1,0:T(8,128)(2,1)}, u32[]{:S(2)}, u32[]{:S(2)}) async-start(bf16[128,128,128]{2,1,0:T(8,128)(2,1)} %get-tuple-element.27), calls=%async_computation.2 | async-start | bytes 8388608 | tf_op jit(solution)/shard_map/all_to_all | solution.py:228
  52.2 32.2 %inverse.1 = f32[512,512]{1,0:T(8,128)S(1)} custom-call(bf16[1280,128]{1,0:T(8,128)(2,1)S(1)} %bitcast.27), custom_call_target="tpu_custom_call" | custom-call | flops 536870912 | bytes 1572864 | tf_op jit(solution)/shard_map/inverse/pallas_call | solution.py:198
  85.5 6.9 %collective-permute-start.1 = (bf16[512,512]{1,0:T(8,128)(2,1)S(1)}, bf16[512,512]{1,0:T(8,128)(2,1)}, u32[]{:S(2)}, u32[]{:S(2)}) collective-permute-start(bf16[512,512]{1,0:T(8,128)(2,1)S(1)} %fusion.refs_0_), channel_id=1, source_target_pairs={{8,10},{16,20},{24,30},{264,266},{272,276},{280,286}} | collective-permute-start | bytes 1572872 | tf_op jit(solution)/shard_map/ppermute | solution.py:337
  96.4 3.6 %collective-permute-start.5 = (bf16[512,512]{1,0:T(8,128)(2,1)S(1)}, bf16[512,512]{1,0:T(8,128)(2,1)S(1)}, u32[]{:S(2)}, u32[]{:S(2)}) collective-permute-start(bf16[512,512]{1,0:T(8,128)(2,1)S(1)} %fusion.refs_0_), channel_id=1, source_target_pairs={{0,4},{8,12},{16,20},{24,28},{32,36},{40,44},{48,52},{56,60},{64,6... | collective-permute-start | bytes 1572872 | tf_op jit(solution)/shard_map/ppermute | solution.py:236
  100.0 3.8 %collective-permute-done.1 = bf16[512,512]{1,0:T(8,128)(2,1)} collective-permute-done((bf16[512,512]{1,0:T(8,128)(2,1)S(1)}, bf16[512,512]{1,0:T(8,128)(2,1)}, u32[]{:S(2)}, u32[]{:S(2)}) %collective-permute-start.1) | collective-permute-done | bytes 524320 | tf_op jit(solution)/shard_map/ppermute | solution.py:337
  105.1 9.9 %collective-permute-done.2.refs_1_ = bf16[512,512]{1,0:T(8,128)(2,1)S(1)} collective-permute-done((bf16[512,512]{1,0:T(8,128)(2,1)S(1)}, bf16[512,512]{1,0:T(8,128)(2,1)S(1)}, u32[]{:S(2)}, u32[]{:S(2)}) %collective-permute-start.2) | collective-permute-done | bytes 524320 | tf_op jit(solution)/shard_map/ppermute | solution.py:236
  116.4 9.9 %collective-permute-done.3.refs_2_ = bf16[512,512]{1,0:T(8,128)(2,1)S(1)} collective-permute-done((bf16[512,512]{1,0:T(8,128)(2,1)S(1)}, bf16[512,512]{1,0:T(8,128)(2,1)S(1)}, u32[]{:S(2)}, u32[]{:S(2)}) %collective-permute-start.3) | collective-permute-done | bytes 524320 | tf_op jit(solution)/shard_map/ppermute | solution.py:236
  126.3 2.1 collective-permute-start.8
  128.4 9.1 %collective-permute-done.4.refs_3_ = bf16[512,512]{1,0:T(8,128)(2,1)S(1)} collective-permute-done((bf16[512,512]{1,0:T(8,128)(2,1)S(1)}, bf16[512,512]{1,0:T(8,128)(2,1)S(1)}, u32[]{:S(2)}, u32[]{:S(2)}) %collective-permute-start.4) | collective-permute-done | bytes 524320 | tf_op jit(solution)/shard_map/ppermute | solution.py:236
  137.5 10.7 %collective-permute-done.5.refs_4_ = bf16[512,512]{1,0:T(8,128)(2,1)S(1)} collective-permute-done((bf16[512,512]{1,0:T(8,128)(2,1)S(1)}, bf16[512,512]{1,0:T(8,128)(2,1)S(1)}, u32[]{:S(2)}, u32[]{:S(2)}) %collective-permute-start.5) | collective-permute-done | bytes 524320 | tf_op jit(solution)/shard_map/ppermute | solution.py:236
  150.0 4.4 %assemble.1.refs_18_ = f32[512,512]{1,0:T(8,128)S(1)} custom-call(s32[128]{0:T(128)S(1)} %reshape.128.tags, bf16[128,128,128]{2,1,0:T(8,128)(2,1)} %all-to-all-done.2.incoming, bf16[1,1024,512]{2,1,0:T(8,128)(2,1)S(1)} %copy-done), custom_call_target="tpu_custom_call" | custom-call | tf_op jit(solution)/shard_map/assemble/pallas_call | solution.py:94
  156.3 3.2 %collective-permute-start.9 = (bf16[512,512]{1,0:T(8,128)(2,1)S(1)}, bf16[512,512]{1,0:T(8,128)(2,1)S(1)}, u32[]{:S(2)}, u32[]{:S(2)}) collective-permute-start(bf16[512,512]{1,0:T(8,128)(2,1)S(1)} %convolution_convert_fusion.1.refs_8_), channel_id=1, source_target_pairs={{0,1},{8,11},{16,21},{24,31},{256,257},{264,267},{272,277},{280,287}} | collective-permute-start | bytes 1572872 | tf_op jit(solution)/shard_map/ppermute | solution.py:337
  159.5 11.0 %collective-permute-done.9 = bf16[512,512]{1,0:T(8,128)(2,1)S(1)} collective-permute-done((bf16[512,512]{1,0:T(8,128)(2,1)S(1)}, bf16[512,512]{1,0:T(8,128)(2,1)S(1)}, u32[]{:S(2)}, u32[]{:S(2)}) %collective-permute-start.9) | collective-permute-done | bytes 524320 | tf_op jit(solution)/shard_map/ppermute | solution.py:337
  170.5 1.9 broadcast_select_fusion
  172.4 10.4 %all-to-all-start.3 = ((bf16[32,16,512]{2,1,0:T(8,128)(2,1)}), bf16[32,16,512]{2,1,0:T(8,128)(2,1)S(1)}, u32[]{:S(2)}, u32[]{:S(2)}) async-start(bf16[32,16,512]{2,1,0:T(8,128)(2,1)} %bitcast.13), calls=%async_computation.3 | async-start | bytes 1048576 | tf_op jit(solution)/shard_map/all_to_all | solution.py:228
  184.1 4.0 %collective-permute-start.11 = (bf16[512,512]{1,0:T(8,128)(2,1)S(1)}, bf16[512,512]{1,0:T(8,128)(2,1)S(1)}, u32[]{:S(2)}, u32[]{:S(2)}) collective-permute-start(bf16[512,512]{1,0:T(8,128)(2,1)S(1)} %convolution_convert_fusion.1.refs_8_), channel_id=1, source_target_pairs={{0,7},{8,15},{16,23},{24,31},{32,39},{40,47},{48,55},{56,63},{64,7... | collective-permute-start | bytes 1572872 | tf_op jit(solution)/shard_map/ppermute | solution.py:236
  188.1 2.1 collective-permute-start.12
  190.2 2.1 collective-permute-start.13
  192.2 4.2 %collective-permute-done.10.refs_9_ = bf16[512,512]{1,0:T(8,128)(2,1)S(1)} collective-permute-done((bf16[512,512]{1,0:T(8,128)(2,1)S(1)}, bf16[512,512]{1,0:T(8,128)(2,1)S(1)}, u32[]{:S(2)}, u32[]{:S(2)}) %collective-permute-start.10) | collective-permute-done | bytes 524320 | tf_op jit(solution)/shard_map/ppermute | solution.py:236
  196.4 4.0 %collective-permute-done.11.refs_15_ = bf16[512,512]{1,0:T(8,128)(2,1)S(1)} collective-permute-done((bf16[512,512]{1,0:T(8,128)(2,1)S(1)}, bf16[512,512]{1,0:T(8,128)(2,1)S(1)}, u32[]{:S(2)}, u32[]{:S(2)}) %collective-permute-start.11) | collective-permute-done | bytes 524320 | tf_op jit(solution)/shard_map/ppermute | solution.py:236
  200.4 4.9 %collective-permute-done.12.refs_10_ = bf16[512,512]{1,0:T(8,128)(2,1)} collective-permute-done((bf16[512,512]{1,0:T(8,128)(2,1)S(1)}, bf16[512,512]{1,0:T(8,128)(2,1)}, u32[]{:S(2)}, u32[]{:S(2)}) %collective-permute-start.12) | collective-permute-done | bytes 524320 | tf_op jit(solution)/shard_map/ppermute | solution.py:236
  205.3 3.7 %collective-permute-done.13.refs_14_ = bf16[512,512]{1,0:T(8,128)(2,1)} collective-permute-done((bf16[512,512]{1,0:T(8,128)(2,1)S(1)}, bf16[512,512]{1,0:T(8,128)(2,1)}, u32[]{:S(2)}, u32[]{:S(2)}) %collective-permute-start.13) | collective-permute-done | bytes 524320 | tf_op jit(solution)/shard_map/ppermute | solution.py:236
  209.8 9.8 %all-to-all-start.4 = ((bf16[32,16,512]{2,1,0:T(8,128)(2,1)}), bf16[32,16,512]{2,1,0:T(8,128)(2,1)S(1)}, u32[]{:S(2)}, u32[]{:S(2)}) async-start(bf16[32,16,512]{2,1,0:T(8,128)(2,1)} %broadcast_in_dim.23), calls=%async_computation.4 | async-start | bytes 1048576 | tf_op jit(solution)/shard_map/all_to_all | solution.py:228
  222.3 2.1 collective-permute-start.16
  225.0 8.2 %collective-permute-done.14.refs_11_ = bf16[512,512]{1,0:T(8,128)(2,1)S(1)} collective-permute-done((bf16[512,512]{1,0:T(8,128)(2,1)S(1)}, bf16[512,512]{1,0:T(8,128)(2,1)S(1)}, u32[]{:S(2)}, u32[]{:S(2)}) %collective-permute-start.14) | collective-permute-done | bytes 524320 | tf_op jit(solution)/shard_map/ppermute | solution.py:236
  233.3 7.4 %collective-permute-done.15.refs_12_ = bf16[512,512]{1,0:T(8,128)(2,1)S(1)} collective-permute-done((bf16[512,512]{1,0:T(8,128)(2,1)S(1)}, bf16[512,512]{1,0:T(8,128)(2,1)S(1)}, u32[]{:S(2)}, u32[]{:S(2)}) %collective-permute-start.15) | collective-permute-done | bytes 524320 | tf_op jit(solution)/shard_map/ppermute | solution.py:236
  242.3 3.8 %finish.1 = bf16[1,1024,512]{2,1,0:T(8,128)(2,1)} custom-call(s32[3]{0:T(128)} %pad_add_fusion.1.state, bf16[512,512]{1,0:T(8,128)(2,1)} %copy-done.4, bf16[512,512]{1,0:T(8,128)(2,1)} %copy-done.5, bf16[512,512]{1,0:T(8,128)(2,1)} %copy-done.6, bf16[512,512]{1,0:T(8,128)(2,1)} %copy-done.7, bf16[512,512]{1,0:T(8,128)(2,1)} %copy-done.8, ...), custom_call_target="tpu_custom_call" | custom-call | tf_op jit(solution)/shard_map/finish/pallas_call | solution.py:283
  (73 shorter events, 23.0 us)
Async XLA Ops:
  1.8 22.9 %all-to-all-start = ((bf16[32,40,128]{2,1,0:T(8,128)(2,1)}), bf16[32,40,128]{2,1,0:T(8,128)(2,1)S(1)}, u32[]{:S(2)}, u32[]{:S(2)}) async-start(bf16[32,40,128]{2,1,0:T(8,128)(2,1)} %bitcast.29), calls=%async_computation | async-start | bytes 655360 | tf_op jit(solution)/shard_map/all_to_all | solution.py:228
  17.7 3.0 %collective-permute-start = (s32[32,2]{0,1:T(2,128)S(1)}, s32[32,2]{0,1:T(2,128)S(1)}, u32[]{:S(2)}, u32[]{:S(2)}) collective-permute-start(s32[32,2]{0,1:T(2,128)S(1)} %copy.30), channel_id=1, source_target_pairs={{0,256},{256,0},{1,257},{257,1},{2,258},{258,2},{3,259},{259,3},{4... | collective-permute-start | bytes 776 | tf_op jit(solution)/shard_map/ppermute | solution.py:314
  45.5 38.9 %copy-start = (bf16[1,1024,512]{2,1,0:T(8,128)(2,1)S(1)}, bf16[1,1024,512]{2,1,0:T(8,128)(2,1)}, u32[]{:S(2)}) copy-start(bf16[1,1024,512]{2,1,0:T(8,128)(2,1)} %refs_17_.1) | copy-start | bytes 3145732
  45.5 104.5 %all-to-all-start.2 = ((bf16[128,128,128]{2,1,0:T(8,128)(2,1)}), bf16[128,128,128]{2,1,0:T(8,128)(2,1)}, u32[]{:S(2)}, u32[]{:S(2)}) async-start(bf16[128,128,128]{2,1,0:T(8,128)(2,1)} %get-tuple-element.27), calls=%async_computation.2 | async-start | bytes 8388608 | tf_op jit(solution)/shard_map/all_to_all | solution.py:228
  85.5 40.8 %copy-start.4 = (bf16[512,512]{1,0:T(8,128)(2,1)}, bf16[512,512]{1,0:T(8,128)(2,1)S(1)}, u32[]{:S(2)}) copy-start(bf16[512,512]{1,0:T(8,128)(2,1)S(1)} %fusion.refs_0_) | copy-start | bytes 1572868
  85.5 18.4 %collective-permute-start.1 = (bf16[512,512]{1,0:T(8,128)(2,1)S(1)}, bf16[512,512]{1,0:T(8,128)(2,1)}, u32[]{:S(2)}, u32[]{:S(2)}) collective-permute-start(bf16[512,512]{1,0:T(8,128)(2,1)S(1)} %fusion.refs_0_), channel_id=1, source_target_pairs={{8,10},{16,20},{24,30},{264,266},{272,276},{280,286}} | collective-permute-start | bytes 1572872 | tf_op jit(solution)/shard_map/ppermute | solution.py:337
  92.4 22.7 %collective-permute-start.2 = (bf16[512,512]{1,0:T(8,128)(2,1)S(1)}, bf16[512,512]{1,0:T(8,128)(2,1)S(1)}, u32[]{:S(2)}, u32[]{:S(2)}) collective-permute-start(bf16[512,512]{1,0:T(8,128)(2,1)S(1)} %fusion.refs_0_), channel_id=1, source_target_pairs={{0,1},{8,9},{16,17},{24,25},{32,33},{40,41},{48,49},{56,57},{64,65... | collective-permute-start | bytes 1572872 | tf_op jit(solution)/shard_map/ppermute | solution.py:236
  93.7 32.6 %collective-permute-start.3 = (bf16[512,512]{1,0:T(8,128)(2,1)S(1)}, bf16[512,512]{1,0:T(8,128)(2,1)S(1)}, u32[]{:S(2)}, u32[]{:S(2)}) collective-permute-start(bf16[512,512]{1,0:T(8,128)(2,1)S(1)} %fusion.refs_0_), channel_id=1, source_target_pairs={{0,2},{8,10},{16,18},{24,26},{32,34},{40,42},{48,50},{56,58},{64,6... | collective-permute-start | bytes 1572872 | tf_op jit(solution)/shard_map/ppermute | solution.py:236
  95.0 42.5 %collective-permute-start.4 = (bf16[512,512]{1,0:T(8,128)(2,1)S(1)}, bf16[512,512]{1,0:T(8,128)(2,1)S(1)}, u32[]{:S(2)}, u32[]{:S(2)}) collective-permute-start(bf16[512,512]{1,0:T(8,128)(2,1)S(1)} %fusion.refs_0_), channel_id=1, source_target_pairs={{0,3},{8,11},{16,19},{24,27},{32,35},{40,43},{48,51},{56,59},{64,6... | collective-permute-start | bytes 1572872 | tf_op jit(solution)/shard_map/ppermute | solution.py:236
  96.4 51.8 %collective-permute-start.5 = (bf16[512,512]{1,0:T(8,128)(2,1)S(1)}, bf16[512,512]{1,0:T(8,128)(2,1)S(1)}, u32[]{:S(2)}, u32[]{:S(2)}) collective-permute-start(bf16[512,512]{1,0:T(8,128)(2,1)S(1)} %fusion.refs_0_), channel_id=1, source_target_pairs={{0,4},{8,12},{16,20},{24,28},{32,36},{40,44},{48,52},{56,60},{64,6... | collective-permute-start | bytes 1572872 | tf_op jit(solution)/shard_map/ppermute | solution.py:236
  103.8 44.4 %collective-permute-start.6 = (bf16[512,512]{1,0:T(8,128)(2,1)S(1)}, bf16[512,512]{1,0:T(8,128)(2,1)S(1)}, u32[]{:S(2)}, u32[]{:S(2)}) collective-permute-start(bf16[512,512]{1,0:T(8,128)(2,1)S(1)} %fusion.refs_0_), channel_id=1, source_target_pairs={{0,5},{8,13},{16,21},{24,29},{32,37},{40,45},{48,53},{56,61},{64,6... | collective-permute-start | bytes 1572872 | tf_op jit(solution)/shard_map/ppermute | solution.py:236
  115.1 33.1 %copy-start.5 = (bf16[512,512]{1,0:T(8,128)(2,1)}, bf16[512,512]{1,0:T(8,128)(2,1)S(1)}, u32[]{:S(2)}) copy-start(bf16[512,512]{1,0:T(8,128)(2,1)S(1)} %collective-permute-done.2.refs_1_) | copy-start | bytes 1572868
  115.1 33.1 %collective-permute-start.7 = (bf16[512,512]{1,0:T(8,128)(2,1)S(1)}, bf16[512,512]{1,0:T(8,128)(2,1)S(1)}, u32[]{:S(2)}, u32[]{:S(2)}) collective-permute-start(bf16[512,512]{1,0:T(8,128)(2,1)S(1)} %fusion.refs_0_), channel_id=1, source_target_pairs={{0,6},{8,14},{16,22},{24,30},{32,38},{40,46},{48,54},{56,62},{64,7... | collective-permute-start | bytes 1572872 | tf_op jit(solution)/shard_map/ppermute | solution.py:236
  126.3 21.9 %copy-start.6 = (bf16[512,512]{1,0:T(8,128)(2,1)}, bf16[512,512]{1,0:T(8,128)(2,1)S(1)}, u32[]{:S(2)}) copy-start(bf16[512,512]{1,0:T(8,128)(2,1)S(1)} %collective-permute-done.3.refs_2_) | copy-start | bytes 1572868
  126.3 23.7 %collective-permute-start.8 = (bf16[512,512]{1,0:T(8,128)(2,1)S(1)}, bf16[512,512]{1,0:T(8,128)(2,1)}, u32[]{:S(2)}, u32[]{:S(2)}) collective-permute-start(bf16[512,512]{1,0:T(8,128)(2,1)S(1)} %fusion.refs_0_), channel_id=1, source_target_pairs={{0,7},{8,15},{16,23},{24,31},{32,39},{40,47},{48,55},{56,63},{64,7... | collective-permute-start | bytes 1572872 | tf_op jit(solution)/shard_map/ppermute | solution.py:236
  137.5 10.7 %copy-start.7 = (bf16[512,512]{1,0:T(8,128)(2,1)}, bf16[512,512]{1,0:T(8,128)(2,1)S(1)}, u32[]{:S(2)}) copy-start(bf16[512,512]{1,0:T(8,128)(2,1)S(1)} %collective-permute-done.4.refs_3_) | copy-start | bytes 1572868
  154.4 87.1 %copy-start.1 = (f32[512,512]{1,0:T(8,128)}, f32[512,512]{1,0:T(8,128)S(1)}, u32[]{:S(2)}) copy-start(f32[512,512]{1,0:T(8,128)S(1)} %assemble.1.refs_18_) | copy-start | bytes 3145732
  154.4 70.0 %copy-start.15 = (s32[1,2,1]{1,2,0:T(1,128)S(1)}, s32[1,2,1]{1,2,0:T(1,128)}, u32[]{:S(2)}) copy-start(s32[1,2,1]{1,2,0:T(1,128)} %param.9) | copy-start | bytes 28
  156.3 85.2 %copy-start.2 = (bf16[512,512]{1,0:T(8,128)(2,1)}, bf16[512,512]{1,0:T(8,128)(2,1)S(1)}, u32[]{:S(2)}) copy-start(bf16[512,512]{1,0:T(8,128)(2,1)S(1)} %convolution_convert_fusion.1.refs_8_) | copy-start | bytes 1572868
  156.3 14.2 %collective-permute-start.9 = (bf16[512,512]{1,0:T(8,128)(2,1)S(1)}, bf16[512,512]{1,0:T(8,128)(2,1)S(1)}, u32[]{:S(2)}, u32[]{:S(2)}) collective-permute-start(bf16[512,512]{1,0:T(8,128)(2,1)S(1)} %convolution_convert_fusion.1.refs_8_), channel_id=1, source_target_pairs={{0,1},{8,11},{16,21},{24,31},{256,257},{264,267},{272,277},{280,287}} | collective-permute-start | bytes 1572872 | tf_op jit(solution)/shard_map/ppermute | solution.py:337
  172.4 36.6 %all-to-all-start.3 = ((bf16[32,16,512]{2,1,0:T(8,128)(2,1)}), bf16[32,16,512]{2,1,0:T(8,128)(2,1)S(1)}, u32[]{:S(2)}, u32[]{:S(2)}) async-start(bf16[32,16,512]{2,1,0:T(8,128)(2,1)} %bitcast.13), calls=%async_computation.3 | async-start | bytes 1048576 | tf_op jit(solution)/shard_map/all_to_all | solution.py:228
  182.8 13.7 %collective-permute-start.10 = (bf16[512,512]{1,0:T(8,128)(2,1)S(1)}, bf16[512,512]{1,0:T(8,128)(2,1)S(1)}, u32[]{:S(2)}, u32[]{:S(2)}) collective-permute-start(bf16[512,512]{1,0:T(8,128)(2,1)S(1)} %convolution_convert_fusion.1.refs_8_), channel_id=1, source_target_pairs={{0,1},{8,9},{16,17},{24,25},{32,33},{40,41},{48,49},{56,57},{64,65... | collective-permute-start | bytes 1572872 | tf_op jit(solution)/shard_map/ppermute | solution.py:236
  184.1 16.3 %collective-permute-start.11 = (bf16[512,512]{1,0:T(8,128)(2,1)S(1)}, bf16[512,512]{1,0:T(8,128)(2,1)S(1)}, u32[]{:S(2)}, u32[]{:S(2)}) collective-permute-start(bf16[512,512]{1,0:T(8,128)(2,1)S(1)} %convolution_convert_fusion.1.refs_8_), channel_id=1, source_target_pairs={{0,7},{8,15},{16,23},{24,31},{32,39},{40,47},{48,55},{56,63},{64,7... | collective-permute-start | bytes 1572872 | tf_op jit(solution)/shard_map/ppermute | solution.py:236
  188.1 17.2 %collective-permute-start.12 = (bf16[512,512]{1,0:T(8,128)(2,1)S(1)}, bf16[512,512]{1,0:T(8,128)(2,1)}, u32[]{:S(2)}, u32[]{:S(2)}) collective-permute-start(bf16[512,512]{1,0:T(8,128)(2,1)S(1)} %convolution_convert_fusion.1.refs_8_), channel_id=1, source_target_pairs={{0,2},{8,10},{16,18},{24,26},{32,34},{40,42},{48,50},{56,58},{64,6... | collective-permute-start | bytes 1572872 | tf_op jit(solution)/shard_map/ppermute | solution.py:236
  190.2 18.8 %collective-permute-start.13 = (bf16[512,512]{1,0:T(8,128)(2,1)S(1)}, bf16[512,512]{1,0:T(8,128)(2,1)}, u32[]{:S(2)}, u32[]{:S(2)}) collective-permute-start(bf16[512,512]{1,0:T(8,128)(2,1)S(1)} %convolution_convert_fusion.1.refs_8_), channel_id=1, source_target_pairs={{0,6},{8,14},{16,22},{24,30},{32,38},{40,46},{48,54},{56,62},{64,7... | collective-permute-start | bytes 1572872 | tf_op jit(solution)/shard_map/ppermute | solution.py:236
  196.4 45.1 %copy-start.11 = (bf16[512,512]{1,0:T(8,128)(2,1)}, bf16[512,512]{1,0:T(8,128)(2,1)S(1)}, u32[]{:S(2)}) copy-start(bf16[512,512]{1,0:T(8,128)(2,1)S(1)} %collective-permute-done.10.refs_9_) | copy-start | bytes 1572868
  200.4 41.1 %copy-start.12 = (bf16[512,512]{1,0:T(8,128)(2,1)}, bf16[512,512]{1,0:T(8,128)(2,1)S(1)}, u32[]{:S(2)}) copy-start(bf16[512,512]{1,0:T(8,128)(2,1)S(1)} %collective-permute-done.11.refs_15_) | copy-start | bytes 1572868
  209.8 31.7 %all-to-all-start.4 = ((bf16[32,16,512]{2,1,0:T(8,128)(2,1)}), bf16[32,16,512]{2,1,0:T(8,128)(2,1)S(1)}, u32[]{:S(2)}, u32[]{:S(2)}) async-start(bf16[32,16,512]{2,1,0:T(8,128)(2,1)} %broadcast_in_dim.23), calls=%async_computation.4 | async-start | bytes 1048576 | tf_op jit(solution)/shard_map/all_to_all | solution.py:228
  219.6 13.7 %collective-permute-start.14 = (bf16[512,512]{1,0:T(8,128)(2,1)S(1)}, bf16[512,512]{1,0:T(8,128)(2,1)S(1)}, u32[]{:S(2)}, u32[]{:S(2)}) collective-permute-start(bf16[512,512]{1,0:T(8,128)(2,1)S(1)} %convolution_convert_fusion.1.refs_8_), channel_id=1, source_target_pairs={{0,3},{8,11},{16,19},{24,27},{32,35},{40,43},{48,51},{56,59},{64,6... | collective-permute-start | bytes 1572872 | tf_op jit(solution)/shard_map/ppermute | solution.py:236
  220.9 19.7 %collective-permute-start.15 = (bf16[512,512]{1,0:T(8,128)(2,1)S(1)}, bf16[512,512]{1,0:T(8,128)(2,1)S(1)}, u32[]{:S(2)}, u32[]{:S(2)}) collective-permute-start(bf16[512,512]{1,0:T(8,128)(2,1)S(1)} %convolution_convert_fusion.1.refs_8_), channel_id=1, source_target_pairs={{0,4},{8,12},{16,20},{24,28},{32,36},{40,44},{48,52},{56,60},{64,6... | collective-permute-start | bytes 1572872 | tf_op jit(solution)/shard_map/ppermute | solution.py:236
  222.3 19.2 %collective-permute-start.16 = (bf16[512,512]{1,0:T(8,128)(2,1)S(1)}, bf16[512,512]{1,0:T(8,128)(2,1)}, u32[]{:S(2)}, u32[]{:S(2)}) collective-permute-start(bf16[512,512]{1,0:T(8,128)(2,1)S(1)} %convolution_convert_fusion.1.refs_8_), channel_id=1, source_target_pairs={{0,5},{8,13},{16,21},{24,29},{32,37},{40,45},{48,53},{56,61},{64,6... | collective-permute-start | bytes 1572872 | tf_op jit(solution)/shard_map/ppermute | solution.py:236
  233.3 7.4 %copy-start.13 = (bf16[512,512]{1,0:T(8,128)(2,1)}, bf16[512,512]{1,0:T(8,128)(2,1)S(1)}, u32[]{:S(2)}) copy-start(bf16[512,512]{1,0:T(8,128)(2,1)S(1)} %collective-permute-done.14.refs_11_) | copy-start | bytes 1572868
  (5 other events, 4.2 us)

commit v6 on v4

--- a/solution.py
+++ b/solution.py
@@ -229,6 +229,7 @@
 
 
 HOLDERS = 4
+QUARTERS = 4
 
 
 def hand_out(parts, axis, devices):
@@ -337,6 +338,7 @@
     columns = lax.axis_size("col")
     front = lax.axis_index("front")
     column = lax.axis_index("col")
+    part_rows = TILE // rows_axis
     first = window[0, :TILE]
     packed = pack_pivot(window).reshape(rows_axis, -1, SB)
     share = packed.shape[1]
@@ -366,10 +368,14 @@
         ).astype(BF16)
 
     def to_plane(lower, odd):
-        pairs = [
-            ((c // 2) * columns, (c // 2) * columns + c) for c in range(max(odd, 1), columns) if c % 2 == odd
-        ]
-        return lax.ppermute(lower, ("row", "col"), pairs)
+        planes = [c for c in range(1, columns) if c % 2 == odd]
+        quarters = lower.reshape(-1, QUARTERS, part_rows, TILE)
+        mine = None
+        for k in range(QUARTERS):
+            pairs = [((c // 2) * columns, k * columns + c) for c in planes]
+            got = lax.ppermute(quarters[:, k], ("row", "col"), pairs)
+            mine = got if mine is None else mine + got
+        return mine
 
     lower_first = solve(first)
     even = to_plane(lower_first, 0)
@@ -379,12 +385,15 @@
     lower_second = solve(added)
     odd = to_plane(lower_second, 1)
     piece = jnp.where(column % 2 == 0, even, odd)
-    piece, under = lax.optimization_barrier((piece, to_holders(lower_second)))
+    groups = [list(range(k, rows_axis, QUARTERS)) for k in range(QUARTERS)]
+    got = lax.all_to_all(
+        piece, "row", split_axis=0, concat_axis=0, axis_index_groups=groups, tiled=True
+    )
+    got, under = lax.optimization_barrier((got, to_holders(lower_second)))
     under = from_holders(under)
-    got = swap(piece.reshape(rows_axis, -1, TILE), "row")
-    got, *under[: HOLDERS + 1] = lax.optimization_barrier((got, *under[: HOLDERS + 1]))
-    owned = lax.dynamic_index_in_dim(got, column // 2, 0)
-    partner = swap(jnp.broadcast_to(owned, got.shape), "row").reshape(TILE, TILE)
+    partner = swap(
+        jnp.broadcast_to(got[:1], (rows_axis, part_rows, TILE)), "row"
+    ).reshape(TILE, TILE)
     state = jnp.concatenate([jnp.full((1,), column, jnp.int32), pattern[0, :, 0]])
     return finish(state, upper, under, partner, window, added)
 

time: 238 us -> 233 us (0.979)
  the two profiles are of different devices: /device:TPU:8 before, /device:TPU:2 now
where the time goes in v6:
time: 233 us; the launch traced here: 231 us
  starting transfers between devices  103 us (44%)
  waiting for transfers between devices  49 us (21%)
  Pallas kernels  47 us (20%)
  blocking collectives  20.1 us (9%)
  local copies, waits for them, and re-layouts  5.38 us (2%)
  other arithmetic  3.23 us (1%)
  matrix products  2.94 us (1%)
    ppermute x14, starting transfers between devices, from_holders(): lax.ppermute(mine, 'col', [(i, (i - t) % size) for i in column_holders()])  34.5 us
    pallas_call x1, Pallas kernels, inverse_factor(): pl.pallas_call(inverse_kernel, out_shape=jax.ShapeDtypeStruct((n, n), F32...  32.2 us
    all_to_all x3, starting transfers between devices, swap(): return lax.all_to_all(block, axis, split_axis=0, concat_axis=0, tiled=True)  24.1 us
    ppermute x8, starting transfers between devices, to_plane(): got = lax.ppermute(quarters[:, k], ('row', 'col'), pairs)  21.6 us
    all_to_all x1, blocking collectives, swap(): return lax.all_to_all(block, axis, split_axis=0, concat_axis=0, tiled=True)  20.1 us
    ppermute x6, starting transfers between devices, hand_out(): mine = mine + lax.ppermute(part, axis, [(0, device)])  17.4 us
    ppermute x14, waiting for transfers between devices, from_holders(): lax.ppermute(mine, 'col', [(i, (i - t) % size) for i in column_holders()])  16.9 us
    all_to_all x3, waiting for transfers between devices, swap(): return lax.all_to_all(block, axis, split_axis=0, concat_axis=0, tiled=True)  12.2 us
  transfers between devices with their start and end apart: 33, of which 16 were waited for; matrix products, arithmetic and copies ran while one was open for 2% of the time, Pallas kernels for 16%

profile of v6, /device:TPU:2, one launch (start us, length us, event | category | flops | bytes accessed | tf_op | source)
XLA Modules:
  0.0 231.5 jit_solution(9202036515983926047)
XLA Ops:
  0.0 1.8 pack.1
  1.8 10.2 %all-to-all-start = ((bf16[32,40,128]{2,1,0:T(8,128)(2,1)}), bf16[32,40,128]{2,1,0:T(8,128)(2,1)S(1)}, u32[]{:S(2)}, u32[]{:S(2)}) async-start(bf16[32,40,128]{2,1,0:T(8,128)(2,1)} %bitcast.64), calls=%async_computation | async-start | bytes 655360 | tf_op jit(solution)/shard_map/all_to_all | solution.py:228
  12.1 4.7 %place.1 = (bf16[128,128,128]{2,1,0:T(8,128)(2,1)}, s32[128]{0:T(128)}) custom-call(s32[64]{0:T(128)} %bitcast.66, s32[64]{0:T(128)} %slots.1, bf16[64,128,128]{2,1,0:T(8,128)(2,1)} %children.1), custom_call_target="tpu_custom_call" | custom-call | tf_op jit(solution)/shard_map/place/pallas_call | solution.py:50
  17.7 1.9 collective-permute-start
  20.9 3.8 %all-to-all-done = bf16[32,40,128]{2,1,0:T(8,128)(2,1)S(1)} async-done(((bf16[32,40,128]{2,1,0:T(8,128)(2,1)}), bf16[32,40,128]{2,1,0:T(8,128)(2,1)S(1)}, u32[]{:S(2)}, u32[]{:S(2)}) %all-to-all-start) | async-done | bytes 327712 | tf_op jit(solution)/shard_map/all_to_all | solution.py:228
  25.0 20.1 %all_to_all.25 = bf16[32,48,128]{2,1,0:T(8,128)(2,1)S(1)} all-to-all(bf16[32,48,128]{2,1,0:T(8,128)(2,1)S(1)} %copy.56), channel_id=1, replica_groups=mesh['front'=2,'row'=32,'col'=8] {'row'}, dimensions={0} | all-to-all | bytes 786432 | tf_op jit(solution)/shard_map/all_to_all | solution.py:228
  45.6 6.7 %all-to-all-start.2 = ((bf16[128,128,128]{2,1,0:T(8,128)(2,1)}), bf16[128,128,128]{2,1,0:T(8,128)(2,1)}, u32[]{:S(2)}, u32[]{:S(2)}) async-start(bf16[128,128,128]{2,1,0:T(8,128)(2,1)} %get-tuple-element.24), calls=%async_computation.2 | async-start | bytes 8388608 | tf_op jit(solution)/shard_map/all_to_all | solution.py:228
  52.3 32.2 %inverse.1 = f32[512,512]{1,0:T(8,128)S(1)} custom-call(bf16[1280,128]{1,0:T(8,128)(2,1)S(1)} %bitcast.58), custom_call_target="tpu_custom_call" | custom-call | flops 536870912 | bytes 1572864 | tf_op jit(solution)/shard_map/inverse/pallas_call | solution.py:198
  85.6 10.9 %collective-permute-start.7 = (bf16[128,512]{1,0:T(8,128)(2,1)S(1)}, bf16[128,512]{1,0:T(8,128)(2,1)S(1)}, u32[]{:S(2)}, u32[]{:S(2)}) collective-permute-start(bf16[128,512]{1,0:T(8,128)(2,1)S(1)} %get-tuple-element.48), channel_id=1, source_target_pairs={{0,6},{8,14},{16,22},{24,30},{32,38},{40,46},{48,54},{56,62},{64,7... | collective-permute-start | bytes 393224 | tf_op jit(solution)/shard_map/ppermute | solution.py:241
  103.8 1.9 collective-permute-start.2
  107.1 1.6 collective-permute-done.4
  108.7 1.9 collective-permute-start.9
  113.1 2.3 %collective-permute-done.1 = bf16[8,16,512]{2,1,0:T(8,128)(2,1)S(1)} collective-permute-done((bf16[8,16,512]{2,1,0:T(8,128)(2,1)}, bf16[8,16,512]{2,1,0:T(8,128)(2,1)S(1)}, u32[]{:S(2)}, u32[]{:S(2)}) %collective-permute-start.1) | collective-permute-done | bytes 131104 | tf_op jit(solution)/shard_map/ppermute | solution.py:376
  115.5 2.5 %collective-permute-start.11 = (bf16[128,512]{1,0:T(8,128)(2,1)S(1)}, bf16[128,512]{1,0:T(8,128)(2,1)S(1)}, u32[]{:S(2)}, u32[]{:S(2)}) collective-permute-start(bf16[128,512]{1,0:T(8,128)(2,1)S(1)} %fusion.15.refs_0_), channel_id=1, source_target_pairs={{0,4},{2,6},{4,0},{6,2},{8,12},{10,14},{12,8},{14,10},{16,20},{18,... | collective-permute-start | bytes 393224 | tf_op jit(solution)/shard_map/ppermute | solution.py:259
  119.7 5.2 %collective-permute-start.13 = (bf16[128,512]{1,0:T(8,128)(2,1)S(1)}, bf16[128,512]{1,0:T(8,128)(2,1)S(1)}, u32[]{:S(2)}, u32[]{:S(2)}) collective-permute-start(bf16[128,512]{1,0:T(8,128)(2,1)S(1)} %fusion.15.refs_0_), channel_id=1, source_target_pairs={{0,2},{2,4},{4,6},{6,0},{8,10},{10,12},{12,14},{14,8},{16,18},{18,... | collective-permute-start | bytes 393224 | tf_op jit(solution)/shard_map/ppermute | solution.py:259
  129.4 6.2 %collective-permute-done.13.refs_6_ = bf16[128,512]{1,0:T(8,128)(2,1)S(1)} collective-permute-done((bf16[128,512]{1,0:T(8,128)(2,1)S(1)}, bf16[128,512]{1,0:T(8,128)(2,1)S(1)}, u32[]{:S(2)}, u32[]{:S(2)}) %collective-permute-start.13) | collective-permute-done | bytes 131104 | tf_op jit(solution)/shard_map/ppermute | solution.py:259
  136.9 8.4 %all-to-all-done.2.incoming = bf16[128,128,128]{2,1,0:T(8,128)(2,1)} async-done(((bf16[128,128,128]{2,1,0:T(8,128)(2,1)}), bf16[128,128,128]{2,1,0:T(8,128)(2,1)}, u32[]{:S(2)}, u32[]{:S(2)}) %all-to-all-start.2) | async-done | bytes 4194336 | tf_op jit(solution)/shard_map/all_to_all | solution.py:228
  145.3 4.4 %assemble.1.refs_18_ = f32[512,512]{1,0:T(8,128)S(1)} custom-call(s32[128]{0:T(128)S(1)} %reshape.149.tags, bf16[128,128,128]{2,1,0:T(8,128)(2,1)} %all-to-all-done.2.incoming, bf16[1,1024,512]{2,1,0:T(8,128)(2,1)S(1)} %copy-done), custom_call_target="tpu_custom_call" | custom-call | tf_op jit(solution)/shard_map/assemble/pallas_call | solution.py:94
  149.7 1.9 convolution_convert_fusion.1
  151.7 11.9 %collective-permute-start.18 = (bf16[8,16,512]{2,1,0:T(8,128)(2,1)S(1)}, bf16[8,16,512]{2,1,0:T(8,128)(2,1)S(1)}, u32[]{:S(2)}, u32[]{:S(2)}) collective-permute-start(bf16[8,16,512]{2,1,0:T(8,128)(2,1)S(1)} %get-tuple-element.45), channel_id=1, source_target_pairs={{0,25},{8,27},{16,29},{24,31},{256,281},{264,283},{272,285},{280,2... | collective-permute-start | bytes 393224 | tf_op jit(solution)/shard_map/ppermute | solution.py:376
  171.5 1.5 collective-permute-done.15
  173.0 2.8 %collective-permute-done.16 = bf16[8,16,512]{2,1,0:T(8,128)(2,1)S(1)} collective-permute-done((bf16[8,16,512]{2,1,0:T(8,128)(2,1)S(1)}, bf16[8,16,512]{2,1,0:T(8,128)(2,1)S(1)}, u32[]{:S(2)}, u32[]{:S(2)}) %collective-permute-start.16) | collective-permute-done | bytes 131104 | tf_op jit(solution)/shard_map/ppermute | solution.py:376
  176.5 3.4 %all-to-all-start.3 = ((bf16[8,16,512]{2,1,0:T(8,128)(2,1)}), bf16[8,16,512]{2,1,0:T(8,128)(2,1)S(1)}, u32[]{:S(2)}, u32[]{:S(2)}) async-start(bf16[8,16,512]{2,1,0:T(8,128)(2,1)} %add_select_fusion), calls=%async_computation.3 | async-start | bytes 262144 | tf_op jit(solution)/shard_map/all_to_all | solution.py:389
  180.8 8.1 %all-to-all-done.3 = bf16[8,16,512]{2,1,0:T(8,128)(2,1)S(1)} async-done(((bf16[8,16,512]{2,1,0:T(8,128)(2,1)}), bf16[8,16,512]{2,1,0:T(8,128)(2,1)S(1)}, u32[]{:S(2)}, u32[]{:S(2)}) %all-to-all-start.3) | async-done | bytes 131104 | tf_op jit(solution)/shard_map/all_to_all | solution.py:389
  189.8 7.1 %all-to-all-start.4 = ((bf16[32,16,512]{2,1,0:T(8,128)(2,1)}), bf16[32,16,512]{2,1,0:T(8,128)(2,1)S(1)}, u32[]{:S(2)}, u32[]{:S(2)}) async-start(bf16[32,16,512]{2,1,0:T(8,128)(2,1)} %broadcast_in_dim.23), calls=%async_computation.4 | async-start | bytes 1048576 | tf_op jit(solution)/shard_map/all_to_all | solution.py:228
  196.9 5.2 %collective-permute-start.22 = (bf16[128,512]{1,0:T(8,128)(2,1)S(1)}, bf16[128,512]{1,0:T(8,128)(2,1)S(1)}, u32[]{:S(2)}, u32[]{:S(2)}) collective-permute-start(bf16[128,512]{1,0:T(8,128)(2,1)S(1)} %fusion.12.refs_8_), channel_id=1, source_target_pairs={{0,7},{2,1},{4,3},{6,5},{8,15},{10,9},{12,11},{14,13},{16,23},{18,... | collective-permute-start | bytes 393224 | tf_op jit(solution)/shard_map/ppermute | solution.py:259
  202.1 4.2 %collective-permute-start.23 = (bf16[128,512]{1,0:T(8,128)(2,1)S(1)}, bf16[128,512]{1,0:T(8,128)(2,1)S(1)}, u32[]{:S(2)}, u32[]{:S(2)}) collective-permute-start(bf16[128,512]{1,0:T(8,128)(2,1)S(1)} %fusion.12.refs_8_), channel_id=1, source_target_pairs={{0,6},{2,0},{4,2},{6,4},{8,14},{10,8},{12,10},{14,12},{16,22},{18,... | collective-permute-start | bytes 393224 | tf_op jit(solution)/shard_map/ppermute | solution.py:259
  207.7 1.9 collective-permute-start.25
  210.9 4.3 %collective-permute-start.27 = (bf16[128,512]{1,0:T(8,128)(2,1)S(1)}, bf16[128,512]{1,0:T(8,128)(2,1)S(1)}, u32[]{:S(2)}, u32[]{:S(2)}) collective-permute-start(bf16[128,512]{1,0:T(8,128)(2,1)S(1)} %fusion.12.refs_8_), channel_id=1, source_target_pairs={{0,2},{2,4},{4,6},{6,0},{8,10},{10,12},{12,14},{14,8},{16,18},{18,... | collective-permute-start | bytes 393224 | tf_op jit(solution)/shard_map/ppermute | solution.py:259
  217.1 7.0 %collective-permute-done.25.refs_12_ = bf16[128,512]{1,0:T(8,128)(2,1)S(1)} collective-permute-done((bf16[128,512]{1,0:T(8,128)(2,1)S(1)}, bf16[128,512]{1,0:T(8,128)(2,1)S(1)}, u32[]{:S(2)}, u32[]{:S(2)}) %collective-permute-start.25) | collective-permute-done | bytes 131104 | tf_op jit(solution)/shard_map/ppermute | solution.py:259
  224.2 2.3 collective-permute-done.27.refs_14_
  227.3 4.0 %finish.1 = bf16[1,1024,512]{2,1,0:T(8,128)(2,1)} custom-call(s32[3]{0:T(128)} %pad_add_fusion.1.state, bf16[128,512]{1,0:T(8,128)(2,1)} %copy-done.3, bf16[128,512]{1,0:T(8,128)(2,1)} %copy-done.5, bf16[128,512]{1,0:T(8,128)(2,1)} %copy-done.6, bf16[128,512]{1,0:T(8,128)(2,1)} %copy-done.7, bf16[128,512]{1,0:T(8,128)(2,1)} %copy-done.8, ...), custom_call_target="tpu_custom_call" | custom-call | tf_op jit(solution)/shard_map/finish/pallas_call | solution.py:318
  (112 shorter events, 38.1 us)
Async XLA Ops:
  1.8 22.9 %all-to-all-start = ((bf16[32,40,128]{2,1,0:T(8,128)(2,1)}), bf16[32,40,128]{2,1,0:T(8,128)(2,1)S(1)}, u32[]{:S(2)}, u32[]{:S(2)}) async-start(bf16[32,40,128]{2,1,0:T(8,128)(2,1)} %bitcast.64), calls=%async_computation | async-start | bytes 655360 | tf_op jit(solution)/shard_map/all_to_all | solution.py:228
  45.6 99.7 %all-to-all-start.2 = ((bf16[128,128,128]{2,1,0:T(8,128)(2,1)}), bf16[128,128,128]{2,1,0:T(8,128)(2,1)}, u32[]{:S(2)}, u32[]{:S(2)}) async-start(bf16[128,128,128]{2,1,0:T(8,128)(2,1)} %get-tuple-element.24), calls=%async_computation.2 | async-start | bytes 8388608 | tf_op jit(solution)/shard_map/all_to_all | solution.py:228
  85.6 16.9 %collective-permute-start.7 = (bf16[128,512]{1,0:T(8,128)(2,1)S(1)}, bf16[128,512]{1,0:T(8,128)(2,1)S(1)}, u32[]{:S(2)}, u32[]{:S(2)}) collective-permute-start(bf16[128,512]{1,0:T(8,128)(2,1)S(1)} %get-tuple-element.48), channel_id=1, source_target_pairs={{0,6},{8,14},{16,22},{24,30},{32,38},{40,46},{48,54},{56,62},{64,7... | collective-permute-start | bytes 393224 | tf_op jit(solution)/shard_map/ppermute | solution.py:241
  96.5 7.3 %collective-permute-start.6 = (bf16[128,512]{1,0:T(8,128)(2,1)S(1)}, bf16[128,512]{1,0:T(8,128)(2,1)S(1)}, u32[]{:S(2)}, u32[]{:S(2)}) collective-permute-start(bf16[128,512]{1,0:T(8,128)(2,1)S(1)} %get-tuple-element.47), channel_id=1, source_target_pairs={{0,4},{8,12},{16,20},{24,28},{32,36},{40,44},{48,52},{56,60},{64,6... | collective-permute-start | bytes 393224 | tf_op jit(solution)/shard_map/ppermute | solution.py:241
  97.8 7.9 %collective-permute-start.5 = (bf16[128,512]{1,0:T(8,128)(2,1)S(1)}, bf16[128,512]{1,0:T(8,128)(2,1)S(1)}, u32[]{:S(2)}, u32[]{:S(2)}) collective-permute-start(bf16[128,512]{1,0:T(8,128)(2,1)S(1)} %get-tuple-element.46), channel_id=1, source_target_pairs={{0,2},{8,10},{16,18},{24,26},{32,34},{40,42},{48,50},{56,58},{64,6... | collective-permute-start | bytes 393224 | tf_op jit(solution)/shard_map/ppermute | solution.py:241
  99.9 8.8 %collective-permute-start.4 = (bf16[8,16,512]{2,1,0:T(8,128)(2,1)S(1)}, bf16[8,16,512]{2,1,0:T(8,128)(2,1)S(1)}, u32[]{:S(2)}, u32[]{:S(2)}) collective-permute-start(bf16[8,16,512]{2,1,0:T(8,128)(2,1)S(1)} %get-tuple-element.51), channel_id=1, source_target_pairs={{8,26},{16,28},{24,30},{264,282},{272,284},{280,286}} | collective-permute-start | bytes 393224 | tf_op jit(solution)/shard_map/ppermute | solution.py:376
  101.2 10.7 %collective-permute-start.3 = (bf16[8,16,512]{2,1,0:T(8,128)(2,1)}, bf16[8,16,512]{2,1,0:T(8,128)(2,1)S(1)}, u32[]{:S(2)}, u32[]{:S(2)}) collective-permute-start(bf16[8,16,512]{2,1,0:T(8,128)(2,1)} %get-tuple-element.52), channel_id=1, source_target_pairs={{8,18},{16,20},{24,22},{264,274},{272,276},{280,278}} | collective-permute-start | bytes 393224 | tf_op jit(solution)/shard_map/ppermute | solution.py:376
  102.5 13.0 %collective-permute-start.1 = (bf16[8,16,512]{2,1,0:T(8,128)(2,1)}, bf16[8,16,512]{2,1,0:T(8,128)(2,1)S(1)}, u32[]{:S(2)}, u32[]{:S(2)}) collective-permute-start(bf16[8,16,512]{2,1,0:T(8,128)(2,1)} %get-tuple-element.50), channel_id=1, source_target_pairs={{8,2},{16,4},{24,6},{264,258},{272,260},{280,262}} | collective-permute-start | bytes 393224 | tf_op jit(solution)/shard_map/ppermute | solution.py:376
  103.8 14.6 %collective-permute-start.2 = (bf16[8,16,512]{2,1,0:T(8,128)(2,1)}, bf16[8,16,512]{2,1,0:T(8,128)(2,1)}, u32[]{:S(2)}, u32[]{:S(2)}) collective-permute-start(bf16[8,16,512]{2,1,0:T(8,128)(2,1)} %get-tuple-element.49), channel_id=1, source_target_pairs={{8,10},{16,12},{24,14},{264,266},{272,268},{280,270}} | collective-permute-start | bytes 393224 | tf_op jit(solution)/shard_map/ppermute | solution.py:376
  105.8 13.9 %collective-permute-start.8 = (bf16[128,512]{1,0:T(8,128)(2,1)S(1)}, bf16[128,512]{1,0:T(8,128)(2,1)S(1)}, u32[]{:S(2)}, u32[]{:S(2)}) collective-permute-start(bf16[128,512]{1,0:T(8,128)(2,1)S(1)} %fusion.15.refs_0_), channel_id=1, source_target_pairs={{0,7},{2,1},{4,3},{6,5},{8,15},{10,9},{12,11},{14,13},{16,23},{18,... | collective-permute-start | bytes 393224 | tf_op jit(solution)/shard_map/ppermute | solution.py:259
  108.7 16.3 %collective-permute-start.9 = (bf16[128,512]{1,0:T(8,128)(2,1)S(1)}, bf16[128,512]{1,0:T(8,128)(2,1)S(1)}, u32[]{:S(2)}, u32[]{:S(2)}) collective-permute-start(bf16[128,512]{1,0:T(8,128)(2,1)S(1)} %fusion.15.refs_0_), channel_id=1, source_target_pairs={{0,6},{2,0},{4,2},{6,4},{8,14},{10,8},{12,10},{14,12},{16,22},{18,... | collective-permute-start | bytes 393224 | tf_op jit(solution)/shard_map/ppermute | solution.py:259
  111.8 16.2 %collective-permute-start.10 = (bf16[128,512]{1,0:T(8,128)(2,1)S(1)}, bf16[128,512]{1,0:T(8,128)(2,1)S(1)}, u32[]{:S(2)}, u32[]{:S(2)}) collective-permute-start(bf16[128,512]{1,0:T(8,128)(2,1)S(1)} %fusion.15.refs_0_), channel_id=1, source_target_pairs={{0,5},{2,7},{4,1},{6,3},{8,13},{10,15},{12,9},{14,11},{16,21},{18,... | collective-permute-start | bytes 393224 | tf_op jit(solution)/shard_map/ppermute | solution.py:259
  115.5 14.0 %collective-permute-start.11 = (bf16[128,512]{1,0:T(8,128)(2,1)S(1)}, bf16[128,512]{1,0:T(8,128)(2,1)S(1)}, u32[]{:S(2)}, u32[]{:S(2)}) collective-permute-start(bf16[128,512]{1,0:T(8,128)(2,1)S(1)} %fusion.15.refs_0_), channel_id=1, source_target_pairs={{0,4},{2,6},{4,0},{6,2},{8,12},{10,14},{12,8},{14,10},{16,20},{18,... | collective-permute-start | bytes 393224 | tf_op jit(solution)/shard_map/ppermute | solution.py:259
  118.4 11.0 %collective-permute-start.12 = (bf16[128,512]{1,0:T(8,128)(2,1)S(1)}, bf16[128,512]{1,0:T(8,128)(2,1)S(1)}, u32[]{:S(2)}, u32[]{:S(2)}) collective-permute-start(bf16[128,512]{1,0:T(8,128)(2,1)S(1)} %fusion.15.refs_0_), channel_id=1, source_target_pairs={{0,3},{2,5},{4,7},{6,1},{8,11},{10,13},{12,15},{14,9},{16,19},{18,... | collective-permute-start | bytes 393224 | tf_op jit(solution)/shard_map/ppermute | solution.py:259
  119.7 15.9 %collective-permute-start.13 = (bf16[128,512]{1,0:T(8,128)(2,1)S(1)}, bf16[128,512]{1,0:T(8,128)(2,1)S(1)}, u32[]{:S(2)}, u32[]{:S(2)}) collective-permute-start(bf16[128,512]{1,0:T(8,128)(2,1)S(1)} %fusion.15.refs_0_), channel_id=1, source_target_pairs={{0,2},{2,4},{4,6},{6,0},{8,10},{10,12},{12,14},{14,8},{16,18},{18,... | collective-permute-start | bytes 393224 | tf_op jit(solution)/shard_map/ppermute | solution.py:259
  125.6 10.0 %collective-permute-start.14 = (bf16[128,512]{1,0:T(8,128)(2,1)S(1)}, bf16[128,512]{1,0:T(8,128)(2,1)S(1)}, u32[]{:S(2)}, u32[]{:S(2)}) collective-permute-start(bf16[128,512]{1,0:T(8,128)(2,1)S(1)} %fusion.15.refs_0_), channel_id=1, source_target_pairs={{0,1},{2,3},{4,5},{6,7},{8,9},{10,11},{12,13},{14,15},{16,17},{18,... | collective-permute-start | bytes 393224 | tf_op jit(solution)/shard_map/ppermute | solution.py:259
  151.7 17.2 %collective-permute-start.18 = (bf16[8,16,512]{2,1,0:T(8,128)(2,1)S(1)}, bf16[8,16,512]{2,1,0:T(8,128)(2,1)S(1)}, u32[]{:S(2)}, u32[]{:S(2)}) collective-permute-start(bf16[8,16,512]{2,1,0:T(8,128)(2,1)S(1)} %get-tuple-element.45), channel_id=1, source_target_pairs={{0,25},{8,27},{16,29},{24,31},{256,281},{264,283},{272,285},{280,2... | collective-permute-start | bytes 393224 | tf_op jit(solution)/shard_map/ppermute | solution.py:376
  163.6 6.6 %collective-permute-start.17 = (bf16[8,16,512]{2,1,0:T(8,128)(2,1)S(1)}, bf16[8,16,512]{2,1,0:T(8,128)(2,1)S(1)}, u32[]{:S(2)}, u32[]{:S(2)}) collective-permute-start(bf16[8,16,512]{2,1,0:T(8,128)(2,1)S(1)} %get-tuple-element.43), channel_id=1, source_target_pairs={{0,17},{8,19},{16,21},{24,23},{256,273},{264,275},{272,277},{280,2... | collective-permute-start | bytes 393224 | tf_op jit(solution)/shard_map/ppermute | solution.py:376
  164.9 8.1 %collective-permute-start.15 = (bf16[8,16,512]{2,1,0:T(8,128)(2,1)S(1)}, bf16[8,16,512]{2,1,0:T(8,128)(2,1)S(1)}, u32[]{:S(2)}, u32[]{:S(2)}) collective-permute-start(bf16[8,16,512]{2,1,0:T(8,128)(2,1)S(1)} %get-tuple-element.44), channel_id=1, source_target_pairs={{0,1},{8,3},{16,5},{24,7},{256,257},{264,259},{272,261},{280,263}} | collective-permute-start | bytes 393224 | tf_op jit(solution)/shard_map/ppermute | solution.py:376
  166.2 9.6 %collective-permute-start.16 = (bf16[8,16,512]{2,1,0:T(8,128)(2,1)S(1)}, bf16[8,16,512]{2,1,0:T(8,128)(2,1)S(1)}, u32[]{:S(2)}, u32[]{:S(2)}) collective-permute-start(bf16[8,16,512]{2,1,0:T(8,128)(2,1)S(1)} %get-tuple-element.42), channel_id=1, source_target_pairs={{0,9},{8,11},{16,13},{24,15},{256,265},{264,267},{272,269},{280,271}} | collective-permute-start | bytes 393224 | tf_op jit(solution)/shard_map/ppermute | solution.py:376
  167.5 12.4 %collective-permute-start.21 = (bf16[128,512]{1,0:T(8,128)(2,1)S(1)}, bf16[128,512]{1,0:T(8,128)(2,1)S(1)}, u32[]{:S(2)}, u32[]{:S(2)}) collective-permute-start(bf16[128,512]{1,0:T(8,128)(2,1)S(1)} %get-tuple-element.40), channel_id=1, source_target_pairs={{0,6},{8,14},{16,22},{24,30},{32,38},{40,46},{48,54},{56,62},{64,7... | collective-permute-start | bytes 393224 | tf_op jit(solution)/shard_map/ppermute | solution.py:241
  168.8 11.1 %collective-permute-start.20 = (bf16[128,512]{1,0:T(8,128)(2,1)S(1)}, bf16[128,512]{1,0:T(8,128)(2,1)S(1)}, u32[]{:S(2)}, u32[]{:S(2)}) collective-permute-start(bf16[128,512]{1,0:T(8,128)(2,1)S(1)} %get-tuple-element.41), channel_id=1, source_target_pairs={{0,4},{8,12},{16,20},{24,28},{32,36},{40,44},{48,52},{56,60},{64,6... | collective-permute-start | bytes 393224 | tf_op jit(solution)/shard_map/ppermute | solution.py:241
  170.2 10.5 %collective-permute-start.19 = (bf16[128,512]{1,0:T(8,128)(2,1)S(1)}, bf16[128,512]{1,0:T(8,128)(2,1)S(1)}, u32[]{:S(2)}, u32[]{:S(2)}) collective-permute-start(bf16[128,512]{1,0:T(8,128)(2,1)S(1)} %get-tuple-element.39), channel_id=1, source_target_pairs={{0,2},{8,10},{16,18},{24,26},{32,34},{40,42},{48,50},{56,58},{64,6... | collective-permute-start | bytes 393224 | tf_op jit(solution)/shard_map/ppermute | solution.py:241
  176.5 12.4 %all-to-all-start.3 = ((bf16[8,16,512]{2,1,0:T(8,128)(2,1)}), bf16[8,16,512]{2,1,0:T(8,128)(2,1)S(1)}, u32[]{:S(2)}, u32[]{:S(2)}) async-start(bf16[8,16,512]{2,1,0:T(8,128)(2,1)} %add_select_fusion), calls=%async_computation.3 | async-start | bytes 262144 | tf_op jit(solution)/shard_map/all_to_all | solution.py:389
  189.8 36.7 %all-to-all-start.4 = ((bf16[32,16,512]{2,1,0:T(8,128)(2,1)}), bf16[32,16,512]{2,1,0:T(8,128)(2,1)S(1)}, u32[]{:S(2)}, u32[]{:S(2)}) async-start(bf16[32,16,512]{2,1,0:T(8,128)(2,1)} %broadcast_in_dim.23), calls=%async_computation.4 | async-start | bytes 1048576 | tf_op jit(solution)/shard_map/all_to_all | solution.py:228
  196.9 14.0 %collective-permute-start.22 = (bf16[128,512]{1,0:T(8,128)(2,1)S(1)}, bf16[128,512]{1,0:T(8,128)(2,1)S(1)}, u32[]{:S(2)}, u32[]{:S(2)}) collective-permute-start(bf16[128,512]{1,0:T(8,128)(2,1)S(1)} %fusion.12.refs_8_), channel_id=1, source_target_pairs={{0,7},{2,1},{4,3},{6,5},{8,15},{10,9},{12,11},{14,13},{16,23},{18,... | collective-permute-start | bytes 393224 | tf_op jit(solution)/shard_map/ppermute | solution.py:259
  202.1 13.1 %collective-permute-start.23 = (bf16[128,512]{1,0:T(8,128)(2,1)S(1)}, bf16[128,512]{1,0:T(8,128)(2,1)S(1)}, u32[]{:S(2)}, u32[]{:S(2)}) collective-permute-start(bf16[128,512]{1,0:T(8,128)(2,1)S(1)} %fusion.12.refs_8_), channel_id=1, source_target_pairs={{0,6},{2,0},{4,2},{6,4},{8,14},{10,8},{12,10},{14,12},{16,22},{18,... | collective-permute-start | bytes 393224 | tf_op jit(solution)/shard_map/ppermute | solution.py:259
  206.4 10.8 %collective-permute-start.24 = (bf16[128,512]{1,0:T(8,128)(2,1)S(1)}, bf16[128,512]{1,0:T(8,128)(2,1)S(1)}, u32[]{:S(2)}, u32[]{:S(2)}) collective-permute-start(bf16[128,512]{1,0:T(8,128)(2,1)S(1)} %fusion.12.refs_8_), channel_id=1, source_target_pairs={{0,5},{2,7},{4,1},{6,3},{8,13},{10,15},{12,9},{14,11},{16,21},{18,... | collective-permute-start | bytes 393224 | tf_op jit(solution)/shard_map/ppermute | solution.py:259
  207.7 16.5 %collective-permute-start.25 = (bf16[128,512]{1,0:T(8,128)(2,1)S(1)}, bf16[128,512]{1,0:T(8,128)(2,1)S(1)}, u32[]{:S(2)}, u32[]{:S(2)}) collective-permute-start(bf16[128,512]{1,0:T(8,128)(2,1)S(1)} %fusion.12.refs_8_), channel_id=1, source_target_pairs={{0,4},{2,6},{4,0},{6,2},{8,12},{10,14},{12,8},{14,10},{16,20},{18,... | collective-permute-start | bytes 393224 | tf_op jit(solution)/shard_map/ppermute | solution.py:259
  209.6 14.6 %collective-permute-start.26 = (bf16[128,512]{1,0:T(8,128)(2,1)S(1)}, bf16[128,512]{1,0:T(8,128)(2,1)S(1)}, u32[]{:S(2)}, u32[]{:S(2)}) collective-permute-start(bf16[128,512]{1,0:T(8,128)(2,1)S(1)} %fusion.12.refs_8_), channel_id=1, source_target_pairs={{0,3},{2,5},{4,7},{6,1},{8,11},{10,13},{12,15},{14,9},{16,19},{18,... | collective-permute-start | bytes 393224 | tf_op jit(solution)/shard_map/ppermute | solution.py:259
  210.9 15.5 %collective-permute-start.27 = (bf16[128,512]{1,0:T(8,128)(2,1)S(1)}, bf16[128,512]{1,0:T(8,128)(2,1)S(1)}, u32[]{:S(2)}, u32[]{:S(2)}) collective-permute-start(bf16[128,512]{1,0:T(8,128)(2,1)S(1)} %fusion.12.refs_8_), channel_id=1, source_target_pairs={{0,2},{2,4},{4,6},{6,0},{8,10},{10,12},{12,14},{14,8},{16,18},{18,... | collective-permute-start | bytes 393224 | tf_op jit(solution)/shard_map/ppermute | solution.py:259
  215.2 11.2 %collective-permute-start.28 = (bf16[128,512]{1,0:T(8,128)(2,1)S(1)}, bf16[128,512]{1,0:T(8,128)(2,1)S(1)}, u32[]{:S(2)}, u32[]{:S(2)}) collective-permute-start(bf16[128,512]{1,0:T(8,128)(2,1)S(1)} %fusion.12.refs_8_), channel_id=1, source_target_pairs={{0,1},{2,3},{4,5},{6,7},{8,9},{10,11},{12,13},{14,15},{16,17},{18,... | collective-permute-start | bytes 393224 | tf_op jit(solution)/shard_map/ppermute | solution.py:259
  (21 other events, 374.1 us)

commit v7 on v6

--- a/solution.py
+++ b/solution.py
@@ -262,12 +262,19 @@
 
 def finish_kernel(size, state, *refs):
     halves = refs[:size], refs[size : 2 * size]
-    partner, base, added, out, parts, sem = refs[2 * size :]
+    partner_at, window, added_at, out, parts, partner, base, added, sem, rest_sem = refs[2 * size :]
     column = state[0]
     step = size // HOLDERS
     rows = TILE // HOLDERS
     shift = lax.rem(step - lax.rem(column, step), step)
     first = lax.div(column + shift, step)
+    others = [
+        pltpu.make_async_copy(partner_at, partner, rest_sem.at[0]),
+        pltpu.make_async_copy(window.at[0, pl.ds(0, TILE), :], base, rest_sem.at[1]),
+        pltpu.make_async_copy(added_at, added, rest_sem.at[2]),
+    ]
+    for copy in others:
+        copy.start()
     for s in range(step):
 
         @pl.when(shift == s)
@@ -284,6 +291,9 @@
             for copy in copies:
                 copy.wait()
 
+    for copy in others:
+        copy.wait()
+
     for k in range(HOLDERS):
         source = lax.rem(first + k, HOLDERS)
         at = pl.ds(pl.multiple_of(source * rows, rows), rows)
@@ -301,7 +311,7 @@
                     part, partner[...], (((1,), (1,)), ((), ())), preferred_element_type=F32
                 )
 
-            upper = base[0, at, :].astype(F32) - state[1].astype(F32) * product(parts[0, k])
+            upper = base[at, :].astype(F32) - state[1].astype(F32) * product(parts[0, k])
             out[0, at, :] = upper.astype(BF16)
             lower = added[at, :] - state[2].astype(F32) * product(parts[1, k])
             out[0, under, :] = lower.astype(BF16)
@@ -309,23 +319,20 @@
 
 def finish(state, upper, under, partner, window, added):
     size = len(upper)
-
-    def whole(x):
-        return pl.BlockSpec(x.shape, lambda i: (0,) * x.ndim)
-
-    tile = pl.BlockSpec((1, TILE, TILE), lambda i: (0, 0, 0))
     out = jax.ShapeDtypeStruct((1, 2 * TILE, TILE), BF16)
     return pl.pallas_call(
         functools.partial(finish_kernel, size),
         out_shape=out,
-        grid=(1,),
         in_specs=[pl.BlockSpec(memory_space=pltpu.SMEM)]
-        + [pl.BlockSpec(memory_space=pl.ANY)] * (2 * size)
-        + [whole(partner), tile, whole(added)],
-        out_specs=whole(out),
+        + [pl.BlockSpec(memory_space=pl.ANY)] * (2 * size + 3),
+        out_specs=pl.BlockSpec(memory_space=pltpu.VMEM),
         scratch_shapes=[
             pltpu.VMEM((2, HOLDERS, TILE // HOLDERS, TILE), BF16),
+            pltpu.VMEM((TILE, TILE), BF16),
+            pltpu.VMEM((TILE, TILE), BF16),
+            pltpu.VMEM((TILE, TILE), F32),
             pltpu.SemaphoreType.DMA((2 * HOLDERS,)),
+            pltpu.SemaphoreType.DMA((3,)),
         ],
         compiler_params=pltpu.CompilerParams(vmem_limit_bytes=56 << 20),
         name="finish",
@@ -391,6 +398,10 @@
     )
     got, under = lax.optimization_barrier((got, to_holders(lower_second)))
     under = from_holders(under)
+    near = [1, columns - 1, 2]
+    got, *arrived = lax.optimization_barrier((got, *(under[t] for t in near)))
+    for t, part in zip(near, arrived):
+        under[t] = part
     partner = swap(
         jnp.broadcast_to(got[:1], (rows_axis, part_rows, TILE)), "row"
     ).reshape(TILE, TILE)

time: 233 us -> 235 us (level)
  starting transfers between devices: 103 us -> 107 us
    ppermute x14, starting transfers between devices: 34.5 us -> 41.7 us  [from_holders(): lax.ppermute(mine, 'col', [(i, (i - t) % size) for i in column_holders()])]
    all_to_all x3, starting transfers between devices: 24.1 us -> 20.6 us  [swap(): return lax.all_to_all(block, axis, split_axis=0, concat_axis=0, tiled=True)]
  transfers between devices with their start and end apart: 33 -> 33, of which waited for: 16 -> 18; matrix products, arithmetic and copies ran while one was open for 2% -> 2% of each run, Pallas kernels for 16% -> 16%
where the time goes in v7:
time: 235 us; the launch traced here: 234 us
  starting transfers between devices  107 us (46%)
  waiting for transfers between devices  47.9 us (20%)
  Pallas kernels  46.7 us (20%)
  blocking collectives  20.2 us (9%)
  local copies, waits for them, and re-layouts  5.35 us (2%)
  other arithmetic  3.23 us (1%)
  matrix products  2.94 us (1%)
    ppermute x14, starting transfers between devices, from_holders(): lax.ppermute(mine, 'col', [(i, (i - t) % size) for i in column_holders()])  41.7 us
    pallas_call x1, Pallas kernels, inverse_factor(): pl.pallas_call(inverse_kernel, out_shape=jax.ShapeDtypeStruct((n, n), F32...  32.2 us
    ppermute x8, starting transfers between devices, to_plane(): got = lax.ppermute(quarters[:, k], ('row', 'col'), pairs)  21.6 us
    all_to_all x3, starting transfers between devices, swap(): return lax.all_to_all(block, axis, split_axis=0, concat_axis=0, tiled=True)  20.6 us
    all_to_all x1, blocking collectives, swap(): return lax.all_to_all(block, axis, split_axis=0, concat_axis=0, tiled=True)  20.2 us
    ppermute x6, starting transfers between devices, hand_out(): mine = mine + lax.ppermute(part, axis, [(0, device)])  17.4 us
    ppermute x14, waiting for transfers between devices, from_holders(): lax.ppermute(mine, 'col', [(i, (i - t) % size) for i in column_holders()])  16 us
    all_to_all x3, waiting for transfers between devices, swap(): return lax.all_to_all(block, axis, split_axis=0, concat_axis=0, tiled=True)  12.2 us
  transfers between devices with their start and end apart: 33, of which 18 were waited for; matrix products, arithmetic and copies ran while one was open for 2% of the time, Pallas kernels for 16%

profile of v7, /device:TPU:2, one launch (start us, length us, event | category | flops | bytes accessed | tf_op | source)
XLA Modules:
  0.0 233.8 jit_solution(9481655285958104889)
XLA Ops:
  0.0 1.8 pack.1
  1.8 10.2 %all-to-all-start = ((bf16[32,40,128]{2,1,0:T(8,128)(2,1)}), bf16[32,40,128]{2,1,0:T(8,128)(2,1)S(1)}, u32[]{:S(2)}, u32[]{:S(2)}) async-start(bf16[32,40,128]{2,1,0:T(8,128)(2,1)} %bitcast.64), calls=%async_computation | async-start | bytes 655360 | tf_op jit(solution)/shard_map/all_to_all | solution.py:228
  12.1 4.7 %place.1 = (bf16[128,128,128]{2,1,0:T(8,128)(2,1)}, s32[128]{0:T(128)}) custom-call(s32[64]{0:T(128)} %bitcast.66, s32[64]{0:T(128)} %slots.1, bf16[64,128,128]{2,1,0:T(8,128)(2,1)} %children.1), custom_call_target="tpu_custom_call" | custom-call | tf_op jit(solution)/shard_map/place/pallas_call | solution.py:50
  17.7 1.9 collective-permute-start
  20.9 3.8 %all-to-all-done = bf16[32,40,128]{2,1,0:T(8,128)(2,1)S(1)} async-done(((bf16[32,40,128]{2,1,0:T(8,128)(2,1)}), bf16[32,40,128]{2,1,0:T(8,128)(2,1)S(1)}, u32[]{:S(2)}, u32[]{:S(2)}) %all-to-all-start) | async-done | bytes 327712 | tf_op jit(solution)/shard_map/all_to_all | solution.py:228
  25.0 20.2 %all_to_all.25 = bf16[32,48,128]{2,1,0:T(8,128)(2,1)S(1)} all-to-all(bf16[32,48,128]{2,1,0:T(8,128)(2,1)S(1)} %copy.56), channel_id=1, replica_groups=mesh['front'=2,'row'=32,'col'=8] {'row'}, dimensions={0} | all-to-all | bytes 786432 | tf_op jit(solution)/shard_map/all_to_all | solution.py:228
  45.6 6.7 %all-to-all-start.2 = ((bf16[128,128,128]{2,1,0:T(8,128)(2,1)}), bf16[128,128,128]{2,1,0:T(8,128)(2,1)}, u32[]{:S(2)}, u32[]{:S(2)}) async-start(bf16[128,128,128]{2,1,0:T(8,128)(2,1)} %get-tuple-element.28), calls=%async_computation.2 | async-start | bytes 8388608 | tf_op jit(solution)/shard_map/all_to_all | solution.py:228
  52.3 32.2 %inverse.1 = f32[512,512]{1,0:T(8,128)S(1)} custom-call(bf16[1280,128]{1,0:T(8,128)(2,1)S(1)} %bitcast.58), custom_call_target="tpu_custom_call" | custom-call | flops 536870912 | bytes 1572864 | tf_op jit(solution)/shard_map/inverse/pallas_call | solution.py:198
  85.6 11.0 %collective-permute-start.7 = (bf16[128,512]{1,0:T(8,128)(2,1)S(1)}, bf16[128,512]{1,0:T(8,128)(2,1)S(1)}, u32[]{:S(2)}, u32[]{:S(2)}) collective-permute-start(bf16[128,512]{1,0:T(8,128)(2,1)S(1)} %get-tuple-element.56), channel_id=1, source_target_pairs={{0,6},{8,14},{16,22},{24,30},{32,38},{40,46},{48,54},{56,62},{64,7... | collective-permute-start | bytes 393224 | tf_op jit(solution)/shard_map/ppermute | solution.py:241
  103.8 1.9 collective-permute-start.2
  107.1 1.6 collective-permute-done.4
  108.7 1.9 collective-permute-start.9
  113.2 2.3 collective-permute-done.1
  115.4 2.5 %collective-permute-start.11 = (bf16[128,512]{1,0:T(8,128)(2,1)S(1)}, bf16[128,512]{1,0:T(8,128)(2,1)S(1)}, u32[]{:S(2)}, u32[]{:S(2)}) collective-permute-start(bf16[128,512]{1,0:T(8,128)(2,1)S(1)} %fusion.15.refs_0_), channel_id=1, source_target_pairs={{0,4},{2,6},{4,0},{6,2},{8,12},{10,14},{12,8},{14,10},{16,20},{18,... | collective-permute-start | bytes 393224 | tf_op jit(solution)/shard_map/ppermute | solution.py:259
  119.5 5.3 %collective-permute-start.13 = (bf16[128,512]{1,0:T(8,128)(2,1)S(1)}, bf16[128,512]{1,0:T(8,128)(2,1)S(1)}, u32[]{:S(2)}, u32[]{:S(2)}) collective-permute-start(bf16[128,512]{1,0:T(8,128)(2,1)S(1)} %fusion.15.refs_0_), channel_id=1, source_target_pairs={{0,2},{2,4},{4,6},{6,0},{8,10},{10,12},{12,14},{14,8},{16,18},{18,... | collective-permute-start | bytes 393224 | tf_op jit(solution)/shard_map/ppermute | solution.py:259
  129.4 6.2 %collective-permute-done.13.refs_6_ = bf16[128,512]{1,0:T(8,128)(2,1)S(1)} collective-permute-done((bf16[128,512]{1,0:T(8,128)(2,1)S(1)}, bf16[128,512]{1,0:T(8,128)(2,1)S(1)}, u32[]{:S(2)}, u32[]{:S(2)}) %collective-permute-start.13) | collective-permute-done | bytes 131104 | tf_op jit(solution)/shard_map/ppermute | solution.py:259
  136.9 8.4 %all-to-all-done.2.incoming = bf16[128,128,128]{2,1,0:T(8,128)(2,1)} async-done(((bf16[128,128,128]{2,1,0:T(8,128)(2,1)}), bf16[128,128,128]{2,1,0:T(8,128)(2,1)}, u32[]{:S(2)}, u32[]{:S(2)}) %all-to-all-start.2) | async-done | bytes 4194336 | tf_op jit(solution)/shard_map/all_to_all | solution.py:228
  145.3 4.4 %assemble.1.refs_18_ = f32[512,512]{1,0:T(8,128)S(1)} custom-call(s32[128]{0:T(128)S(1)} %reshape.149.tags, bf16[128,128,128]{2,1,0:T(8,128)(2,1)} %all-to-all-done.2.incoming, bf16[1,1024,512]{2,1,0:T(8,128)(2,1)S(1)} %copy-done), custom_call_target="tpu_custom_call" | custom-call | tf_op jit(solution)/shard_map/assemble/pallas_call | solution.py:94
  149.7 1.9 convolution_convert_fusion.1
  151.7 11.9 %collective-permute-start.18 = (bf16[8,16,512]{2,1,0:T(8,128)(2,1)S(1)}, bf16[8,16,512]{2,1,0:T(8,128)(2,1)S(1)}, u32[]{:S(2)}, u32[]{:S(2)}) collective-permute-start(bf16[8,16,512]{2,1,0:T(8,128)(2,1)S(1)} %get-tuple-element.53), channel_id=1, source_target_pairs={{0,25},{8,27},{16,29},{24,31},{256,281},{264,283},{272,285},{280,2... | collective-permute-start | bytes 393224 | tf_op jit(solution)/shard_map/ppermute | solution.py:383
  173.1 2.8 %collective-permute-done.16 = bf16[8,16,512]{2,1,0:T(8,128)(2,1)S(1)} collective-permute-done((bf16[8,16,512]{2,1,0:T(8,128)(2,1)S(1)}, bf16[8,16,512]{2,1,0:T(8,128)(2,1)S(1)}, u32[]{:S(2)}, u32[]{:S(2)}) %collective-permute-start.16) | collective-permute-done | bytes 131104 | tf_op jit(solution)/shard_map/ppermute | solution.py:383
  176.6 3.4 %all-to-all-start.3 = ((bf16[8,16,512]{2,1,0:T(8,128)(2,1)}), bf16[8,16,512]{2,1,0:T(8,128)(2,1)S(1)}, u32[]{:S(2)}, u32[]{:S(2)}) async-start(bf16[8,16,512]{2,1,0:T(8,128)(2,1)} %add_select_fusion), calls=%async_computation.3 | async-start | bytes 262144 | tf_op jit(solution)/shard_map/all_to_all | solution.py:396
  180.5 8.5 %all-to-all-done.3 = bf16[8,16,512]{2,1,0:T(8,128)(2,1)S(1)} async-done(((bf16[8,16,512]{2,1,0:T(8,128)(2,1)}), bf16[8,16,512]{2,1,0:T(8,128)(2,1)S(1)}, u32[]{:S(2)}, u32[]{:S(2)}) %all-to-all-start.3) | async-done | bytes 131104 | tf_op jit(solution)/shard_map/all_to_all | solution.py:396
  188.9 8.7 %collective-permute-start.22 = (bf16[128,512]{1,0:T(8,128)(2,1)S(1)}, bf16[128,512]{1,0:T(8,128)(2,1)S(1)}, u32[]{:S(2)}, u32[]{:S(2)}) collective-permute-start(bf16[128,512]{1,0:T(8,128)(2,1)S(1)} %fusion.12.refs_8_), channel_id=1, source_target_pairs={{0,7},{2,1},{4,3},{6,5},{8,15},{10,9},{12,11},{14,13},{16,23},{18,... | collective-permute-start | bytes 393224 | tf_op jit(solution)/shard_map/ppermute | solution.py:259
  198.9 4.3 %collective-permute-start.24 = (bf16[128,512]{1,0:T(8,128)(2,1)S(1)}, bf16[128,512]{1,0:T(8,128)(2,1)S(1)}, u32[]{:S(2)}, u32[]{:S(2)}) collective-permute-start(bf16[128,512]{1,0:T(8,128)(2,1)S(1)} %fusion.12.refs_8_), channel_id=1, source_target_pairs={{0,6},{2,0},{4,2},{6,4},{8,14},{10,8},{12,10},{14,12},{16,22},{18,... | collective-permute-start | bytes 393224 | tf_op jit(solution)/shard_map/ppermute | solution.py:259
  203.2 3.5 %collective-permute-done.24.refs_10_ = bf16[128,512]{1,0:T(8,128)(2,1)S(1)} collective-permute-done((bf16[128,512]{1,0:T(8,128)(2,1)S(1)}, bf16[128,512]{1,0:T(8,128)(2,1)S(1)}, u32[]{:S(2)}, u32[]{:S(2)}) %collective-permute-start.24) | collective-permute-done | bytes 131104 | tf_op jit(solution)/shard_map/ppermute | solution.py:259
  207.6 3.7 %all-to-all-start.4 = ((bf16[32,16,512]{2,1,0:T(8,128)(2,1)}), bf16[32,16,512]{2,1,0:T(8,128)(2,1)S(1)}, u32[]{:S(2)}, u32[]{:S(2)}) async-start(bf16[32,16,512]{2,1,0:T(8,128)(2,1)} %broadcast_in_dim.23), calls=%async_computation.4 | async-start | bytes 1048576 | tf_op jit(solution)/shard_map/all_to_all | solution.py:228
  212.5 5.1 %collective-permute-start.26 = (bf16[128,512]{1,0:T(8,128)(2,1)S(1)}, bf16[128,512]{1,0:T(8,128)(2,1)S(1)}, u32[]{:S(2)}, u32[]{:S(2)}) collective-permute-start(bf16[128,512]{1,0:T(8,128)(2,1)S(1)} %fusion.12.refs_8_), channel_id=1, source_target_pairs={{0,4},{2,6},{4,0},{6,2},{8,12},{10,14},{12,8},{14,10},{16,20},{18,... | collective-permute-start | bytes 393224 | tf_op jit(solution)/shard_map/ppermute | solution.py:259
  219.0 4.6 %collective-permute-start.28 = (bf16[128,512]{1,0:T(8,128)(2,1)S(1)}, bf16[128,512]{1,0:T(8,128)(2,1)S(1)}, u32[]{:S(2)}, u32[]{:S(2)}) collective-permute-start(bf16[128,512]{1,0:T(8,128)(2,1)S(1)} %fusion.12.refs_8_), channel_id=1, source_target_pairs={{0,2},{2,4},{4,6},{6,0},{8,10},{10,12},{12,14},{14,8},{16,18},{18,... | collective-permute-start | bytes 393224 | tf_op jit(solution)/shard_map/ppermute | solution.py:259
  224.5 2.3 collective-permute-done.27.refs_13_
  226.7 2.4 %collective-permute-done.28.refs_14_ = bf16[128,512]{1,0:T(8,128)(2,1)S(1)} collective-permute-done((bf16[128,512]{1,0:T(8,128)(2,1)S(1)}, bf16[128,512]{1,0:T(8,128)(2,1)S(1)}, u32[]{:S(2)}, u32[]{:S(2)}) %collective-permute-start.28) | collective-permute-done | bytes 131104 | tf_op jit(solution)/shard_map/ppermute | solution.py:259
  230.0 3.7 %finish.1 = bf16[1,1024,512]{2,1,0:T(8,128)(2,1)} custom-call(s32[3]{0:T(128)} %pad_add_fusion.1.state, bf16[128,512]{1,0:T(8,128)(2,1)} %copy-done.3, bf16[128,512]{1,0:T(8,128)(2,1)} %copy-done.5, bf16[128,512]{1,0:T(8,128)(2,1)} %copy-done.6, bf16[128,512]{1,0:T(8,128)(2,1)} %copy-done.7, bf16[128,512]{1,0:T(8,128)(2,1)} %copy-done.8, ...), custom_call_target="tpu_custom_call" | custom-call | tf_op jit(solution)/shard_map/finish/pallas_call | solution.py:323
  (112 shorter events, 39.4 us)
Async XLA Ops:
  1.8 22.9 %all-to-all-start = ((bf16[32,40,128]{2,1,0:T(8,128)(2,1)}), bf16[32,40,128]{2,1,0:T(8,128)(2,1)S(1)}, u32[]{:S(2)}, u32[]{:S(2)}) async-start(bf16[32,40,128]{2,1,0:T(8,128)(2,1)} %bitcast.64), calls=%async_computation | async-start | bytes 655360 | tf_op jit(solution)/shard_map/all_to_all | solution.py:228
  45.6 99.7 %all-to-all-start.2 = ((bf16[128,128,128]{2,1,0:T(8,128)(2,1)}), bf16[128,128,128]{2,1,0:T(8,128)(2,1)}, u32[]{:S(2)}, u32[]{:S(2)}) async-start(bf16[128,128,128]{2,1,0:T(8,128)(2,1)} %get-tuple-element.28), calls=%async_computation.2 | async-start | bytes 8388608 | tf_op jit(solution)/shard_map/all_to_all | solution.py:228
  85.6 16.9 %collective-permute-start.7 = (bf16[128,512]{1,0:T(8,128)(2,1)S(1)}, bf16[128,512]{1,0:T(8,128)(2,1)S(1)}, u32[]{:S(2)}, u32[]{:S(2)}) collective-permute-start(bf16[128,512]{1,0:T(8,128)(2,1)S(1)} %get-tuple-element.56), channel_id=1, source_target_pairs={{0,6},{8,14},{16,22},{24,30},{32,38},{40,46},{48,54},{56,62},{64,7... | collective-permute-start | bytes 393224 | tf_op jit(solution)/shard_map/ppermute | solution.py:241
  96.6 7.3 %collective-permute-start.6 = (bf16[128,512]{1,0:T(8,128)(2,1)S(1)}, bf16[128,512]{1,0:T(8,128)(2,1)S(1)}, u32[]{:S(2)}, u32[]{:S(2)}) collective-permute-start(bf16[128,512]{1,0:T(8,128)(2,1)S(1)} %get-tuple-element.55), channel_id=1, source_target_pairs={{0,4},{8,12},{16,20},{24,28},{32,36},{40,44},{48,52},{56,60},{64,6... | collective-permute-start | bytes 393224 | tf_op jit(solution)/shard_map/ppermute | solution.py:241
  97.9 7.9 %collective-permute-start.5 = (bf16[128,512]{1,0:T(8,128)(2,1)S(1)}, bf16[128,512]{1,0:T(8,128)(2,1)S(1)}, u32[]{:S(2)}, u32[]{:S(2)}) collective-permute-start(bf16[128,512]{1,0:T(8,128)(2,1)S(1)} %get-tuple-element.54), channel_id=1, source_target_pairs={{0,2},{8,10},{16,18},{24,26},{32,34},{40,42},{48,50},{56,58},{64,6... | collective-permute-start | bytes 393224 | tf_op jit(solution)/shard_map/ppermute | solution.py:241
  99.9 8.8 %collective-permute-start.4 = (bf16[8,16,512]{2,1,0:T(8,128)(2,1)S(1)}, bf16[8,16,512]{2,1,0:T(8,128)(2,1)S(1)}, u32[]{:S(2)}, u32[]{:S(2)}) collective-permute-start(bf16[8,16,512]{2,1,0:T(8,128)(2,1)S(1)} %get-tuple-element.59), channel_id=1, source_target_pairs={{8,26},{16,28},{24,30},{264,282},{272,284},{280,286}} | collective-permute-start | bytes 393224 | tf_op jit(solution)/shard_map/ppermute | solution.py:383
  101.2 10.7 %collective-permute-start.3 = (bf16[8,16,512]{2,1,0:T(8,128)(2,1)}, bf16[8,16,512]{2,1,0:T(8,128)(2,1)S(1)}, u32[]{:S(2)}, u32[]{:S(2)}) collective-permute-start(bf16[8,16,512]{2,1,0:T(8,128)(2,1)} %get-tuple-element.60), channel_id=1, source_target_pairs={{8,18},{16,20},{24,22},{264,274},{272,276},{280,278}} | collective-permute-start | bytes 393224 | tf_op jit(solution)/shard_map/ppermute | solution.py:383
  102.5 12.9 %collective-permute-start.1 = (bf16[8,16,512]{2,1,0:T(8,128)(2,1)}, bf16[8,16,512]{2,1,0:T(8,128)(2,1)S(1)}, u32[]{:S(2)}, u32[]{:S(2)}) collective-permute-start(bf16[8,16,512]{2,1,0:T(8,128)(2,1)} %get-tuple-element.58), channel_id=1, source_target_pairs={{8,2},{16,4},{24,6},{264,258},{272,260},{280,262}} | collective-permute-start | bytes 393224 | tf_op jit(solution)/shard_map/ppermute | solution.py:383
  103.8 14.4 %collective-permute-start.2 = (bf16[8,16,512]{2,1,0:T(8,128)(2,1)}, bf16[8,16,512]{2,1,0:T(8,128)(2,1)}, u32[]{:S(2)}, u32[]{:S(2)}) collective-permute-start(bf16[8,16,512]{2,1,0:T(8,128)(2,1)} %get-tuple-element.57), channel_id=1, source_target_pairs={{8,10},{16,12},{24,14},{264,266},{272,268},{280,270}} | collective-permute-start | bytes 393224 | tf_op jit(solution)/shard_map/ppermute | solution.py:383
  105.8 13.7 %collective-permute-start.8 = (bf16[128,512]{1,0:T(8,128)(2,1)S(1)}, bf16[128,512]{1,0:T(8,128)(2,1)S(1)}, u32[]{:S(2)}, u32[]{:S(2)}) collective-permute-start(bf16[128,512]{1,0:T(8,128)(2,1)S(1)} %fusion.15.refs_0_), channel_id=1, source_target_pairs={{0,7},{2,1},{4,3},{6,5},{8,15},{10,9},{12,11},{14,13},{16,23},{18,... | collective-permute-start | bytes 393224 | tf_op jit(solution)/shard_map/ppermute | solution.py:259
  108.7 16.2 %collective-permute-start.9 = (bf16[128,512]{1,0:T(8,128)(2,1)S(1)}, bf16[128,512]{1,0:T(8,128)(2,1)S(1)}, u32[]{:S(2)}, u32[]{:S(2)}) collective-permute-start(bf16[128,512]{1,0:T(8,128)(2,1)S(1)} %fusion.15.refs_0_), channel_id=1, source_target_pairs={{0,6},{2,0},{4,2},{6,4},{8,14},{10,8},{12,10},{14,12},{16,22},{18,... | collective-permute-start | bytes 393224 | tf_op jit(solution)/shard_map/ppermute | solution.py:259
  111.9 16.1 %collective-permute-start.10 = (bf16[128,512]{1,0:T(8,128)(2,1)S(1)}, bf16[128,512]{1,0:T(8,128)(2,1)S(1)}, u32[]{:S(2)}, u32[]{:S(2)}) collective-permute-start(bf16[128,512]{1,0:T(8,128)(2,1)S(1)} %fusion.15.refs_0_), channel_id=1, source_target_pairs={{0,5},{2,7},{4,1},{6,3},{8,13},{10,15},{12,9},{14,11},{16,21},{18,... | collective-permute-start | bytes 393224 | tf_op jit(solution)/shard_map/ppermute | solution.py:259
  115.4 14.0 %collective-permute-start.11 = (bf16[128,512]{1,0:T(8,128)(2,1)S(1)}, bf16[128,512]{1,0:T(8,128)(2,1)S(1)}, u32[]{:S(2)}, u32[]{:S(2)}) collective-permute-start(bf16[128,512]{1,0:T(8,128)(2,1)S(1)} %fusion.15.refs_0_), channel_id=1, source_target_pairs={{0,4},{2,6},{4,0},{6,2},{8,12},{10,14},{12,8},{14,10},{16,20},{18,... | collective-permute-start | bytes 393224 | tf_op jit(solution)/shard_map/ppermute | solution.py:259
  118.2 11.2 %collective-permute-start.12 = (bf16[128,512]{1,0:T(8,128)(2,1)S(1)}, bf16[128,512]{1,0:T(8,128)(2,1)S(1)}, u32[]{:S(2)}, u32[]{:S(2)}) collective-permute-start(bf16[128,512]{1,0:T(8,128)(2,1)S(1)} %fusion.15.refs_0_), channel_id=1, source_target_pairs={{0,3},{2,5},{4,7},{6,1},{8,11},{10,13},{12,15},{14,9},{16,19},{18,... | collective-permute-start | bytes 393224 | tf_op jit(solution)/shard_map/ppermute | solution.py:259
  119.5 16.1 %collective-permute-start.13 = (bf16[128,512]{1,0:T(8,128)(2,1)S(1)}, bf16[128,512]{1,0:T(8,128)(2,1)S(1)}, u32[]{:S(2)}, u32[]{:S(2)}) collective-permute-start(bf16[128,512]{1,0:T(8,128)(2,1)S(1)} %fusion.15.refs_0_), channel_id=1, source_target_pairs={{0,2},{2,4},{4,6},{6,0},{8,10},{10,12},{12,14},{14,8},{16,18},{18,... | collective-permute-start | bytes 393224 | tf_op jit(solution)/shard_map/ppermute | solution.py:259
  125.5 10.0 %collective-permute-start.14 = (bf16[128,512]{1,0:T(8,128)(2,1)S(1)}, bf16[128,512]{1,0:T(8,128)(2,1)S(1)}, u32[]{:S(2)}, u32[]{:S(2)}) collective-permute-start(bf16[128,512]{1,0:T(8,128)(2,1)S(1)} %fusion.15.refs_0_), channel_id=1, source_target_pairs={{0,1},{2,3},{4,5},{6,7},{8,9},{10,11},{12,13},{14,15},{16,17},{18,... | collective-permute-start | bytes 393224 | tf_op jit(solution)/shard_map/ppermute | solution.py:259
  151.7 17.2 %collective-permute-start.18 = (bf16[8,16,512]{2,1,0:T(8,128)(2,1)S(1)}, bf16[8,16,512]{2,1,0:T(8,128)(2,1)S(1)}, u32[]{:S(2)}, u32[]{:S(2)}) collective-permute-start(bf16[8,16,512]{2,1,0:T(8,128)(2,1)S(1)} %get-tuple-element.53), channel_id=1, source_target_pairs={{0,25},{8,27},{16,29},{24,31},{256,281},{264,283},{272,285},{280,2... | collective-permute-start | bytes 393224 | tf_op jit(solution)/shard_map/ppermute | solution.py:383
  163.6 6.7 %collective-permute-start.17 = (bf16[8,16,512]{2,1,0:T(8,128)(2,1)S(1)}, bf16[8,16,512]{2,1,0:T(8,128)(2,1)S(1)}, u32[]{:S(2)}, u32[]{:S(2)}) collective-permute-start(bf16[8,16,512]{2,1,0:T(8,128)(2,1)S(1)} %get-tuple-element.51), channel_id=1, source_target_pairs={{0,17},{8,19},{16,21},{24,23},{256,273},{264,275},{272,277},{280,2... | collective-permute-start | bytes 393224 | tf_op jit(solution)/shard_map/ppermute | solution.py:383
  164.9 8.2 %collective-permute-start.15 = (bf16[8,16,512]{2,1,0:T(8,128)(2,1)S(1)}, bf16[8,16,512]{2,1,0:T(8,128)(2,1)S(1)}, u32[]{:S(2)}, u32[]{:S(2)}) collective-permute-start(bf16[8,16,512]{2,1,0:T(8,128)(2,1)S(1)} %get-tuple-element.52), channel_id=1, source_target_pairs={{0,1},{8,3},{16,5},{24,7},{256,257},{264,259},{272,261},{280,263}} | collective-permute-start | bytes 393224 | tf_op jit(solution)/shard_map/ppermute | solution.py:383
  166.2 9.7 %collective-permute-start.16 = (bf16[8,16,512]{2,1,0:T(8,128)(2,1)S(1)}, bf16[8,16,512]{2,1,0:T(8,128)(2,1)S(1)}, u32[]{:S(2)}, u32[]{:S(2)}) collective-permute-start(bf16[8,16,512]{2,1,0:T(8,128)(2,1)S(1)} %get-tuple-element.50), channel_id=1, source_target_pairs={{0,9},{8,11},{16,13},{24,15},{256,265},{264,267},{272,269},{280,271}} | collective-permute-start | bytes 393224 | tf_op jit(solution)/shard_map/ppermute | solution.py:383
  167.5 12.4 %collective-permute-start.21 = (bf16[128,512]{1,0:T(8,128)(2,1)S(1)}, bf16[128,512]{1,0:T(8,128)(2,1)S(1)}, u32[]{:S(2)}, u32[]{:S(2)}) collective-permute-start(bf16[128,512]{1,0:T(8,128)(2,1)S(1)} %get-tuple-element.48), channel_id=1, source_target_pairs={{0,6},{8,14},{16,22},{24,30},{32,38},{40,46},{48,54},{56,62},{64,7... | collective-permute-start | bytes 393224 | tf_op jit(solution)/shard_map/ppermute | solution.py:241
  168.8 11.1 %collective-permute-start.20 = (bf16[128,512]{1,0:T(8,128)(2,1)S(1)}, bf16[128,512]{1,0:T(8,128)(2,1)S(1)}, u32[]{:S(2)}, u32[]{:S(2)}) collective-permute-start(bf16[128,512]{1,0:T(8,128)(2,1)S(1)} %get-tuple-element.49), channel_id=1, source_target_pairs={{0,4},{8,12},{16,20},{24,28},{32,36},{40,44},{48,52},{56,60},{64,6... | collective-permute-start | bytes 393224 | tf_op jit(solution)/shard_map/ppermute | solution.py:241
  170.3 10.2 %collective-permute-start.19 = (bf16[128,512]{1,0:T(8,128)(2,1)S(1)}, bf16[128,512]{1,0:T(8,128)(2,1)S(1)}, u32[]{:S(2)}, u32[]{:S(2)}) collective-permute-start(bf16[128,512]{1,0:T(8,128)(2,1)S(1)} %get-tuple-element.47), channel_id=1, source_target_pairs={{0,2},{8,10},{16,18},{24,26},{32,34},{40,42},{48,50},{56,58},{64,6... | collective-permute-start | bytes 393224 | tf_op jit(solution)/shard_map/ppermute | solution.py:241
  176.6 12.4 %all-to-all-start.3 = ((bf16[8,16,512]{2,1,0:T(8,128)(2,1)}), bf16[8,16,512]{2,1,0:T(8,128)(2,1)S(1)}, u32[]{:S(2)}, u32[]{:S(2)}) async-start(bf16[8,16,512]{2,1,0:T(8,128)(2,1)} %add_select_fusion), calls=%async_computation.3 | async-start | bytes 262144 | tf_op jit(solution)/shard_map/all_to_all | solution.py:396
  188.9 14.2 %collective-permute-start.22 = (bf16[128,512]{1,0:T(8,128)(2,1)S(1)}, bf16[128,512]{1,0:T(8,128)(2,1)S(1)}, u32[]{:S(2)}, u32[]{:S(2)}) collective-permute-start(bf16[128,512]{1,0:T(8,128)(2,1)S(1)} %fusion.12.refs_8_), channel_id=1, source_target_pairs={{0,7},{2,1},{4,3},{6,5},{8,15},{10,9},{12,11},{14,13},{16,23},{18,... | collective-permute-start | bytes 393224 | tf_op jit(solution)/shard_map/ppermute | solution.py:259
  197.6 5.6 %collective-permute-start.23 = (bf16[128,512]{1,0:T(8,128)(2,1)S(1)}, bf16[128,512]{1,0:T(8,128)(2,1)S(1)}, u32[]{:S(2)}, u32[]{:S(2)}) collective-permute-start(bf16[128,512]{1,0:T(8,128)(2,1)S(1)} %fusion.12.refs_8_), channel_id=1, source_target_pairs={{0,1},{2,3},{4,5},{6,7},{8,9},{10,11},{12,13},{14,15},{16,17},{18,... | collective-permute-start | bytes 393224 | tf_op jit(solution)/shard_map/ppermute | solution.py:259
  198.9 7.8 %collective-permute-start.24 = (bf16[128,512]{1,0:T(8,128)(2,1)S(1)}, bf16[128,512]{1,0:T(8,128)(2,1)S(1)}, u32[]{:S(2)}, u32[]{:S(2)}) collective-permute-start(bf16[128,512]{1,0:T(8,128)(2,1)S(1)} %fusion.12.refs_8_), channel_id=1, source_target_pairs={{0,6},{2,0},{4,2},{6,4},{8,14},{10,8},{12,10},{14,12},{16,22},{18,... | collective-permute-start | bytes 393224 | tf_op jit(solution)/shard_map/ppermute | solution.py:259
  207.6 21.6 %all-to-all-start.4 = ((bf16[32,16,512]{2,1,0:T(8,128)(2,1)}), bf16[32,16,512]{2,1,0:T(8,128)(2,1)S(1)}, u32[]{:S(2)}, u32[]{:S(2)}) async-start(bf16[32,16,512]{2,1,0:T(8,128)(2,1)} %broadcast_in_dim.23), calls=%async_computation.4 | async-start | bytes 1048576 | tf_op jit(solution)/shard_map/all_to_all | solution.py:228
  211.2 13.0 %collective-permute-start.25 = (bf16[128,512]{1,0:T(8,128)(2,1)S(1)}, bf16[128,512]{1,0:T(8,128)(2,1)S(1)}, u32[]{:S(2)}, u32[]{:S(2)}) collective-permute-start(bf16[128,512]{1,0:T(8,128)(2,1)S(1)} %fusion.12.refs_8_), channel_id=1, source_target_pairs={{0,5},{2,7},{4,1},{6,3},{8,13},{10,15},{12,9},{14,11},{16,21},{18,... | collective-permute-start | bytes 393224 | tf_op jit(solution)/shard_map/ppermute | solution.py:259
  212.5 11.9 %collective-permute-start.26 = (bf16[128,512]{1,0:T(8,128)(2,1)S(1)}, bf16[128,512]{1,0:T(8,128)(2,1)S(1)}, u32[]{:S(2)}, u32[]{:S(2)}) collective-permute-start(bf16[128,512]{1,0:T(8,128)(2,1)S(1)} %fusion.12.refs_8_), channel_id=1, source_target_pairs={{0,4},{2,6},{4,0},{6,2},{8,12},{10,14},{12,8},{14,10},{16,20},{18,... | collective-permute-start | bytes 393224 | tf_op jit(solution)/shard_map/ppermute | solution.py:259
  217.7 9.0 %collective-permute-start.27 = (bf16[128,512]{1,0:T(8,128)(2,1)S(1)}, bf16[128,512]{1,0:T(8,128)(2,1)S(1)}, u32[]{:S(2)}, u32[]{:S(2)}) collective-permute-start(bf16[128,512]{1,0:T(8,128)(2,1)S(1)} %fusion.12.refs_8_), channel_id=1, source_target_pairs={{0,3},{2,5},{4,7},{6,1},{8,11},{10,13},{12,15},{14,9},{16,19},{18,... | collective-permute-start | bytes 393224 | tf_op jit(solution)/shard_map/ppermute | solution.py:259
  219.0 10.1 %collective-permute-start.28 = (bf16[128,512]{1,0:T(8,128)(2,1)S(1)}, bf16[128,512]{1,0:T(8,128)(2,1)S(1)}, u32[]{:S(2)}, u32[]{:S(2)}) collective-permute-start(bf16[128,512]{1,0:T(8,128)(2,1)S(1)} %fusion.12.refs_8_), channel_id=1, source_target_pairs={{0,2},{2,4},{4,6},{6,0},{8,10},{10,12},{12,14},{14,8},{16,18},{18,... | collective-permute-start | bytes 393224 | tf_op jit(solution)/shard_map/ppermute | solution.py:259
  (21 other events, 431.8 us)

commit v8 on v7

--- a/solution.py
+++ b/solution.py
@@ -60,48 +60,59 @@
     )(routes, slots, children)
 
 
-def assemble_kernel(tags, incoming, base, out, acc):
+def assemble_kernel(tags, incoming, window, out, blocks, base, acc, sem):
     side = TILE // SB
-    step = pl.program_id(0)
-    blocks = incoming.shape[0]
-
-    @pl.when(step == 0)
-    def _():
-        acc[...] = jnp.zeros_like(acc)
+    pieces = sem.shape[0] - 1
+    size = incoming.shape[0] // pieces
+    copies = [
+        pltpu.make_async_copy(
+            incoming.at[pl.ds(p * size, size)], blocks.at[pl.ds(p * size, size)], sem.at[p]
+        )
+        for p in range(pieces)
+    ]
+    copies.append(
+        pltpu.make_async_copy(window.at[0, pl.ds(TILE, TILE), :], base, sem.at[pieces])
+    )
+    for copy in copies:
+        copy.start()
+    acc[...] = jnp.zeros_like(acc)
 
     def add(s, _):
-        t = tags[step * blocks + s]
+        t = tags[s]
 
         @pl.when(t > 0)
         def _():
-            acc[t - 1] = acc[t - 1] + incoming[s].astype(F32)
+            acc[t - 1] = acc[t - 1] + blocks[s].astype(F32)
 
         return 0
 
-    lax.fori_loop(0, blocks, add, 0)
-
-    @pl.when(step == pl.num_programs(0) - 1)
-    def _():
-        for i in range(side):
-            for j in range(side):
-                rows, cols = slice(i * SB, (i + 1) * SB), slice(j * SB, (j + 1) * SB)
-                out[rows, cols] = base[0, rows, cols].astype(F32) + acc[i * side + j]
+    for p in range(pieces):
+        copies[p].wait()
+        lax.fori_loop(p * size, (p + 1) * size, add, 0)
+    copies[pieces].wait()
+    for i in range(side):
+        for j in range(side):
+            rows, cols = slice(i * SB, (i + 1) * SB), slice(j * SB, (j + 1) * SB)
+            out[rows, cols] = base[rows, cols].astype(F32) + acc[i * side + j]
 
 
 def assemble(tags, incoming, window):
-    steps = 1
-    blocks = incoming.shape[0] // steps
+    pieces = 4
     return pl.pallas_call(
         assemble_kernel,
         out_shape=jax.ShapeDtypeStruct((TILE, TILE), F32),
-        grid=(steps,),
         in_specs=[
             pl.BlockSpec(memory_space=pltpu.SMEM),
-            pl.BlockSpec((blocks, SB, SB), lambda i: (i, 0, 0)),
-            pl.BlockSpec((1, TILE, TILE), lambda i: (0, 1, 0)),
+            pl.BlockSpec(memory_space=pl.ANY),
+            pl.BlockSpec(memory_space=pl.ANY),
         ],
-        out_specs=pl.BlockSpec((TILE, TILE), lambda i: (0, 0)),
-        scratch_shapes=[pltpu.VMEM(((TILE // SB) ** 2, SB, SB), F32)],
+        out_specs=pl.BlockSpec(memory_space=pltpu.VMEM),
+        scratch_shapes=[
+            pltpu.VMEM(incoming.shape, BF16),
+            pltpu.VMEM((TILE, TILE), BF16),
+            pltpu.VMEM(((TILE // SB) ** 2, SB, SB), F32),
+            pltpu.SemaphoreType.DMA((pieces + 1,)),
+        ],
         compiler_params=pltpu.CompilerParams(vmem_limit_bytes=24 << 20),
         name="assemble",
     )(tags, incoming, window)
@@ -396,9 +407,8 @@
     got = lax.all_to_all(
         piece, "row", split_axis=0, concat_axis=0, axis_index_groups=groups, tiled=True
     )
-    got, under = lax.optimization_barrier((got, to_holders(lower_second)))
-    under = from_holders(under)
-    near = [1, columns - 1, 2]
+    under = from_holders(to_holders(lower_second))
+    near = [1, columns - 1]
     got, *arrived = lax.optimization_barrier((got, *(under[t] for t in near)))
     for t, part in zip(near, arrived):
         under[t] = part

time: 235 us -> 232 us (0.987)
  waiting for transfers between devices: 47.9 us -> 42.3 us
    all_to_all x1, waiting for transfers between devices: 8.47 us -> 0.01 us  [shards(): lax.all_to_all(piece, 'row', split_axis=0, concat_axis=0, axis_index_grou...]
    all_to_all x3, starting transfers between devices: 20.6 us -> 25.7 us  [swap(): return lax.all_to_all(block, axis, split_axis=0, concat_axis=0, tiled=True)]
    ppermute x14, waiting for transfers between devices: 16 us -> 19 us  [from_holders(): lax.ppermute(mine, 'col', [(i, (i - t) % size) for i in column_holders()])]
  transfers between devices with their start and end apart: 33 -> 33, of which waited for: 18 -> 17; matrix products, arithmetic and copies ran while one was open for 2% -> 2% of each run, Pallas kernels for 16% -> 16%
where the time goes in v8:
time: 232 us; the launch traced here: 231 us
  starting transfers between devices  109 us (47%)
  Pallas kernels  46.3 us (20%)
  waiting for transfers between devices  42.3 us (18%)
  blocking collectives  20.2 us (9%)
  local copies, waits for them, and re-layouts  5.35 us (2%)
  other arithmetic  3.23 us (1%)
  matrix products  2.94 us (1%)
    ppermute x14, starting transfers between devices, from_holders(): lax.ppermute(mine, 'col', [(i, (i - t) % size) for i in column_holders()])  39.4 us
    pallas_call x1, Pallas kernels, inverse_factor(): pl.pallas_call(inverse_kernel, out_shape=jax.ShapeDtypeStruct((n, n), F32...  32.2 us
    all_to_all x3, starting transfers between devices, swap(): return lax.all_to_all(block, axis, split_axis=0, concat_axis=0, tiled=True)  25.7 us
    ppermute x8, starting transfers between devices, to_plane(): got = lax.ppermute(quarters[:, k], ('row', 'col'), pairs)  21.6 us
    all_to_all x1, blocking collectives, swap(): return lax.all_to_all(block, axis, split_axis=0, concat_axis=0, tiled=True)  20.2 us
    ppermute x14, waiting for transfers between devices, from_holders(): lax.ppermute(mine, 'col', [(i, (i - t) % size) for i in column_holders()])  19 us
    ppermute x6, starting transfers between devices, hand_out(): mine = mine + lax.ppermute(part, axis, [(0, device)])  17.4 us
    all_to_all x3, waiting for transfers between devices, swap(): return lax.all_to_all(block, axis, split_axis=0, concat_axis=0, tiled=True)  12.3 us
  transfers between devices with their start and end apart: 33, of which 17 were waited for; matrix products, arithmetic and copies ran while one was open for 2% of the time, Pallas kernels for 16%

profile of v8, /device:TPU:2, one launch (start us, length us, event | category | flops | bytes accessed | tf_op | source)
XLA Modules:
  0.0 230.5 jit_solution(17199569987699633584)
XLA Ops:
  0.0 1.8 pack.1
  1.8 10.2 %all-to-all-start = ((bf16[32,40,128]{2,1,0:T(8,128)(2,1)}), bf16[32,40,128]{2,1,0:T(8,128)(2,1)S(1)}, u32[]{:S(2)}, u32[]{:S(2)}) async-start(bf16[32,40,128]{2,1,0:T(8,128)(2,1)} %bitcast.64), calls=%async_computation | async-start | bytes 655360 | tf_op jit(solution)/shard_map/all_to_all | solution.py:239
  12.1 4.7 %place.1 = (bf16[128,128,128]{2,1,0:T(8,128)(2,1)}, s32[128]{0:T(128)}) custom-call(s32[64]{0:T(128)} %bitcast.66, s32[64]{0:T(128)} %slots.1, bf16[64,128,128]{2,1,0:T(8,128)(2,1)} %children.1), custom_call_target="tpu_custom_call" | custom-call | tf_op jit(solution)/shard_map/place/pallas_call | solution.py:50
  17.8 1.9 collective-permute-start
  20.9 3.8 %all-to-all-done = bf16[32,40,128]{2,1,0:T(8,128)(2,1)S(1)} async-done(((bf16[32,40,128]{2,1,0:T(8,128)(2,1)}), bf16[32,40,128]{2,1,0:T(8,128)(2,1)S(1)}, u32[]{:S(2)}, u32[]{:S(2)}) %all-to-all-start) | async-done | bytes 327712 | tf_op jit(solution)/shard_map/all_to_all | solution.py:239
  25.0 20.2 %all_to_all.25 = bf16[32,48,128]{2,1,0:T(8,128)(2,1)S(1)} all-to-all(bf16[32,48,128]{2,1,0:T(8,128)(2,1)S(1)} %copy.56), channel_id=1, replica_groups=mesh['front'=2,'row'=32,'col'=8] {'row'}, dimensions={0} | all-to-all | bytes 786432 | tf_op jit(solution)/shard_map/all_to_all | solution.py:239
  45.6 6.7 %all-to-all-start.2 = ((bf16[128,128,128]{2,1,0:T(8,128)(2,1)}), bf16[128,128,128]{2,1,0:T(8,128)(2,1)}, u32[]{:S(2)}, u32[]{:S(2)}) async-start(bf16[128,128,128]{2,1,0:T(8,128)(2,1)} %get-tuple-element.25), calls=%async_computation.2 | async-start | bytes 8388608 | tf_op jit(solution)/shard_map/all_to_all | solution.py:239
  52.4 32.2 %inverse.1 = f32[512,512]{1,0:T(8,128)S(1)} custom-call(bf16[1280,128]{1,0:T(8,128)(2,1)S(1)} %bitcast.58), custom_call_target="tpu_custom_call" | custom-call | flops 536870912 | bytes 1572864 | tf_op jit(solution)/shard_map/inverse/pallas_call | solution.py:209
  85.7 10.9 %collective-permute-start.7 = (bf16[128,512]{1,0:T(8,128)(2,1)S(1)}, bf16[128,512]{1,0:T(8,128)(2,1)S(1)}, u32[]{:S(2)}, u32[]{:S(2)}) collective-permute-start(bf16[128,512]{1,0:T(8,128)(2,1)S(1)} %get-tuple-element.50), channel_id=1, source_target_pairs={{0,6},{8,14},{16,22},{24,30},{32,38},{40,46},{48,54},{56,62},{64,7... | collective-permute-start | bytes 393224 | tf_op jit(solution)/shard_map/ppermute | solution.py:252
  103.8 1.9 collective-permute-start.2
  107.2 1.6 collective-permute-done.4
  108.8 1.9 collective-permute-start.9
  113.2 2.3 collective-permute-done.1
  115.4 2.6 %collective-permute-start.11 = (bf16[128,512]{1,0:T(8,128)(2,1)S(1)}, bf16[128,512]{1,0:T(8,128)(2,1)S(1)}, u32[]{:S(2)}, u32[]{:S(2)}) collective-permute-start(bf16[128,512]{1,0:T(8,128)(2,1)S(1)} %fusion.15.refs_0_), channel_id=1, source_target_pairs={{0,4},{2,6},{4,0},{6,2},{8,12},{10,14},{12,8},{14,10},{16,20},{18,... | collective-permute-start | bytes 393224 | tf_op jit(solution)/shard_map/ppermute | solution.py:270
  119.5 5.3 %collective-permute-start.13 = (bf16[128,512]{1,0:T(8,128)(2,1)S(1)}, bf16[128,512]{1,0:T(8,128)(2,1)S(1)}, u32[]{:S(2)}, u32[]{:S(2)}) collective-permute-start(bf16[128,512]{1,0:T(8,128)(2,1)S(1)} %fusion.15.refs_0_), channel_id=1, source_target_pairs={{0,2},{2,4},{4,6},{6,0},{8,10},{10,12},{12,14},{14,8},{16,18},{18,... | collective-permute-start | bytes 393224 | tf_op jit(solution)/shard_map/ppermute | solution.py:270
  129.0 6.6 %collective-permute-done.13.refs_6_ = bf16[128,512]{1,0:T(8,128)(2,1)S(1)} collective-permute-done((bf16[128,512]{1,0:T(8,128)(2,1)S(1)}, bf16[128,512]{1,0:T(8,128)(2,1)S(1)}, u32[]{:S(2)}, u32[]{:S(2)}) %collective-permute-start.13) | collective-permute-done | bytes 131104 | tf_op jit(solution)/shard_map/ppermute | solution.py:270
  136.9 8.5 %all-to-all-done.2.incoming = bf16[128,128,128]{2,1,0:T(8,128)(2,1)} async-done(((bf16[128,128,128]{2,1,0:T(8,128)(2,1)}), bf16[128,128,128]{2,1,0:T(8,128)(2,1)}, u32[]{:S(2)}, u32[]{:S(2)}) %all-to-all-start.2) | async-done | bytes 4194336 | tf_op jit(solution)/shard_map/all_to_all | solution.py:239
  145.4 3.9 %assemble.1.refs_18_ = f32[512,512]{1,0:T(8,128)S(1)} custom-call(s32[128]{0:T(128)S(1)} %reshape.149.tags, bf16[128,128,128]{2,1,0:T(8,128)(2,1)} %all-to-all-done.2.incoming, bf16[1,1024,512]{2,1,0:T(8,128)(2,1)S(1)} %copy-done), custom_call_target="tpu_custom_call" | custom-call | tf_op jit(solution)/shard_map/assemble/pallas_call | solution.py:101
  149.3 1.9 convolution_convert_fusion.1
  151.2 11.9 %collective-permute-start.21 = (bf16[8,16,512]{2,1,0:T(8,128)(2,1)S(1)}, bf16[8,16,512]{2,1,0:T(8,128)(2,1)S(1)}, u32[]{:S(2)}, u32[]{:S(2)}) collective-permute-start(bf16[8,16,512]{2,1,0:T(8,128)(2,1)S(1)} %get-tuple-element.43), channel_id=1, source_target_pairs={{0,25},{8,27},{16,29},{24,31},{256,281},{264,283},{272,285},{280,2... | collective-permute-start | bytes 393224 | tf_op jit(solution)/shard_map/ppermute | solution.py:394
  171.2 1.5 collective-permute-done.18
  172.7 2.8 %collective-permute-done.19 = bf16[8,16,512]{2,1,0:T(8,128)(2,1)S(1)} collective-permute-done((bf16[8,16,512]{2,1,0:T(8,128)(2,1)S(1)}, bf16[8,16,512]{2,1,0:T(8,128)(2,1)S(1)}, u32[]{:S(2)}, u32[]{:S(2)}) %collective-permute-start.19) | collective-permute-done | bytes 131104 | tf_op jit(solution)/shard_map/ppermute | solution.py:394
  176.2 3.4 %all-to-all-start.3 = ((bf16[8,16,512]{2,1,0:T(8,128)(2,1)}), bf16[8,16,512]{2,1,0:T(8,128)(2,1)S(1)}, u32[]{:S(2)}, u32[]{:S(2)}) async-start(bf16[8,16,512]{2,1,0:T(8,128)(2,1)} %add_select_fusion), calls=%async_computation.3 | async-start | bytes 262144 | tf_op jit(solution)/shard_map/all_to_all | solution.py:407
  179.9 8.4 %collective-permute-start.22 = (bf16[128,512]{1,0:T(8,128)(2,1)S(1)}, bf16[128,512]{1,0:T(8,128)(2,1)S(1)}, u32[]{:S(2)}, u32[]{:S(2)}) collective-permute-start(bf16[128,512]{1,0:T(8,128)(2,1)S(1)} %fusion.12.refs_8_), channel_id=1, source_target_pairs={{0,7},{2,1},{4,3},{6,5},{8,15},{10,9},{12,11},{14,13},{16,23},{18,... | collective-permute-start | bytes 393224 | tf_op jit(solution)/shard_map/ppermute | solution.py:270
  193.0 8.7 %all-to-all-start.4 = ((bf16[32,16,512]{2,1,0:T(8,128)(2,1)}), bf16[32,16,512]{2,1,0:T(8,128)(2,1)S(1)}, u32[]{:S(2)}, u32[]{:S(2)}) async-start(bf16[32,16,512]{2,1,0:T(8,128)(2,1)} %broadcast_in_dim.23), calls=%async_computation.4 | async-start | bytes 1048576 | tf_op jit(solution)/shard_map/all_to_all | solution.py:239
  201.7 4.2 %collective-permute-start.24 = (bf16[128,512]{1,0:T(8,128)(2,1)S(1)}, bf16[128,512]{1,0:T(8,128)(2,1)S(1)}, u32[]{:S(2)}, u32[]{:S(2)}) collective-permute-start(bf16[128,512]{1,0:T(8,128)(2,1)S(1)} %fusion.12.refs_8_), channel_id=1, source_target_pairs={{0,6},{2,0},{4,2},{6,4},{8,14},{10,8},{12,10},{14,12},{16,22},{18,... | collective-permute-start | bytes 393224 | tf_op jit(solution)/shard_map/ppermute | solution.py:270
  205.9 2.5 %collective-permute-start.25 = (bf16[128,512]{1,0:T(8,128)(2,1)S(1)}, bf16[128,512]{1,0:T(8,128)(2,1)S(1)}, u32[]{:S(2)}, u32[]{:S(2)}) collective-permute-start(bf16[128,512]{1,0:T(8,128)(2,1)S(1)} %fusion.12.refs_8_), channel_id=1, source_target_pairs={{0,5},{2,7},{4,1},{6,3},{8,13},{10,15},{12,9},{14,11},{16,21},{18,... | collective-permute-start | bytes 393224 | tf_op jit(solution)/shard_map/ppermute | solution.py:270
  208.5 4.7 %collective-permute-start.26 = (bf16[128,512]{1,0:T(8,128)(2,1)S(1)}, bf16[128,512]{1,0:T(8,128)(2,1)S(1)}, u32[]{:S(2)}, u32[]{:S(2)}) collective-permute-start(bf16[128,512]{1,0:T(8,128)(2,1)S(1)} %fusion.12.refs_8_), channel_id=1, source_target_pairs={{0,4},{2,6},{4,0},{6,2},{8,12},{10,14},{12,8},{14,10},{16,20},{18,... | collective-permute-start | bytes 393224 | tf_op jit(solution)/shard_map/ppermute | solution.py:270
  214.4 1.9 collective-permute-start.28
  217.0 5.6 %collective-permute-done.26.refs_12_ = bf16[128,512]{1,0:T(8,128)(2,1)S(1)} collective-permute-done((bf16[128,512]{1,0:T(8,128)(2,1)S(1)}, bf16[128,512]{1,0:T(8,128)(2,1)S(1)}, u32[]{:S(2)}, u32[]{:S(2)}) %collective-permute-start.26) | collective-permute-done | bytes 131104 | tf_op jit(solution)/shard_map/ppermute | solution.py:270
  222.6 3.2 %collective-permute-done.28.refs_14_ = bf16[128,512]{1,0:T(8,128)(2,1)S(1)} collective-permute-done((bf16[128,512]{1,0:T(8,128)(2,1)S(1)}, bf16[128,512]{1,0:T(8,128)(2,1)S(1)}, u32[]{:S(2)}, u32[]{:S(2)}) %collective-permute-start.28) | collective-permute-done | bytes 131104 | tf_op jit(solution)/shard_map/ppermute | solution.py:270
  226.7 3.7 %finish.1 = bf16[1,1024,512]{2,1,0:T(8,128)(2,1)} custom-call(s32[3]{0:T(128)} %pad_add_fusion.1.state, bf16[128,512]{1,0:T(8,128)(2,1)} %copy-done.3, bf16[128,512]{1,0:T(8,128)(2,1)} %copy-done.5, bf16[128,512]{1,0:T(8,128)(2,1)} %copy-done.6, bf16[128,512]{1,0:T(8,128)(2,1)} %copy-done.7, bf16[128,512]{1,0:T(8,128)(2,1)} %copy-done.8, ...), custom_call_target="tpu_custom_call" | custom-call | tf_op jit(solution)/shard_map/finish/pallas_call | solution.py:334
  (112 shorter events, 38.2 us)
Async XLA Ops:
  1.8 22.9 %all-to-all-start = ((bf16[32,40,128]{2,1,0:T(8,128)(2,1)}), bf16[32,40,128]{2,1,0:T(8,128)(2,1)S(1)}, u32[]{:S(2)}, u32[]{:S(2)}) async-start(bf16[32,40,128]{2,1,0:T(8,128)(2,1)} %bitcast.64), calls=%async_computation | async-start | bytes 655360 | tf_op jit(solution)/shard_map/all_to_all | solution.py:239
  45.6 99.7 %all-to-all-start.2 = ((bf16[128,128,128]{2,1,0:T(8,128)(2,1)}), bf16[128,128,128]{2,1,0:T(8,128)(2,1)}, u32[]{:S(2)}, u32[]{:S(2)}) async-start(bf16[128,128,128]{2,1,0:T(8,128)(2,1)} %get-tuple-element.25), calls=%async_computation.2 | async-start | bytes 8388608 | tf_op jit(solution)/shard_map/all_to_all | solution.py:239
  85.7 16.9 %collective-permute-start.7 = (bf16[128,512]{1,0:T(8,128)(2,1)S(1)}, bf16[128,512]{1,0:T(8,128)(2,1)S(1)}, u32[]{:S(2)}, u32[]{:S(2)}) collective-permute-start(bf16[128,512]{1,0:T(8,128)(2,1)S(1)} %get-tuple-element.50), channel_id=1, source_target_pairs={{0,6},{8,14},{16,22},{24,30},{32,38},{40,46},{48,54},{56,62},{64,7... | collective-permute-start | bytes 393224 | tf_op jit(solution)/shard_map/ppermute | solution.py:252
  96.6 7.3 %collective-permute-start.6 = (bf16[128,512]{1,0:T(8,128)(2,1)S(1)}, bf16[128,512]{1,0:T(8,128)(2,1)S(1)}, u32[]{:S(2)}, u32[]{:S(2)}) collective-permute-start(bf16[128,512]{1,0:T(8,128)(2,1)S(1)} %get-tuple-element.49), channel_id=1, source_target_pairs={{0,4},{8,12},{16,20},{24,28},{32,36},{40,44},{48,52},{56,60},{64,6... | collective-permute-start | bytes 393224 | tf_op jit(solution)/shard_map/ppermute | solution.py:252
  97.9 7.9 %collective-permute-start.5 = (bf16[128,512]{1,0:T(8,128)(2,1)S(1)}, bf16[128,512]{1,0:T(8,128)(2,1)S(1)}, u32[]{:S(2)}, u32[]{:S(2)}) collective-permute-start(bf16[128,512]{1,0:T(8,128)(2,1)S(1)} %get-tuple-element.48), channel_id=1, source_target_pairs={{0,2},{8,10},{16,18},{24,26},{32,34},{40,42},{48,50},{56,58},{64,6... | collective-permute-start | bytes 393224 | tf_op jit(solution)/shard_map/ppermute | solution.py:252
  99.9 8.8 %collective-permute-start.4 = (bf16[8,16,512]{2,1,0:T(8,128)(2,1)S(1)}, bf16[8,16,512]{2,1,0:T(8,128)(2,1)S(1)}, u32[]{:S(2)}, u32[]{:S(2)}) collective-permute-start(bf16[8,16,512]{2,1,0:T(8,128)(2,1)S(1)} %get-tuple-element.54), channel_id=1, source_target_pairs={{8,26},{16,28},{24,30},{264,282},{272,284},{280,286}} | collective-permute-start | bytes 393224 | tf_op jit(solution)/shard_map/ppermute | solution.py:394
  101.2 10.7 %collective-permute-start.3 = (bf16[8,16,512]{2,1,0:T(8,128)(2,1)}, bf16[8,16,512]{2,1,0:T(8,128)(2,1)S(1)}, u32[]{:S(2)}, u32[]{:S(2)}) collective-permute-start(bf16[8,16,512]{2,1,0:T(8,128)(2,1)} %get-tuple-element.52), channel_id=1, source_target_pairs={{8,18},{16,20},{24,22},{264,274},{272,276},{280,278}} | collective-permute-start | bytes 393224 | tf_op jit(solution)/shard_map/ppermute | solution.py:394
  102.5 12.9 %collective-permute-start.1 = (bf16[8,16,512]{2,1,0:T(8,128)(2,1)}, bf16[8,16,512]{2,1,0:T(8,128)(2,1)S(1)}, u32[]{:S(2)}, u32[]{:S(2)}) collective-permute-start(bf16[8,16,512]{2,1,0:T(8,128)(2,1)} %get-tuple-element.53), channel_id=1, source_target_pairs={{8,2},{16,4},{24,6},{264,258},{272,260},{280,262}} | collective-permute-start | bytes 393224 | tf_op jit(solution)/shard_map/ppermute | solution.py:394
  103.8 14.4 %collective-permute-start.2 = (bf16[8,16,512]{2,1,0:T(8,128)(2,1)}, bf16[8,16,512]{2,1,0:T(8,128)(2,1)}, u32[]{:S(2)}, u32[]{:S(2)}) collective-permute-start(bf16[8,16,512]{2,1,0:T(8,128)(2,1)} %get-tuple-element.51), channel_id=1, source_target_pairs={{8,10},{16,12},{24,14},{264,266},{272,268},{280,270}} | collective-permute-start | bytes 393224 | tf_op jit(solution)/shard_map/ppermute | solution.py:394
  105.8 13.7 %collective-permute-start.8 = (bf16[128,512]{1,0:T(8,128)(2,1)S(1)}, bf16[128,512]{1,0:T(8,128)(2,1)S(1)}, u32[]{:S(2)}, u32[]{:S(2)}) collective-permute-start(bf16[128,512]{1,0:T(8,128)(2,1)S(1)} %fusion.15.refs_0_), channel_id=1, source_target_pairs={{0,7},{2,1},{4,3},{6,5},{8,15},{10,9},{12,11},{14,13},{16,23},{18,... | collective-permute-start | bytes 393224 | tf_op jit(solution)/shard_map/ppermute | solution.py:270
  108.8 16.1 %collective-permute-start.9 = (bf16[128,512]{1,0:T(8,128)(2,1)S(1)}, bf16[128,512]{1,0:T(8,128)(2,1)S(1)}, u32[]{:S(2)}, u32[]{:S(2)}) collective-permute-start(bf16[128,512]{1,0:T(8,128)(2,1)S(1)} %fusion.15.refs_0_), channel_id=1, source_target_pairs={{0,6},{2,0},{4,2},{6,4},{8,14},{10,8},{12,10},{14,12},{16,22},{18,... | collective-permute-start | bytes 393224 | tf_op jit(solution)/shard_map/ppermute | solution.py:270
  111.9 16.1 %collective-permute-start.10 = (bf16[128,512]{1,0:T(8,128)(2,1)S(1)}, bf16[128,512]{1,0:T(8,128)(2,1)S(1)}, u32[]{:S(2)}, u32[]{:S(2)}) collective-permute-start(bf16[128,512]{1,0:T(8,128)(2,1)S(1)} %fusion.15.refs_0_), channel_id=1, source_target_pairs={{0,5},{2,7},{4,1},{6,3},{8,13},{10,15},{12,9},{14,11},{16,21},{18,... | collective-permute-start | bytes 393224 | tf_op jit(solution)/shard_map/ppermute | solution.py:270
  115.4 13.6 %collective-permute-start.11 = (bf16[128,512]{1,0:T(8,128)(2,1)S(1)}, bf16[128,512]{1,0:T(8,128)(2,1)S(1)}, u32[]{:S(2)}, u32[]{:S(2)}) collective-permute-start(bf16[128,512]{1,0:T(8,128)(2,1)S(1)} %fusion.15.refs_0_), channel_id=1, source_target_pairs={{0,4},{2,6},{4,0},{6,2},{8,12},{10,14},{12,8},{14,10},{16,20},{18,... | collective-permute-start | bytes 393224 | tf_op jit(solution)/shard_map/ppermute | solution.py:270
  118.2 10.8 %collective-permute-start.12 = (bf16[128,512]{1,0:T(8,128)(2,1)S(1)}, bf16[128,512]{1,0:T(8,128)(2,1)S(1)}, u32[]{:S(2)}, u32[]{:S(2)}) collective-permute-start(bf16[128,512]{1,0:T(8,128)(2,1)S(1)} %fusion.15.refs_0_), channel_id=1, source_target_pairs={{0,3},{2,5},{4,7},{6,1},{8,11},{10,13},{12,15},{14,9},{16,19},{18,... | collective-permute-start | bytes 393224 | tf_op jit(solution)/shard_map/ppermute | solution.py:270
  119.5 16.0 %collective-permute-start.13 = (bf16[128,512]{1,0:T(8,128)(2,1)S(1)}, bf16[128,512]{1,0:T(8,128)(2,1)S(1)}, u32[]{:S(2)}, u32[]{:S(2)}) collective-permute-start(bf16[128,512]{1,0:T(8,128)(2,1)S(1)} %fusion.15.refs_0_), channel_id=1, source_target_pairs={{0,2},{2,4},{4,6},{6,0},{8,10},{10,12},{12,14},{14,8},{16,18},{18,... | collective-permute-start | bytes 393224 | tf_op jit(solution)/shard_map/ppermute | solution.py:270
  125.5 10.0 %collective-permute-start.14 = (bf16[128,512]{1,0:T(8,128)(2,1)S(1)}, bf16[128,512]{1,0:T(8,128)(2,1)S(1)}, u32[]{:S(2)}, u32[]{:S(2)}) collective-permute-start(bf16[128,512]{1,0:T(8,128)(2,1)S(1)} %fusion.15.refs_0_), channel_id=1, source_target_pairs={{0,1},{2,3},{4,5},{6,7},{8,9},{10,11},{12,13},{14,15},{16,17},{18,... | collective-permute-start | bytes 393224 | tf_op jit(solution)/shard_map/ppermute | solution.py:270
  151.2 17.2 %collective-permute-start.21 = (bf16[8,16,512]{2,1,0:T(8,128)(2,1)S(1)}, bf16[8,16,512]{2,1,0:T(8,128)(2,1)S(1)}, u32[]{:S(2)}, u32[]{:S(2)}) collective-permute-start(bf16[8,16,512]{2,1,0:T(8,128)(2,1)S(1)} %get-tuple-element.43), channel_id=1, source_target_pairs={{0,25},{8,27},{16,29},{24,31},{256,281},{264,283},{272,285},{280,2... | collective-permute-start | bytes 393224 | tf_op jit(solution)/shard_map/ppermute | solution.py:394
  163.2 6.7 %collective-permute-start.20 = (bf16[8,16,512]{2,1,0:T(8,128)(2,1)S(1)}, bf16[8,16,512]{2,1,0:T(8,128)(2,1)S(1)}, u32[]{:S(2)}, u32[]{:S(2)}) collective-permute-start(bf16[8,16,512]{2,1,0:T(8,128)(2,1)S(1)} %get-tuple-element.44), channel_id=1, source_target_pairs={{0,17},{8,19},{16,21},{24,23},{256,273},{264,275},{272,277},{280,2... | collective-permute-start | bytes 393224 | tf_op jit(solution)/shard_map/ppermute | solution.py:394
  164.5 8.2 %collective-permute-start.18 = (bf16[8,16,512]{2,1,0:T(8,128)(2,1)S(1)}, bf16[8,16,512]{2,1,0:T(8,128)(2,1)S(1)}, u32[]{:S(2)}, u32[]{:S(2)}) collective-permute-start(bf16[8,16,512]{2,1,0:T(8,128)(2,1)S(1)} %get-tuple-element.42), channel_id=1, source_target_pairs={{0,1},{8,3},{16,5},{24,7},{256,257},{264,259},{272,261},{280,263}} | collective-permute-start | bytes 393224 | tf_op jit(solution)/shard_map/ppermute | solution.py:394
  165.8 9.7 %collective-permute-start.19 = (bf16[8,16,512]{2,1,0:T(8,128)(2,1)S(1)}, bf16[8,16,512]{2,1,0:T(8,128)(2,1)S(1)}, u32[]{:S(2)}, u32[]{:S(2)}) collective-permute-start(bf16[8,16,512]{2,1,0:T(8,128)(2,1)S(1)} %get-tuple-element.41), channel_id=1, source_target_pairs={{0,9},{8,11},{16,13},{24,15},{256,265},{264,267},{272,269},{280,271}} | collective-permute-start | bytes 393224 | tf_op jit(solution)/shard_map/ppermute | solution.py:394
  167.1 12.4 %collective-permute-start.17 = (bf16[128,512]{1,0:T(8,128)(2,1)S(1)}, bf16[128,512]{1,0:T(8,128)(2,1)S(1)}, u32[]{:S(2)}, u32[]{:S(2)}) collective-permute-start(bf16[128,512]{1,0:T(8,128)(2,1)S(1)} %get-tuple-element.46), channel_id=1, source_target_pairs={{0,6},{8,14},{16,22},{24,30},{32,38},{40,46},{48,54},{56,62},{64,7... | collective-permute-start | bytes 393224 | tf_op jit(solution)/shard_map/ppermute | solution.py:252
  168.4 11.1 %collective-permute-start.16 = (bf16[128,512]{1,0:T(8,128)(2,1)S(1)}, bf16[128,512]{1,0:T(8,128)(2,1)S(1)}, u32[]{:S(2)}, u32[]{:S(2)}) collective-permute-start(bf16[128,512]{1,0:T(8,128)(2,1)S(1)} %get-tuple-element.47), channel_id=1, source_target_pairs={{0,4},{8,12},{16,20},{24,28},{32,36},{40,44},{48,52},{56,60},{64,6... | collective-permute-start | bytes 393224 | tf_op jit(solution)/shard_map/ppermute | solution.py:252
  169.9 10.0 %collective-permute-start.15 = (bf16[128,512]{1,0:T(8,128)(2,1)S(1)}, bf16[128,512]{1,0:T(8,128)(2,1)S(1)}, u32[]{:S(2)}, u32[]{:S(2)}) collective-permute-start(bf16[128,512]{1,0:T(8,128)(2,1)S(1)} %get-tuple-element.45), channel_id=1, source_target_pairs={{0,2},{8,10},{16,18},{24,26},{32,34},{40,42},{48,50},{56,58},{64,6... | collective-permute-start | bytes 393224 | tf_op jit(solution)/shard_map/ppermute | solution.py:252
  176.2 15.9 %all-to-all-start.3 = ((bf16[8,16,512]{2,1,0:T(8,128)(2,1)}), bf16[8,16,512]{2,1,0:T(8,128)(2,1)S(1)}, u32[]{:S(2)}, u32[]{:S(2)}) async-start(bf16[8,16,512]{2,1,0:T(8,128)(2,1)} %add_select_fusion), calls=%async_computation.3 | async-start | bytes 262144 | tf_op jit(solution)/shard_map/all_to_all | solution.py:407
  179.9 10.9 %collective-permute-start.22 = (bf16[128,512]{1,0:T(8,128)(2,1)S(1)}, bf16[128,512]{1,0:T(8,128)(2,1)S(1)}, u32[]{:S(2)}, u32[]{:S(2)}) collective-permute-start(bf16[128,512]{1,0:T(8,128)(2,1)S(1)} %fusion.12.refs_8_), channel_id=1, source_target_pairs={{0,7},{2,1},{4,3},{6,5},{8,15},{10,9},{12,11},{14,13},{16,23},{18,... | collective-permute-start | bytes 393224 | tf_op jit(solution)/shard_map/ppermute | solution.py:270
  188.3 3.8 %collective-permute-start.23 = (bf16[128,512]{1,0:T(8,128)(2,1)S(1)}, bf16[128,512]{1,0:T(8,128)(2,1)S(1)}, u32[]{:S(2)}, u32[]{:S(2)}) collective-permute-start(bf16[128,512]{1,0:T(8,128)(2,1)S(1)} %fusion.12.refs_8_), channel_id=1, source_target_pairs={{0,1},{2,3},{4,5},{6,7},{8,9},{10,11},{12,13},{14,15},{16,17},{18,... | collective-permute-start | bytes 393224 | tf_op jit(solution)/shard_map/ppermute | solution.py:270
  193.0 32.9 %all-to-all-start.4 = ((bf16[32,16,512]{2,1,0:T(8,128)(2,1)}), bf16[32,16,512]{2,1,0:T(8,128)(2,1)S(1)}, u32[]{:S(2)}, u32[]{:S(2)}) async-start(bf16[32,16,512]{2,1,0:T(8,128)(2,1)} %broadcast_in_dim.23), calls=%async_computation.4 | async-start | bytes 1048576 | tf_op jit(solution)/shard_map/all_to_all | solution.py:239
  201.7 15.3 %collective-permute-start.24 = (bf16[128,512]{1,0:T(8,128)(2,1)S(1)}, bf16[128,512]{1,0:T(8,128)(2,1)S(1)}, u32[]{:S(2)}, u32[]{:S(2)}) collective-permute-start(bf16[128,512]{1,0:T(8,128)(2,1)S(1)} %fusion.12.refs_8_), channel_id=1, source_target_pairs={{0,6},{2,0},{4,2},{6,4},{8,14},{10,8},{12,10},{14,12},{16,22},{18,... | collective-permute-start | bytes 393224 | tf_op jit(solution)/shard_map/ppermute | solution.py:270
  205.9 11.1 %collective-permute-start.25 = (bf16[128,512]{1,0:T(8,128)(2,1)S(1)}, bf16[128,512]{1,0:T(8,128)(2,1)S(1)}, u32[]{:S(2)}, u32[]{:S(2)}) collective-permute-start(bf16[128,512]{1,0:T(8,128)(2,1)S(1)} %fusion.12.refs_8_), channel_id=1, source_target_pairs={{0,5},{2,7},{4,1},{6,3},{8,13},{10,15},{12,9},{14,11},{16,21},{18,... | collective-permute-start | bytes 393224 | tf_op jit(solution)/shard_map/ppermute | solution.py:270
  208.5 14.2 %collective-permute-start.26 = (bf16[128,512]{1,0:T(8,128)(2,1)S(1)}, bf16[128,512]{1,0:T(8,128)(2,1)S(1)}, u32[]{:S(2)}, u32[]{:S(2)}) collective-permute-start(bf16[128,512]{1,0:T(8,128)(2,1)S(1)} %fusion.12.refs_8_), channel_id=1, source_target_pairs={{0,4},{2,6},{4,0},{6,2},{8,12},{10,14},{12,8},{14,10},{16,20},{18,... | collective-permute-start | bytes 393224 | tf_op jit(solution)/shard_map/ppermute | solution.py:270
  213.1 9.5 %collective-permute-start.27 = (bf16[128,512]{1,0:T(8,128)(2,1)S(1)}, bf16[128,512]{1,0:T(8,128)(2,1)S(1)}, u32[]{:S(2)}, u32[]{:S(2)}) collective-permute-start(bf16[128,512]{1,0:T(8,128)(2,1)S(1)} %fusion.12.refs_8_), channel_id=1, source_target_pairs={{0,3},{2,5},{4,7},{6,1},{8,11},{10,13},{12,15},{14,9},{16,19},{18,... | collective-permute-start | bytes 393224 | tf_op jit(solution)/shard_map/ppermute | solution.py:270
  214.4 11.4 %collective-permute-start.28 = (bf16[128,512]{1,0:T(8,128)(2,1)S(1)}, bf16[128,512]{1,0:T(8,128)(2,1)S(1)}, u32[]{:S(2)}, u32[]{:S(2)}) collective-permute-start(bf16[128,512]{1,0:T(8,128)(2,1)S(1)} %fusion.12.refs_8_), channel_id=1, source_target_pairs={{0,2},{2,4},{4,6},{6,0},{8,10},{10,12},{12,14},{14,8},{16,18},{18,... | collective-permute-start | bytes 393224 | tf_op jit(solution)/shard_map/ppermute | solution.py:270
  (21 other events, 426.1 us)

commit v9 on v8

--- a/solution.py
+++ b/solution.py
@@ -239,7 +239,6 @@
     return lax.all_to_all(block, axis, split_axis=0, concat_axis=0, tiled=True)
 
 
-HOLDERS = 4
 QUARTERS = 4
 
 
@@ -253,101 +252,70 @@
     return mine
 
 
-def column_holders():
+def to_columns(block):
     size = lax.axis_size("col")
-    return list(range(0, size, size // HOLDERS))
-
-
-def to_holders(block):
-    parts = list(block.reshape(HOLDERS, -1, block.shape[1]))
-    return hand_out(parts, "col", column_holders())
-
-
-def from_holders(mine):
-    size = lax.axis_size("col")
-    got = [mine]
-    for t in range(1, size):
-        got.append(lax.ppermute(mine, "col", [(i, (i - t) % size) for i in column_holders()]))
-    return got
-
-
-def finish_kernel(size, state, *refs):
-    halves = refs[:size], refs[size : 2 * size]
-    partner_at, window, added_at, out, parts, partner, base, added, sem, rest_sem = refs[2 * size :]
+    return hand_out(list(block.reshape(size, -1, block.shape[1])), "col", range(size))
+
+
+def finish_kernel(
+    state, lower_at, first, second, partner_at, window, added_at, out, lower, partner, base, added, sem
+):
     column = state[0]
-    step = size // HOLDERS
-    rows = TILE // HOLDERS
-    shift = lax.rem(step - lax.rem(column, step), step)
-    first = lax.div(column + shift, step)
-    others = [
-        pltpu.make_async_copy(partner_at, partner, rest_sem.at[0]),
-        pltpu.make_async_copy(window.at[0, pl.ds(0, TILE), :], base, rest_sem.at[1]),
-        pltpu.make_async_copy(added_at, added, rest_sem.at[2]),
-    ]
-    for copy in others:
-        copy.start()
-    for s in range(step):
-
-        @pl.when(shift == s)
-        def _():
-            copies = [
-                pltpu.make_async_copy(
-                    halves[h][k * step + s], parts.at[h, k], sem.at[h * HOLDERS + k]
-                )
-                for h in range(2)
-                for k in range(HOLDERS)
-            ]
-            for copy in copies:
-                copy.start()
-            for copy in copies:
-                copy.wait()
-
-    for copy in others:
-        copy.wait()
-
-    for k in range(HOLDERS):
-        source = lax.rem(first + k, HOLDERS)
-        at = pl.ds(pl.multiple_of(source * rows, rows), rows)
-        under = pl.ds(pl.multiple_of(source * rows + TILE, rows), rows)
-
-        @pl.when(column == 0)
-        def _():
-            out[0, at, :] = parts[0, k]
-            out[0, under, :] = parts[1, k]
-
-        @pl.when(column != 0)
-        def _():
-            def product(part):
-                return lax.dot_general(
-                    part, partner[...], (((1,), (1,)), ((), ())), preferred_element_type=F32
-                )
-
-            upper = base[at, :].astype(F32) - state[1].astype(F32) * product(parts[0, k])
+
+    @pl.when(column == 0)
+    def _():
+        copies = [
+            pltpu.make_async_copy(first, out.at[0, pl.ds(0, TILE), :], sem.at[0]),
+            pltpu.make_async_copy(second, out.at[0, pl.ds(TILE, TILE), :], sem.at[1]),
+        ]
+        for copy in copies:
+            copy.start()
+        for copy in copies:
+            copy.wait()
+
+    @pl.when(column != 0)
+    def _():
+        copies = [
+            pltpu.make_async_copy(lower_at, lower, sem.at[0]),
+            pltpu.make_async_copy(partner_at, partner, sem.at[1]),
+            pltpu.make_async_copy(window.at[0, pl.ds(0, TILE), :], base, sem.at[2]),
+            pltpu.make_async_copy(added_at, added, sem.at[3]),
+        ]
+        for copy in copies:
+            copy.start()
+        for copy in copies:
+            copy.wait()
+        size, both, _ = lower.shape
+        rows = both // 2
+        for p in range(size):
+            product = lax.dot_general(
+                lower[p], partner[...], (((1,), (1,)), ((), ())), preferred_element_type=F32
+            )
+            at = slice(p * rows, (p + 1) * rows)
+            under = slice(TILE + p * rows, TILE + (p + 1) * rows)
+            upper = base[at, :].astype(F32) - state[1].astype(F32) * product[:rows]
             out[0, at, :] = upper.astype(BF16)
-            lower = added[at, :] - state[2].astype(F32) * product(parts[1, k])
-            out[0, under, :] = lower.astype(BF16)
-
-
-def finish(state, upper, under, partner, window, added):
-    size = len(upper)
-    out = jax.ShapeDtypeStruct((1, 2 * TILE, TILE), BF16)
-    return pl.pallas_call(
-        functools.partial(finish_kernel, size),
-        out_shape=out,
+            result = added[at, :] - state[2].astype(F32) * product[rows:]
+            out[0, under, :] = result.astype(BF16)
+
+
+def finish(state, lower, first, second, partner, window, added):
+    return pl.pallas_call(
+        finish_kernel,
+        out_shape=jax.ShapeDtypeStruct((1, 2 * TILE, TILE), BF16),
         in_specs=[pl.BlockSpec(memory_space=pltpu.SMEM)]
-        + [pl.BlockSpec(memory_space=pl.ANY)] * (2 * size + 3),
+        + [pl.BlockSpec(memory_space=pl.ANY)] * 6,
         out_specs=pl.BlockSpec(memory_space=pltpu.VMEM),
         scratch_shapes=[
-            pltpu.VMEM((2, HOLDERS, TILE // HOLDERS, TILE), BF16),
+            pltpu.VMEM(lower.shape, BF16),
             pltpu.VMEM((TILE, TILE), BF16),
             pltpu.VMEM((TILE, TILE), BF16),
             pltpu.VMEM((TILE, TILE), F32),
-            pltpu.SemaphoreType.DMA((2 * HOLDERS,)),
-            pltpu.SemaphoreType.DMA((3,)),
+            pltpu.SemaphoreType.DMA((4,)),
         ],
         compiler_params=pltpu.CompilerParams(vmem_limit_bytes=56 << 20),
         name="finish",
-    )(state, *upper, *under, partner, window, added)
+    )(state, lower, first, second, partner, window, added)
 
 
 def shards(window, children, routes, slots, pattern):
@@ -397,7 +365,7 @@
 
     lower_first = solve(first)
     even = to_plane(lower_first, 0)
-    upper = from_holders(to_holders(lower_first))
+    upper = to_columns(lower_first)
     incoming, even, upper = lax.optimization_barrier((incoming, even, upper))
     added = assemble(tags, incoming, window)
     lower_second = solve(added)
@@ -407,16 +375,15 @@
     got = lax.all_to_all(
         piece, "row", split_axis=0, concat_axis=0, axis_index_groups=groups, tiled=True
     )
-    under = from_holders(to_holders(lower_second))
-    near = [1, columns - 1]
-    got, *arrived = lax.optimization_barrier((got, *(under[t] for t in near)))
-    for t, part in zip(near, arrived):
-        under[t] = part
+    under = to_columns(lower_second)
+    lower = lax.all_gather(jnp.concatenate([upper, under]), "col", tiled=True)
+    lower = lower.reshape(columns, -1, TILE)
+    got, under = lax.optimization_barrier((got, under))
     partner = swap(
         jnp.broadcast_to(got[:1], (rows_axis, part_rows, TILE)), "row"
     ).reshape(TILE, TILE)
     state = jnp.concatenate([jnp.full((1,), column, jnp.int32), pattern[0, :, 0]])
-    return finish(state, upper, under, partner, window, added)
+    return finish(state, lower, lower_first, lower_second, partner, window, added)
 
 
 def solution(mesh):

time: 232 us -> 239 us (1.030)
  the two profiles are of different devices: /device:TPU:2 before, /device:TPU:8 now
where the time goes in v9:
time: 239 us; the launch traced here: 238 us
  starting transfers between devices  71.2 us (30%)
  waiting for transfers between devices  57.8 us (24%)
  Pallas kernels  45.8 us (19%)
  blocking collectives  41 us (17%)
  between operations  14 us (6%)
  matrix products  2.94 us (1%)
  local copies, waits for them, and re-layouts  2.74 us (1%)
  other arithmetic  2.43 us (1%)
    all_to_all x3, waiting for transfers between devices, swap(): return lax.all_to_all(block, axis, split_axis=0, concat_axis=0, tiled=True)  56.8 us
    ppermute x14, starting transfers between devices, hand_out(): mine = mine + lax.ppermute(part, axis, [(0, device)])  37.4 us
    pallas_call x1, Pallas kernels, inverse_factor(): pl.pallas_call(inverse_kernel, out_shape=jax.ShapeDtypeStruct((n, n), F32...  32.2 us
    all_to_all x3, starting transfers between devices, swap(): return lax.all_to_all(block, axis, split_axis=0, concat_axis=0, tiled=True)  26.3 us
    all_to_all x1, blocking collectives, shards(): lax.all_to_all(piece, 'row', split_axis=0, concat_axis=0, axis_index_grou...  20.9 us
    all_to_all x1, blocking collectives, swap(): return lax.all_to_all(block, axis, split_axis=0, concat_axis=0, tiled=True)  20.1 us
    ppermute x8, starting transfers between devices, to_plane(): got = lax.ppermute(quarters[:, k], ('row', 'col'), pairs)  5.53 us
  transfers between devices with their start and end apart: 27, of which 4 were waited for; matrix products, arithmetic and copies ran while one was open for 2% of the time, Pallas kernels for 15%

profile of v9, /device:TPU:8, one launch (start us, length us, event | category | flops | bytes accessed | tf_op | source)
XLA Modules:
  0.0 238.0 jit_solution(9726955219717973758)
XLA Ops:
  6.5 1.8 pack.1
  8.4 10.2 %all-to-all-start = ((bf16[32,40,128]{2,1,0:T(8,128)(2,1)}), bf16[32,40,128]{2,1,0:T(8,128)(2,1)S(1)}, u32[]{:S(2)}, u32[]{:S(2)}) async-start(bf16[32,40,128]{2,1,0:T(8,128)(2,1)} %bitcast.66), calls=%async_computation | async-start | bytes 655360 | tf_op jit(solution)/shard_map/all_to_all | solution.py:239
  18.5 4.7 %place.1 = (bf16[128,128,128]{2,1,0:T(8,128)(2,1)}, s32[128]{0:T(128)}) custom-call(s32[64]{0:T(128)} %bitcast.69, s32[64]{0:T(128)} %slots.1, bf16[64,128,128]{2,1,0:T(8,128)(2,1)} %children.1), custom_call_target="tpu_custom_call" | custom-call | tf_op jit(solution)/shard_map/place/pallas_call | solution.py:50
  24.3 1.9 collective-permute-start
  26.3 1.0 collective-permute-done
  27.4 4.5 %all-to-all-done = bf16[32,40,128]{2,1,0:T(8,128)(2,1)S(1)} async-done(((bf16[32,40,128]{2,1,0:T(8,128)(2,1)}), bf16[32,40,128]{2,1,0:T(8,128)(2,1)S(1)}, u32[]{:S(2)}, u32[]{:S(2)}) %all-to-all-start) | async-done | bytes 327712 | tf_op jit(solution)/shard_map/all_to_all | solution.py:239
  32.3 20.1 %all_to_all.25 = bf16[32,48,128]{2,1,0:T(8,128)(2,1)S(1)} all-to-all(bf16[32,48,128]{2,1,0:T(8,128)(2,1)S(1)} %copy.56), channel_id=1, replica_groups=mesh['front'=2,'row'=32,'col'=8] {'row'}, dimensions={0} | all-to-all | bytes 786432 | tf_op jit(solution)/shard_map/all_to_all | solution.py:239
  52.8 6.1 %all-to-all-start.2 = ((bf16[128,128,128]{2,1,0:T(8,128)(2,1)}), bf16[128,128,128]{2,1,0:T(8,128)(2,1)}, u32[]{:S(2)}, u32[]{:S(2)}) async-start(bf16[128,128,128]{2,1,0:T(8,128)(2,1)} %get-tuple-element.16), calls=%async_computation.2 | async-start | bytes 8388608 | tf_op jit(solution)/shard_map/all_to_all | solution.py:239
  58.9 32.2 %inverse.1 = f32[512,512]{1,0:T(8,128)S(1)} custom-call(bf16[1280,128]{1,0:T(8,128)(2,1)S(1)} %bitcast.59), custom_call_target="tpu_custom_call" | custom-call | flops 536870912 | bytes 1572864 | tf_op jit(solution)/shard_map/inverse/pallas_call | solution.py:209
  91.1 1.1 convolution_convert_fusion
  92.2 10.9 %collective-permute-start.11 = (bf16[64,512]{1,0:T(8,128)(2,1)S(1)}, bf16[64,512]{1,0:T(8,128)(2,1)S(1)}, u32[]{:S(2)}, u32[]{:S(2)}) collective-permute-start(bf16[64,512]{1,0:T(8,128)(2,1)S(1)} %get-tuple-element.35), channel_id=1, source_target_pairs={{0,7},{8,15},{16,23},{24,31},{32,39},{40,47},{48,55},{56,63},{64,7... | collective-permute-start | bytes 196616 | tf_op jit(solution)/shard_map/ppermute | solution.py:251
  103.2 1.3 collective-permute-start.10
  104.5 1.3 collective-permute-start.9
  105.8 1.3 collective-permute-start.8
  107.1 1.3 collective-permute-start.7
  108.4 1.3 collective-permute-start.6
  109.7 1.3 collective-permute-start.5
  114.1 38.9 %all-to-all-done.2.incoming = bf16[128,128,128]{2,1,0:T(8,128)(2,1)} async-done(((bf16[128,128,128]{2,1,0:T(8,128)(2,1)}), bf16[128,128,128]{2,1,0:T(8,128)(2,1)}, u32[]{:S(2)}, u32[]{:S(2)}) %all-to-all-start.2) | async-done | bytes 4194336 | tf_op jit(solution)/shard_map/all_to_all | solution.py:239
  153.0 4.3 %assemble.1.added_at = f32[512,512]{1,0:T(8,128)S(1)} custom-call(s32[128]{0:T(128)S(1)} %reshape.168.tags, bf16[128,128,128]{2,1,0:T(8,128)(2,1)} %all-to-all-done.2.incoming, bf16[1,1024,512]{2,1,0:T(8,128)(2,1)S(1)} %copy-done), custom_call_target="tpu_custom_call" | custom-call | tf_op jit(solution)/shard_map/assemble/pallas_call | solution.py:101
  157.3 1.9 convolution_convert_fusion.1.second
  159.2 10.9 %collective-permute-start.18 = (bf16[64,512]{1,0:T(8,128)(2,1)S(1)}, bf16[64,512]{1,0:T(8,128)(2,1)S(1)}, u32[]{:S(2)}, u32[]{:S(2)}) collective-permute-start(bf16[64,512]{1,0:T(8,128)(2,1)S(1)} %get-tuple-element.28), channel_id=1, source_target_pairs={{0,7},{8,15},{16,23},{24,31},{32,39},{40,47},{48,55},{56,63},{64,7... | collective-permute-start | bytes 196616 | tf_op jit(solution)/shard_map/ppermute | solution.py:251
  170.1 1.3 collective-permute-start.17
  171.4 1.3 collective-permute-start.16
  172.7 1.3 collective-permute-start.15
  174.0 1.3 collective-permute-start.14
  175.3 1.3 collective-permute-start.13
  176.7 1.3 collective-permute-start.12
  181.6 20.9 %all_to_all.26 = bf16[8,16,512]{2,1,0:T(8,128)(2,1)S(1)} all-to-all(bf16[8,16,512]{2,1,0:T(8,128)(2,1)S(1)} %add_select_fusion), channel_id=1, replica_groups={{0,32,64,96,128,160,192,224},{8,40,72,104,136,168,200,232},{16,48,80,11..., dimensions={0} | all-to-all | bytes 262144 | tf_op jit(solution)/shard_map/all_to_all | solution.py:375
  202.5 0.9 broadcast_in_dim.23
  203.4 10.1 %all-to-all-start.4 = ((bf16[32,16,512]{2,1,0:T(8,128)(2,1)}), bf16[32,16,512]{2,1,0:T(8,128)(2,1)S(1)}, u32[]{:S(2)}, u32[]{:S(2)}) async-start(bf16[32,16,512]{2,1,0:T(8,128)(2,1)} %broadcast_in_dim.23), calls=%async_computation.4 | async-start | bytes 1048576 | tf_op jit(solution)/shard_map/all_to_all | solution.py:239
  214.1 13.3 %all-to-all-done.4 = bf16[32,16,512]{2,1,0:T(8,128)(2,1)S(1)} async-done(((bf16[32,16,512]{2,1,0:T(8,128)(2,1)}), bf16[32,16,512]{2,1,0:T(8,128)(2,1)S(1)}, u32[]{:S(2)}, u32[]{:S(2)}) %all-to-all-start.4) | async-done | bytes 524320 | tf_op jit(solution)/shard_map/all_to_all | solution.py:239
  228.2 2.9 %finish.1 = bf16[1,1024,512]{2,1,0:T(8,128)(2,1)} custom-call(s32[3]{0:T(128)} %pad_add_fusion.1.state, bf16[8,128,512]{2,1,0:T(8,128)(2,1)} %bitcast.67, bf16[512,512]{1,0:T(8,128)(2,1)} %bitcast.64, bf16[512,512]{1,0:T(8,128)(2,1)} %copy-done.2, bf16[512,512]{1,0:T(8,128)(2,1)} %bitcast.65, bf16[1,1024,512]{2,1,0:T(8,128)(2,1)} %window.3, f32[512,512]{1,0:T(8,128)} %copy-done.1), custom_call_target="tpu_custom_call" | custom-call | tf_op jit(solution)/shard_map/finish/pallas_call | solution.py:303
  (75 shorter events, 10.0 us)
Async XLA Ops:
  8.4 23.6 %all-to-all-start = ((bf16[32,40,128]{2,1,0:T(8,128)(2,1)}), bf16[32,40,128]{2,1,0:T(8,128)(2,1)S(1)}, u32[]{:S(2)}, u32[]{:S(2)}) async-start(bf16[32,40,128]{2,1,0:T(8,128)(2,1)} %bitcast.66), calls=%async_computation | async-start | bytes 655360 | tf_op jit(solution)/shard_map/all_to_all | solution.py:239
  24.3 3.0 %collective-permute-start = (s32[32,2]{0,1:T(2,128)S(1)}, s32[32,2]{0,1:T(2,128)S(1)}, u32[]{:S(2)}, u32[]{:S(2)}) collective-permute-start(s32[32,2]{0,1:T(2,128)S(1)} %copy.54), channel_id=1, source_target_pairs={{0,256},{256,0},{1,257},{257,1},{2,258},{258,2},{3,259},{259,3},{4... | collective-permute-start | bytes 776 | tf_op jit(solution)/shard_map/ppermute | solution.py:336
  52.8 38.3 %copy-start = (bf16[1,1024,512]{2,1,0:T(8,128)(2,1)S(1)}, bf16[1,1024,512]{2,1,0:T(8,128)(2,1)}, u32[]{:S(2)}) copy-start(bf16[1,1024,512]{2,1,0:T(8,128)(2,1)} %window.3) | copy-start | bytes 3145732
  52.8 100.2 %all-to-all-start.2 = ((bf16[128,128,128]{2,1,0:T(8,128)(2,1)}), bf16[128,128,128]{2,1,0:T(8,128)(2,1)}, u32[]{:S(2)}, u32[]{:S(2)}) async-start(bf16[128,128,128]{2,1,0:T(8,128)(2,1)} %get-tuple-element.16), calls=%async_computation.2 | async-start | bytes 8388608 | tf_op jit(solution)/shard_map/all_to_all | solution.py:239
  58.9 168.6 %all-gather.2.cloned.1.call-start = ((), (), s32[]{:S(2)}) async-start(), calls=%async_computation.5 | async-start | bytes 1179648 | tf_op jit(solution)/shard_map/all_gather | solution.py:379
  92.2 21.9 %copy-start.3 = (bf16[512,512]{0,1:T(8,128)(2,1)}, bf16[512,512]{0,1:T(8,128)(2,1)S(1)}, u32[]{:S(2)}) copy-start(bf16[512,512]{0,1:T(8,128)(2,1)S(1)} %convolution_convert_fusion) | copy-start | bytes 1572868
  92.2 16.2 %collective-permute-start.11 = (bf16[64,512]{1,0:T(8,128)(2,1)S(1)}, bf16[64,512]{1,0:T(8,128)(2,1)S(1)}, u32[]{:S(2)}, u32[]{:S(2)}) collective-permute-start(bf16[64,512]{1,0:T(8,128)(2,1)S(1)} %get-tuple-element.35), channel_id=1, source_target_pairs={{0,7},{8,15},{16,23},{24,31},{32,39},{40,47},{48,55},{56,63},{64,7... | collective-permute-start | bytes 196616 | tf_op jit(solution)/shard_map/ppermute | solution.py:251
  103.2 6.5 %collective-permute-start.10 = (bf16[64,512]{1,0:T(8,128)(2,1)S(1)}, bf16[64,512]{1,0:T(8,128)(2,1)S(1)}, u32[]{:S(2)}, u32[]{:S(2)}) collective-permute-start(bf16[64,512]{1,0:T(8,128)(2,1)S(1)} %get-tuple-element.36), channel_id=1, source_target_pairs={{0,6},{8,14},{16,22},{24,30},{32,38},{40,46},{48,54},{56,62},{64,7... | collective-permute-start | bytes 196616 | tf_op jit(solution)/shard_map/ppermute | solution.py:251
  104.5 6.6 %collective-permute-start.9 = (bf16[64,512]{1,0:T(8,128)(2,1)S(1)}, bf16[64,512]{1,0:T(8,128)(2,1)S(1)}, u32[]{:S(2)}, u32[]{:S(2)}) collective-permute-start(bf16[64,512]{1,0:T(8,128)(2,1)S(1)} %get-tuple-element.37), channel_id=1, source_target_pairs={{0,5},{8,13},{16,21},{24,29},{32,37},{40,45},{48,53},{56,61},{64,6... | collective-permute-start | bytes 196616 | tf_op jit(solution)/shard_map/ppermute | solution.py:251
  105.8 6.0 %collective-permute-start.8 = (bf16[64,512]{1,0:T(8,128)(2,1)S(1)}, bf16[64,512]{1,0:T(8,128)(2,1)S(1)}, u32[]{:S(2)}, u32[]{:S(2)}) collective-permute-start(bf16[64,512]{1,0:T(8,128)(2,1)S(1)} %get-tuple-element.38), channel_id=1, source_target_pairs={{0,4},{8,12},{16,20},{24,28},{32,36},{40,44},{48,52},{56,60},{64,6... | collective-permute-start | bytes 196616 | tf_op jit(solution)/shard_map/ppermute | solution.py:251
  107.1 5.3 %collective-permute-start.7 = (bf16[64,512]{1,0:T(8,128)(2,1)S(1)}, bf16[64,512]{1,0:T(8,128)(2,1)S(1)}, u32[]{:S(2)}, u32[]{:S(2)}) collective-permute-start(bf16[64,512]{1,0:T(8,128)(2,1)S(1)} %get-tuple-element.39), channel_id=1, source_target_pairs={{0,3},{8,11},{16,19},{24,27},{32,35},{40,43},{48,51},{56,59},{64,6... | collective-permute-start | bytes 196616 | tf_op jit(solution)/shard_map/ppermute | solution.py:251
  108.4 4.7 %collective-permute-start.6 = (bf16[64,512]{1,0:T(8,128)(2,1)S(1)}, bf16[64,512]{1,0:T(8,128)(2,1)S(1)}, u32[]{:S(2)}, u32[]{:S(2)}) collective-permute-start(bf16[64,512]{1,0:T(8,128)(2,1)S(1)} %get-tuple-element.40), channel_id=1, source_target_pairs={{0,2},{8,10},{16,18},{24,26},{32,34},{40,42},{48,50},{56,58},{64,6... | collective-permute-start | bytes 196616 | tf_op jit(solution)/shard_map/ppermute | solution.py:251
  109.7 4.3 %collective-permute-start.5 = (bf16[64,512]{1,0:T(8,128)(2,1)S(1)}, bf16[64,512]{1,0:T(8,128)(2,1)S(1)}, u32[]{:S(2)}, u32[]{:S(2)}) collective-permute-start(bf16[64,512]{1,0:T(8,128)(2,1)S(1)} %get-tuple-element.34), channel_id=1, source_target_pairs={{0,1},{8,9},{16,17},{24,25},{32,33},{40,41},{48,49},{56,57},{64,65... | collective-permute-start | bytes 196616 | tf_op jit(solution)/shard_map/ppermute | solution.py:251
  111.0 3.0 %collective-permute-start.4 = (bf16[8,16,512]{2,1,0:T(8,128)(2,1)S(1)}, bf16[8,16,512]{2,1,0:T(8,128)(2,1)S(1)}, u32[]{:S(2)}, u32[]{:S(2)}) collective-permute-start(bf16[8,16,512]{2,1,0:T(8,128)(2,1)S(1)} %get-tuple-element.44), channel_id=1, source_target_pairs={{8,26},{16,28},{24,30},{264,282},{272,284},{280,286}} | collective-permute-start | bytes 393224 | tf_op jit(solution)/shard_map/ppermute | solution.py:362
  111.7 2.3 collective-permute-start.3
  112.4 1.6 collective-permute-start.1
  113.1 0.9 collective-permute-start.2
  157.3 70.2 %copy-start.1 = (f32[512,512]{1,0:T(8,128)}, f32[512,512]{1,0:T(8,128)S(1)}, u32[]{:S(2)}) copy-start(f32[512,512]{1,0:T(8,128)S(1)} %assemble.1.added_at) | copy-start | bytes 3145732
  157.3 56.2 %copy-start.5 = (s32[1,2,1]{1,2,0:T(1,128)S(1)}, s32[1,2,1]{1,2,0:T(1,128)}, u32[]{:S(2)}) copy-start(s32[1,2,1]{1,2,0:T(1,128)} %param.9) | copy-start | bytes 28
  159.1 68.3 %copy-start.2 = (bf16[512,512]{1,0:T(8,128)(2,1)}, bf16[512,512]{1,0:T(8,128)(2,1)S(1)}, u32[]{:S(2)}) copy-start(bf16[512,512]{1,0:T(8,128)(2,1)S(1)} %convolution_convert_fusion.1.second) | copy-start | bytes 1572868
  159.2 16.1 %collective-permute-start.18 = (bf16[64,512]{1,0:T(8,128)(2,1)S(1)}, bf16[64,512]{1,0:T(8,128)(2,1)S(1)}, u32[]{:S(2)}, u32[]{:S(2)}) collective-permute-start(bf16[64,512]{1,0:T(8,128)(2,1)S(1)} %get-tuple-element.28), channel_id=1, source_target_pairs={{0,7},{8,15},{16,23},{24,31},{32,39},{40,47},{48,55},{56,63},{64,7... | collective-permute-start | bytes 196616 | tf_op jit(solution)/shard_map/ppermute | solution.py:251
  170.1 6.5 %collective-permute-start.17 = (bf16[64,512]{1,0:T(8,128)(2,1)S(1)}, bf16[64,512]{1,0:T(8,128)(2,1)S(1)}, u32[]{:S(2)}, u32[]{:S(2)}) collective-permute-start(bf16[64,512]{1,0:T(8,128)(2,1)S(1)} %get-tuple-element.29), channel_id=1, source_target_pairs={{0,6},{8,14},{16,22},{24,30},{32,38},{40,46},{48,54},{56,62},{64,7... | collective-permute-start | bytes 196616 | tf_op jit(solution)/shard_map/ppermute | solution.py:251
  171.4 6.6 %collective-permute-start.16 = (bf16[64,512]{1,0:T(8,128)(2,1)S(1)}, bf16[64,512]{1,0:T(8,128)(2,1)S(1)}, u32[]{:S(2)}, u32[]{:S(2)}) collective-permute-start(bf16[64,512]{1,0:T(8,128)(2,1)S(1)} %get-tuple-element.30), channel_id=1, source_target_pairs={{0,5},{8,13},{16,21},{24,29},{32,37},{40,45},{48,53},{56,61},{64,6... | collective-permute-start | bytes 196616 | tf_op jit(solution)/shard_map/ppermute | solution.py:251
  172.7 6.0 %collective-permute-start.15 = (bf16[64,512]{1,0:T(8,128)(2,1)S(1)}, bf16[64,512]{1,0:T(8,128)(2,1)S(1)}, u32[]{:S(2)}, u32[]{:S(2)}) collective-permute-start(bf16[64,512]{1,0:T(8,128)(2,1)S(1)} %get-tuple-element.31), channel_id=1, source_target_pairs={{0,4},{8,12},{16,20},{24,28},{32,36},{40,44},{48,52},{56,60},{64,6... | collective-permute-start | bytes 196616 | tf_op jit(solution)/shard_map/ppermute | solution.py:251
  174.0 5.3 %collective-permute-start.14 = (bf16[64,512]{1,0:T(8,128)(2,1)S(1)}, bf16[64,512]{1,0:T(8,128)(2,1)S(1)}, u32[]{:S(2)}, u32[]{:S(2)}) collective-permute-start(bf16[64,512]{1,0:T(8,128)(2,1)S(1)} %get-tuple-element.32), channel_id=1, source_target_pairs={{0,3},{8,11},{16,19},{24,27},{32,35},{40,43},{48,51},{56,59},{64,6... | collective-permute-start | bytes 196616 | tf_op jit(solution)/shard_map/ppermute | solution.py:251
  175.3 4.7 %collective-permute-start.13 = (bf16[64,512]{1,0:T(8,128)(2,1)S(1)}, bf16[64,512]{1,0:T(8,128)(2,1)S(1)}, u32[]{:S(2)}, u32[]{:S(2)}) collective-permute-start(bf16[64,512]{1,0:T(8,128)(2,1)S(1)} %get-tuple-element.33), channel_id=1, source_target_pairs={{0,2},{8,10},{16,18},{24,26},{32,34},{40,42},{48,50},{56,58},{64,6... | collective-permute-start | bytes 196616 | tf_op jit(solution)/shard_map/ppermute | solution.py:251
  176.7 4.1 %collective-permute-start.12 = (bf16[64,512]{1,0:T(8,128)(2,1)S(1)}, bf16[64,512]{1,0:T(8,128)(2,1)S(1)}, u32[]{:S(2)}, u32[]{:S(2)}) collective-permute-start(bf16[64,512]{1,0:T(8,128)(2,1)S(1)} %get-tuple-element.27), channel_id=1, source_target_pairs={{0,1},{8,9},{16,17},{24,25},{32,33},{40,41},{48,49},{56,57},{64,65... | collective-permute-start | bytes 196616 | tf_op jit(solution)/shard_map/ppermute | solution.py:251
  178.0 3.5 %collective-permute-start.22 = (bf16[8,16,512]{2,1,0:T(8,128)(2,1)S(1)}, bf16[8,16,512]{2,1,0:T(8,128)(2,1)S(1)}, u32[]{:S(2)}, u32[]{:S(2)}) collective-permute-start(bf16[8,16,512]{2,1,0:T(8,128)(2,1)S(1)} %get-tuple-element.25), channel_id=1, source_target_pairs={{0,25},{8,27},{16,29},{24,31},{256,281},{264,283},{272,285},{280,2... | collective-permute-start | bytes 393224 | tf_op jit(solution)/shard_map/ppermute | solution.py:362
  178.7 2.8 %collective-permute-start.21 = (bf16[8,16,512]{2,1,0:T(8,128)(2,1)S(1)}, bf16[8,16,512]{2,1,0:T(8,128)(2,1)S(1)}, u32[]{:S(2)}, u32[]{:S(2)}) collective-permute-start(bf16[8,16,512]{2,1,0:T(8,128)(2,1)S(1)} %get-tuple-element.26), channel_id=1, source_target_pairs={{0,17},{8,19},{16,21},{24,23},{256,273},{264,275},{272,277},{280,2... | collective-permute-start | bytes 393224 | tf_op jit(solution)/shard_map/ppermute | solution.py:362
  179.4 2.1 collective-permute-start.19
  180.1 1.5 collective-permute-start.20
  203.4 24.1 %all-to-all-start.4 = ((bf16[32,16,512]{2,1,0:T(8,128)(2,1)}), bf16[32,16,512]{2,1,0:T(8,128)(2,1)S(1)}, u32[]{:S(2)}, u32[]{:S(2)}) async-start(bf16[32,16,512]{2,1,0:T(8,128)(2,1)} %broadcast_in_dim.23), calls=%async_computation.4 | async-start | bytes 1048576 | tf_op jit(solution)/shard_map/all_to_all | solution.py:239
  (1 other events, 0.8 us)
Sparse Core Ops, SparseCore 0:
  181.6 40.0 all-gather.1

commit v10 on v8

--- a/solution.py
+++ b/solution.py
@@ -273,50 +273,61 @@
 
 def finish_kernel(size, state, *refs):
     halves = refs[:size], refs[size : 2 * size]
-    partner_at, window, added_at, out, parts, partner, base, added, sem, rest_sem = refs[2 * size :]
+    own = refs[2 * size : 2 * size + 2]
+    rest = refs[2 * size + 2 :]
+    partner_at, window, added_at, out, parts, partner, base, added, sem, rest_sem = rest
     column = state[0]
     step = size // HOLDERS
     rows = TILE // HOLDERS
     shift = lax.rem(step - lax.rem(column, step), step)
     first = lax.div(column + shift, step)
-    others = [
-        pltpu.make_async_copy(partner_at, partner, rest_sem.at[0]),
-        pltpu.make_async_copy(window.at[0, pl.ds(0, TILE), :], base, rest_sem.at[1]),
-        pltpu.make_async_copy(added_at, added, rest_sem.at[2]),
-    ]
-    for copy in others:
-        copy.start()
-    for s in range(step):
-
-        @pl.when(shift == s)
-        def _():
-            copies = [
-                pltpu.make_async_copy(
-                    halves[h][k * step + s], parts.at[h, k], sem.at[h * HOLDERS + k]
-                )
-                for h in range(2)
-                for k in range(HOLDERS)
-            ]
-            for copy in copies:
-                copy.start()
-            for copy in copies:
-                copy.wait()
-
-    for copy in others:
-        copy.wait()
-
-    for k in range(HOLDERS):
-        source = lax.rem(first + k, HOLDERS)
-        at = pl.ds(pl.multiple_of(source * rows, rows), rows)
-        under = pl.ds(pl.multiple_of(source * rows + TILE, rows), rows)
-
-        @pl.when(column == 0)
-        def _():
-            out[0, at, :] = parts[0, k]
-            out[0, under, :] = parts[1, k]
-
-        @pl.when(column != 0)
-        def _():
+
+    @pl.when(column == 0)
+    def _():
+        copies = [
+            pltpu.make_async_copy(
+                own[h], out.at[0, pl.ds(h * TILE, TILE), :], rest_sem.at[h]
+            )
+            for h in range(2)
+        ]
+        for copy in copies:
+            copy.start()
+        for copy in copies:
+            copy.wait()
+
+    @pl.when(column != 0)
+    def _():
+        others = [
+            pltpu.make_async_copy(partner_at, partner, rest_sem.at[0]),
+            pltpu.make_async_copy(window.at[0, pl.ds(0, TILE), :], base, rest_sem.at[1]),
+            pltpu.make_async_copy(added_at, added, rest_sem.at[2]),
+        ]
+        for copy in others:
+            copy.start()
+        for s in range(step):
+
+            @pl.when(shift == s)
+            def _():
+                copies = [
+                    pltpu.make_async_copy(
+                        halves[h][k * step + s], parts.at[h, k], sem.at[h * HOLDERS + k]
+                    )
+                    for h in range(2)
+                    for k in range(HOLDERS)
+                ]
+                for copy in copies:
+                    copy.start()
+                for copy in copies:
+                    copy.wait()
+
+        for copy in others:
+            copy.wait()
+
+        for k in range(HOLDERS):
+            source = lax.rem(first + k, HOLDERS)
+            at = pl.ds(pl.multiple_of(source * rows, rows), rows)
+            under = pl.ds(pl.multiple_of(source * rows + TILE, rows), rows)
+
             def product(part):
                 return lax.dot_general(
                     part, partner[...], (((1,), (1,)), ((), ())), preferred_element_type=F32
@@ -328,14 +339,14 @@
             out[0, under, :] = lower.astype(BF16)
 
 
-def finish(state, upper, under, partner, window, added):
+def finish(state, upper, under, own, partner, window, added):
     size = len(upper)
     out = jax.ShapeDtypeStruct((1, 2 * TILE, TILE), BF16)
     return pl.pallas_call(
         functools.partial(finish_kernel, size),
         out_shape=out,
         in_specs=[pl.BlockSpec(memory_space=pltpu.SMEM)]
-        + [pl.BlockSpec(memory_space=pl.ANY)] * (2 * size + 3),
+        + [pl.BlockSpec(memory_space=pl.ANY)] * (2 * size + 5),
         out_specs=pl.BlockSpec(memory_space=pltpu.VMEM),
         scratch_shapes=[
             pltpu.VMEM((2, HOLDERS, TILE // HOLDERS, TILE), BF16),
@@ -347,7 +358,7 @@
         ],
         compiler_params=pltpu.CompilerParams(vmem_limit_bytes=56 << 20),
         name="finish",
-    )(state, *upper, *under, partner, window, added)
+    )(state, *upper, *under, *own, partner, window, added)
 
 
 def shards(window, children, routes, slots, pattern):
@@ -408,7 +419,7 @@
         piece, "row", split_axis=0, concat_axis=0, axis_index_groups=groups, tiled=True
     )
     under = from_holders(to_holders(lower_second))
-    near = [1, columns - 1]
+    near = [1, columns - 1, 2, columns - 2]
     got, *arrived = lax.optimization_barrier((got, *(under[t] for t in near)))
     for t, part in zip(near, arrived):
         under[t] = part
@@ -416,7 +427,7 @@
         jnp.broadcast_to(got[:1], (rows_axis, part_rows, TILE)), "row"
     ).reshape(TILE, TILE)
     state = jnp.concatenate([jnp.full((1,), column, jnp.int32), pattern[0, :, 0]])
-    return finish(state, upper, under, partner, window, added)
+    return finish(state, upper, under, (lower_first, lower_second), partner, window, added)
 
 
 def solution(mesh):

time: 232 us -> 232 us (level)
  the two profiles are of different devices: /device:TPU:2 before, /device:TPU:66 now
where the time goes in v10:
time: 232 us; the launch traced here: 231 us
  waiting for transfers between devices  93.6 us (40%)
  starting transfers between devices  58.1 us (25%)
  Pallas kernels  47.7 us (21%)
  blocking collectives  20.2 us (9%)
  local copies, waits for them, and re-layouts  4.1 us (2%)
  other arithmetic  3.48 us (2%)
  matrix products  2.94 us (1%)
    ppermute x14, waiting for transfers between devices, from_holders(): lax.ppermute(mine, 'col', [(i, (i - t) % size) for i in column_holders()])  62.4 us
    pallas_call x1, Pallas kernels, inverse_factor(): pl.pallas_call(inverse_kernel, out_shape=jax.ShapeDtypeStruct((n, n), F32...  32.2 us
    all_to_all x3, starting transfers between devices, swap(): return lax.all_to_all(block, axis, split_axis=0, concat_axis=0, tiled=True)  25.7 us
    all_to_all x1, blocking collectives, swap(): return lax.all_to_all(block, axis, split_axis=0, concat_axis=0, tiled=True)  20.2 us
    ppermute x8, waiting for transfers between devices, to_plane(): got = lax.ppermute(quarters[:, k], ('row', 'col'), pairs)  15.9 us
    ppermute x14, starting transfers between devices, from_holders(): lax.ppermute(mine, 'col', [(i, (i - t) % size) for i in column_holders()])  14.5 us
    all_to_all x3, waiting for transfers between devices, swap(): return lax.all_to_all(block, axis, split_axis=0, concat_axis=0, tiled=True)  14.4 us
    ppermute x8, starting transfers between devices, to_plane(): got = lax.ppermute(quarters[:, k], ('row', 'col'), pairs)  8.58 us
  transfers between devices with their start and end apart: 33, of which 12 were waited for; matrix products, arithmetic and copies ran while one was open for 2% of the time, Pallas kernels for 16%

profile of v10, /device:TPU:66, one launch (start us, length us, event | category | flops | bytes accessed | tf_op | source)
XLA Modules:
  0.0 231.0 jit_solution(948983528158916563)
XLA Ops:
  0.0 1.8 pack.1
  1.8 10.2 %all-to-all-start = ((bf16[32,40,128]{2,1,0:T(8,128)(2,1)}), bf16[32,40,128]{2,1,0:T(8,128)(2,1)S(1)}, u32[]{:S(2)}, u32[]{:S(2)}) async-start(bf16[32,40,128]{2,1,0:T(8,128)(2,1)} %bitcast.65), calls=%async_computation | async-start | bytes 655360 | tf_op jit(solution)/shard_map/all_to_all | solution.py:239
  12.1 4.7 %place.1 = (bf16[128,128,128]{2,1,0:T(8,128)(2,1)}, s32[128]{0:T(128)}) custom-call(s32[64]{0:T(128)} %bitcast.67, s32[64]{0:T(128)} %slots.1, bf16[64,128,128]{2,1,0:T(8,128)(2,1)} %children.1), custom_call_target="tpu_custom_call" | custom-call | tf_op jit(solution)/shard_map/place/pallas_call | solution.py:50
  17.8 1.9 collective-permute-start
  21.0 3.7 %all-to-all-done = bf16[32,40,128]{2,1,0:T(8,128)(2,1)S(1)} async-done(((bf16[32,40,128]{2,1,0:T(8,128)(2,1)}), bf16[32,40,128]{2,1,0:T(8,128)(2,1)S(1)}, u32[]{:S(2)}, u32[]{:S(2)}) %all-to-all-start) | async-done | bytes 327712 | tf_op jit(solution)/shard_map/all_to_all | solution.py:239
  25.0 20.2 %all_to_all.25 = bf16[32,48,128]{2,1,0:T(8,128)(2,1)S(1)} all-to-all(bf16[32,48,128]{2,1,0:T(8,128)(2,1)S(1)} %copy.56), channel_id=1, replica_groups=mesh['front'=2,'row'=32,'col'=8] {'row'}, dimensions={0} | all-to-all | bytes 786432 | tf_op jit(solution)/shard_map/all_to_all | solution.py:239
  45.7 6.7 %all-to-all-start.2 = ((bf16[128,128,128]{2,1,0:T(8,128)(2,1)}), bf16[128,128,128]{2,1,0:T(8,128)(2,1)}, u32[]{:S(2)}, u32[]{:S(2)}) async-start(bf16[128,128,128]{2,1,0:T(8,128)(2,1)} %get-tuple-element.27), calls=%async_computation.2 | async-start | bytes 8388608 | tf_op jit(solution)/shard_map/all_to_all | solution.py:239
  52.4 32.2 %inverse.1 = f32[512,512]{1,0:T(8,128)S(1)} custom-call(bf16[1280,128]{1,0:T(8,128)(2,1)S(1)} %bitcast.58), custom_call_target="tpu_custom_call" | custom-call | flops 536870912 | bytes 1572864 | tf_op jit(solution)/shard_map/inverse/pallas_call | solution.py:209
  88.4 1.3 collective-permute-start.4
  89.8 1.3 collective-permute-start.3
  91.1 1.3 collective-permute-start.1
  92.4 1.3 collective-permute-start.2
  93.8 1.3 collective-permute-start.8
  95.8 1.3 collective-permute-start.10
  97.8 1.3 collective-permute-start.12
  99.1 11.3 %collective-permute-done.8.refs_1_ = bf16[128,512]{1,0:T(8,128)(2,1)S(1)} collective-permute-done((bf16[128,512]{1,0:T(8,128)(2,1)S(1)}, bf16[128,512]{1,0:T(8,128)(2,1)S(1)}, u32[]{:S(2)}, u32[]{:S(2)}) %collective-permute-start.8) | collective-permute-done | bytes 131104 | tf_op jit(solution)/shard_map/ppermute | solution.py:270
  111.7 1.5 collective-permute-start.14
  114.3 6.8 %collective-permute-done.10.refs_3_ = bf16[128,512]{1,0:T(8,128)(2,1)S(1)} collective-permute-done((bf16[128,512]{1,0:T(8,128)(2,1)S(1)}, bf16[128,512]{1,0:T(8,128)(2,1)S(1)}, u32[]{:S(2)}, u32[]{:S(2)}) %collective-permute-start.10) | collective-permute-done | bytes 131104 | tf_op jit(solution)/shard_map/ppermute | solution.py:270
  121.1 10.7 %collective-permute-done.12.refs_5_ = bf16[128,512]{1,0:T(8,128)(2,1)S(1)} collective-permute-done((bf16[128,512]{1,0:T(8,128)(2,1)S(1)}, bf16[128,512]{1,0:T(8,128)(2,1)S(1)}, u32[]{:S(2)}, u32[]{:S(2)}) %collective-permute-start.12) | collective-permute-done | bytes 131104 | tf_op jit(solution)/shard_map/ppermute | solution.py:270
  131.8 3.0 %collective-permute-done.14.refs_7_ = bf16[128,512]{1,0:T(8,128)(2,1)} collective-permute-done((bf16[128,512]{1,0:T(8,128)(2,1)S(1)}, bf16[128,512]{1,0:T(8,128)(2,1)}, u32[]{:S(2)}, u32[]{:S(2)}) %collective-permute-start.14) | collective-permute-done | bytes 131104 | tf_op jit(solution)/shard_map/ppermute | solution.py:270
  134.8 10.6 %all-to-all-done.2.incoming = bf16[128,128,128]{2,1,0:T(8,128)(2,1)} async-done(((bf16[128,128,128]{2,1,0:T(8,128)(2,1)}), bf16[128,128,128]{2,1,0:T(8,128)(2,1)}, u32[]{:S(2)}, u32[]{:S(2)}) %all-to-all-start.2) | async-done | bytes 4194336 | tf_op jit(solution)/shard_map/all_to_all | solution.py:239
  145.4 3.9 %assemble.1.refs_20_ = f32[512,512]{1,0:T(8,128)S(1)} custom-call(s32[128]{0:T(128)S(1)} %reshape.149.tags, bf16[128,128,128]{2,1,0:T(8,128)(2,1)} %all-to-all-done.2.incoming, bf16[1,1024,512]{2,1,0:T(8,128)(2,1)S(1)} %copy-done), custom_call_target="tpu_custom_call" | custom-call | tf_op jit(solution)/shard_map/assemble/pallas_call | solution.py:101
  149.4 1.9 convolution_convert_fusion.1.refs_17_
  153.4 1.3 collective-permute-start.19
  156.8 15.8 %collective-permute-done.19 = bf16[8,16,512]{2,1,0:T(8,128)(2,1)S(1)} collective-permute-done((bf16[8,16,512]{2,1,0:T(8,128)(2,1)S(1)}, bf16[8,16,512]{2,1,0:T(8,128)(2,1)S(1)}, u32[]{:S(2)}, u32[]{:S(2)}) %collective-permute-start.19) | collective-permute-done | bytes 131104 | tf_op jit(solution)/shard_map/ppermute | solution.py:405
  173.3 3.4 %all-to-all-start.3 = ((bf16[8,16,512]{2,1,0:T(8,128)(2,1)}), bf16[8,16,512]{2,1,0:T(8,128)(2,1)S(1)}, u32[]{:S(2)}, u32[]{:S(2)}) async-start(bf16[8,16,512]{2,1,0:T(8,128)(2,1)} %add_select_fusion), calls=%async_computation.3 | async-start | bytes 262144 | tf_op jit(solution)/shard_map/all_to_all | solution.py:418
  180.7 5.1 %collective-permute-done.22.refs_9_ = bf16[128,512]{1,0:T(8,128)(2,1)S(1)} collective-permute-done((bf16[128,512]{1,0:T(8,128)(2,1)S(1)}, bf16[128,512]{1,0:T(8,128)(2,1)S(1)}, u32[]{:S(2)}, u32[]{:S(2)}) %collective-permute-start.22) | collective-permute-done | bytes 131104 | tf_op jit(solution)/shard_map/ppermute | solution.py:270
  185.8 6.4 %collective-permute-done.23.refs_15_ = bf16[128,512]{1,0:T(8,128)(2,1)S(1)} collective-permute-done((bf16[128,512]{1,0:T(8,128)(2,1)S(1)}, bf16[128,512]{1,0:T(8,128)(2,1)S(1)}, u32[]{:S(2)}, u32[]{:S(2)}) %collective-permute-start.23) | collective-permute-done | bytes 131104 | tf_op jit(solution)/shard_map/ppermute | solution.py:270
  193.1 8.7 %all-to-all-start.4 = ((bf16[32,16,512]{2,1,0:T(8,128)(2,1)}), bf16[32,16,512]{2,1,0:T(8,128)(2,1)S(1)}, u32[]{:S(2)}, u32[]{:S(2)}) async-start(bf16[32,16,512]{2,1,0:T(8,128)(2,1)} %broadcast_in_dim.23), calls=%async_computation.4 | async-start | bytes 1048576 | tf_op jit(solution)/shard_map/all_to_all | solution.py:239
  205.7 11.5 %collective-permute-done.26.refs_11_ = bf16[128,512]{1,0:T(8,128)(2,1)S(1)} collective-permute-done((bf16[128,512]{1,0:T(8,128)(2,1)S(1)}, bf16[128,512]{1,0:T(8,128)(2,1)S(1)}, u32[]{:S(2)}, u32[]{:S(2)}) %collective-permute-start.26) | collective-permute-done | bytes 131104 | tf_op jit(solution)/shard_map/ppermute | solution.py:270
  217.2 7.8 %collective-permute-done.28.refs_13_ = bf16[128,512]{1,0:T(8,128)(2,1)S(1)} collective-permute-done((bf16[128,512]{1,0:T(8,128)(2,1)S(1)}, bf16[128,512]{1,0:T(8,128)(2,1)S(1)}, u32[]{:S(2)}, u32[]{:S(2)}) %collective-permute-start.28) | collective-permute-done | bytes 131104 | tf_op jit(solution)/shard_map/ppermute | solution.py:270
  225.9 5.0 %finish.1 = bf16[1,1024,512]{2,1,0:T(8,128)(2,1)} custom-call(s32[3]{0:T(128)} %pad_add_fusion.1.state, bf16[128,512]{1,0:T(8,128)(2,1)} %copy-done.5, bf16[128,512]{1,0:T(8,128)(2,1)} %copy-done.7, bf16[128,512]{1,0:T(8,128)(2,1)} %copy-done.8, bf16[128,512]{1,0:T(8,128)(2,1)} %copy-done.9, bf16[128,512]{1,0:T(8,128)(2,1)} %copy-done.10, ...), custom_call_target="tpu_custom_call" | custom-call | tf_op jit(solution)/shard_map/finish/pallas_call | solution.py:345
  (114 shorter events, 24.9 us)
Async XLA Ops:
  1.8 22.9 %all-to-all-start = ((bf16[32,40,128]{2,1,0:T(8,128)(2,1)}), bf16[32,40,128]{2,1,0:T(8,128)(2,1)S(1)}, u32[]{:S(2)}, u32[]{:S(2)}) async-start(bf16[32,40,128]{2,1,0:T(8,128)(2,1)} %bitcast.65), calls=%async_computation | async-start | bytes 655360 | tf_op jit(solution)/shard_map/all_to_all | solution.py:239
  45.7 99.8 %all-to-all-start.2 = ((bf16[128,128,128]{2,1,0:T(8,128)(2,1)}), bf16[128,128,128]{2,1,0:T(8,128)(2,1)}, u32[]{:S(2)}, u32[]{:S(2)}) async-start(bf16[128,128,128]{2,1,0:T(8,128)(2,1)} %get-tuple-element.27), calls=%async_computation.2 | async-start | bytes 8388608 | tf_op jit(solution)/shard_map/all_to_all | solution.py:239
  85.7 5.4 %collective-permute-start.7 = (bf16[128,512]{1,0:T(8,128)(2,1)S(1)}, bf16[128,512]{1,0:T(8,128)(2,1)S(1)}, u32[]{:S(2)}, u32[]{:S(2)}) collective-permute-start(bf16[128,512]{1,0:T(8,128)(2,1)S(1)} %get-tuple-element.53), channel_id=1, source_target_pairs={{0,6},{8,14},{16,22},{24,30},{32,38},{40,46},{48,54},{56,62},{64,7... | collective-permute-start | bytes 393224 | tf_op jit(solution)/shard_map/ppermute | solution.py:252
  86.4 6.0 %collective-permute-start.6 = (bf16[128,512]{1,0:T(8,128)(2,1)S(1)}, bf16[128,512]{1,0:T(8,128)(2,1)S(1)}, u32[]{:S(2)}, u32[]{:S(2)}) collective-permute-start(bf16[128,512]{1,0:T(8,128)(2,1)S(1)} %get-tuple-element.54), channel_id=1, source_target_pairs={{0,4},{8,12},{16,20},{24,28},{32,36},{40,44},{48,52},{56,60},{64,6... | collective-permute-start | bytes 393224 | tf_op jit(solution)/shard_map/ppermute | solution.py:252
  87.0 6.7 %collective-permute-start.5 = (bf16[128,512]{1,0:T(8,128)(2,1)S(1)}, bf16[128,512]{1,0:T(8,128)(2,1)S(1)}, u32[]{:S(2)}, u32[]{:S(2)}) collective-permute-start(bf16[128,512]{1,0:T(8,128)(2,1)S(1)} %get-tuple-element.52), channel_id=1, source_target_pairs={{0,2},{8,10},{16,18},{24,26},{32,34},{40,42},{48,50},{56,58},{64,6... | collective-permute-start | bytes 393224 | tf_op jit(solution)/shard_map/ppermute | solution.py:252
  88.4 6.6 %collective-permute-start.4 = (bf16[8,16,512]{2,1,0:T(8,128)(2,1)S(1)}, bf16[8,16,512]{2,1,0:T(8,128)(2,1)}, u32[]{:S(2)}, u32[]{:S(2)}) collective-permute-start(bf16[8,16,512]{2,1,0:T(8,128)(2,1)S(1)} %get-tuple-element.58), channel_id=1, source_target_pairs={{8,26},{16,28},{24,30},{264,282},{272,284},{280,286}} | collective-permute-start | bytes 393224 | tf_op jit(solution)/shard_map/ppermute | solution.py:405
  89.8 6.0 %collective-permute-start.3 = (bf16[8,16,512]{2,1,0:T(8,128)(2,1)}, bf16[8,16,512]{2,1,0:T(8,128)(2,1)}, u32[]{:S(2)}, u32[]{:S(2)}) collective-permute-start(bf16[8,16,512]{2,1,0:T(8,128)(2,1)} %get-tuple-element.56), channel_id=1, source_target_pairs={{8,18},{16,20},{24,22},{264,274},{272,276},{280,278}} | collective-permute-start | bytes 393224 | tf_op jit(solution)/shard_map/ppermute | solution.py:405
  91.1 6.0 %collective-permute-start.1 = (bf16[8,16,512]{2,1,0:T(8,128)(2,1)}, bf16[8,16,512]{2,1,0:T(8,128)(2,1)}, u32[]{:S(2)}, u32[]{:S(2)}) collective-permute-start(bf16[8,16,512]{2,1,0:T(8,128)(2,1)} %get-tuple-element.57), channel_id=1, source_target_pairs={{8,2},{16,4},{24,6},{264,258},{272,260},{280,262}} | collective-permute-start | bytes 393224 | tf_op jit(solution)/shard_map/ppermute | solution.py:405
  92.4 5.4 %collective-permute-start.2 = (bf16[8,16,512]{2,1,0:T(8,128)(2,1)S(1)}, bf16[8,16,512]{2,1,0:T(8,128)(2,1)}, u32[]{:S(2)}, u32[]{:S(2)}) collective-permute-start(bf16[8,16,512]{2,1,0:T(8,128)(2,1)S(1)} %get-tuple-element.55), channel_id=1, source_target_pairs={{8,10},{16,12},{24,14},{264,266},{272,268},{280,270}} | collective-permute-start | bytes 393224 | tf_op jit(solution)/shard_map/ppermute | solution.py:405
  93.8 16.6 %collective-permute-start.8 = (bf16[128,512]{1,0:T(8,128)(2,1)S(1)}, bf16[128,512]{1,0:T(8,128)(2,1)S(1)}, u32[]{:S(2)}, u32[]{:S(2)}) collective-permute-start(bf16[128,512]{1,0:T(8,128)(2,1)S(1)} %fusion.15.refs_0_), channel_id=1, source_target_pairs={{0,7},{2,1},{4,3},{6,5},{8,15},{10,9},{12,11},{14,13},{16,23},{18,... | collective-permute-start | bytes 393224 | tf_op jit(solution)/shard_map/ppermute | solution.py:270
  95.1 15.9 %collective-permute-start.9 = (bf16[128,512]{1,0:T(8,128)(2,1)S(1)}, bf16[128,512]{1,0:T(8,128)(2,1)S(1)}, u32[]{:S(2)}, u32[]{:S(2)}) collective-permute-start(bf16[128,512]{1,0:T(8,128)(2,1)S(1)} %fusion.15.refs_0_), channel_id=1, source_target_pairs={{0,6},{2,0},{4,2},{6,4},{8,14},{10,8},{12,10},{14,12},{16,22},{18,... | collective-permute-start | bytes 393224 | tf_op jit(solution)/shard_map/ppermute | solution.py:270
  95.8 25.3 %collective-permute-start.10 = (bf16[128,512]{1,0:T(8,128)(2,1)S(1)}, bf16[128,512]{1,0:T(8,128)(2,1)S(1)}, u32[]{:S(2)}, u32[]{:S(2)}) collective-permute-start(bf16[128,512]{1,0:T(8,128)(2,1)S(1)} %fusion.15.refs_0_), channel_id=1, source_target_pairs={{0,5},{2,7},{4,1},{6,3},{8,13},{10,15},{12,9},{14,11},{16,21},{18,... | collective-permute-start | bytes 393224 | tf_op jit(solution)/shard_map/ppermute | solution.py:270
  97.1 24.0 %collective-permute-start.11 = (bf16[128,512]{1,0:T(8,128)(2,1)S(1)}, bf16[128,512]{1,0:T(8,128)(2,1)S(1)}, u32[]{:S(2)}, u32[]{:S(2)}) collective-permute-start(bf16[128,512]{1,0:T(8,128)(2,1)S(1)} %fusion.15.refs_0_), channel_id=1, source_target_pairs={{0,4},{2,6},{4,0},{6,2},{8,12},{10,14},{12,8},{14,10},{16,20},{18,... | collective-permute-start | bytes 393224 | tf_op jit(solution)/shard_map/ppermute | solution.py:270
  97.8 34.0 %collective-permute-start.12 = (bf16[128,512]{1,0:T(8,128)(2,1)S(1)}, bf16[128,512]{1,0:T(8,128)(2,1)S(1)}, u32[]{:S(2)}, u32[]{:S(2)}) collective-permute-start(bf16[128,512]{1,0:T(8,128)(2,1)S(1)} %fusion.15.refs_0_), channel_id=1, source_target_pairs={{0,3},{2,5},{4,7},{6,1},{8,11},{10,13},{12,15},{14,9},{16,19},{18,... | collective-permute-start | bytes 393224 | tf_op jit(solution)/shard_map/ppermute | solution.py:270
  110.4 21.4 %collective-permute-start.13 = (bf16[128,512]{1,0:T(8,128)(2,1)S(1)}, bf16[128,512]{1,0:T(8,128)(2,1)S(1)}, u32[]{:S(2)}, u32[]{:S(2)}) collective-permute-start(bf16[128,512]{1,0:T(8,128)(2,1)S(1)} %fusion.15.refs_0_), channel_id=1, source_target_pairs={{0,2},{2,4},{4,6},{6,0},{8,10},{10,12},{12,14},{14,8},{16,18},{18,... | collective-permute-start | bytes 393224 | tf_op jit(solution)/shard_map/ppermute | solution.py:270
  111.7 23.0 %collective-permute-start.14 = (bf16[128,512]{1,0:T(8,128)(2,1)S(1)}, bf16[128,512]{1,0:T(8,128)(2,1)}, u32[]{:S(2)}, u32[]{:S(2)}) collective-permute-start(bf16[128,512]{1,0:T(8,128)(2,1)S(1)} %fusion.15.refs_0_), channel_id=1, source_target_pairs={{0,1},{2,3},{4,5},{6,7},{8,9},{10,11},{12,13},{14,15},{16,17},{18,... | collective-permute-start | bytes 393224 | tf_op jit(solution)/shard_map/ppermute | solution.py:270
  151.3 4.0 %collective-permute-start.21 = (bf16[8,16,512]{2,1,0:T(8,128)(2,1)S(1)}, bf16[8,16,512]{2,1,0:T(8,128)(2,1)S(1)}, u32[]{:S(2)}, u32[]{:S(2)}) collective-permute-start(bf16[8,16,512]{2,1,0:T(8,128)(2,1)S(1)} %get-tuple-element.47), channel_id=1, source_target_pairs={{0,25},{8,27},{16,29},{24,31},{256,281},{264,283},{272,285},{280,2... | collective-permute-start | bytes 393224 | tf_op jit(solution)/shard_map/ppermute | solution.py:405
  152.0 4.1 %collective-permute-start.20 = (bf16[8,16,512]{2,1,0:T(8,128)(2,1)S(1)}, bf16[8,16,512]{2,1,0:T(8,128)(2,1)S(1)}, u32[]{:S(2)}, u32[]{:S(2)}) collective-permute-start(bf16[8,16,512]{2,1,0:T(8,128)(2,1)S(1)} %get-tuple-element.48), channel_id=1, source_target_pairs={{0,17},{8,19},{16,21},{24,23},{256,273},{264,275},{272,277},{280,2... | collective-permute-start | bytes 393224 | tf_op jit(solution)/shard_map/ppermute | solution.py:405
  152.7 4.1 %collective-permute-start.18 = (bf16[8,16,512]{2,1,0:T(8,128)(2,1)S(1)}, bf16[8,16,512]{2,1,0:T(8,128)(2,1)S(1)}, u32[]{:S(2)}, u32[]{:S(2)}) collective-permute-start(bf16[8,16,512]{2,1,0:T(8,128)(2,1)S(1)} %get-tuple-element.46), channel_id=1, source_target_pairs={{0,1},{8,3},{16,5},{24,7},{256,257},{264,259},{272,261},{280,263}} | collective-permute-start | bytes 393224 | tf_op jit(solution)/shard_map/ppermute | solution.py:405
  153.4 19.2 %collective-permute-start.19 = (bf16[8,16,512]{2,1,0:T(8,128)(2,1)S(1)}, bf16[8,16,512]{2,1,0:T(8,128)(2,1)S(1)}, u32[]{:S(2)}, u32[]{:S(2)}) collective-permute-start(bf16[8,16,512]{2,1,0:T(8,128)(2,1)S(1)} %get-tuple-element.45), channel_id=1, source_target_pairs={{0,9},{8,11},{16,13},{24,15},{256,265},{264,267},{272,269},{280,271}} | collective-permute-start | bytes 393224 | tf_op jit(solution)/shard_map/ppermute | solution.py:405
  154.7 22.0 %collective-permute-start.17 = (bf16[128,512]{1,0:T(8,128)(2,1)S(1)}, bf16[128,512]{1,0:T(8,128)(2,1)S(1)}, u32[]{:S(2)}, u32[]{:S(2)}) collective-permute-start(bf16[128,512]{1,0:T(8,128)(2,1)S(1)} %get-tuple-element.50), channel_id=1, source_target_pairs={{0,6},{8,14},{16,22},{24,30},{32,38},{40,46},{48,54},{56,62},{64,7... | collective-permute-start | bytes 393224 | tf_op jit(solution)/shard_map/ppermute | solution.py:252
  155.4 21.3 %collective-permute-start.16 = (bf16[128,512]{1,0:T(8,128)(2,1)S(1)}, bf16[128,512]{1,0:T(8,128)(2,1)S(1)}, u32[]{:S(2)}, u32[]{:S(2)}) collective-permute-start(bf16[128,512]{1,0:T(8,128)(2,1)S(1)} %get-tuple-element.51), channel_id=1, source_target_pairs={{0,4},{8,12},{16,20},{24,28},{32,36},{40,44},{48,52},{56,60},{64,6... | collective-permute-start | bytes 393224 | tf_op jit(solution)/shard_map/ppermute | solution.py:252
  156.1 20.6 %collective-permute-start.15 = (bf16[128,512]{1,0:T(8,128)(2,1)S(1)}, bf16[128,512]{1,0:T(8,128)(2,1)S(1)}, u32[]{:S(2)}, u32[]{:S(2)}) collective-permute-start(bf16[128,512]{1,0:T(8,128)(2,1)S(1)} %get-tuple-element.49), channel_id=1, source_target_pairs={{0,2},{8,10},{16,18},{24,26},{32,34},{40,42},{48,50},{56,58},{64,6... | collective-permute-start | bytes 393224 | tf_op jit(solution)/shard_map/ppermute | solution.py:252
  173.3 18.9 %all-to-all-start.3 = ((bf16[8,16,512]{2,1,0:T(8,128)(2,1)}), bf16[8,16,512]{2,1,0:T(8,128)(2,1)S(1)}, u32[]{:S(2)}, u32[]{:S(2)}) async-start(bf16[8,16,512]{2,1,0:T(8,128)(2,1)} %add_select_fusion), calls=%async_computation.3 | async-start | bytes 262144 | tf_op jit(solution)/shard_map/all_to_all | solution.py:418
  176.7 9.1 %collective-permute-start.22 = (bf16[128,512]{1,0:T(8,128)(2,1)S(1)}, bf16[128,512]{1,0:T(8,128)(2,1)S(1)}, u32[]{:S(2)}, u32[]{:S(2)}) collective-permute-start(bf16[128,512]{1,0:T(8,128)(2,1)S(1)} %fusion.12.refs_8_), channel_id=1, source_target_pairs={{0,7},{2,1},{4,3},{6,5},{8,15},{10,9},{12,11},{14,13},{16,23},{18,... | collective-permute-start | bytes 393224 | tf_op jit(solution)/shard_map/ppermute | solution.py:270
  178.0 14.1 %collective-permute-start.23 = (bf16[128,512]{1,0:T(8,128)(2,1)S(1)}, bf16[128,512]{1,0:T(8,128)(2,1)S(1)}, u32[]{:S(2)}, u32[]{:S(2)}) collective-permute-start(bf16[128,512]{1,0:T(8,128)(2,1)S(1)} %fusion.12.refs_8_), channel_id=1, source_target_pairs={{0,1},{2,3},{4,5},{6,7},{8,9},{10,11},{12,13},{14,15},{16,17},{18,... | collective-permute-start | bytes 393224 | tf_op jit(solution)/shard_map/ppermute | solution.py:270
  179.3 12.8 %collective-permute-start.24 = (bf16[128,512]{1,0:T(8,128)(2,1)S(1)}, bf16[128,512]{1,0:T(8,128)(2,1)S(1)}, u32[]{:S(2)}, u32[]{:S(2)}) collective-permute-start(bf16[128,512]{1,0:T(8,128)(2,1)S(1)} %fusion.12.refs_8_), channel_id=1, source_target_pairs={{0,6},{2,0},{4,2},{6,4},{8,14},{10,8},{12,10},{14,12},{16,22},{18,... | collective-permute-start | bytes 393224 | tf_op jit(solution)/shard_map/ppermute | solution.py:270
  180.0 12.1 %collective-permute-start.25 = (bf16[128,512]{1,0:T(8,128)(2,1)S(1)}, bf16[128,512]{1,0:T(8,128)(2,1)S(1)}, u32[]{:S(2)}, u32[]{:S(2)}) collective-permute-start(bf16[128,512]{1,0:T(8,128)(2,1)S(1)} %fusion.12.refs_8_), channel_id=1, source_target_pairs={{0,2},{2,4},{4,6},{6,0},{8,10},{10,12},{12,14},{14,8},{16,18},{18,... | collective-permute-start | bytes 393224 | tf_op jit(solution)/shard_map/ppermute | solution.py:270
  193.1 31.9 %all-to-all-start.4 = ((bf16[32,16,512]{2,1,0:T(8,128)(2,1)}), bf16[32,16,512]{2,1,0:T(8,128)(2,1)S(1)}, u32[]{:S(2)}, u32[]{:S(2)}) async-start(bf16[32,16,512]{2,1,0:T(8,128)(2,1)} %broadcast_in_dim.23), calls=%async_computation.4 | async-start | bytes 1048576 | tf_op jit(solution)/shard_map/all_to_all | solution.py:239
  201.8 15.4 %collective-permute-start.26 = (bf16[128,512]{1,0:T(8,128)(2,1)S(1)}, bf16[128,512]{1,0:T(8,128)(2,1)S(1)}, u32[]{:S(2)}, u32[]{:S(2)}) collective-permute-start(bf16[128,512]{1,0:T(8,128)(2,1)S(1)} %fusion.12.refs_8_), channel_id=1, source_target_pairs={{0,5},{2,7},{4,1},{6,3},{8,13},{10,15},{12,9},{14,11},{16,21},{18,... | collective-permute-start | bytes 393224 | tf_op jit(solution)/shard_map/ppermute | solution.py:270
  203.1 14.1 %collective-permute-start.27 = (bf16[128,512]{1,0:T(8,128)(2,1)S(1)}, bf16[128,512]{1,0:T(8,128)(2,1)S(1)}, u32[]{:S(2)}, u32[]{:S(2)}) collective-permute-start(bf16[128,512]{1,0:T(8,128)(2,1)S(1)} %fusion.12.refs_8_), channel_id=1, source_target_pairs={{0,4},{2,6},{4,0},{6,2},{8,12},{10,14},{12,8},{14,10},{16,20},{18,... | collective-permute-start | bytes 393224 | tf_op jit(solution)/shard_map/ppermute | solution.py:270
  203.8 21.2 %collective-permute-start.28 = (bf16[128,512]{1,0:T(8,128)(2,1)S(1)}, bf16[128,512]{1,0:T(8,128)(2,1)S(1)}, u32[]{:S(2)}, u32[]{:S(2)}) collective-permute-start(bf16[128,512]{1,0:T(8,128)(2,1)S(1)} %fusion.12.refs_8_), channel_id=1, source_target_pairs={{0,3},{2,5},{4,7},{6,1},{8,11},{10,13},{12,15},{14,9},{16,19},{18,... | collective-permute-start | bytes 393224 | tf_op jit(solution)/shard_map/ppermute | solution.py:270
  (22 other events, 632.0 us)

commit v11 on v10

--- a/solution.py
+++ b/solution.py
@@ -267,7 +267,8 @@
     size = lax.axis_size("col")
     got = [mine]
     for t in range(1, size):
-        got.append(lax.ppermute(mine, "col", [(i, (i - t) % size) for i in column_holders()]))
+        pairs = [(i, (i - t) % size) for i in column_holders() if (i - t) % size]
+        got.append(lax.ppermute(mine, "col", pairs))
     return got
 
 
@@ -419,7 +420,7 @@
         piece, "row", split_axis=0, concat_axis=0, axis_index_groups=groups, tiled=True
     )
     under = from_holders(to_holders(lower_second))
-    near = [1, columns - 1, 2, columns - 2]
+    near = [columns // 2, columns // 2 - 1]
     got, *arrived = lax.optimization_barrier((got, *(under[t] for t in near)))
     for t, part in zip(near, arrived):
         under[t] = part

time: 232 us -> 231 us (level)
  no operation moved by 1% of the time
where the time goes in v11:
time: 231 us; the launch traced here: 228 us
  waiting for transfers between devices  92.2 us (40%)
  starting transfers between devices  56.7 us (25%)
  Pallas kernels  47.6 us (21%)
  blocking collectives  20.2 us (9%)
  local copies, waits for them, and re-layouts  4.08 us (2%)
  other arithmetic  3.48 us (2%)
  matrix products  2.94 us (1%)
    ppermute x14, waiting for transfers between devices, from_holders(): got.append(lax.ppermute(mine, 'col', pairs))  60.8 us
    pallas_call x1, Pallas kernels, inverse_factor(): pl.pallas_call(inverse_kernel, out_shape=jax.ShapeDtypeStruct((n, n), F32...  32.2 us
    all_to_all x3, starting transfers between devices, swap(): return lax.all_to_all(block, axis, split_axis=0, concat_axis=0, tiled=True)  24.3 us
    all_to_all x1, blocking collectives, swap(): return lax.all_to_all(block, axis, split_axis=0, concat_axis=0, tiled=True)  20.2 us
    ppermute x8, waiting for transfers between devices, to_plane(): got = lax.ppermute(quarters[:, k], ('row', 'col'), pairs)  15.9 us
    ppermute x14, starting transfers between devices, from_holders(): got.append(lax.ppermute(mine, 'col', pairs))  14.5 us
    all_to_all x3, waiting for transfers between devices, swap(): return lax.all_to_all(block, axis, split_axis=0, concat_axis=0, tiled=True)  14.5 us
    ppermute x8, starting transfers between devices, to_plane(): got = lax.ppermute(quarters[:, k], ('row', 'col'), pairs)  8.58 us
  transfers between devices with their start and end apart: 33, of which 12 were waited for; matrix products, arithmetic and copies ran while one was open for 2% of the time, Pallas kernels for 16%

profile of v11, /device:TPU:66, one launch (start us, length us, event | category | flops | bytes accessed | tf_op | source)
XLA Modules:
  0.0 228.1 jit_solution(5511235862933485892)
XLA Ops:
  0.0 1.8 pack.1
  1.8 10.2 %all-to-all-start = ((bf16[32,40,128]{2,1,0:T(8,128)(2,1)}), bf16[32,40,128]{2,1,0:T(8,128)(2,1)S(1)}, u32[]{:S(2)}, u32[]{:S(2)}) async-start(bf16[32,40,128]{2,1,0:T(8,128)(2,1)} %bitcast.65), calls=%async_computation | async-start | bytes 655360 | tf_op jit(solution)/shard_map/all_to_all | solution.py:239
  12.1 4.7 %place.1 = (bf16[128,128,128]{2,1,0:T(8,128)(2,1)}, s32[128]{0:T(128)}) custom-call(s32[64]{0:T(128)} %bitcast.67, s32[64]{0:T(128)} %slots.1, bf16[64,128,128]{2,1,0:T(8,128)(2,1)} %children.1), custom_call_target="tpu_custom_call" | custom-call | tf_op jit(solution)/shard_map/place/pallas_call | solution.py:50
  17.8 1.9 collective-permute-start
  20.9 3.8 %all-to-all-done = bf16[32,40,128]{2,1,0:T(8,128)(2,1)S(1)} async-done(((bf16[32,40,128]{2,1,0:T(8,128)(2,1)}), bf16[32,40,128]{2,1,0:T(8,128)(2,1)S(1)}, u32[]{:S(2)}, u32[]{:S(2)}) %all-to-all-start) | async-done | bytes 327712 | tf_op jit(solution)/shard_map/all_to_all | solution.py:239
  25.0 20.2 %all_to_all.25 = bf16[32,48,128]{2,1,0:T(8,128)(2,1)S(1)} all-to-all(bf16[32,48,128]{2,1,0:T(8,128)(2,1)S(1)} %copy.56), channel_id=1, replica_groups=mesh['front'=2,'row'=32,'col'=8] {'row'}, dimensions={0} | all-to-all | bytes 786432 | tf_op jit(solution)/shard_map/all_to_all | solution.py:239
  45.6 6.7 %all-to-all-start.2 = ((bf16[128,128,128]{2,1,0:T(8,128)(2,1)}), bf16[128,128,128]{2,1,0:T(8,128)(2,1)}, u32[]{:S(2)}, u32[]{:S(2)}) async-start(bf16[128,128,128]{2,1,0:T(8,128)(2,1)} %get-tuple-element.25), calls=%async_computation.2 | async-start | bytes 8388608 | tf_op jit(solution)/shard_map/all_to_all | solution.py:239
  52.3 32.2 %inverse.1 = f32[512,512]{1,0:T(8,128)S(1)} custom-call(bf16[1280,128]{1,0:T(8,128)(2,1)S(1)} %bitcast.58), custom_call_target="tpu_custom_call" | custom-call | flops 536870912 | bytes 1572864 | tf_op jit(solution)/shard_map/inverse/pallas_call | solution.py:209
  88.4 1.3 collective-permute-start.4
  89.7 1.3 collective-permute-start.3
  91.0 1.3 collective-permute-start.1
  92.3 1.3 collective-permute-start.2
  93.7 1.3 collective-permute-start.8
  95.7 1.3 collective-permute-start.10
  97.7 1.3 collective-permute-start.12
  99.0 11.7 %collective-permute-done.8.refs_1_ = bf16[128,512]{1,0:T(8,128)(2,1)S(1)} collective-permute-done((bf16[128,512]{1,0:T(8,128)(2,1)S(1)}, bf16[128,512]{1,0:T(8,128)(2,1)S(1)}, u32[]{:S(2)}, u32[]{:S(2)}) %collective-permute-start.8) | collective-permute-done | bytes 131104 | tf_op jit(solution)/shard_map/ppermute | solution.py:271
  112.1 1.5 collective-permute-start.14
  114.7 6.3 %collective-permute-done.10.refs_3_ = bf16[128,512]{1,0:T(8,128)(2,1)S(1)} collective-permute-done((bf16[128,512]{1,0:T(8,128)(2,1)S(1)}, bf16[128,512]{1,0:T(8,128)(2,1)S(1)}, u32[]{:S(2)}, u32[]{:S(2)}) %collective-permute-start.10) | collective-permute-done | bytes 131104 | tf_op jit(solution)/shard_map/ppermute | solution.py:271
  121.0 9.7 %collective-permute-done.12.refs_5_ = bf16[128,512]{1,0:T(8,128)(2,1)S(1)} collective-permute-done((bf16[128,512]{1,0:T(8,128)(2,1)S(1)}, bf16[128,512]{1,0:T(8,128)(2,1)S(1)}, u32[]{:S(2)}, u32[]{:S(2)}) %collective-permute-start.12) | collective-permute-done | bytes 131104 | tf_op jit(solution)/shard_map/ppermute | solution.py:271
  130.7 3.9 %collective-permute-done.14.refs_7_ = bf16[128,512]{1,0:T(8,128)(2,1)} collective-permute-done((bf16[128,512]{1,0:T(8,128)(2,1)S(1)}, bf16[128,512]{1,0:T(8,128)(2,1)}, u32[]{:S(2)}, u32[]{:S(2)}) %collective-permute-start.14) | collective-permute-done | bytes 131104 | tf_op jit(solution)/shard_map/ppermute | solution.py:271
  134.6 10.7 %all-to-all-done.2.incoming = bf16[128,128,128]{2,1,0:T(8,128)(2,1)} async-done(((bf16[128,128,128]{2,1,0:T(8,128)(2,1)}), bf16[128,128,128]{2,1,0:T(8,128)(2,1)}, u32[]{:S(2)}, u32[]{:S(2)}) %all-to-all-start.2) | async-done | bytes 4194336 | tf_op jit(solution)/shard_map/all_to_all | solution.py:239
  145.3 3.9 %assemble.1.refs_20_ = f32[512,512]{1,0:T(8,128)S(1)} custom-call(s32[128]{0:T(128)S(1)} %reshape.149.tags, bf16[128,128,128]{2,1,0:T(8,128)(2,1)} %all-to-all-done.2.incoming, bf16[1,1024,512]{2,1,0:T(8,128)(2,1)S(1)} %copy-done), custom_call_target="tpu_custom_call" | custom-call | tf_op jit(solution)/shard_map/assemble/pallas_call | solution.py:101
  149.3 1.9 convolution_convert_fusion.1.refs_17_
  156.7 15.9 %collective-permute-done.21 = bf16[8,16,512]{2,1,0:T(8,128)(2,1)S(1)} collective-permute-done((bf16[8,16,512]{2,1,0:T(8,128)(2,1)S(1)}, bf16[8,16,512]{2,1,0:T(8,128)(2,1)S(1)}, u32[]{:S(2)}, u32[]{:S(2)}) %collective-permute-start.21) | collective-permute-done | bytes 131104 | tf_op jit(solution)/shard_map/ppermute | solution.py:406
  173.2 3.4 %all-to-all-start.3 = ((bf16[8,16,512]{2,1,0:T(8,128)(2,1)}), bf16[8,16,512]{2,1,0:T(8,128)(2,1)S(1)}, u32[]{:S(2)}, u32[]{:S(2)}) async-start(bf16[8,16,512]{2,1,0:T(8,128)(2,1)} %add_select_fusion), calls=%async_computation.3 | async-start | bytes 262144 | tf_op jit(solution)/shard_map/all_to_all | solution.py:419
  177.3 1.3 collective-permute-start.25
  178.7 9.9 %collective-permute-done.25.refs_11_ = bf16[128,512]{1,0:T(8,128)(2,1)S(1)} collective-permute-done((bf16[128,512]{1,0:T(8,128)(2,1)S(1)}, bf16[128,512]{1,0:T(8,128)(2,1)S(1)}, u32[]{:S(2)}, u32[]{:S(2)}) %collective-permute-start.25) | collective-permute-done | bytes 131104 | tf_op jit(solution)/shard_map/ppermute | solution.py:271
  189.4 7.4 %all-to-all-start.4 = ((bf16[32,16,512]{2,1,0:T(8,128)(2,1)}), bf16[32,16,512]{2,1,0:T(8,128)(2,1)S(1)}, u32[]{:S(2)}, u32[]{:S(2)}) async-start(bf16[32,16,512]{2,1,0:T(8,128)(2,1)} %broadcast_in_dim.23), calls=%async_computation.4 | async-start | bytes 1048576 | tf_op jit(solution)/shard_map/all_to_all | solution.py:239
  202.7 3.2 %collective-permute-done.18.refs_9_ = bf16[128,512]{1,0:T(8,128)(2,1)S(1)} collective-permute-done((bf16[128,512]{1,0:T(8,128)(2,1)S(1)}, bf16[128,512]{1,0:T(8,128)(2,1)S(1)}, u32[]{:S(2)}, u32[]{:S(2)}) %collective-permute-start.18) | collective-permute-done | bytes 131104 | tf_op jit(solution)/shard_map/ppermute | solution.py:271
  205.9 12.5 %collective-permute-done.26.refs_13_ = bf16[128,512]{1,0:T(8,128)(2,1)S(1)} collective-permute-done((bf16[128,512]{1,0:T(8,128)(2,1)S(1)}, bf16[128,512]{1,0:T(8,128)(2,1)S(1)}, u32[]{:S(2)}, u32[]{:S(2)}) %collective-permute-start.26) | collective-permute-done | bytes 131104 | tf_op jit(solution)/shard_map/ppermute | solution.py:271
  218.4 3.7 %collective-permute-done.28.refs_15_ = bf16[128,512]{1,0:T(8,128)(2,1)S(1)} collective-permute-done((bf16[128,512]{1,0:T(8,128)(2,1)S(1)}, bf16[128,512]{1,0:T(8,128)(2,1)S(1)}, u32[]{:S(2)}, u32[]{:S(2)}) %collective-permute-start.28) | collective-permute-done | bytes 131104 | tf_op jit(solution)/shard_map/ppermute | solution.py:271
  222.9 5.0 %finish.1 = bf16[1,1024,512]{2,1,0:T(8,128)(2,1)} custom-call(s32[3]{0:T(128)} %pad_add_fusion.1.state, bf16[128,512]{1,0:T(8,128)(2,1)} %copy-done.5, bf16[128,512]{1,0:T(8,128)(2,1)} %copy-done.7, bf16[128,512]{1,0:T(8,128)(2,1)} %copy-done.8, bf16[128,512]{1,0:T(8,128)(2,1)} %copy-done.9, bf16[128,512]{1,0:T(8,128)(2,1)} %copy-done.10, ...), custom_call_target="tpu_custom_call" | custom-call | tf_op jit(solution)/shard_map/finish/pallas_call | solution.py:346
  (114 shorter events, 24.9 us)
Async XLA Ops:
  1.8 22.9 %all-to-all-start = ((bf16[32,40,128]{2,1,0:T(8,128)(2,1)}), bf16[32,40,128]{2,1,0:T(8,128)(2,1)S(1)}, u32[]{:S(2)}, u32[]{:S(2)}) async-start(bf16[32,40,128]{2,1,0:T(8,128)(2,1)} %bitcast.65), calls=%async_computation | async-start | bytes 655360 | tf_op jit(solution)/shard_map/all_to_all | solution.py:239
  17.8 3.0 %collective-permute-start = (s32[32,2]{0,1:T(2,128)S(1)}, s32[32,2]{0,1:T(2,128)S(1)}, u32[]{:S(2)}, u32[]{:S(2)}) collective-permute-start(s32[32,2]{0,1:T(2,128)S(1)} %copy.54), channel_id=1, source_target_pairs={{0,256},{256,0},{1,257},{257,1},{2,258},{258,2},{3,259},{259,3},{4... | collective-permute-start | bytes 776 | tf_op jit(solution)/shard_map/ppermute | solution.py:380
  45.6 99.8 %all-to-all-start.2 = ((bf16[128,128,128]{2,1,0:T(8,128)(2,1)}), bf16[128,128,128]{2,1,0:T(8,128)(2,1)}, u32[]{:S(2)}, u32[]{:S(2)}) async-start(bf16[128,128,128]{2,1,0:T(8,128)(2,1)} %get-tuple-element.25), calls=%async_computation.2 | async-start | bytes 8388608 | tf_op jit(solution)/shard_map/all_to_all | solution.py:239
  85.6 5.4 %collective-permute-start.7 = (bf16[128,512]{1,0:T(8,128)(2,1)S(1)}, bf16[128,512]{1,0:T(8,128)(2,1)S(1)}, u32[]{:S(2)}, u32[]{:S(2)}) collective-permute-start(bf16[128,512]{1,0:T(8,128)(2,1)S(1)} %get-tuple-element.49), channel_id=1, source_target_pairs={{0,6},{8,14},{16,22},{24,30},{32,38},{40,46},{48,54},{56,62},{64,7... | collective-permute-start | bytes 393224 | tf_op jit(solution)/shard_map/ppermute | solution.py:252
  86.3 6.0 %collective-permute-start.6 = (bf16[128,512]{1,0:T(8,128)(2,1)S(1)}, bf16[128,512]{1,0:T(8,128)(2,1)S(1)}, u32[]{:S(2)}, u32[]{:S(2)}) collective-permute-start(bf16[128,512]{1,0:T(8,128)(2,1)S(1)} %get-tuple-element.50), channel_id=1, source_target_pairs={{0,4},{8,12},{16,20},{24,28},{32,36},{40,44},{48,52},{56,60},{64,6... | collective-permute-start | bytes 393224 | tf_op jit(solution)/shard_map/ppermute | solution.py:252
  87.0 6.7 %collective-permute-start.5 = (bf16[128,512]{1,0:T(8,128)(2,1)S(1)}, bf16[128,512]{1,0:T(8,128)(2,1)S(1)}, u32[]{:S(2)}, u32[]{:S(2)}) collective-permute-start(bf16[128,512]{1,0:T(8,128)(2,1)S(1)} %get-tuple-element.48), channel_id=1, source_target_pairs={{0,2},{8,10},{16,18},{24,26},{32,34},{40,42},{48,50},{56,58},{64,6... | collective-permute-start | bytes 393224 | tf_op jit(solution)/shard_map/ppermute | solution.py:252
  88.4 6.6 %collective-permute-start.4 = (bf16[8,16,512]{2,1,0:T(8,128)(2,1)S(1)}, bf16[8,16,512]{2,1,0:T(8,128)(2,1)}, u32[]{:S(2)}, u32[]{:S(2)}) collective-permute-start(bf16[8,16,512]{2,1,0:T(8,128)(2,1)S(1)} %get-tuple-element.54), channel_id=1, source_target_pairs={{8,26},{16,28},{24,30},{264,282},{272,284},{280,286}} | collective-permute-start | bytes 393224 | tf_op jit(solution)/shard_map/ppermute | solution.py:406
  89.7 6.0 %collective-permute-start.3 = (bf16[8,16,512]{2,1,0:T(8,128)(2,1)}, bf16[8,16,512]{2,1,0:T(8,128)(2,1)}, u32[]{:S(2)}, u32[]{:S(2)}) collective-permute-start(bf16[8,16,512]{2,1,0:T(8,128)(2,1)} %get-tuple-element.52), channel_id=1, source_target_pairs={{8,18},{16,20},{24,22},{264,274},{272,276},{280,278}} | collective-permute-start | bytes 393224 | tf_op jit(solution)/shard_map/ppermute | solution.py:406
  91.0 6.0 %collective-permute-start.1 = (bf16[8,16,512]{2,1,0:T(8,128)(2,1)}, bf16[8,16,512]{2,1,0:T(8,128)(2,1)}, u32[]{:S(2)}, u32[]{:S(2)}) collective-permute-start(bf16[8,16,512]{2,1,0:T(8,128)(2,1)} %get-tuple-element.53), channel_id=1, source_target_pairs={{8,2},{16,4},{24,6},{264,258},{272,260},{280,262}} | collective-permute-start | bytes 393224 | tf_op jit(solution)/shard_map/ppermute | solution.py:406
  92.3 5.4 %collective-permute-start.2 = (bf16[8,16,512]{2,1,0:T(8,128)(2,1)S(1)}, bf16[8,16,512]{2,1,0:T(8,128)(2,1)}, u32[]{:S(2)}, u32[]{:S(2)}) collective-permute-start(bf16[8,16,512]{2,1,0:T(8,128)(2,1)S(1)} %get-tuple-element.51), channel_id=1, source_target_pairs={{8,10},{16,12},{24,14},{264,266},{272,268},{280,270}} | collective-permute-start | bytes 393224 | tf_op jit(solution)/shard_map/ppermute | solution.py:406
  93.7 17.0 %collective-permute-start.8 = (bf16[128,512]{1,0:T(8,128)(2,1)S(1)}, bf16[128,512]{1,0:T(8,128)(2,1)S(1)}, u32[]{:S(2)}, u32[]{:S(2)}) collective-permute-start(bf16[128,512]{1,0:T(8,128)(2,1)S(1)} %fusion.15.refs_0_), channel_id=1, source_target_pairs={{0,7},{2,1},{4,3},{6,5},{8,15},{10,9},{12,11},{14,13},{16,23},{18,... | collective-permute-start | bytes 393224 | tf_op jit(solution)/shard_map/ppermute | solution.py:271
  95.0 16.4 %collective-permute-start.9 = (bf16[128,512]{1,0:T(8,128)(2,1)S(1)}, bf16[128,512]{1,0:T(8,128)(2,1)S(1)}, u32[]{:S(2)}, u32[]{:S(2)}) collective-permute-start(bf16[128,512]{1,0:T(8,128)(2,1)S(1)} %fusion.15.refs_0_), channel_id=1, source_target_pairs={{0,6},{4,2},{6,4},{8,14},{12,10},{14,12},{16,22},{20,18},{22,20},{... | collective-permute-start | bytes 393224 | tf_op jit(solution)/shard_map/ppermute | solution.py:271
  95.7 25.2 %collective-permute-start.10 = (bf16[128,512]{1,0:T(8,128)(2,1)S(1)}, bf16[128,512]{1,0:T(8,128)(2,1)S(1)}, u32[]{:S(2)}, u32[]{:S(2)}) collective-permute-start(bf16[128,512]{1,0:T(8,128)(2,1)S(1)} %fusion.15.refs_0_), channel_id=1, source_target_pairs={{0,5},{2,7},{4,1},{6,3},{8,13},{10,15},{12,9},{14,11},{16,21},{18,... | collective-permute-start | bytes 393224 | tf_op jit(solution)/shard_map/ppermute | solution.py:271
  97.0 23.9 %collective-permute-start.11 = (bf16[128,512]{1,0:T(8,128)(2,1)S(1)}, bf16[128,512]{1,0:T(8,128)(2,1)S(1)}, u32[]{:S(2)}, u32[]{:S(2)}) collective-permute-start(bf16[128,512]{1,0:T(8,128)(2,1)S(1)} %fusion.15.refs_0_), channel_id=1, source_target_pairs={{0,4},{2,6},{6,2},{8,12},{10,14},{14,10},{16,20},{18,22},{22,18},{... | collective-permute-start | bytes 393224 | tf_op jit(solution)/shard_map/ppermute | solution.py:271
  97.7 33.0 %collective-permute-start.12 = (bf16[128,512]{1,0:T(8,128)(2,1)S(1)}, bf16[128,512]{1,0:T(8,128)(2,1)S(1)}, u32[]{:S(2)}, u32[]{:S(2)}) collective-permute-start(bf16[128,512]{1,0:T(8,128)(2,1)S(1)} %fusion.15.refs_0_), channel_id=1, source_target_pairs={{0,3},{2,5},{4,7},{6,1},{8,11},{10,13},{12,15},{14,9},{16,19},{18,... | collective-permute-start | bytes 393224 | tf_op jit(solution)/shard_map/ppermute | solution.py:271
  110.8 19.9 %collective-permute-start.13 = (bf16[128,512]{1,0:T(8,128)(2,1)S(1)}, bf16[128,512]{1,0:T(8,128)(2,1)S(1)}, u32[]{:S(2)}, u32[]{:S(2)}) collective-permute-start(bf16[128,512]{1,0:T(8,128)(2,1)S(1)} %fusion.15.refs_0_), channel_id=1, source_target_pairs={{0,2},{2,4},{4,6},{8,10},{10,12},{12,14},{16,18},{18,20},{20,22},{... | collective-permute-start | bytes 393224 | tf_op jit(solution)/shard_map/ppermute | solution.py:271
  112.1 22.5 %collective-permute-start.14 = (bf16[128,512]{1,0:T(8,128)(2,1)S(1)}, bf16[128,512]{1,0:T(8,128)(2,1)}, u32[]{:S(2)}, u32[]{:S(2)}) collective-permute-start(bf16[128,512]{1,0:T(8,128)(2,1)S(1)} %fusion.15.refs_0_), channel_id=1, source_target_pairs={{0,1},{2,3},{4,5},{6,7},{8,9},{10,11},{12,13},{14,15},{16,17},{18,... | collective-permute-start | bytes 393224 | tf_op jit(solution)/shard_map/ppermute | solution.py:271
  151.2 4.0 %collective-permute-start.23 = (bf16[8,16,512]{2,1,0:T(8,128)(2,1)S(1)}, bf16[8,16,512]{2,1,0:T(8,128)(2,1)S(1)}, u32[]{:S(2)}, u32[]{:S(2)}) collective-permute-start(bf16[8,16,512]{2,1,0:T(8,128)(2,1)S(1)} %get-tuple-element.43), channel_id=1, source_target_pairs={{0,25},{8,27},{16,29},{24,31},{256,281},{264,283},{272,285},{280,2... | collective-permute-start | bytes 393224 | tf_op jit(solution)/shard_map/ppermute | solution.py:406
  151.9 4.1 %collective-permute-start.22 = (bf16[8,16,512]{2,1,0:T(8,128)(2,1)S(1)}, bf16[8,16,512]{2,1,0:T(8,128)(2,1)S(1)}, u32[]{:S(2)}, u32[]{:S(2)}) collective-permute-start(bf16[8,16,512]{2,1,0:T(8,128)(2,1)S(1)} %get-tuple-element.44), channel_id=1, source_target_pairs={{0,17},{8,19},{16,21},{24,23},{256,273},{264,275},{272,277},{280,2... | collective-permute-start | bytes 393224 | tf_op jit(solution)/shard_map/ppermute | solution.py:406
  152.6 4.1 %collective-permute-start.20 = (bf16[8,16,512]{2,1,0:T(8,128)(2,1)S(1)}, bf16[8,16,512]{2,1,0:T(8,128)(2,1)S(1)}, u32[]{:S(2)}, u32[]{:S(2)}) collective-permute-start(bf16[8,16,512]{2,1,0:T(8,128)(2,1)S(1)} %get-tuple-element.42), channel_id=1, source_target_pairs={{0,1},{8,3},{16,5},{24,7},{256,257},{264,259},{272,261},{280,263}} | collective-permute-start | bytes 393224 | tf_op jit(solution)/shard_map/ppermute | solution.py:406
  153.3 19.3 %collective-permute-start.21 = (bf16[8,16,512]{2,1,0:T(8,128)(2,1)S(1)}, bf16[8,16,512]{2,1,0:T(8,128)(2,1)S(1)}, u32[]{:S(2)}, u32[]{:S(2)}) collective-permute-start(bf16[8,16,512]{2,1,0:T(8,128)(2,1)S(1)} %get-tuple-element.41), channel_id=1, source_target_pairs={{0,9},{8,11},{16,13},{24,15},{256,265},{264,267},{272,269},{280,271}} | collective-permute-start | bytes 393224 | tf_op jit(solution)/shard_map/ppermute | solution.py:406
  154.6 22.0 %collective-permute-start.17 = (bf16[128,512]{1,0:T(8,128)(2,1)S(1)}, bf16[128,512]{1,0:T(8,128)(2,1)S(1)}, u32[]{:S(2)}, u32[]{:S(2)}) collective-permute-start(bf16[128,512]{1,0:T(8,128)(2,1)S(1)} %get-tuple-element.46), channel_id=1, source_target_pairs={{0,6},{8,14},{16,22},{24,30},{32,38},{40,46},{48,54},{56,62},{64,7... | collective-permute-start | bytes 393224 | tf_op jit(solution)/shard_map/ppermute | solution.py:252
  155.3 21.3 %collective-permute-start.16 = (bf16[128,512]{1,0:T(8,128)(2,1)S(1)}, bf16[128,512]{1,0:T(8,128)(2,1)S(1)}, u32[]{:S(2)}, u32[]{:S(2)}) collective-permute-start(bf16[128,512]{1,0:T(8,128)(2,1)S(1)} %get-tuple-element.47), channel_id=1, source_target_pairs={{0,4},{8,12},{16,20},{24,28},{32,36},{40,44},{48,52},{56,60},{64,6... | collective-permute-start | bytes 393224 | tf_op jit(solution)/shard_map/ppermute | solution.py:252
  156.0 20.6 %collective-permute-start.15 = (bf16[128,512]{1,0:T(8,128)(2,1)S(1)}, bf16[128,512]{1,0:T(8,128)(2,1)S(1)}, u32[]{:S(2)}, u32[]{:S(2)}) collective-permute-start(bf16[128,512]{1,0:T(8,128)(2,1)S(1)} %get-tuple-element.45), channel_id=1, source_target_pairs={{0,2},{8,10},{16,18},{24,26},{32,34},{40,42},{48,50},{56,58},{64,6... | collective-permute-start | bytes 393224 | tf_op jit(solution)/shard_map/ppermute | solution.py:252
  173.2 15.4 %all-to-all-start.3 = ((bf16[8,16,512]{2,1,0:T(8,128)(2,1)}), bf16[8,16,512]{2,1,0:T(8,128)(2,1)S(1)}, u32[]{:S(2)}, u32[]{:S(2)}) async-start(bf16[8,16,512]{2,1,0:T(8,128)(2,1)} %add_select_fusion), calls=%async_computation.3 | async-start | bytes 262144 | tf_op jit(solution)/shard_map/all_to_all | solution.py:419
  177.3 11.2 %collective-permute-start.25 = (bf16[128,512]{1,0:T(8,128)(2,1)S(1)}, bf16[128,512]{1,0:T(8,128)(2,1)S(1)}, u32[]{:S(2)}, u32[]{:S(2)}) collective-permute-start(bf16[128,512]{1,0:T(8,128)(2,1)S(1)} %fusion.12.refs_8_), channel_id=1, source_target_pairs={{0,5},{2,7},{4,1},{6,3},{8,13},{10,15},{12,9},{14,11},{16,21},{18,... | collective-permute-start | bytes 393224 | tf_op jit(solution)/shard_map/ppermute | solution.py:271
  189.4 32.7 %all-to-all-start.4 = ((bf16[32,16,512]{2,1,0:T(8,128)(2,1)}), bf16[32,16,512]{2,1,0:T(8,128)(2,1)S(1)}, u32[]{:S(2)}, u32[]{:S(2)}) async-start(bf16[32,16,512]{2,1,0:T(8,128)(2,1)} %broadcast_in_dim.23), calls=%async_computation.4 | async-start | bytes 1048576 | tf_op jit(solution)/shard_map/all_to_all | solution.py:239
  196.8 9.0 %collective-permute-start.18 = (bf16[128,512]{1,0:T(8,128)(2,1)S(1)}, bf16[128,512]{1,0:T(8,128)(2,1)S(1)}, u32[]{:S(2)}, u32[]{:S(2)}) collective-permute-start(bf16[128,512]{1,0:T(8,128)(2,1)S(1)} %fusion.12.refs_8_), channel_id=1, source_target_pairs={{0,7},{2,1},{4,3},{6,5},{8,15},{10,9},{12,11},{14,13},{16,23},{18,... | collective-permute-start | bytes 393224 | tf_op jit(solution)/shard_map/ppermute | solution.py:271
  198.1 7.8 %collective-permute-start.19 = (bf16[128,512]{1,0:T(8,128)(2,1)S(1)}, bf16[128,512]{1,0:T(8,128)(2,1)S(1)}, u32[]{:S(2)}, u32[]{:S(2)}) collective-permute-start(bf16[128,512]{1,0:T(8,128)(2,1)S(1)} %fusion.12.refs_8_), channel_id=1, source_target_pairs={{0,6},{4,2},{6,4},{8,14},{12,10},{14,12},{16,22},{20,18},{22,20},{... | collective-permute-start | bytes 393224 | tf_op jit(solution)/shard_map/ppermute | solution.py:271
  198.8 19.6 %collective-permute-start.26 = (bf16[128,512]{1,0:T(8,128)(2,1)S(1)}, bf16[128,512]{1,0:T(8,128)(2,1)S(1)}, u32[]{:S(2)}, u32[]{:S(2)}) collective-permute-start(bf16[128,512]{1,0:T(8,128)(2,1)S(1)} %fusion.12.refs_8_), channel_id=1, source_target_pairs={{0,3},{2,5},{4,7},{6,1},{8,11},{10,13},{12,15},{14,9},{16,19},{18,... | collective-permute-start | bytes 393224 | tf_op jit(solution)/shard_map/ppermute | solution.py:271
  200.1 18.3 %collective-permute-start.27 = (bf16[128,512]{1,0:T(8,128)(2,1)S(1)}, bf16[128,512]{1,0:T(8,128)(2,1)S(1)}, u32[]{:S(2)}, u32[]{:S(2)}) collective-permute-start(bf16[128,512]{1,0:T(8,128)(2,1)S(1)} %fusion.12.refs_8_), channel_id=1, source_target_pairs={{0,2},{2,4},{4,6},{8,10},{10,12},{12,14},{16,18},{18,20},{20,22},{... | collective-permute-start | bytes 393224 | tf_op jit(solution)/shard_map/ppermute | solution.py:271
  200.8 21.3 %collective-permute-start.28 = (bf16[128,512]{1,0:T(8,128)(2,1)S(1)}, bf16[128,512]{1,0:T(8,128)(2,1)S(1)}, u32[]{:S(2)}, u32[]{:S(2)}) collective-permute-start(bf16[128,512]{1,0:T(8,128)(2,1)S(1)} %fusion.12.refs_8_), channel_id=1, source_target_pairs={{0,1},{2,3},{4,5},{6,7},{8,9},{10,11},{12,13},{14,15},{16,17},{18,... | collective-permute-start | bytes 393224 | tf_op jit(solution)/shard_map/ppermute | solution.py:271
  (22 other events, 584.0 us)
